TPU v7x, 32 devices: a whole 2x2x4 slice. The times are simulated.
32 devices in a mesh: dp: 8 (over z, x), tensor: 4 (over y, core).
Axes of the slice: x: 2, y: 2, z: 4, core: 2. Of those that a mesh axis runs over, the one named last changes fastest.
Arguments:
- inputs: bfloat16 [16, 1024, 768], P('dp'), may hold values from -6 to 6
- cotangent: bfloat16 [16, 1024, 768], P('dp', 'tensor'), may hold values from -6 to 6
- lengths: int32 [16], P('dp'), may hold values from 512 to 1024, as said below
- qkv_weight: bfloat16 [768, 3, 768], P(None, None, 'tensor'), may hold values from -0.21875 to 0.21875
- qkv_bias: bfloat16 [2, 768], P(None, 'tensor'), may hold values from -0.29882812 to 0.29882812
- out_weight: bfloat16 [768, 768], P('tensor'), may hold values from -4 to 4
- out_bias: bfloat16 [768], replicated, may hold values from -0.59765625 to 0.59765625
- first_gain: bfloat16 [768], replicated, may hold values from 0.5 to 1.5
- first_shift: bfloat16 [768], replicated, may hold values from -0.59765625 to 0.59765625
- up_weight: bfloat16 [768, 3072], P(None, 'tensor'), may hold values from -0.21875 to 0.21875
- up_bias: bfloat16 [3072], P('tensor'), may hold values from -0.59765625 to 0.59765625
- down_weight: bfloat16 [3072, 768], P('tensor'), may hold values from -0.109375 to 0.109375
- down_bias: bfloat16 [768], replicated, may hold values from -0.59765625 to 0.59765625
- second_gain: bfloat16 [768], replicated, may hold values from 0.5 to 1.5
- second_shift: bfloat16 [768], replicated, may hold values from -0.59765625 to 0.59765625
Outputs:
- outputs: bfloat16 [16, 1024, 768], P('dp', 'tensor')
- input_grad: bfloat16 [16, 1024, 768], P('dp', 'tensor')
- qkv_weight_grad: float32 [768, 3, 768], P('dp', None, 'tensor')
- qkv_bias_grad: float32 [2, 768], P(None, 'tensor')
- out_weight_grad: float32 [768, 768], P(('tensor', 'dp'))
- out_bias_grad: float32 [768], replicated
- first_gain_grad: float32 [768], replicated
- first_shift_grad: float32 [768], replicated
- up_weight_grad: float32 [768, 3072], P('dp', 'tensor')
- up_bias_grad: float32 [3072], P('tensor')
- down_weight_grad: float32 [3072, 768], P(('tensor', 'dp'))
- down_bias_grad: float32 [768], replicated
- second_gain_grad: float32 [768], replicated
- second_shift_grad: float32 [768], replicated
Inputs may be any that keep to these rules, and one draw needn't show every extreme that they name: `lengths`: each sequence has at least half of 1024 valid slots; in every draw some sequence has all 1024 slots valid and some has exactly half of 1024.
All inputs are finite; a program needn't handle non-finite values.
Results may differ from a plain program's by a relative error of at most 0.018.
Values may be sent and summed in bfloat16 or wider, within the bound.
No kernel may reach another device: no remote copies, remote signals or barrier semaphores. Data moves between devices by JAX's collectives and lax.ppermute only.
A program may use at most 192 MiB of HBM per device.

v0:
```python
import functools

import jax
import jax.numpy as jnp
from jax import lax
from jax.experimental import pallas as pl
from jax.experimental.pallas import tpu as pltpu
from jax.sharding import PartitionSpec as P

HEAD = 64
WIDE, LANES = 192, 256
NEAR = 30
NT = (((1,), (1,)), ((), ()))
NN = (((1,), (0,)), ((), ()))
TN = (((0,), (0,)), ((), ()))
bf16 = jnp.bfloat16
f32 = jnp.float32
VM = pl.BlockSpec(memory_space=pltpu.VMEM)
SDS = jax.ShapeDtypeStruct


def mm(a, b, dims=NN):
    return lax.dot_general(a, b, dims, preferred_element_type=f32)


class Fetch:
    def __init__(self, src, dst, sem):
        self.dst, self.copy = dst, pltpu.make_async_copy(src, dst, sem)
        self.copy.start()
        self.waiting = True

    def __call__(self):
        if self.waiting:
            self.copy.wait()
            self.waiting = False
        return self.dst


class Flush:
    def __init__(self, src, dst, sem):
        self.src, self.copy = src, pltpu.make_async_copy(src, dst, sem)
        self.started = False

    def start(self):
        if not self.started:
            self.copy.start()
        self.started = True


def call(name, body, info, ins, outs, scratch=(), vmem=58, which=0, **static):
    far_in = [i for i, a in enumerate(ins) if isinstance(a, tuple)]
    pinned = [i for i in far_in if len(ins[i]) == 2]
    far_out = [i for i, o in enumerate(outs) if isinstance(o, list)]
    raw_in = [i for i, a in enumerate(ins) if isinstance(a, Raw)]
    raw_out = [i for i, o in enumerate(outs) if isinstance(o, Raw)]
    pinned += raw_in
    arrays = [a[0] if isinstance(a, tuple) else a.value if isinstance(a, Raw) else a for a in ins]
    shapes = [o[0] if isinstance(o, list) else o.value if isinstance(o, Raw) else o for o in outs]
    picked = [a[1] if isinstance(a, tuple) else None for a in ins]
    n_in, n_out = len(ins), len(outs)

    def kernel(lengths_ref, which_ref, *refs):
        dp = lax.axis_index("dp")
        at = which_ref[0]
        info_ref = (lengths_ref[0], lengths_ref[1], lax.axis_index("tensor"), dp & 1, (dp >> 1) & 1, at, lengths_ref[at], lengths_ref)
        in_refs, refs = refs[:n_in], refs[n_in:]
        out_refs, refs = refs[:n_out], refs[n_out:]
        sem, refs = refs[-1], refs[:-1]
        buffers, rest = refs[: len(far_in) + len(far_out)], refs[len(far_in) + len(far_out) :]
        args = list(in_refs)
        for j, i in enumerate(far_in):
            view = picked[i][1]
            args[i] = Fetch(view(in_refs[i], info_ref), buffers[j], sem.at[j])
        results = list(out_refs)
        flushes = []
        for j, i in enumerate(far_out):
            at = len(far_in) + j
            results[i] = Flush(buffers[at], out_refs[i], sem.at[at])
            flushes.append(results[i])
        body(info_ref, *args, *results, *rest, **static)
        for i in far_in:
            args[i]()
        for f in flushes:
            f.start()
        for f in flushes:
            f.copy.wait()

    hbm = pl.BlockSpec(memory_space=pltpu.HBM)
    buffers = [pltpu.VMEM(picked[i][0], arrays[i].dtype) for i in far_in]
    buffers += [pltpu.VMEM(shapes[i].shape, shapes[i].dtype) for i in far_out]
    return pl.pallas_call(
        kernel,
        out_shape=[pltpu.HBM(o.shape, o.dtype) if i in far_out + raw_out else o for i, o in enumerate(shapes)],
        grid_spec=pltpu.PrefetchScalarGridSpec(
            num_scalar_prefetch=2,
            grid=(1,),
            in_specs=[hbm if i in pinned else pl.BlockSpec(memory_space=pl.ANY) if i in far_in else VM for i in range(n_in)],
            out_specs=[hbm if i in far_out + raw_out else VM for i in range(n_out)],
            scratch_shapes=[*buffers, *scratch, pltpu.SemaphoreType.DMA((max(1, len(far_in) + len(far_out)),))],
        ),
        compiler_params=pltpu.CompilerParams(vmem_limit_bytes=vmem << 20),
        cost_estimate=pl.CostEstimate(flops=1000, bytes_accessed=1000, transcendentals=0),
        name=name,
    )(info, jnp.full((1,), which, jnp.int32), *[pltpu.with_memory_space_constraint(a, pltpu.HBM) if i in pinned else a for i, a in enumerate(arrays)])


class Raw:
    def __init__(self, value):
        self.value = value


def ref(x):
    return x() if isinstance(x, Fetch) else x.src if isinstance(x, Flush) else x


def whole(a):
    return (a, (a.shape, lambda ref, info: ref))


def loose(a):
    return (*whole(a), None)


def prepare_kernel(info, out_in, bias, up_in, dn_in, pack, up_half, dn_half):
    for src, dst in ((up_in, up_half), (dn_in, dn_half)):
        dst.src[...] = src()[...]
        dst.start()
    out_w = out_in()
    width, d = out_w.shape
    pack.src[0:width, :] = out_w[...]
    pack.src[width : width + 8, :] = jnp.broadcast_to(bias[...], (8, d))


def prepare(info, out_w, bias, up, dn):
    width, d = out_w.shape
    half = up.shape[0] // 2
    view = lambda ref, info: ref.at[pl.ds(pl.multiple_of(info[3] * half, half), half)]
    view2 = lambda ref, info: ref.at[pl.ds(pl.multiple_of(info[4] * half, half), half)]
    ins = [whole(out_w), bias, (up, ((half, d), view)), (dn, ((half, d), view2))]
    return call("prepare", prepare_kernel, info, ins, [[SDS((width + 8, d), bf16)]] + [[SDS((half, d), bf16)]] * 2)


def head_cols(a, h, extra=()):
    lane = lax.broadcasted_iota(jnp.int32, a.shape, 1)
    out = jnp.where((lane >= HEAD * h) & (lane < HEAD * (h + 1)), a, jnp.zeros_like(a))
    for i, e in enumerate(extra):
        out = jnp.where(lane == WIDE + i, e, out)
    return out


def tail_cols(rows, values):
    lane = lax.broadcasted_iota(jnp.int32, (rows, LANES - WIDE), 1)
    out = jnp.zeros((rows, LANES - WIDE), f32)
    for i, v in enumerate(values):
        out = jnp.where(lane == i, v, out)
    return out.astype(bf16)


def attend_fwd_kernel(info, x_hbm, w_ref, b_ref, *rest):
    far, outs = rest[:5], rest[5:9]
    x_all, *near, v_t, s_all, sem_in, sem_out = rest[9:]
    q_all, k_all, v_all, lse_all, c_all = near
    me = info[2]
    batch, peers, width, block = c_all.shape
    seq = peers * block
    heads = width // HEAD

    def fetch(s):
        return pltpu.make_async_copy(x_hbm.at[s], x_all.at[s], sem_in.at[s])

    def flush(s, i):
        return pltpu.make_async_copy(near[i].at[s], far[i].at[s], sem_out.at[s, i])

    for s in range(batch):
        fetch(s).start()
    w = w_ref()

    def one_sequence(s, carry):
        length = info[7][s]
        fetch(s).wait()
        x = x_all[s]
        k_all[s, :, 0:WIDE] = mm(x, w[1], NT).astype(bf16)
        row = lax.broadcasted_iota(jnp.int32, (seq, 1), 0)
        k_all[s, :, WIDE:LANES] = tail_cols(seq, (jnp.where(row < length, 0.0, -1e30),))
        q = mm(x, w[0], NT) + b_ref[0:1, :].astype(f32)
        q_all[s, :, 0:WIDE] = q.astype(bf16) * jnp.asarray(0.125, bf16)
        q_all[s, :, WIDE:LANES] = tail_cols(seq, (1.0,))
        v = (mm(x, w[2], NT) + b_ref[1:2, :].astype(f32)).astype(bf16)
        v_all[s] = v
        v_t[...] = v.T
        for i in range(3):
            flush(s, i).start()

        def two_blocks(n, carry):
            qb = q_all[s, pl.ds(pl.multiple_of(n * 2 * block, 2 * block), 2 * block), :]
            one = jnp.ones_like(qb[:, 0:1])
            for h in range(heads):
                s_all[h] = mm(k_all[s], head_cols(qb, h, (one,)), NT)
            for h in range(heads):
                top = jnp.max(s_all[h], axis=0, keepdims=True)
                p = jnp.exp(s_all[h] - top)
                total = jnp.sum(p, axis=0, keepdims=True)
                rows = slice(HEAD * h, HEAD * (h + 1))
                out = (mm(v_t[rows, :], p.astype(bf16)) * (1.0 / total)).astype(bf16)
                lse = top + jnp.log(total)
                for j in range(2):
                    cols = slice(block * j, block * (j + 1))
                    c_all[s, 2 * n + j, rows, :] = out[:, cols]
                    lse_all[s, 2 * n + j, h : h + 1, :] = lse[:, cols]
            return carry

        lax.fori_loop(0, peers // 2, two_blocks, 0)
        for i in range(3, 5):
            flush(s, i).start()
        for k, out in enumerate(outs):
            out.src[s] = c_all[s, me ^ k]
        return carry

    lax.fori_loop(0, batch, one_sequence, 0)
    for out in outs:
        out.start()
    for s in range(batch):
        for i in range(5):
            flush(s, i).wait()


def attend_fwd(info, inputs, w_t, bias, peers):
    batch, seq, d = inputs.shape
    width = w_t.shape[1]
    block = seq // peers
    far = [SDS((batch, seq, LANES), bf16)] * 2 + [SDS((batch, seq, width), bf16)]
    far += [SDS((batch, peers, 8, block), f32), SDS((batch, peers, width, block), bf16)]
    scratch = [pltpu.VMEM(inputs.shape, bf16), *[pltpu.VMEM(o.shape, o.dtype) for o in far]]
    scratch += [pltpu.VMEM((width, seq), bf16), pltpu.VMEM((width // HEAD, seq, 2 * block), f32)]
    scratch += [pltpu.SemaphoreType.DMA((batch,)), pltpu.SemaphoreType.DMA((batch, 5))]
    return call(
        "attend_fwd",
        attend_fwd_kernel,
        info,
        [Raw(inputs), whole(w_t), bias],
        [Raw(o) for o in far] + [[SDS((batch, width, block), bf16)]] * peers,
        scratch,
    )


def of_sequence(a):
    return (a, (a.shape[1:], lambda ref, info: ref.at[info[5]]))


def attend_bwd_kernel(info, x_ref, q_in, k_in, v_in, lse_in, c_in, *rest):
    w_ref = x_ref
    peers = 4
    gs, rest = rest[:peers], rest[peers:]
    keep, send, low_out, db_ref, dq_t, dk, dv, k_t, g_ref = rest
    low = low_out.src
    length = info[6]
    me = info[2]
    k_ref, q_ref, v_ref = k_in(), q_in(), v_in()
    lse_ref, c_ref = lse_in(), c_in()
    _, width, block = c_ref.shape
    heads = width // HEAD
    k_t[...] = k_ref[:, 0:WIDE].T
    dk[...] = jnp.zeros_like(dk)
    dv[...] = jnp.zeros_like(dv)
    for k in range(peers):
        g_ref[me ^ k] = gs[k]()[...]

    def one_block(s, carry):
        at = pl.multiple_of(s * block, block)

        @pl.when(at >= length)
        def _():
            dq_t[:, pl.ds(at, block)] = jnp.zeros((width, block), f32)

        @pl.when(at < length)
        def _():
            qb = q_ref[pl.ds(at, block), :]
            g_t = g_ref[s]
            g = g_t.T
            prod_t = g_t.astype(f32) * c_ref[s].astype(f32)
            for h in range(heads):
                rows = slice(HEAD * h, HEAD * (h + 1))
                qh = head_cols(qb, h)
                gh = head_cols(g, h)
                scores = mm(k_ref[...], qh, NT)
                row = lax.broadcasted_iota(jnp.int32, scores.shape, 0)
                p = jnp.where(row < length, jnp.exp(scores - lse_ref[s, h : h + 1, :]), 0.0)
                dp = mm(v_ref[...], gh, NT)
                inner = jnp.sum(prod_t[rows], axis=0, keepdims=True)
                ds = (p * (dp - inner)).astype(bf16)
                dv[...] += mm(p.astype(bf16), gh)
                dk[...] += mm(ds, qh)
                dq_t[rows, pl.ds(at, block)] = mm(k_t[rows, :], ds) * 0.125

        return carry

    lax.fori_loop(0, peers, one_block, 0)
    low[0] = dq_t[...].T.astype(bf16)
    low[1] = dk[:, 0:WIDE].astype(bf16)
    low[2] = dv[...].astype(bf16)
    w = w_ref()
    for s in range(peers):
        at = pl.multiple_of((me ^ s) * block, block)
        total = sum(mm(low[i, pl.ds(at, block), :], w[i]) for i in range(3))
        (send if s % 2 else keep).src[s // 2] = total.astype(bf16)
    send.start()
    keep.start()
    db_ref[...] = jnp.concatenate([rowsum(low[i].astype(f32)) for i in (0, 2)], axis=1)


def attend_bwd(which, info, w_t, q, k, v, lse, c, gs, d):
    _, peers, width, block = c.shape
    seq = peers * block
    outs = [[SDS((2, block, d), bf16)]] * 2 + [[SDS((3, seq, width), bf16)], SDS((1, 2 * width), f32)]
    scratch = [
        pltpu.VMEM((width, seq), f32),
        pltpu.VMEM((seq, LANES), f32),
        pltpu.VMEM((seq, width), f32),
        pltpu.VMEM((width, seq), bf16),
        pltpu.VMEM((peers, width, block), bf16),
    ]
    ins = [whole(w_t)] + [of_sequence(a) for a in (q, k, v, lse, c)]
    ins += [(g, ((width, block), lambda ref, info: ref.at[info[5]]), None) for g in gs]
    return call("attend_bwd", attend_bwd_kernel, info, ins, outs, scratch, which=which)


def project_grads_kernel(info, x_in, low0, low1, db0, db1, keep, send, db_ref, dw, *, parts):
    lows = (low0(), low1())
    x = x_in()
    _, d, width = dw.shape
    step = 256
    for i in range(3):
        for m in range(0, d, step):
            cols = slice(m, m + step)
            dw[i, cols, :] = mm(x[0, :, cols], lows[0][i], TN) + mm(x[1, :, cols], lows[1][i], TN)
    rows = d // parts
    half = 3 * rows // 2
    for b in range(parts):
        flat = dw[:, b * rows : (b + 1) * rows, :].reshape(3 * rows, width)
        flat = jnp.concatenate([flat[0:half], flat[half : 2 * half]], axis=1).astype(bf16)
        at = ((b >> 2) * 2 + (b & 1)) * half
        mine = ((b >> 1) & 1) == info[4]

        @pl.when(mine)
        def _():
            keep.src[at : at + half, :] = flat

        @pl.when(jnp.logical_not(mine))
        def _():
            send.src[at : at + half, :] = flat

    db = db0[...] + db1[...]
    db_ref[...] = db
    high = db.astype(bf16)
    n = keep.src.shape[0]
    send.src[n : n + 8, :] = jnp.concatenate(
        [high, (db - high.astype(f32)).astype(bf16), jnp.zeros((6, 2 * width), bf16)], axis=0
    )
    send.start()


def gelu_parts(h):
    t = 1.0 / (1.0 + (0.3275911 * 0.7071067811865476) * jnp.abs(h))
    poly = t * (0.127414796 + t * (-0.142248368 + t * (0.7107068705 + t * (-0.7265760135 + t * 0.5307027145))))
    bell = jnp.exp2((-0.5 * 1.4426950408889634) * (h * h))
    tail = poly * bell
    cum = jnp.where(h < 0, tail, 1.0 - tail)
    return h * cum, cum + h * (bell * 0.3989422804014327)


def norm_parts(v):
    center = v - jnp.mean(v, axis=1, keepdims=True)
    r = lax.rsqrt(jnp.mean(center * center, axis=1, keepdims=True) + 1e-12)
    return center * r, r


def norm_back(u, gain, nv, r):
    gu = u * gain
    return r * (gu - jnp.mean(gu, axis=1, keepdims=True) - nv * jnp.mean(gu * nv, axis=1, keepdims=True))


def rowsum(v):
    return jnp.sum(v, axis=0, keepdims=True)


def first_norm_kernel(info, x_in, par, *rest):
    nv_ref, r_ref, low = rest[8:]
    cs, packs = [c() for c in rest[:4]], [p() for p in rest[4:8]]
    x_ref = x_in()
    batch, rows = x_ref.shape[:2]
    width = cs[0].shape[1]

    def one_sequence(s, carry):
        here = pl.ds(pl.multiple_of(s * rows, rows), rows)
        total = par[0:1, :] + x_ref[s].astype(f32)
        for k in range(4):
            total = total + mm(cs[k][s], packs[k][0:width, :], TN)
        nv, r = norm_parts(total)
        nv_ref[here, :] = nv
        r_ref[here, :] = r
        low[here, :] = (nv * par[1:2, :] + par[2:3, :]).astype(bf16)
        return carry

    lax.fori_loop(0, batch, one_sequence, 0)


def feed_kernel(info, low, low2, pack, *rest, width, far):
    if far:
        u_a, u_b, d_a, d_b, p_own, p_sib, act_out, slope_out, own, sib, both, up, dn = rest
        half = u_a.dst.shape[0]
        assemble(info[3], up, u_a(), u_b(), half)
    else:
        u_in, d_in, act_out, slope_out, own, sib, both = rest
        up = u_in()
    act, slope = ref(act_out), ref(slope_out)
    units = up.shape[1]
    bias = pack()
    step = 256
    both[0] = low[...]
    both[1] = low2[...]

    def side(j, carry):
        def chunk(n, carry):
            cols = pl.ds(pl.multiple_of(n * step, step), step)
            hidden = mm(both[j], up[:, cols]) + bias[width : width + 1, cols].astype(f32)
            a, g = gelu_parts(hidden)
            act[j, :, cols] = a.astype(bf16)
            slope[j, :, cols] = g.astype(bf16)
            return carry

        return lax.fori_loop(0, units // step, chunk, carry)

    lax.fori_loop(0, 2, side, 0)
    if far:
        assemble(info[4], dn, d_a(), d_b(), half)
        sib[...] = (p_sib[...] + mm(act[1], dn[...])).astype(bf16)
        own[...] = p_own[...] + mm(act[0], dn[...])
    else:
        dn = d_in()
        own[...] = mm(act[0], dn[...])
        sib[...] = mm(act[1], dn[...])


def assemble(bit, dst, a, b, half):
    dst[pl.ds(pl.multiple_of(bit * half, half), half)] = a[...]
    dst[pl.ds(pl.multiple_of((1 - bit) * half, half), half)] = b[...]


def second_norm_kernel(info, cot_in, par, nv_in, own, got, outs, gsec_out, gs_low, small):
    cot, nv_ref, gsec = cot_in(), ref(nv_in), ref(gsec_out)
    batch, rows, d = cot.shape

    def one_sequence(s, sums):
        here = pl.ds(pl.multiple_of(s * rows, rows), rows)
        total = own[here, :] + got[here, :].astype(f32) + par[3:4, :] + (nv_ref[here, :] * par[1:2, :] + par[2:3, :])
        nv, r = norm_parts(total)
        outs.src[s] = (nv * par[4:5, :] + par[5:6, :]).astype(bf16)
        at = info[2] * rows + lax.broadcasted_iota(jnp.int32, (rows, 1), 0)
        seed = jnp.where(at < info[7][s], cot[s].astype(f32), 0.0)
        g = norm_back(seed, par[4:5, :], nv, r)
        gsec[here, :] = g
        gs_low[here, :] = g.astype(bf16)
        return tuple(a + rowsum(b) for a, b in zip(sums, (g, seed * nv, seed)))

    sums = lax.fori_loop(0, batch, one_sequence, (jnp.zeros((1, d), f32),) * 3)
    small[...] = jnp.concatenate([*sums, jnp.zeros((5, d), f32)], axis=0)


def feed_back_kernel(info, gs, gs2, slope0, slope1, up0, dn0, u_a, u_b, d_a, d_b, gh_out, own, sib, ub, sides, up2, dn2):
    gh = ref(gh_out)
    half = u_a.dst.shape[0]
    units = up0.dst.shape[1]
    ub[...] = jnp.zeros_like(ub)
    sides[0] = gs[...]
    sides[1] = gs2[...]
    step = 256
    for k, slope in enumerate((ref(slope0), ref(slope1))):
        if k:
            assemble(info[4], dn2, d_a(), d_b(), half)
            dn = dn2
        else:
            dn = dn0()

        def side(j, carry):
            def chunk(n, carry):
                cols = pl.ds(pl.multiple_of(n * step, step), step)
                ga = mm(sides[j], dn[cols, :], NT)
                h = (ga * slope[j, :, cols].astype(f32)).astype(bf16)
                gh[k, j, :, cols] = h
                ub[k : k + 1, cols] += rowsum(h.astype(f32))
                return carry

            return lax.fori_loop(0, units // step, chunk, carry)

        lax.fori_loop(0, 2, side, 0)
    assemble(info[3], up2, u_a(), u_b(), half)
    up = up0()
    sib[...] = (mm(gh[0, 1], up[...], NT) + mm(gh[1, 1], up2[...], NT)).astype(bf16)
    own[...] = mm(gh[0, 0], up[...], NT) + mm(gh[1, 0], up2[...], NT)


def first_back_kernel(info, par, nv_in, r_ref, own, got, gsec_in, small2, *rest):
    cs, packs = [c() for c in rest[:4]], rest[4:8]
    gfi, g0, g1, g2, g3, okeep, osend, small, ga_low = rest[8:]
    nv_ref, gsec = ref(nv_in), ref(gsec_in)
    packs = [p() for p in packs]
    n, d = own.shape
    rows = n // 2
    width = cs[0].shape[1]

    def one_sequence(s, sums):
        here = pl.ds(pl.multiple_of(s * rows, rows), rows)
        u = own[here, :] + got[here, :].astype(f32) + gsec[here, :]
        nv = nv_ref[here, :]
        g = norm_back(u, par[1:2, :], nv, r_ref[here, :])
        gfi.src[here, :] = g
        low = g.astype(bf16)
        ga_low[here, :] = low
        for k, out in enumerate((g0, g1, g2, g3)):
            out.src[s] = mm(packs[k][0:width, :], low, NT).astype(bf16)
        return tuple(a + rowsum(b) for a, b in zip(sums, (g, u * nv, u)))

    sums = lax.fori_loop(0, 2, one_sequence, (jnp.zeros((1, d), f32),) * 3)
    for out in (g3, g2, g1, g0, gfi):
        out.start()
    for k in range(4):
        total = mm(cs[k][0], ga_low[0:rows, :]) + mm(cs[k][1], ga_low[rows:n, :])
        (osend if k % 2 else okeep).src[k // 2, 0:width, :] = total.astype(bf16)
    both = jnp.concatenate([*sums, small2[0:3, :], jnp.zeros((2, d), f32)], axis=0)
    small[...] = both
    high = both.astype(bf16)
    osend.src[0, width : width + 8, :] = high
    osend.src[1, width : width + 8, :] = (both - high.astype(f32)).astype(bf16)


def down_grads_kernel(info, act0, act1, gs, gs2, far_keep, far_send, keep, send, scr, *, parts):
    units = act0.shape[2]
    block = units // parts
    step = 384
    for act, mine, theirs in ((act1, far_keep, far_send), (act0, keep, send)):

        def chunk(m, carry):
            cols = pl.ds(pl.multiple_of(m * step, step), step)
            total = mm(act[0, :, cols], gs[...], TN) + mm(act[1, :, cols], gs2[...], TN)
            total = total.astype(bf16)
            for i in range(step // block):
                scr[(i & 1) ^ info[3], m * (step // block // 2) + (i >> 1)] = total[i * block : (i + 1) * block]
            return carry

        lax.fori_loop(0, units // step, chunk, 0)
        theirs.src[...] = scr[1]
        theirs.start()
        mine.src[...] = scr[0]
        mine.start()


def up_grads_kernel(
    info, low, low2, gh_in, okeep, ogot, small, ub, far_keep, far_send, keep, send, sums, scr, *, parts, width
):
    gh = ref(gh_in)
    units = low.shape[1]
    block = units // parts
    extra = width // parts
    joint = block + extra
    n = parts // 2 * joint
    step = 384
    got = ogot()
    both = small[...] + got[0, width : width + 8, :].astype(f32) + got[1, width : width + 8, :].astype(f32)
    both = jnp.concatenate([both[0:6], ub[0:2, :]], axis=0)
    sums[...] = both
    high = both.astype(bf16)
    far_send.src[n : n + 8, :] = high
    far_send.src[n + 8 : n + 16, :] = (both - high.astype(f32)).astype(bf16)
    for k, mine, theirs in ((1, far_keep, far_send), (0, keep, send)):

        def chunk(m, carry):
            cols = pl.ds(pl.multiple_of(m * step, step), step)
            total = mm(low[:, cols], gh[k, 0], TN) + mm(low2[:, cols], gh[k, 1], TN)
            total = total.astype(bf16)
            for i in range(step // block):
                at = (m * (step // block // 4) + (i >> 2)) * 2 + (i & 1)
                scr[((i >> 1) & 1) ^ info[4], at, 0:block, :] = total[i * block : (i + 1) * block]
            return carry

        lax.fori_loop(0, units // step, chunk, 0)
        o = (okeep()[k, 0:width, :].astype(f32) + got[k, 0:width, :].astype(f32)).astype(bf16)
        for b in range(parts):
            at = (b >> 2) * 2 + (b & 1)
            scr[((b >> 1) & 1) ^ info[4], at, block:joint, :] = o[b * extra : (b + 1) * extra]
        for b in range(parts // 2):
            theirs.src[b * joint : (b + 1) * joint, :] = scr[1, b]
            mine.src[b * joint : (b + 1) * joint, :] = scr[0, b]
        theirs.start()
        mine.start()


def swap(x, axis, bit):
    size = lax.axis_size(axis)
    return lax.ppermute(x, axis, [(i, i ^ bit) for i in range(size)])


def summed(parts):
    return sum(p.astype(f32) for p in parts)


def spread(array, axis, parts):
    bits = parts.bit_length() - 1
    return array.reshape(*array.shape[:axis], *([2] * bits), array.shape[axis] // parts, *array.shape[axis + 1 :])


def halve_sum(terms, axis, mine):
    other = [lax.dynamic_index_in_dim(t, 1 - mine, axis, keepdims=False) for t in terms]
    kept = [lax.dynamic_index_in_dim(t, mine, axis, keepdims=False) for t in terms]
    return kept, summed(other).astype(bf16)


def halve(terms, axis, bit, mine):
    other = [lax.dynamic_index_in_dim(t, 1 - mine, axis, keepdims=False) for t in terms]
    kept = [lax.dynamic_index_in_dim(t, mine, axis, keepdims=False) for t in terms]
    other = summed(other).astype(bf16)
    return kept + [swap(other, "dp", bit)], other


def body(
    inputs,
    cotangent,
    lengths,
    qkv_weight,
    qkv_bias,
    out_weight,
    out_bias,
    first_gain,
    first_shift,
    up_weight,
    up_bias,
    down_weight,
    down_bias,
    second_gain,
    second_shift,
):
    batch, seq, d = inputs.shape
    rows = cotangent.shape[1]
    n = batch * rows
    width = out_weight.shape[0]
    units = up_weight.shape[1]
    peers = lax.axis_size("tensor")
    parts = lax.axis_size("dp")
    bits = parts.bit_length() - 1
    t = lax.axis_index("tensor")
    dp = lax.axis_index("dp")
    bit_of = [(dp >> i) & 1 for i in range(bits)]
    info = lengths
    par = jnp.concatenate([out_bias, first_gain, first_shift, down_bias, second_gain, second_shift])
    par = par.reshape(6, d).astype(f32)
    w_t = jnp.transpose(qkv_weight, (1, 2, 0))
    pack, up_half, dn_half = prepare(info, out_weight, up_bias[None], up_weight, down_weight)
    pack2 = swap(pack, "tensor", 2)
    pack1 = swap(pack, "tensor", 1)
    u2a = swap(up_half, "tensor", 2)
    q, k, v, lse, c, *cs = attend_fwd(info, inputs, w_t, qkv_bias, peers)
    saved = (q, k, v, lse, c)
    *cs, pack1, pack2, u2a = after(*cs, pack1, pack2, u2a)
    ctx = [cs[0]] + [swap(cs[j], "tensor", j) for j in range(1, peers)]
    pack3 = swap(pack2, "tensor", 1)
    *ctx, pack3, dn_half = after(*ctx, pack3, dn_half)
    d2a = swap(dn_half, "tensor", 2)
    packs = [pack, pack1, pack2, pack3]
    u2b = swap(u2a, "dp", 1)
    d2b = swap(d2a, "dp", 2)
    far_ctx = [whole(ctx[0])] + [loose(x) for x in ctx[1:]]
    far_packs = [whole(pack)] + [loose(p) for p in packs[1:]]
    share = (inputs, ((batch, rows, d), lambda ref, info: ref.at[:, pl.ds(pl.multiple_of(info[2] * rows, rows), rows), :]))
    nv1, r1, low = call(
        "first_norm",
        first_norm_kernel,
        info,
        [share, par, *far_ctx, *far_packs],
        [SDS((n, d), f32), SDS((n, 1), f32), SDS((n, d), bf16)],
        vmem=NEAR,
    )
    low2 = swap(low, "tensor", 1)
    pair = SDS((2, n, units), bf16)
    part = SDS((n, d), f32)
    sides = pltpu.VMEM((2, n, d), bf16)
    act0, slope0, own, sib = call(
        "feed",
        feed_kernel,
        info,
        [low, low2, far_packs[0], whole(up_weight), whole(down_weight)],
        [pair, pair, part, part],
        [sides],
        vmem=NEAR,
        width=width,
        far=False,
    )
    halves = [loose(x) for x in (u2a, u2b, d2a, d2b)]
    both = [pltpu.VMEM((d, units), bf16), pltpu.VMEM((units, d), bf16)]
    act1, slope1, own, sib = call(
        "feed",
        feed_kernel,
        info,
        [low, low2, far_packs[2], *halves, own, sib],
        [pair, pair, part, SDS((n, d), bf16)],
        [sides, *both],
        vmem=NEAR,
        width=width,
        far=True,
    )
    got = swap(sib, "tensor", 1)
    outputs, gsec, gs_low, small2 = call(
        "second_norm",
        second_norm_kernel,
        info,
        [whole(cotangent), par, nv1, own, got],
        [[SDS((batch, rows, d), bf16)], part, SDS((n, d), bf16), SDS((8, d), f32)],
        vmem=NEAR,
    )
    gs_low2 = swap(gs_low, "tensor", 1)
    gh, own, sib, ub = call(
        "feed_back",
        feed_back_kernel,
        info,
        [gs_low, gs_low2, slope0, slope1, whole(up_weight), whole(down_weight), *halves],
        [SDS((2, 2, n, units), bf16), part, SDS((n, d), bf16), SDS((8, d), f32)],
        [sides, *both],
        vmem=NEAR,
    )
    got = swap(sib, "tensor", 1)
    block = units // parts
    downs = call(
        "down_grads",
        down_grads_kernel,
        info,
        [act0, act1, gs_low, gs_low2],
        [[SDS((parts // 2, block, d), bf16)]] * 4,
        [pltpu.VMEM((2, parts // 2, block, d), bf16)],
        vmem=NEAR,
        parts=parts,
    )
    down_far_keep, down_far_send, down_keep, down_send = downs
    down_far_got = swap(down_far_send, "dp", 1)
    gfi, g0, g1, g2, g3, okeep, osend, small1 = call(
        "first_back",
        first_back_kernel,
        info,
        [par, nv1, r1, own, got, gsec, small2, *far_ctx, *far_packs],
        [
            [part],
            *[[SDS((batch, width, rows), bf16)]] * 4,
            *[[SDS((2, width + 8, d), bf16)]] * 2,
            SDS((8, d), f32),
        ],
        [pltpu.VMEM((n, d), bf16)],
        vmem=NEAR,
    )
    gctx = [g0] + [swap(g, "tensor", j) for j, g in ((1, g1), (2, g2), (3, g3))]
    got_o = swap(osend, "tensor", 1)
    joint = block + width // parts
    cut = parts // 2 * joint
    up_far_keep, up_far_send, up_keep, up_send, small = call(
        "up_grads",
        up_grads_kernel,
        info,
        [low, low2, gh, whole(okeep), loose(got_o), small1, ub],
        [
            [SDS((cut, d), bf16)],
            [SDS((cut + 16, d), bf16)],
            [SDS((cut, d), bf16)],
            [SDS((cut, d), bf16)],
            SDS((8, d), f32),
        ],
        [pltpu.VMEM((2, parts // 2, joint, d), bf16)],
        vmem=NEAR,
        parts=parts,
        width=width,
    )
    *gctx, up_far_send = after(*gctx, up_far_send)
    down_far_sum = summed([down_far_keep, down_far_got]).astype(bf16)
    *gctx, down_far_sum, up_far_keep = after(*gctx, down_far_sum, up_far_keep)
    up_far_got = swap(up_far_send, "dp", 2)
    down_y = swap(down_far_sum, "tensor", 2)
    down_got = swap(down_send, "dp", 1)
    lows, biases, terms_of = [], [], []
    for s in range(batch):
        keep, send, low_grads, db = attend_bwd(s, info, w_t, *saved, gctx, d)
        if s == 0:
            send, up_far_got, down_y, down_got = after(send, up_far_got, down_y, down_got)
        else:
            send, low_grads, up_got, up_more, far = after(send, low_grads, up_got, up_more, far)
            terms_of[0].append(far)
        near = swap(send, "tensor", 1)
        in_sum = summed([keep[1], near[1]]).astype(bf16)
        terms_of.append([keep[0], near[0]])
        lows.append(low_grads)
        biases.append(db)
        if s:
            continue
        shape = ([2] * (bits - 1)) + [block, d]
        down_terms = [x.reshape(shape) for x in (down_keep, down_got, down_y)]
        down_kept, down_next = halve_sum(down_terms, bits - 2, bit_of[1])
        shape = ([2] * (bits - 1)) + [joint, d]
        small = small + pair_sum(up_far_got, cut, 8)
        terms = [x.reshape(shape) for x in (up_far_keep, up_far_got[:cut])]
        up_far_kept, up_far_next = halve_sum(terms, bits - 2, bit_of[0])
        up_far_rows = with_rows(up_far_next, small)
        tied = after(down_next, up_far_rows, in_sum, up_send, *gctx)
        (down_next, up_far_rows, in_sum, up_send), gctx = tied[:4], tied[4:]
        up_got = swap(up_send, "dp", 2)
        down_more = swap(down_next, "dp", 2)
        up_more = swap(up_far_rows, "dp", 1)
        far = swap(in_sum, "tensor", 2)
    terms_of[1].append(swap(in_sum, "tensor", 2))
    first_terms, last_terms = terms_of
    m = 3 * d // 4
    w_keep, w_send, db = call(
        "project_grads",
        project_grads_kernel,
        info,
        [whole(inputs), *[whole(a) for a in lows], *biases],
        [[SDS((m, 2 * width), bf16)], [SDS((m + 8, 2 * width), bf16)], SDS((1, 2 * width), f32)],
        [pltpu.VMEM((3, d, width), f32)],
        parts=parts,
    )
    w_send, down_more = after(w_send, down_more)
    down_terms = down_kept + [down_more]
    order = [1, 0] + list(range(2, bits))
    row = 3 * (d // parts) // 2
    got = swap(w_send, "dp", 2)
    got, in_sum = after(got, in_sum)
    got, up_got, up_more, *down_terms = after(got, up_got, up_more, *down_terms)
    at = up_far_next.size // d
    up_far_terms = up_far_kept + [up_more[:at].reshape(up_far_next.shape)]
    small_x = pair_sum(up_more, at, 8)
    small = small + small_x
    small = jnp.concatenate([small[0:6], small[7:8], small[6:7]])
    send = summed(up_far_terms).astype(bf16)
    up_y_sent = with_rows(send, small)
    up_y = swap(up_y_sent, "tensor", 2)
    at = send.size // d
    small = jnp.concatenate([small[0:6], small[7:8], small[7:8]]) + pair_sum(up_y, at, 8)
    shape = ([2] * (bits - 1)) + [joint, d]
    terms, up_next = halve([x.reshape(shape) for x in (up_keep, up_got)], bits - 2, 1, bit_of[0])
    terms.append(up_y[:at].reshape(send.shape))
    for i in range(2, bits):
        terms, sent, more = halve_with(terms, terms[0].ndim - 3, small, "dp", 1 << i, bit_of[i])
        small = small + more
    up_sum = summed(terms)
    mine = small
    for i in range(2, bits):
        down_terms, sent = halve(down_terms, bits - 1 - i, 1 << i, bit_of[i])
    down_sum = summed(down_terms)
    at = parts // 2 * row
    shape = ([2] * (bits - 1)) + [row, 2 * width]
    terms = [x.reshape(shape) for x in (w_keep, got[:at])]
    db = db + got[at : at + 1].astype(f32) + got[at + 1 : at + 2].astype(f32)
    for i in order[1:]:
        kept, sent, more = halve_with(terms, terms[0].ndim - 3, db, "dp", 1 << i, bit_of[i])
        terms, db = kept, db + more
    qkv_sum = summed(terms)
    qkv_sum = jnp.concatenate([qkv_sum[:, :width], qkv_sum[:, width:]], axis=0).reshape(3, -1, width)
    qkv_sum = jnp.transpose(qkv_sum, (1, 0, 2))
    db = db.reshape(2, width)
    input_list = [
        (summed(x) + gfi[s * rows : (s + 1) * rows]).astype(bf16)
        for s, x in enumerate((first_terms, last_terms))
    ]
    return (
        outputs,
        jnp.stack(input_list, 0),
        qkv_sum,
        db,
        up_sum[block:],
        mine[0],
        mine[1],
        mine[2],
        up_sum[:block],
        mine[6],
        down_sum,
        mine[3],
        mine[4],
        mine[5],
    )


def pair_sum(array, at, n):
    return array[at : at + n].astype(f32) + array[at + n : at + 2 * n].astype(f32)


def with_rows(array, rows):
    flat = array.reshape(-1, array.shape[-1])
    high = rows.astype(bf16)
    low = (rows - high.astype(f32)).astype(bf16)
    return jnp.concatenate([flat, high, low], axis=0)


def halve_with(terms, axis, rows, name, bit, mine):
    other = [lax.dynamic_index_in_dim(t, 1 - mine, axis, keepdims=False) for t in terms]
    kept = [lax.dynamic_index_in_dim(t, mine, axis, keepdims=False) for t in terms]
    other = summed(other).astype(bf16)
    sent = with_rows(other, rows)
    got = swap(sent, name, bit)
    cut = other.size // other.shape[-1]
    return kept + [got[:cut].reshape(other.shape)], sent, pair_sum(got, cut, rows.shape[0])


def after(*values):
    return lax.optimization_barrier(values)


def solution(mesh):
    in_specs = (
        P("dp", None, None),
        P("dp", "tensor", None),
        P("dp"),
        P(None, None, "tensor"),
        P(None, "tensor"),
        P("tensor", None),
        P(),
        P(),
        P(),
        P(None, "tensor"),
        P("tensor"),
        P("tensor", None),
        P(),
        P(),
        P(),
    )
    out_specs = (
        P("dp", "tensor", None),
        P("dp", "tensor", None),
        P("dp", None, "tensor"),
        P(None, "tensor"),
        P(("tensor", "dp"), None),
        P(),
        P(),
        P(),
        P("dp", "tensor"),
        P("tensor"),
        P(("tensor", "dp"), None),
        P(),
        P(),
        P(),
    )
    return jax.shard_map(body, mesh=mesh, in_specs=in_specs, out_specs=out_specs, check_vma=False)
```

profile of v0, /device:TPU:0, one launch (start us, length us, event | category | flops | bytes accessed | tf_op | source)
XLA Modules:
  0.0 237.5 jit_solution(17410168519756428519)
XLA Ops:
  0.6 1.3 broadcast_in_dim.3.refs_1_
  1.9 3.7 %prepare.1 = (bf16[200,768]{1,0:T(8,128)(2,1)}, bf16[384,768]{1,0:T(8,128)(2,1)}, bf16[384,768]{1,0:T(8,128)(2,1)}) custom-call(s32[2]{0:T(128)} %lengths_ref.25, s32[1]{0:T(128)} %constant.264.clone.1.which_ref, bf16[192,768]{1,0:T(8,128)(2,1)} %refs_0_.6, bf16[1,768]{1,0:T(2,128)(2,1)} %broadcast_in_dim.3.refs_1_, bf16[768,768]{1,0:T(8,128)(2,1)} %refs_4_.3, ...), custom_call_target="tpu_custom_call" | custom-call | flops 1000 | bytes 1000 | tf_op jit(solution)/shard_map/prepare/pallas_call | solution.py:91
  5.6 3.0 %collective-permute-start.2 = (bf16[384,768]{1,0:T(8,128)(2,1)}, bf16[384,768]{1,0:T(8,128)(2,1)S(1)}, u32[]{:S(2)}, u32[]{:S(2)}) collective-permute-start(bf16[384,768]{1,0:T(8,128)(2,1)} %get-tuple-element.129), channel_id=1, source_target_pairs={{0,2},{1,3},{2,0},{3,1},{4,6},{5,7},{6,4},{7,5},{8,10},{9,11},{10,... | collective-permute-start | bytes 1769480 | tf_op jit(solution)/shard_map/ppermute | solution.py:599
  8.9 16.4 %attend_fwd.1 = (bf16[2,1024,256]{2,1,0:T(8,128)(2,1)}, bf16[2,1024,256]{2,1,0:T(8,128)(2,1)}, bf16[2,1024,192]{2,1,0:T(8,128)(2,1)}, f32[2,4,8,256]{3,2,1,0:T(8...) custom-call(s32[2]{0:T(128)} %lengths_ref.25, ...), custom_call_target="tpu_custom_call" | custom-call | flops 1000 | bytes 1000 | tf_op jit(solution)/shard_map/attend_fwd/pallas_call | solution.py:91
  25.3 3.5 %collective-permute-done.1.refs_8_.refs_2_.refs_13_ = bf16[200,768]{1,0:T(8,128)(2,1)S(1)} collective-permute-done((bf16[200,768]{1,0:T(8,128)(2,1)}, bf16[200,768]{1,0:T(8,128)(2,1)S(1)}, u32[]{:S(2)}, u32[]{:S(2)}) %collective-permute-start.1) | collective-permute-done | bytes 307232 | tf_op jit(solution)/shard_map/ppermute | solution.py:599
  29.3 1.7 collective-permute-start.4
  31.0 6.2 %collective-permute-done.4.refs_4_.refs_9_ = bf16[2,192,256]{2,1,0:T(8,128)(2,1)S(1)} collective-permute-done((bf16[2,192,256]{2,1,0:T(8,128)(2,1)}, bf16[2,192,256]{2,1,0:T(8,128)(2,1)S(1)}, u32[]{:S(2)}, u32[]{:S(2)}) %collective-permute-start.4) | collective-permute-done | bytes 196640 | tf_op jit(solution)/shard_map/ppermute | solution.py:599
  37.3 2.6 %collective-permute-done.5.refs_5_.refs_10_ = bf16[2,192,256]{2,1,0:T(8,128)(2,1)S(1)} collective-permute-done((bf16[2,192,256]{2,1,0:T(8,128)(2,1)}, bf16[2,192,256]{2,1,0:T(8,128)(2,1)S(1)}, u32[]{:S(2)}, u32[]{:S(2)}) %collective-permute-start.5) | collective-permute-done | bytes 196640 | tf_op jit(solution)/shard_map/ppermute | solution.py:599
  39.9 1.4 collective-permute-start.9
  42.6 4.1 %first_norm.1 = (f32[512,768]{1,0:T(8,128)S(1)}, f32[512,1]{1,0:T(8,128)S(1)}, bf16[512,768]{1,0:T(8,128)(2,1)S(1)}) custom-call(s32[2]{0:T(128)S(1)} %copy-done, s32[1]{0:T(128)} %constant.264.clone.1.which_ref, bf16[2,1024,768]{2,1,0:T(8,128)(2,1)} %refs_0_.9, f32[6,768]{1,0:T(8,128)S(1)} %reshape.183.refs_1_.refs_0_, ...), custom_call_target="tpu_custom_call" | custom-call | flops 1000 | bytes 1000 | tf_op jit(solution)/shard_map/first_norm/pallas_call | solution.py:91
  46.7 0.6 collective-permute-start.7
  47.3 1.5 collective-permute-start.8
  48.8 6.8 %collective-permute-done.9.refs_5_.refs_8_ = bf16[384,768]{1,0:T(8,128)(2,1)S(1)} collective-permute-done((bf16[384,768]{1,0:T(8,128)(2,1)S(1)}, bf16[384,768]{1,0:T(8,128)(2,1)S(1)}, u32[]{:S(2)}, u32[]{:S(2)}) %collective-permute-start.9) | collective-permute-done | bytes 589856 | tf_op jit(solution)/shard_map/ppermute | solution.py:599
  55.6 1.8 collective-permute-start.10
  57.4 7.6 %feed.2 = (bf16[2,512,768]{2,1,0:T(8,128)(2,1)S(1)}, bf16[2,512,768]{2,1,0:T(8,128)(2,1)S(1)}, f32[512,768]{1,0:T(8,128)S(1)}, f32[512,768]{1,0:T(8,128)S(1)}) custom-call(s32[2]{0:T(128)S(1)} %copy-done, s32[1]{0:T(128)} %constant.264.clone.1.which_ref, bf16[512,768]{1,0:T(8,128)(2,1)S(1)} %get-tuple-element.143.refs_0_, ...), custom_call_target="tpu_custom_call" | custom-call | flops 1000 | bytes 1000 | tf_op jit(solution)/shard_map/feed/pallas_call | solution.py:91
  65.0 5.6 %collective-permute-done.10.refs_6_.refs_9_ = bf16[384,768]{1,0:T(8,128)(2,1)S(1)} collective-permute-done((bf16[384,768]{1,0:T(8,128)(2,1)S(1)}, bf16[384,768]{1,0:T(8,128)(2,1)S(1)}, u32[]{:S(2)}, u32[]{:S(2)}) %collective-permute-start.10) | collective-permute-done | bytes 589856 | tf_op jit(solution)/shard_map/ppermute | solution.py:599
  70.7 7.0 %feed.3 = (bf16[2,512,768]{2,1,0:T(8,128)(2,1)S(1)}, bf16[2,512,768]{2,1,0:T(8,128)(2,1)S(1)}, f32[512,768]{1,0:T(8,128)S(1)}, bf16[512,768]{1,0:T(8,128)(2,1)S(1)}) custom-call(s32[2]{0:T(128)S(1)} %copy-done, s32[1]{0:T(128)} %constant.264.clone.1.which_ref, bf16[512,768]{1,0:T(8,128)(2,1)S(1)} %get-tuple-element.143.refs_0_, ...), custom_call_target="tpu_custom_call" | custom-call | flops 1000 | bytes 1000 | tf_op jit(solution)/shard_map/feed/pallas_call | solution.py:91
  77.8 2.3 collective-permute-done.11.refs_4_
  80.0 4.1 %second_norm.1 = (bf16[2,256,768]{2,1,0:T(8,128)(2,1)}, f32[512,768]{1,0:T(8,128)S(1)}, bf16[512,768]{1,0:T(8,128)(2,1)S(1)}, f32[8,768]{1,0:T(8,128)S(1)}) custom-call(s32[2]{0:T(128)S(1)} %copy-done, s32[1]{0:T(128)} %constant.264.clone.1.which_ref, bf16[2,256,768]{2,1,0:T(8,128)(2,1)} %refs_0_.8, f32[6,768]{1,0:T(8,128)S(1)} %reshape.183.refs_1_.refs_0_, ...), custom_call_target="tpu_custom_call" | custom-call | flops 1000 | bytes 1000 | tf_op jit(solution)/shard_map/second_norm/pallas_call | solution.py:91
  84.3 2.1 collective-permute-done.12.refs_1_.refs_3_
  86.5 10.3 %feed_back.1 = (bf16[2,2,512,768]{3,2,1,0:T(8,128)(2,1)S(1)}, f32[512,768]{1,0:T(8,128)S(1)}, bf16[512,768]{1,0:T(8,128)(2,1)S(1)}, f32[8,768]{1,0:T(8,128)S(1)}) custom-call(s32[2]{0:T(128)S(1)} %copy-done, s32[1]{0:T(128)} %constant.264.clone.1.which_ref, bf16[512,768]{1,0:T(8,128)(2,1)S(1)} %get-tuple-element.157.refs_0_.refs_2_, ...), custom_call_target="tpu_custom_call" | custom-call | flops 1000 | bytes 1000 | tf_op jit(solution)/shard_map/feed_back/pallas_call | solution.py:91
  96.9 2.1 collective-permute-done.13.refs_4_
  99.1 7.0 %first_back.1 = (f32[512,768]{1,0:T(8,128)}, bf16[2,192,256]{2,1,0:T(8,128)(2,1)}, bf16[2,192,256]{2,1,0:T(8,128)(2,1)}, bf16[2,192,256]{2,1,0:T(8,128)(2,1)}, b...) custom-call(s32[2]{0:T(128)S(1)} %copy-done, ...), custom_call_target="tpu_custom_call" | custom-call | flops 1000 | bytes 1000 | tf_op jit(solution)/shard_map/first_back/pallas_call | solution.py:91
  106.3 5.0 %down_grads.1 = (bf16[4,96,768]{2,1,0:T(8,128)(2,1)}, bf16[4,96,768]{2,1,0:T(8,128)(2,1)}, bf16[4,96,768]{2,1,0:T(8,128)(2,1)}, bf16[4,96,768]{2,1,0:T(8,128)(2,1)}) custom-call(s32[2]{0:T(128)S(1)} %copy-done, s32[1]{0:T(128)} %constant.264.clone.1.which_ref, bf16[2,512,768]{2,1,0:T(8,128)(2,1)S(1)} %get-tuple-element.178.refs_0_, ...), custom_call_target="tpu_custom_call" | custom-call | flops 1000 | bytes 1000 | tf_op jit(solution)/shard_map/down_grads/pallas_call | solution.py:91
  111.3 1.7 collective-permute-start.18
  113.1 1.6 collective-permute-start.15
  115.4 5.6 %up_grads.1 = (bf16[480,768]{1,0:T(8,128)(2,1)}, bf16[496,768]{1,0:T(8,128)(2,1)}, bf16[480,768]{1,0:T(8,128)(2,1)}, bf16[480,768]{1,0:T(8,128)(2,1)}, f32[8,768]{1,0:T(8,128)S(1)}) custom-call(s32[2]{0:T(128)S(1)} %copy-done, s32[1]{0:T(128)} %constant.264.clone.1.which_ref, bf16[512,768]{1,0:T(8,128)(2,1)S(1)} %get-tuple-element.143.refs_0_, ...), custom_call_target="tpu_custom_call" | custom-call | flops 1000 | bytes 1000 | tf_op jit(solution)/shard_map/up_grads/pallas_call | solution.py:91
  121.1 3.1 %collective-permute-done.16.refs_9_ = bf16[2,192,256]{2,1,0:T(8,128)(2,1)S(1)} collective-permute-done((bf16[2,192,256]{2,1,0:T(8,128)(2,1)S(1)}, bf16[2,192,256]{2,1,0:T(8,128)(2,1)S(1)}, u32[]{:S(2)}, u32[]{:S(2)}) %collective-permute-start.16) | collective-permute-done | bytes 196640 | tf_op jit(solution)/shard_map/ppermute | solution.py:599
  124.1 1.6 collective-permute-start.19
  125.7 2.0 collective-permute-done.18
  127.9 1.9 collective-permute-start.20
  129.8 16.3 %attend_bwd.2 = (bf16[2,256,768]{2,1,0:T(8,128)(2,1)}, bf16[2,256,768]{2,1,0:T(8,128)(2,1)}, bf16[3,1024,192]{2,1,0:T(8,128)(2,1)}, f32[1,384]{1,0:T(1,128)}) custom-call(s32[2]{0:T(128)} %lengths_ref.25, s32[1]{0:T(128)} %constant.264.clone.1.which_ref, bf16[3,192,768]{2,1,0:T(8,128)(2,1)} %bitcast.102, bf16[2,1024,256]{2,1,0:T(8,128)(2,1)} %get-tuple-element.151.refs_1_, ...), custom_call_target="tpu_custom_call" | custom-call | flops 1000 | bytes 1000 | tf_op jit(solution)/shard_map/attend_bwd/pallas_call | solution.py:91
  146.2 1.2 copy-done.11
  147.4 0.8 fusion.12
  148.3 1.3 convert_add_fusion
  149.8 0.9 copy-done.27
  150.7 0.8 collective-permute-start.24
  151.9 13.8 %attend_bwd.3 = (bf16[2,256,768]{2,1,0:T(8,128)(2,1)}, bf16[2,256,768]{2,1,0:T(8,128)(2,1)}, bf16[3,1024,192]{2,1,0:T(8,128)(2,1)}, f32[1,384]{1,0:T(1,128)}) custom-call(s32[2]{0:T(128)} %lengths_ref.25, s32[1]{0:T(128)} %constant.265.clone.1.which_ref, bf16[3,192,768]{2,1,0:T(8,128)(2,1)} %bitcast.103, bf16[2,1024,256]{2,1,0:T(8,128)(2,1)} %get-tuple-element.151.refs_1_, ...), custom_call_target="tpu_custom_call" | custom-call | flops 1000 | bytes 1000 | tf_op jit(solution)/shard_map/attend_bwd/pallas_call | solution.py:91
  165.7 0.7 copy-done.18
  166.5 2.1 collective-permute-done.23
  168.8 9.5 %project_grads.1 = (bf16[576,384]{1,0:T(8,128)(2,1)}, bf16[584,384]{1,0:T(8,128)(2,1)}, f32[1,384]{1,0:T(1,128)}) custom-call(s32[2]{0:T(128)} %lengths_ref.25, s32[1]{0:T(128)} %constant.264.clone.1.which_ref, bf16[2,1024,768]{2,1,0:T(8,128)(2,1)} %refs_0_.9, bf16[3,1024,192]{2,1,0:T(8,128)(2,1)} %get-tuple-element.213.refs_1_, ...), custom_call_target="tpu_custom_call" | custom-call | flops 1000 | bytes 1000 | tf_op jit(solution)/shard_map/project_grads/pallas_call | solution.py:91
  178.3 1.8 collective-permute-start.29
  180.3 1.9 fusion.6
  182.4 8.6 %collective-permute-done.29 = bf16[584,384]{1,0:T(8,128)(2,1)S(1)} collective-permute-done((bf16[584,384]{1,0:T(8,128)(2,1)}, bf16[584,384]{1,0:T(8,128)(2,1)S(1)}, u32[]{:S(2)}, u32[]{:S(2)}) %collective-permute-start.29) | collective-permute-done | bytes 448544 | tf_op jit(solution)/shard_map/ppermute | solution.py:599
  191.0 1.0 fusion.15
  192.0 5.4 %collective-permute-start.35 = (bf16[96,768]{1,0:T(8,128)(2,1)S(1)}, bf16[96,768]{1,0:T(8,128)(2,1)S(1)}, u32[]{:S(2)}, u32[]{:S(2)}) collective-permute-start(bf16[96,768]{1,0:T(8,128)(2,1)S(1)} %fusion.15), channel_id=1, source_target_pairs={{0,16},{4,20},{8,24},{12,28},{16,0},{20,4},{24,8},{28,12},{1,17},{... | collective-permute-start | bytes 442376 | tf_op jit(solution)/shard_map/ppermute | solution.py:599
  197.4 1.9 fusion.9
  199.7 2.0 collective-permute-start.30
  201.7 1.7 collective-permute-start.33
  203.5 10.6 %collective-permute-done.30 = bf16[290,384]{1,0:T(8,128)(2,1)S(1)} collective-permute-done((bf16[290,384]{1,0:T(8,128)(2,1)S(1)}, bf16[290,384]{1,0:T(8,128)(2,1)S(1)}, u32[]{:S(2)}, u32[]{:S(2)}) %collective-permute-start.30) | collective-permute-done | bytes 222752 | tf_op jit(solution)/shard_map/ppermute | solution.py:599
  214.6 1.7 bitcast_add_fusion.3
  216.3 4.8 %collective-permute-done.31 = bf16[146,384]{1,0:T(8,128)(2,1)S(1)} collective-permute-done((bf16[146,384]{1,0:T(8,128)(2,1)S(1)}, bf16[146,384]{1,0:T(8,128)(2,1)S(1)}, u32[]{:S(2)}, u32[]{:S(2)}) %collective-permute-start.31) | collective-permute-done | bytes 112160 | tf_op jit(solution)/shard_map/ppermute | solution.py:599
  221.2 0.7 reshape.179
  222.0 0.7 pad_maximum_fusion.3
  222.7 1.0 slice.199
  223.8 1.1 fusion.10
  224.9 0.7 subtract_convert_fusion
  225.8 1.5 fusion.7
  227.3 0.9 pad_maximum_fusion
  228.3 6.1 %collective-permute-done.34 = bf16[136,768]{1,0:T(8,128)(2,1)S(1)} collective-permute-done((bf16[136,768]{1,0:T(8,128)(2,1)S(1)}, bf16[136,768]{1,0:T(8,128)(2,1)S(1)}, u32[]{:S(2)}, u32[]{:S(2)}) %collective-permute-start.34) | collective-permute-done | bytes 208928 | tf_op jit(solution)/shard_map/ppermute | solution.py:599
  234.3 1.1 fusion.11
  235.4 0.7 slice.210
  236.2 0.6 slice.204
  236.8 0.7 slice_reduce_fusion
  (139 shorter events, 6.1 us)
Async XLA Ops:
  5.6 23.2 %collective-permute-start.2 = (bf16[384,768]{1,0:T(8,128)(2,1)}, bf16[384,768]{1,0:T(8,128)(2,1)S(1)}, u32[]{:S(2)}, u32[]{:S(2)}) collective-permute-start(bf16[384,768]{1,0:T(8,128)(2,1)} %get-tuple-element.129), channel_id=1, source_target_pairs={{0,2},{1,3},{2,0},{3,1},{4,6},{5,7},{6,4},{7,5},{8,10},{9,11},{10,... | collective-permute-start | bytes 1769480 | tf_op jit(solution)/shard_map/ppermute | solution.py:599
  8.6 16.7 %collective-permute-start = (bf16[200,768]{1,0:T(8,128)(2,1)}, bf16[200,768]{1,0:T(8,128)(2,1)S(1)}, u32[]{:S(2)}, u32[]{:S(2)}) collective-permute-start(bf16[200,768]{1,0:T(8,128)(2,1)} %get-tuple-element.128.refs_6_.refs_2_.refs_11_), channel_id=1, source_target_pairs={{0,1},{1,0},{2,3},{3,2},{4,5},{5,4},{6,7},{7,6},{8,9},{9,8},{10,11... | collective-permute-start | bytes 921608 | tf_op jit(solution)/shard_map/ppermute | solution.py:599
  8.7 20.1 %collective-permute-start.1 = (bf16[200,768]{1,0:T(8,128)(2,1)}, bf16[200,768]{1,0:T(8,128)(2,1)S(1)}, u32[]{:S(2)}, u32[]{:S(2)}) collective-permute-start(bf16[200,768]{1,0:T(8,128)(2,1)} %get-tuple-element.128.refs_6_.refs_2_.refs_11_), channel_id=1, source_target_pairs={{0,2},{1,3},{2,0},{3,1},{4,6},{5,7},{6,4},{7,5},{8,10},{9,11},{10,... | collective-permute-start | bytes 921608 | tf_op jit(solution)/shard_map/ppermute | solution.py:599
  8.8 31.1 %copy-start.28 = (bf16[384,768]{1,0:T(8,128)(2,1)S(1)}, bf16[384,768]{1,0:T(8,128)(2,1)}, u32[]{:S(2)}) copy-start(bf16[384,768]{1,0:T(8,128)(2,1)} %get-tuple-element.145) | copy-start | bytes 1769476
  8.8 32.5 %copy-start.20 = (bf16[768]{0:T(1024)(128)(2,1)S(1)}, bf16[768]{0:T(1024)(128)(2,1)}, u32[]{:S(2)}) copy-start(bf16[768]{0:T(1024)(128)(2,1)} %param.21) | copy-start | bytes 4612
  8.8 32.7 %copy-start.21 = (bf16[768]{0:T(1024)(128)(2,1)S(1)}, bf16[768]{0:T(1024)(128)(2,1)}, u32[]{:S(2)}) copy-start(bf16[768]{0:T(1024)(128)(2,1)} %param.22) | copy-start | bytes 4612
  8.8 32.9 %copy-start.22 = (bf16[768]{0:T(1024)(128)(2,1)S(1)}, bf16[768]{0:T(1024)(128)(2,1)}, u32[]{:S(2)}) copy-start(bf16[768]{0:T(1024)(128)(2,1)} %param.23) | copy-start | bytes 4612
  8.8 33.1 %copy-start.23 = (bf16[768]{0:T(1024)(128)(2,1)S(1)}, bf16[768]{0:T(1024)(128)(2,1)}, u32[]{:S(2)}) copy-start(bf16[768]{0:T(1024)(128)(2,1)} %param.27) | copy-start | bytes 4612
  8.8 33.3 %copy-start.24 = (bf16[768]{0:T(1024)(128)(2,1)S(1)}, bf16[768]{0:T(1024)(128)(2,1)}, u32[]{:S(2)}) copy-start(bf16[768]{0:T(1024)(128)(2,1)} %param.28) | copy-start | bytes 4612
  8.8 33.5 %copy-start.25 = (bf16[768]{0:T(1024)(128)(2,1)S(1)}, bf16[768]{0:T(1024)(128)(2,1)}, u32[]{:S(2)}) copy-start(bf16[768]{0:T(1024)(128)(2,1)} %param.29) | copy-start | bytes 4612
  8.9 33.7 %copy-start = (s32[2]{0:T(128)S(1)}, s32[2]{0:T(128)}, u32[]{:S(2)}) copy-start(s32[2]{0:T(128)} %lengths_ref.25) | copy-start | bytes 28
  28.8 11.1 %collective-permute-start.6 = (bf16[200,768]{1,0:T(8,128)(2,1)S(1)}, bf16[200,768]{1,0:T(8,128)(2,1)S(1)}, u32[]{:S(2)}, u32[]{:S(2)}) collective-permute-start(bf16[200,768]{1,0:T(8,128)(2,1)S(1)} %collective-permute-done.1.refs_8_.refs_2_.refs_13_), channel_id=1, source_target_pairs={{0,1},{1,0},{2,3},{3,2},{4,5},{5,4},{6,7},{7,6},{8,9},{9,8},{10,11... | collective-permute-start | bytes 921608 | tf_op jit(solution)/shard_map/ppermute | solution.py:599
  28.8 2.3 collective-permute-start.3
  29.3 8.0 %collective-permute-start.4 = (bf16[2,192,256]{2,1,0:T(8,128)(2,1)}, bf16[2,192,256]{2,1,0:T(8,128)(2,1)S(1)}, u32[]{:S(2)}, u32[]{:S(2)}) collective-permute-start(bf16[2,192,256]{2,1,0:T(8,128)(2,1)} %get-tuple-element.132), channel_id=1, source_target_pairs={{0,2},{1,3},{2,0},{3,1},{4,6},{5,7},{6,4},{7,5},{8,10},{9,11},{10,... | collective-permute-start | bytes 589832 | tf_op jit(solution)/shard_map/ppermute | solution.py:599
  31.0 8.9 %collective-permute-start.5 = (bf16[2,192,256]{2,1,0:T(8,128)(2,1)}, bf16[2,192,256]{2,1,0:T(8,128)(2,1)S(1)}, u32[]{:S(2)}, u32[]{:S(2)}) collective-permute-start(bf16[2,192,256]{2,1,0:T(8,128)(2,1)} %get-tuple-element.133), channel_id=1, source_target_pairs={{0,3},{1,2},{2,1},{3,0},{4,7},{5,6},{6,5},{7,4},{8,11},{9,10},{10,... | collective-permute-start | bytes 589832 | tf_op jit(solution)/shard_map/ppermute | solution.py:599
  39.9 15.7 %collective-permute-start.9 = (bf16[384,768]{1,0:T(8,128)(2,1)S(1)}, bf16[384,768]{1,0:T(8,128)(2,1)S(1)}, u32[]{:S(2)}, u32[]{:S(2)}) collective-permute-start(bf16[384,768]{1,0:T(8,128)(2,1)S(1)} %copy-done.28), channel_id=1, source_target_pairs={{0,2},{1,3},{2,0},{3,1},{4,6},{5,7},{6,4},{7,5},{8,10},{9,11},{10,... | collective-permute-start | bytes 1769480 | tf_op jit(solution)/shard_map/ppermute | solution.py:599
  46.7 10.7 %collective-permute-start.7 = (bf16[512,768]{1,0:T(8,128)(2,1)S(1)}, bf16[512,768]{1,0:T(8,128)(2,1)S(1)}, u32[]{:S(2)}, u32[]{:S(2)}) collective-permute-start(bf16[512,768]{1,0:T(8,128)(2,1)S(1)} %get-tuple-element.143.refs_0_), channel_id=1, source_target_pairs={{0,1},{1,0},{2,3},{3,2},{4,5},{5,4},{6,7},{7,6},{8,9},{9,8},{10,11... | collective-permute-start | bytes 2359304 | tf_op jit(solution)/shard_map/ppermute | solution.py:599
  47.3 17.8 %collective-permute-start.8 = (bf16[384,768]{1,0:T(8,128)(2,1)S(1)}, bf16[384,768]{1,0:T(8,128)(2,1)S(1)}, u32[]{:S(2)}, u32[]{:S(2)}) collective-permute-start(bf16[384,768]{1,0:T(8,128)(2,1)S(1)} %collective-permute-done.2.refs_3_.refs_6_), channel_id=1, source_target_pairs={{0,4},{4,0},{8,12},{12,8},{16,20},{20,16},{24,28},{28,24},{1,5},{5... | collective-permute-start | bytes 1769480 | tf_op jit(solution)/shard_map/ppermute | solution.py:599
  55.6 15.1 %collective-permute-start.10 = (bf16[384,768]{1,0:T(8,128)(2,1)S(1)}, bf16[384,768]{1,0:T(8,128)(2,1)S(1)}, u32[]{:S(2)}, u32[]{:S(2)}) collective-permute-start(bf16[384,768]{1,0:T(8,128)(2,1)S(1)} %collective-permute-done.9.refs_5_.refs_8_), channel_id=1, source_target_pairs={{0,8},{4,12},{8,0},{12,4},{16,24},{20,28},{24,16},{28,20},{1,9},{5... | collective-permute-start | bytes 1769480 | tf_op jit(solution)/shard_map/ppermute | solution.py:599
  77.7 2.4 collective-permute-start.11
  84.1 2.4 collective-permute-start.12
  96.7 2.4 collective-permute-start.13
  106.1 8.9 %collective-permute-start.17 = (bf16[2,200,768]{2,1,0:T(8,128)(2,1)}, bf16[2,200,768]{2,1,0:T(8,128)(2,1)S(1)}, u32[]{:S(2)}, u32[]{:S(2)}) collective-permute-start(bf16[2,200,768]{2,1,0:T(8,128)(2,1)} %get-tuple-element.170), channel_id=1, source_target_pairs={{0,1},{1,0},{2,3},{3,2},{4,5},{5,4},{6,7},{7,6},{8,9},{9,8},{10,11... | collective-permute-start | bytes 1843208 | tf_op jit(solution)/shard_map/ppermute | solution.py:599
  106.3 6.8 %copy-start.31 = (bf16[2,192,256]{2,1,0:T(8,128)(2,1)S(1)}, bf16[2,192,256]{2,1,0:T(8,128)(2,1)}, u32[]{:S(2)}) copy-start(bf16[2,192,256]{2,1,0:T(8,128)(2,1)} %get-tuple-element.165) | copy-start | bytes 589828
  106.3 6.9 %copy-start.30 = (bf16[2,192,256]{2,1,0:T(8,128)(2,1)S(1)}, bf16[2,192,256]{2,1,0:T(8,128)(2,1)}, u32[]{:S(2)}) copy-start(bf16[2,192,256]{2,1,0:T(8,128)(2,1)} %get-tuple-element.166) | copy-start | bytes 589828
  106.3 8.5 %copy-start.29 = (bf16[2,192,256]{2,1,0:T(8,128)(2,1)S(1)}, bf16[2,192,256]{2,1,0:T(8,128)(2,1)}, u32[]{:S(2)}) copy-start(bf16[2,192,256]{2,1,0:T(8,128)(2,1)} %get-tuple-element.167) | copy-start | bytes 589828
  111.3 16.4 %collective-permute-start.18 = (bf16[4,96,768]{2,1,0:T(8,128)(2,1)}, bf16[4,96,768]{2,1,0:T(8,128)(2,1)S(1)}, u32[]{:S(2)}, u32[]{:S(2)}) collective-permute-start(bf16[4,96,768]{2,1,0:T(8,128)(2,1)} %get-tuple-element.181), channel_id=1, source_target_pairs={{0,4},{4,0},{8,12},{12,8},{16,20},{20,16},{24,28},{28,24},{1,5},{5... | collective-permute-start | bytes 1769480 | tf_op jit(solution)/shard_map/ppermute | solution.py:599
  113.0 8.0 %collective-permute-start.14 = (bf16[2,192,256]{2,1,0:T(8,128)(2,1)S(1)}, bf16[2,192,256]{2,1,0:T(8,128)(2,1)S(1)}, u32[]{:S(2)}, u32[]{:S(2)}) collective-permute-start(bf16[2,192,256]{2,1,0:T(8,128)(2,1)S(1)} %copy-done.31), channel_id=1, source_target_pairs={{0,1},{1,0},{2,3},{3,2},{4,5},{5,4},{6,7},{7,6},{8,9},{9,8},{10,11... | collective-permute-start | bytes 589832 | tf_op jit(solution)/shard_map/ppermute | solution.py:599
  113.1 7.9 %collective-permute-start.15 = (bf16[2,192,256]{2,1,0:T(8,128)(2,1)S(1)}, bf16[2,192,256]{2,1,0:T(8,128)(2,1)S(1)}, u32[]{:S(2)}, u32[]{:S(2)}) collective-permute-start(bf16[2,192,256]{2,1,0:T(8,128)(2,1)S(1)} %copy-done.30), channel_id=1, source_target_pairs={{0,2},{1,3},{2,0},{3,1},{4,6},{5,7},{6,4},{7,5},{8,10},{9,11},{10,... | collective-permute-start | bytes 589832 | tf_op jit(solution)/shard_map/ppermute | solution.py:599
  114.7 9.4 %collective-permute-start.16 = (bf16[2,192,256]{2,1,0:T(8,128)(2,1)S(1)}, bf16[2,192,256]{2,1,0:T(8,128)(2,1)S(1)}, u32[]{:S(2)}, u32[]{:S(2)}) collective-permute-start(bf16[2,192,256]{2,1,0:T(8,128)(2,1)S(1)} %copy-done.29), channel_id=1, source_target_pairs={{0,3},{1,2},{2,1},{3,0},{4,7},{5,6},{6,5},{7,4},{8,11},{9,10},{10,... | collective-permute-start | bytes 589832 | tf_op jit(solution)/shard_map/ppermute | solution.py:599
  114.9 31.1 %collective-permute-start.21 = (bf16[4,96,768]{2,1,0:T(8,128)(2,1)}, bf16[4,96,768]{2,1,0:T(8,128)(2,1)S(1)}, u32[]{:S(2)}, u32[]{:S(2)}) collective-permute-start(bf16[4,96,768]{2,1,0:T(8,128)(2,1)} %get-tuple-element.191), channel_id=1, source_target_pairs={{0,4},{4,0},{8,12},{12,8},{16,20},{20,16},{24,28},{28,24},{1,5},{5... | collective-permute-start | bytes 1769480 | tf_op jit(solution)/shard_map/ppermute | solution.py:599
  115.4 12.3 %copy-start.10 = (bf16[4,96,768]{2,1,0:T(8,128)(2,1)S(1)}, bf16[4,96,768]{2,1,0:T(8,128)(2,1)}, u32[]{:S(2)}) copy-start(bf16[4,96,768]{2,1,0:T(8,128)(2,1)} %get-tuple-element.180) | copy-start | bytes 1769476
  121.0 8.7 %copy-start.2 = (bf16[2,192,256]{2,1,0:T(8,128)(2,1)}, bf16[2,192,256]{2,1,0:T(8,128)(2,1)S(1)}, u32[]{:S(2)}) copy-start(bf16[2,192,256]{2,1,0:T(8,128)(2,1)S(1)} %collective-permute-done.14.refs_7_) | copy-start | bytes 589828
  121.0 8.7 %copy-start.3 = (bf16[2,192,256]{2,1,0:T(8,128)(2,1)}, bf16[2,192,256]{2,1,0:T(8,128)(2,1)S(1)}, u32[]{:S(2)}) copy-start(bf16[2,192,256]{2,1,0:T(8,128)(2,1)S(1)} %collective-permute-done.15.refs_8_) | copy-start | bytes 589828
  124.1 5.6 %copy-start.4 = (bf16[2,192,256]{2,1,0:T(8,128)(2,1)}, bf16[2,192,256]{2,1,0:T(8,128)(2,1)S(1)}, u32[]{:S(2)}) copy-start(bf16[2,192,256]{2,1,0:T(8,128)(2,1)S(1)} %collective-permute-done.16.refs_9_) | copy-start | bytes 589828
  124.1 21.9 %collective-permute-start.19 = (bf16[496,768]{1,0:T(8,128)(2,1)}, bf16[496,768]{1,0:T(8,128)(2,1)S(1)}, u32[]{:S(2)}, u32[]{:S(2)}) collective-permute-start(bf16[496,768]{1,0:T(8,128)(2,1)} %get-tuple-element.189), channel_id=1, source_target_pairs={{0,8},{4,12},{8,0},{12,4},{16,24},{20,28},{24,16},{28,20},{1,9},{5... | collective-permute-start | bytes 2285576 | tf_op jit(solution)/shard_map/ppermute | solution.py:599
  127.9 18.2 %collective-permute-start.20 = (bf16[4,96,768]{2,1,0:T(8,128)(2,1)S(1)}, bf16[4,96,768]{2,1,0:T(8,128)(2,1)S(1)}, u32[]{:S(2)}, u32[]{:S(2)}) collective-permute-start(bf16[4,96,768]{2,1,0:T(8,128)(2,1)S(1)} %add_convert_fusion), channel_id=1, source_target_pairs={{0,2},{1,3},{2,0},{3,1},{4,6},{5,7},{6,4},{7,5},{8,10},{9,11},{10,... | collective-permute-start | bytes 1769480 | tf_op jit(solution)/shard_map/ppermute | solution.py:599
  146.0 2.2 copy-start.13
  146.1 2.2 copy-start.15
  146.1 3.6 %collective-permute-start.22 = (bf16[2,256,768]{2,1,0:T(8,128)(2,1)}, bf16[2,256,768]{2,1,0:T(8,128)(2,1)S(1)}, u32[]{:S(2)}, u32[]{:S(2)}) collective-permute-start(bf16[2,256,768]{2,1,0:T(8,128)(2,1)} %get-tuple-element.192), channel_id=1, source_target_pairs={{0,1},{1,0},{2,3},{3,2},{4,5},{5,4},{6,7},{7,6},{8,9},{9,8},{10,11... | collective-permute-start | bytes 2359304 | tf_op jit(solution)/shard_map/ppermute | solution.py:599
  150.7 17.8 %collective-permute-start.23 = (bf16[480,768]{1,0:T(8,128)(2,1)S(1)}, bf16[480,768]{1,0:T(8,128)(2,1)}, u32[]{:S(2)}, u32[]{:S(2)}) collective-permute-start(bf16[480,768]{1,0:T(8,128)(2,1)S(1)} %copy-done.27), channel_id=1, source_target_pairs={{0,8},{4,12},{8,0},{12,4},{16,24},{20,28},{24,16},{28,20},{1,9},{5... | collective-permute-start | bytes 2211848 | tf_op jit(solution)/shard_map/ppermute | solution.py:599
  150.7 15.0 %collective-permute-start.24 = (bf16[256,768]{1,0:T(8,128)(2,1)S(1)}, bf16[256,768]{1,0:T(8,128)(2,1)S(1)}, u32[]{:S(2)}, u32[]{:S(2)}) collective-permute-start(bf16[256,768]{1,0:T(8,128)(2,1)S(1)} %pad_maximum_fusion.1), channel_id=1, source_target_pairs={{0,4},{4,0},{8,12},{12,8},{16,20},{20,16},{24,28},{28,24},{1,5},{5... | collective-permute-start | bytes 1179656 | tf_op jit(solution)/shard_map/ppermute | solution.py:599
  151.5 14.2 %collective-permute-start.25 = (bf16[256,768]{1,0:T(8,128)(2,1)S(1)}, bf16[256,768]{1,0:T(8,128)(2,1)S(1)}, u32[]{:S(2)}, u32[]{:S(2)}) collective-permute-start(bf16[256,768]{1,0:T(8,128)(2,1)S(1)} %fusion.5), channel_id=1, source_target_pairs={{0,2},{1,3},{2,0},{3,1},{4,6},{5,7},{6,4},{7,5},{8,10},{9,11},{10,... | collective-permute-start | bytes 1179656 | tf_op jit(solution)/shard_map/ppermute | solution.py:599
  168.5 11.7 %collective-permute-start.26 = (bf16[2,256,768]{2,1,0:T(8,128)(2,1)}, bf16[2,256,768]{2,1,0:T(8,128)(2,1)}, u32[]{:S(2)}, u32[]{:S(2)}) collective-permute-start(bf16[2,256,768]{2,1,0:T(8,128)(2,1)} %get-tuple-element.212), channel_id=1, source_target_pairs={{0,1},{1,0},{2,3},{3,2},{4,5},{5,4},{6,7},{7,6},{8,9},{9,8},{10,11... | collective-permute-start | bytes 2359304 | tf_op jit(solution)/shard_map/ppermute | solution.py:599
  168.5 9.8 %collective-permute-start.28 = (bf16[2,96,768]{2,1,0:T(8,128)(2,1)}, bf16[2,96,768]{2,1,0:T(8,128)(2,1)}, u32[]{:S(2)}, u32[]{:S(2)}) collective-permute-start(bf16[2,96,768]{2,1,0:T(8,128)(2,1)} %fusion.12), channel_id=1, source_target_pairs={{0,8},{4,12},{8,0},{12,4},{16,24},{20,28},{24,16},{28,20},{1,9},{5... | collective-permute-start | bytes 884744 | tf_op jit(solution)/shard_map/ppermute | solution.py:599
  168.8 11.3 %copy-start.12 = (bf16[4,96,768]{2,1,0:T(8,128)(2,1)S(1)}, bf16[4,96,768]{2,1,0:T(8,128)(2,1)}, u32[]{:S(2)}) copy-start(bf16[4,96,768]{2,1,0:T(8,128)(2,1)} %get-tuple-element.193) | copy-start | bytes 1769476
  168.8 11.3 %copy-start.14 = (bf16[4,96,768]{2,1,0:T(8,128)(2,1)S(1)}, bf16[4,96,768]{2,1,0:T(8,128)(2,1)}, u32[]{:S(2)}) copy-start(bf16[4,96,768]{2,1,0:T(8,128)(2,1)} %copy-done.13) | copy-start | bytes 1769476
  168.8 11.3 %copy-start.16 = (bf16[4,96,768]{2,1,0:T(8,128)(2,1)S(1)}, bf16[4,96,768]{2,1,0:T(8,128)(2,1)}, u32[]{:S(2)}) copy-start(bf16[4,96,768]{2,1,0:T(8,128)(2,1)} %copy-done.15) | copy-start | bytes 1769476
  178.3 2.0 copy-start.6
  178.3 12.7 %collective-permute-start.29 = (bf16[584,384]{1,0:T(8,128)(2,1)}, bf16[584,384]{1,0:T(8,128)(2,1)S(1)}, u32[]{:S(2)}, u32[]{:S(2)}) collective-permute-start(bf16[584,384]{1,0:T(8,128)(2,1)} %get-tuple-element.220), channel_id=1, source_target_pairs={{0,8},{4,12},{8,0},{12,4},{16,24},{20,28},{24,16},{28,20},{1,9},{5... | collective-permute-start | bytes 1345544 | tf_op jit(solution)/shard_map/ppermute | solution.py:599
  180.2 17.2 %copy-start.8 = (bf16[480,768]{1,0:T(8,128)(2,1)S(1)}, bf16[480,768]{1,0:T(8,128)(2,1)}, u32[]{:S(2)}) copy-start(bf16[480,768]{1,0:T(8,128)(2,1)} %get-tuple-element.227) | copy-start | bytes 2211844
  180.2 19.1 %copy-start.19 = (bf16[256,768]{1,0:T(8,128)(2,1)S(1)}, bf16[256,768]{1,0:T(8,128)(2,1)}, u32[]{:S(2)}) copy-start(bf16[256,768]{1,0:T(8,128)(2,1)} %copy-done.18) | copy-start | bytes 1179652
  182.2 43.6 %collective-permute-start.27 = (bf16[256,768]{1,0:T(8,128)(2,1)}, bf16[256,768]{1,0:T(8,128)(2,1)}, u32[]{:S(2)}, u32[]{:S(2)}) collective-permute-start(bf16[256,768]{1,0:T(8,128)(2,1)} %fusion.6), channel_id=1, source_target_pairs={{0,2},{1,3},{2,0},{3,1},{4,6},{5,7},{6,4},{7,5},{8,10},{9,11},{10,... | collective-permute-start | bytes 1179656 | tf_op jit(solution)/shard_map/ppermute | solution.py:599
  192.0 22.6 %collective-permute-start.35 = (bf16[96,768]{1,0:T(8,128)(2,1)S(1)}, bf16[96,768]{1,0:T(8,128)(2,1)S(1)}, u32[]{:S(2)}, u32[]{:S(2)}) collective-permute-start(bf16[96,768]{1,0:T(8,128)(2,1)S(1)} %fusion.15), channel_id=1, source_target_pairs={{0,16},{4,20},{8,24},{12,28},{16,0},{20,4},{24,8},{28,12},{1,17},{... | collective-permute-start | bytes 442376 | tf_op jit(solution)/shard_map/ppermute | solution.py:599
  197.4 2.2 copy-start.26
  197.4 2.2 copy-start.17
  199.3 24.5 %collective-permute-start.32 = (bf16[2,120,768]{2,1,0:T(8,128)(2,1)}, bf16[2,120,768]{2,1,0:T(8,128)(2,1)}, u32[]{:S(2)}, u32[]{:S(2)}) collective-permute-start(bf16[2,120,768]{2,1,0:T(8,128)(2,1)} %fusion.9), channel_id=1, source_target_pairs={{0,4},{4,0},{8,12},{12,8},{16,20},{20,16},{24,28},{28,24},{1,5},{5... | collective-permute-start | bytes 1105928 | tf_op jit(solution)/shard_map/ppermute | solution.py:599
  199.7 14.4 %collective-permute-start.30 = (bf16[290,384]{1,0:T(8,128)(2,1)S(1)}, bf16[290,384]{1,0:T(8,128)(2,1)S(1)}, u32[]{:S(2)}, u32[]{:S(2)}) collective-permute-start(bf16[290,384]{1,0:T(8,128)(2,1)S(1)} %pad_maximum_fusion.4), channel_id=1, source_target_pairs={{0,4},{4,0},{8,12},{12,8},{16,20},{20,16},{24,28},{28,24},{1,5},{5... | collective-permute-start | bytes 668168 | tf_op jit(solution)/shard_map/ppermute | solution.py:599
  201.7 21.0 %collective-permute-start.33 = (bf16[256,768]{1,0:T(8,128)(2,1)S(1)}, bf16[256,768]{1,0:T(8,128)(2,1)}, u32[]{:S(2)}, u32[]{:S(2)}) collective-permute-start(bf16[256,768]{1,0:T(8,128)(2,1)S(1)} %pad_maximum_fusion.2), channel_id=1, source_target_pairs={{0,2},{1,3},{2,0},{3,1},{4,6},{5,7},{6,4},{7,5},{8,10},{9,11},{10,... | collective-permute-start | bytes 1179656 | tf_op jit(solution)/shard_map/ppermute | solution.py:599
  214.2 9.5 %copy-start.9 = (bf16[480,768]{1,0:T(8,128)(2,1)S(1)}, bf16[480,768]{1,0:T(8,128)(2,1)}, u32[]{:S(2)}) copy-start(bf16[480,768]{1,0:T(8,128)(2,1)} %get-tuple-element.227) | copy-start | bytes 2211844
  214.2 6.9 %collective-permute-start.31 = (bf16[146,384]{1,0:T(8,128)(2,1)S(1)}, bf16[146,384]{1,0:T(8,128)(2,1)S(1)}, u32[]{:S(2)}, u32[]{:S(2)}) collective-permute-start(bf16[146,384]{1,0:T(8,128)(2,1)S(1)} %pad_maximum_fusion.6), channel_id=1, source_target_pairs={{0,16},{4,20},{8,24},{12,28},{16,0},{20,4},{24,8},{28,12},{1,17},{... | collective-permute-start | bytes 336392 | tf_op jit(solution)/shard_map/ppermute | solution.py:599
  221.9 3.9 %copy-start.1 = (f32[512,768]{1,0:T(8,128)S(1)}, f32[512,768]{1,0:T(8,128)}, u32[]{:S(2)}) copy-start(f32[512,768]{1,0:T(8,128)} %get-tuple-element.210) | copy-start | bytes 4718596
  221.9 3.9 %copy-start.7 = (bf16[2,256,768]{2,1,0:T(8,128)(2,1)S(1)}, bf16[2,256,768]{2,1,0:T(8,128)(2,1)}, u32[]{:S(2)}) copy-start(bf16[2,256,768]{2,1,0:T(8,128)(2,1)} %get-tuple-element.211) | copy-start | bytes 2359300
  225.7 8.7 %collective-permute-start.34 = (bf16[136,768]{1,0:T(8,128)(2,1)S(1)}, bf16[136,768]{1,0:T(8,128)(2,1)S(1)}, u32[]{:S(2)}, u32[]{:S(2)}) collective-permute-start(bf16[136,768]{1,0:T(8,128)(2,1)S(1)} %pad_maximum_fusion.5), channel_id=1, source_target_pairs={{0,16},{4,20},{8,24},{12,28},{16,0},{20,4},{24,8},{28,12},{1,17},{... | collective-permute-start | bytes 626696 | tf_op jit(solution)/shard_map/ppermute | solution.py:599
  (4 other events, 4.7 us)
where the time goes:
time: 238 us; the launch traced here: 237 us
  Pallas kernels  110 us (46%)
  waiting for transfers between devices  68.6 us (29%)
  starting transfers between devices  32.1 us (13%)
  other arithmetic  15.6 us (7%)
  local copies, waits for them, and re-layouts  9.51 us (4%)
    pallas_call x13, Pallas kernels, call(): pl.pallas_call(kernel, out_shape=[pltpu.HBM(o.shape, o.dtype) if i in far...  110 us
    ppermute x36, waiting for transfers between devices, swap(): return lax.ppermute(x, axis, [(i, i ^ bit) for i in range(size)])  68.6 us
    ppermute x36, starting transfers between devices, swap(): return lax.ppermute(x, axis, [(i, i ^ bit) for i in range(size)])  32.1 us
    add x5, other arithmetic, summed(): return sum((p.astype(f32) for p in parts))  5.24 us
  transfers between devices with their start and end apart: 36, of which 15 were waited for; matrix products, arithmetic and copies ran while one was open for 7% of the time, Pallas kernels for 33%

commit v1 on v0

--- a/solution.py
+++ b/solution.py
@@ -324,35 +324,32 @@
     return call("attend_bwd", attend_bwd_kernel, info, ins, outs, scratch, which=which)
 
 
-def project_grads_kernel(info, x_in, low0, low1, db0, db1, keep, send, db_ref, dw, *, parts):
+def project_grads_kernel(info, x_in, low0, low1, db0, db1, keep, send, db_ref, dw, pair, *, parts):
+    x = x_in()
     lows = (low0(), low1())
-    x = x_in()
     _, d, width = dw.shape
     step = 256
-    for i in range(3):
-        for m in range(0, d, step):
-            cols = slice(m, m + step)
-            dw[i, cols, :] = mm(x[0, :, cols], lows[0][i], TN) + mm(x[1, :, cols], lows[1][i], TN)
+
+    def chunk(m, carry):
+        cols = pl.ds(pl.multiple_of(m * step, step), step)
+        x_t = (x[0, :, cols].T, x[1, :, cols].T)
+        for i in range(3):
+            dw[i, cols, :] = mm(x_t[0], lows[0][i]) + mm(x_t[1], lows[1][i])
+        return carry
+
+    lax.fori_loop(0, d // step, chunk, 0)
     rows = d // parts
     half = 3 * rows // 2
     for b in range(parts):
         flat = dw[:, b * rows : (b + 1) * rows, :].reshape(3 * rows, width)
         flat = jnp.concatenate([flat[0:half], flat[half : 2 * half]], axis=1).astype(bf16)
-        at = ((b >> 2) * 2 + (b & 1)) * half
-        mine = ((b >> 1) & 1) == info[4]
-
-        @pl.when(mine)
-        def _():
-            keep.src[at : at + half, :] = flat
-
-        @pl.when(jnp.logical_not(mine))
-        def _():
-            send.src[at : at + half, :] = flat
-
+        pair[(b & 1) ^ info[3], (b >> 1) * half : (b // 2 + 1) * half, :] = flat
+    n = keep.src.shape[0]
+    send.src[0:n, :] = pair[1]
+    keep.src[...] = pair[0]
     db = db0[...] + db1[...]
     db_ref[...] = db
     high = db.astype(bf16)
-    n = keep.src.shape[0]
     send.src[n : n + 8, :] = jnp.concatenate(
         [high, (db - high.astype(f32)).astype(bf16), jnp.zeros((6, 2 * width), bf16)], axis=0
     )
@@ -533,11 +530,11 @@
     osend.src[1, width : width + 8, :] = (both - high.astype(f32)).astype(bf16)
 
 
-def down_grads_kernel(info, act0, act1, gs, gs2, far_keep, far_send, keep, send, scr, *, parts):
+def down_grads_kernel(info, act0, act1, gs, gs2, far_keep, keep, send, scr, *, parts):
     units = act0.shape[2]
     block = units // parts
     step = 384
-    for act, mine, theirs in ((act1, far_keep, far_send), (act0, keep, send)):
+    for k, (act, mine) in enumerate(((act1, far_keep), (act0, keep))):
 
         def chunk(m, carry):
             cols = pl.ds(pl.multiple_of(m * step, step), step)
@@ -548,10 +545,9 @@
             return carry
 
         lax.fori_loop(0, units // step, chunk, 0)
-        theirs.src[...] = scr[1]
-        theirs.start()
+        send.src[k] = scr[1]
         mine.src[...] = scr[0]
-        mine.start()
+    send.start()
 
 
 def up_grads_kernel(
@@ -727,18 +723,18 @@
     )
     got = swap(sib, "tensor", 1)
     block = units // parts
-    downs = call(
+    half_shape = (parts // 2, block, d)
+    down_far_keep, down_keep, down_send = call(
         "down_grads",
         down_grads_kernel,
         info,
         [act0, act1, gs_low, gs_low2],
-        [[SDS((parts // 2, block, d), bf16)]] * 4,
-        [pltpu.VMEM((2, parts // 2, block, d), bf16)],
+        [[SDS(half_shape, bf16)], [SDS(half_shape, bf16)], [SDS((2, *half_shape), bf16)]],
+        [pltpu.VMEM((2, *half_shape), bf16)],
         vmem=NEAR,
         parts=parts,
     )
-    down_far_keep, down_far_send, down_keep, down_send = downs
-    down_far_got = swap(down_far_send, "dp", 1)
+    down_got = swap(down_send, "dp", 1)
     gfi, g0, g1, g2, g3, okeep, osend, small1 = call(
         "first_back",
         first_back_kernel,
@@ -775,42 +771,49 @@
         width=width,
     )
     *gctx, up_far_send = after(*gctx, up_far_send)
-    down_far_sum = summed([down_far_keep, down_far_got]).astype(bf16)
-    *gctx, down_far_sum, up_far_keep = after(*gctx, down_far_sum, up_far_keep)
     up_far_got = swap(up_far_send, "dp", 2)
-    down_y = swap(down_far_sum, "tensor", 2)
-    down_got = swap(down_send, "dp", 1)
+    *gctx, up_far_keep = after(*gctx, up_far_keep)
     lows, biases, terms_of = [], [], []
     for s in range(batch):
         keep, send, low_grads, db = attend_bwd(s, info, w_t, *saved, gctx, d)
+        biases.append(db)
         if s == 0:
-            send, up_far_got, down_y, down_got = after(send, up_far_got, down_y, down_got)
+            send, up_far_got, down_got = after(send, up_far_got, down_got)
         else:
-            send, low_grads, up_got, up_more, far = after(send, low_grads, up_got, up_more, far)
+            send, low_grads, down_y, up_got, up_more, far = after(send, low_grads, down_y, up_got, up_more, far)
             terms_of[0].append(far)
         near = swap(send, "tensor", 1)
         in_sum = summed([keep[1], near[1]]).astype(bf16)
         terms_of.append([keep[0], near[0]])
-        lows.append(low_grads)
-        biases.append(db)
-        if s:
-            continue
-        shape = ([2] * (bits - 1)) + [block, d]
-        down_terms = [x.reshape(shape) for x in (down_keep, down_got, down_y)]
-        down_kept, down_next = halve_sum(down_terms, bits - 2, bit_of[1])
-        shape = ([2] * (bits - 1)) + [joint, d]
-        small = small + pair_sum(up_far_got, cut, 8)
-        terms = [x.reshape(shape) for x in (up_far_keep, up_far_got[:cut])]
-        up_far_kept, up_far_next = halve_sum(terms, bits - 2, bit_of[0])
-        up_far_rows = with_rows(up_far_next, small)
-        tied = after(down_next, up_far_rows, in_sum, up_send, *gctx)
-        (down_next, up_far_rows, in_sum, up_send), gctx = tied[:4], tied[4:]
-        up_got = swap(up_send, "dp", 2)
-        down_more = swap(down_next, "dp", 2)
-        up_more = swap(up_far_rows, "dp", 1)
-        far = swap(in_sum, "tensor", 2)
-    terms_of[1].append(swap(in_sum, "tensor", 2))
-    first_terms, last_terms = terms_of
+        if s == 0:
+            lows.append(low_grads)
+            down_sum = summed([down_far_keep, down_got[0]]).astype(bf16)
+            shape = ([2] * (bits - 1)) + [joint, d]
+            small = small + pair_sum(up_far_got, cut, 8)
+            terms = [x.reshape(shape) for x in (up_far_keep, up_far_got[:cut])]
+            up_far_kept, up_far_next = halve_sum(terms, bits - 2, bit_of[0])
+            up_far_rows = with_rows(up_far_next, small)
+            tied = after(down_sum, up_far_rows, in_sum, up_send, *gctx)
+            (down_sum, up_far_rows, in_sum, up_send), gctx = tied[:4], tied[4:]
+            down_y = swap(down_sum, "tensor", 2)
+            up_got = swap(up_send, "dp", 2)
+            up_more = swap(up_far_rows, "dp", 1)
+            far = swap(in_sum, "tensor", 2)
+    shape = ([2] * (bits - 1)) + [block, d]
+    down_terms = [x.reshape(shape) for x in (down_keep, down_got[1], down_y)]
+    down_kept, down_next = halve_sum(down_terms, bits - 2, bit_of[1])
+    at = up_far_next.size // d
+    small = small + pair_sum(up_more, at, 8)
+    small = jnp.concatenate([small[0:6], small[7:8], small[6:7]])
+    up_y_next = summed(up_far_kept + [up_more[:at].reshape(up_far_next.shape)]).astype(bf16)
+    up_y_rows = with_rows(up_y_next, small)
+    shape = ([2] * (bits - 1)) + [joint, d]
+    up_kept, up_next = halve_sum([x.reshape(shape) for x in (up_keep, up_got)], bits - 2, bit_of[0])
+    low_grads, down_next, up_y_rows, up_next = after(low_grads, down_next, up_y_rows, up_next)
+    lows.append(low_grads)
+    down_more = swap(down_next, "dp", 2)
+    up_y = swap(up_y_rows, "tensor", 2)
+    up_more = swap(up_next, "dp", 1)
     m = 3 * d // 4
     w_keep, w_send, db = call(
         "project_grads",
@@ -818,42 +821,32 @@
         info,
         [whole(inputs), *[whole(a) for a in lows], *biases],
         [[SDS((m, 2 * width), bf16)], [SDS((m + 8, 2 * width), bf16)], SDS((1, 2 * width), f32)],
-        [pltpu.VMEM((3, d, width), f32)],
+        [pltpu.VMEM((3, d, width), f32), pltpu.VMEM((2, m, 2 * width), bf16)],
         parts=parts,
     )
-    w_send, down_more = after(w_send, down_more)
+    w_send, down_more, up_y, up_more = after(w_send, down_more, up_y, up_more)
+    down_more, up_y, up_more, in_sum = after(down_more, up_y, up_more, in_sum)
+    got = swap(w_send, "dp", 1)
+    got, far = after(got, swap(in_sum, "tensor", 2))
+    terms_of[1].append(far)
     down_terms = down_kept + [down_more]
-    order = [1, 0] + list(range(2, bits))
-    row = 3 * (d // parts) // 2
-    got = swap(w_send, "dp", 2)
-    got, in_sum = after(got, in_sum)
-    got, up_got, up_more, *down_terms = after(got, up_got, up_more, *down_terms)
-    at = up_far_next.size // d
-    up_far_terms = up_far_kept + [up_more[:at].reshape(up_far_next.shape)]
-    small_x = pair_sum(up_more, at, 8)
-    small = small + small_x
-    small = jnp.concatenate([small[0:6], small[7:8], small[6:7]])
-    send = summed(up_far_terms).astype(bf16)
-    up_y_sent = with_rows(send, small)
-    up_y = swap(up_y_sent, "tensor", 2)
-    at = send.size // d
+    for i in range(2, bits):
+        down_terms, sent = halve(down_terms, bits - 1 - i, 1 << i, bit_of[i])
+    down_sum = summed(down_terms)
+    at = up_y_next.size // d
     small = jnp.concatenate([small[0:6], small[7:8], small[7:8]]) + pair_sum(up_y, at, 8)
-    shape = ([2] * (bits - 1)) + [joint, d]
-    terms, up_next = halve([x.reshape(shape) for x in (up_keep, up_got)], bits - 2, 1, bit_of[0])
-    terms.append(up_y[:at].reshape(send.shape))
+    terms = up_kept + [up_more, up_y[:at].reshape(up_y_next.shape)]
     for i in range(2, bits):
         terms, sent, more = halve_with(terms, terms[0].ndim - 3, small, "dp", 1 << i, bit_of[i])
         small = small + more
     up_sum = summed(terms)
     mine = small
-    for i in range(2, bits):
-        down_terms, sent = halve(down_terms, bits - 1 - i, 1 << i, bit_of[i])
-    down_sum = summed(down_terms)
+    row = 3 * (d // parts) // 2
     at = parts // 2 * row
     shape = ([2] * (bits - 1)) + [row, 2 * width]
     terms = [x.reshape(shape) for x in (w_keep, got[:at])]
     db = db + got[at : at + 1].astype(f32) + got[at + 1 : at + 2].astype(f32)
-    for i in order[1:]:
+    for i in range(1, bits):
         kept, sent, more = halve_with(terms, terms[0].ndim - 3, db, "dp", 1 << i, bit_of[i])
         terms, db = kept, db + more
     qkv_sum = summed(terms)
@@ -862,7 +855,7 @@
     db = db.reshape(2, width)
     input_list = [
         (summed(x) + gfi[s * rows : (s + 1) * rows]).astype(bf16)
-        for s, x in enumerate((first_terms, last_terms))
+        for s, x in enumerate(terms_of)
     ]
     return (
         outputs,

time: 238 us -> 234 us (0.983)
  local copies, waits for them, and re-layouts: 9.51 us -> 5.6 us
  other arithmetic: 15.6 us -> 18.2 us
    unnamed x69 -> x55, local copies, waits for them, and re-layouts: 4.02 us -> 1.12 us
    add x5 -> x4, other arithmetic: 5.24 us -> 4.18 us  [summed(): return sum((p.astype(f32) for p in parts))]
    ppermute x36 -> x35, waiting for transfers between devices: 68.6 us -> 67.7 us  [swap(): return lax.ppermute(x, axis, [(i, i ^ bit) for i in range(size)])]
    ppermute x36 -> x35, starting transfers between devices: 32.1 us -> 32.1 us  [swap(): return lax.ppermute(x, axis, [(i, i ^ bit) for i in range(size)])]
  transfers between devices with their start and end apart: 36 -> 35, of which waited for: 15 -> 18; matrix products, arithmetic and copies ran while one was open for 7% -> 8% of each run, Pallas kernels for 33% -> 33%
where the time goes in v1:
time: 234 us; the launch traced here: 233 us
  Pallas kernels  108 us (46%)
  waiting for transfers between devices  67.7 us (29%)
  starting transfers between devices  32.1 us (14%)
  other arithmetic  18.2 us (8%)
  local copies, waits for them, and re-layouts  5.6 us (2%)
    pallas_call x13, Pallas kernels, call(): pl.pallas_call(kernel, out_shape=[pltpu.HBM(o.shape, o.dtype) if i in far...  108 us
    ppermute x35, waiting for transfers between devices, swap(): return lax.ppermute(x, axis, [(i, i ^ bit) for i in range(size)])  67.7 us
    ppermute x35, starting transfers between devices, swap(): return lax.ppermute(x, axis, [(i, i ^ bit) for i in range(size)])  32.1 us
  transfers between devices with their start and end apart: 35, of which 18 were waited for; matrix products, arithmetic and copies ran while one was open for 8% of the time, Pallas kernels for 33%

profile of v1, /device:TPU:0, one launch (start us, length us, event | category | flops | bytes accessed | tf_op | source)
XLA Modules:
  0.0 233.2 jit_solution(13069089399806018834)
XLA Ops:
  0.6 1.3 broadcast_in_dim.3.refs_1_
  1.9 3.7 %prepare.1 = (bf16[200,768]{1,0:T(8,128)(2,1)}, bf16[384,768]{1,0:T(8,128)(2,1)}, bf16[384,768]{1,0:T(8,128)(2,1)}) custom-call(s32[2]{0:T(128)} %lengths_ref.25, s32[1]{0:T(128)} %constant.384.clone.1.which_ref, bf16[192,768]{1,0:T(8,128)(2,1)} %refs_0_.6, bf16[1,768]{1,0:T(2,128)(2,1)} %broadcast_in_dim.3.refs_1_, bf16[768,768]{1,0:T(8,128)(2,1)} %refs_4_.3, ...), custom_call_target="tpu_custom_call" | custom-call | flops 1000 | bytes 1000 | tf_op jit(solution)/shard_map/prepare/pallas_call | solution.py:91
  5.6 3.0 %collective-permute-start.2 = (bf16[384,768]{1,0:T(8,128)(2,1)}, bf16[384,768]{1,0:T(8,128)(2,1)S(1)}, u32[]{:S(2)}, u32[]{:S(2)}) collective-permute-start(bf16[384,768]{1,0:T(8,128)(2,1)} %get-tuple-element.131), channel_id=1, source_target_pairs={{0,2},{1,3},{2,0},{3,1},{4,6},{5,7},{6,4},{7,5},{8,10},{9,11},{10,... | collective-permute-start | bytes 1769480 | tf_op jit(solution)/shard_map/ppermute | solution.py:595
  8.8 16.4 %attend_fwd.1 = (bf16[2,1024,256]{2,1,0:T(8,128)(2,1)}, bf16[2,1024,256]{2,1,0:T(8,128)(2,1)}, bf16[2,1024,192]{2,1,0:T(8,128)(2,1)}, f32[2,4,8,256]{3,2,1,0:T(8...) custom-call(s32[2]{0:T(128)} %lengths_ref.25, ...), custom_call_target="tpu_custom_call" | custom-call | flops 1000 | bytes 1000 | tf_op jit(solution)/shard_map/attend_fwd/pallas_call | solution.py:91
  25.3 3.5 %collective-permute-done.1.refs_8_.refs_2_.refs_13_ = bf16[200,768]{1,0:T(8,128)(2,1)S(1)} collective-permute-done((bf16[200,768]{1,0:T(8,128)(2,1)}, bf16[200,768]{1,0:T(8,128)(2,1)S(1)}, u32[]{:S(2)}, u32[]{:S(2)}) %collective-permute-start.1) | collective-permute-done | bytes 307232 | tf_op jit(solution)/shard_map/ppermute | solution.py:595
  29.3 1.7 collective-permute-start.4
  31.0 6.2 %collective-permute-done.4.refs_4_.refs_9_ = bf16[2,192,256]{2,1,0:T(8,128)(2,1)S(1)} collective-permute-done((bf16[2,192,256]{2,1,0:T(8,128)(2,1)}, bf16[2,192,256]{2,1,0:T(8,128)(2,1)S(1)}, u32[]{:S(2)}, u32[]{:S(2)}) %collective-permute-start.4) | collective-permute-done | bytes 196640 | tf_op jit(solution)/shard_map/ppermute | solution.py:595
  37.3 2.7 %collective-permute-done.5.refs_5_.refs_10_ = bf16[2,192,256]{2,1,0:T(8,128)(2,1)S(1)} collective-permute-done((bf16[2,192,256]{2,1,0:T(8,128)(2,1)}, bf16[2,192,256]{2,1,0:T(8,128)(2,1)S(1)}, u32[]{:S(2)}, u32[]{:S(2)}) %collective-permute-start.5) | collective-permute-done | bytes 196640 | tf_op jit(solution)/shard_map/ppermute | solution.py:595
  40.0 1.5 collective-permute-start.9
  42.7 4.1 %first_norm.1 = (f32[512,768]{1,0:T(8,128)S(1)}, f32[512,1]{1,0:T(8,128)S(1)}, bf16[512,768]{1,0:T(8,128)(2,1)S(1)}) custom-call(s32[2]{0:T(128)S(1)} %copy-done, s32[1]{0:T(128)} %constant.384.clone.1.which_ref, bf16[2,1024,768]{2,1,0:T(8,128)(2,1)} %refs_0_.9, f32[6,768]{1,0:T(8,128)S(1)} %reshape.192.refs_1_.refs_0_, ...), custom_call_target="tpu_custom_call" | custom-call | flops 1000 | bytes 1000 | tf_op jit(solution)/shard_map/first_norm/pallas_call | solution.py:91
  47.3 1.5 collective-permute-start.8
  48.8 6.8 %collective-permute-done.9.refs_5_.refs_8_ = bf16[384,768]{1,0:T(8,128)(2,1)S(1)} collective-permute-done((bf16[384,768]{1,0:T(8,128)(2,1)S(1)}, bf16[384,768]{1,0:T(8,128)(2,1)S(1)}, u32[]{:S(2)}, u32[]{:S(2)}) %collective-permute-start.9) | collective-permute-done | bytes 589856 | tf_op jit(solution)/shard_map/ppermute | solution.py:595
  55.7 1.8 collective-permute-start.10
  57.5 7.6 %feed.2 = (bf16[2,512,768]{2,1,0:T(8,128)(2,1)S(1)}, bf16[2,512,768]{2,1,0:T(8,128)(2,1)S(1)}, f32[512,768]{1,0:T(8,128)S(1)}, f32[512,768]{1,0:T(8,128)S(1)}) custom-call(s32[2]{0:T(128)S(1)} %copy-done, s32[1]{0:T(128)} %constant.384.clone.1.which_ref, bf16[512,768]{1,0:T(8,128)(2,1)S(1)} %get-tuple-element.145.refs_0_, ...), custom_call_target="tpu_custom_call" | custom-call | flops 1000 | bytes 1000 | tf_op jit(solution)/shard_map/feed/pallas_call | solution.py:91
  65.1 5.6 %collective-permute-done.10.refs_6_.refs_9_ = bf16[384,768]{1,0:T(8,128)(2,1)S(1)} collective-permute-done((bf16[384,768]{1,0:T(8,128)(2,1)S(1)}, bf16[384,768]{1,0:T(8,128)(2,1)S(1)}, u32[]{:S(2)}, u32[]{:S(2)}) %collective-permute-start.10) | collective-permute-done | bytes 589856 | tf_op jit(solution)/shard_map/ppermute | solution.py:595
  70.8 7.0 %feed.3 = (bf16[2,512,768]{2,1,0:T(8,128)(2,1)S(1)}, bf16[2,512,768]{2,1,0:T(8,128)(2,1)S(1)}, f32[512,768]{1,0:T(8,128)S(1)}, bf16[512,768]{1,0:T(8,128)(2,1)S(1)}) custom-call(s32[2]{0:T(128)S(1)} %copy-done, s32[1]{0:T(128)} %constant.384.clone.1.which_ref, bf16[512,768]{1,0:T(8,128)(2,1)S(1)} %get-tuple-element.145.refs_0_, ...), custom_call_target="tpu_custom_call" | custom-call | flops 1000 | bytes 1000 | tf_op jit(solution)/shard_map/feed/pallas_call | solution.py:91
  77.9 2.3 collective-permute-done.11.refs_4_
  80.1 4.1 %second_norm.1 = (bf16[2,256,768]{2,1,0:T(8,128)(2,1)}, f32[512,768]{1,0:T(8,128)S(1)}, bf16[512,768]{1,0:T(8,128)(2,1)S(1)}, f32[8,768]{1,0:T(8,128)S(1)}) custom-call(s32[2]{0:T(128)S(1)} %copy-done, s32[1]{0:T(128)} %constant.384.clone.1.which_ref, bf16[2,256,768]{2,1,0:T(8,128)(2,1)} %refs_0_.8, f32[6,768]{1,0:T(8,128)S(1)} %reshape.192.refs_1_.refs_0_, ...), custom_call_target="tpu_custom_call" | custom-call | flops 1000 | bytes 1000 | tf_op jit(solution)/shard_map/second_norm/pallas_call | solution.py:91
  84.4 2.1 collective-permute-done.12.refs_1_.refs_3_
  86.6 10.3 %feed_back.1 = (bf16[2,2,512,768]{3,2,1,0:T(8,128)(2,1)S(1)}, f32[512,768]{1,0:T(8,128)S(1)}, bf16[512,768]{1,0:T(8,128)(2,1)S(1)}, f32[8,768]{1,0:T(8,128)S(1)}) custom-call(s32[2]{0:T(128)S(1)} %copy-done, s32[1]{0:T(128)} %constant.384.clone.1.which_ref, bf16[512,768]{1,0:T(8,128)(2,1)S(1)} %get-tuple-element.159.refs_0_.refs_2_, ...), custom_call_target="tpu_custom_call" | custom-call | flops 1000 | bytes 1000 | tf_op jit(solution)/shard_map/feed_back/pallas_call | solution.py:91
  97.0 2.2 collective-permute-done.13.refs_4_
  99.2 7.1 %first_back.1 = (f32[512,768]{1,0:T(8,128)}, bf16[2,192,256]{2,1,0:T(8,128)(2,1)}, bf16[2,192,256]{2,1,0:T(8,128)(2,1)}, bf16[2,192,256]{2,1,0:T(8,128)(2,1)}, b...) custom-call(s32[2]{0:T(128)S(1)} %copy-done, ...), custom_call_target="tpu_custom_call" | custom-call | flops 1000 | bytes 1000 | tf_op jit(solution)/shard_map/first_back/pallas_call | solution.py:91
  106.5 5.3 %down_grads.1 = (bf16[4,96,768]{2,1,0:T(8,128)(2,1)}, bf16[4,96,768]{2,1,0:T(8,128)(2,1)}, bf16[2,4,96,768]{3,2,1,0:T(8,128)(2,1)}) custom-call(s32[2]{0:T(128)S(1)} %copy-done, s32[1]{0:T(128)} %constant.384.clone.1.which_ref, bf16[2,512,768]{2,1,0:T(8,128)(2,1)S(1)} %get-tuple-element.188.refs_0_, bf16[2,512,768]{2,1,0:T(8,128)(2,1)S(1)} %get-tuple-element.189.refs_1_, ...), custom_call_target="tpu_custom_call" | custom-call | flops 1000 | bytes 1000 | tf_op jit(solution)/shard_map/down_grads/pallas_call | solution.py:91
  111.9 1.7 collective-permute-start.19
  113.7 1.6 collective-permute-start.15
  115.5 5.7 %up_grads.1 = (bf16[480,768]{1,0:T(8,128)(2,1)}, bf16[496,768]{1,0:T(8,128)(2,1)}, bf16[480,768]{1,0:T(8,128)(2,1)}, bf16[480,768]{1,0:T(8,128)(2,1)}, f32[8,768]{1,0:T(8,128)S(1)}) custom-call(s32[2]{0:T(128)S(1)} %copy-done, s32[1]{0:T(128)} %constant.384.clone.1.which_ref, bf16[512,768]{1,0:T(8,128)(2,1)S(1)} %get-tuple-element.145.refs_0_, ...), custom_call_target="tpu_custom_call" | custom-call | flops 1000 | bytes 1000 | tf_op jit(solution)/shard_map/up_grads/pallas_call | solution.py:91
  121.4 3.3 %collective-permute-done.16.refs_9_ = bf16[2,192,256]{2,1,0:T(8,128)(2,1)S(1)} collective-permute-done((bf16[2,192,256]{2,1,0:T(8,128)(2,1)S(1)}, bf16[2,192,256]{2,1,0:T(8,128)(2,1)S(1)}, u32[]{:S(2)}, u32[]{:S(2)}) %collective-permute-start.16) | collective-permute-done | bytes 196640 | tf_op jit(solution)/shard_map/ppermute | solution.py:595
  124.7 1.6 collective-permute-start.18
  126.3 14.0 %attend_bwd.2 = (bf16[2,256,768]{2,1,0:T(8,128)(2,1)}, bf16[2,256,768]{2,1,0:T(8,128)(2,1)}, bf16[3,1024,192]{2,1,0:T(8,128)(2,1)}, f32[1,384]{1,0:T(1,128)}) custom-call(s32[2]{0:T(128)} %lengths_ref.25, s32[1]{0:T(128)} %constant.384.clone.1.which_ref, bf16[3,192,768]{2,1,0:T(8,128)(2,1)} %bitcast.99, bf16[2,1024,256]{2,1,0:T(8,128)(2,1)} %get-tuple-element.153.refs_1_, ...), custom_call_target="tpu_custom_call" | custom-call | flops 1000 | bytes 1000 | tf_op jit(solution)/shard_map/attend_bwd/pallas_call | solution.py:91
  140.4 4.0 %collective-permute-done.18 = bf16[496,768]{1,0:T(8,128)(2,1)S(1)} collective-permute-done((bf16[496,768]{1,0:T(8,128)(2,1)}, bf16[496,768]{1,0:T(8,128)(2,1)S(1)}, u32[]{:S(2)}, u32[]{:S(2)}) %collective-permute-start.18) | collective-permute-done | bytes 761888 | tf_op jit(solution)/shard_map/ppermute | solution.py:595
  144.5 1.3 convert_add_fusion.1
  145.8 0.8 pad_maximum_fusion.1
  146.6 1.0 fusion
  147.6 1.8 fusion.6
  149.4 1.6 collective-permute-start.22
  151.0 1.5 collective-permute-start.21
  152.6 0.5 collective-permute-start.23
  153.7 13.9 %attend_bwd.3 = (bf16[2,256,768]{2,1,0:T(8,128)(2,1)}, bf16[2,256,768]{2,1,0:T(8,128)(2,1)}, bf16[3,1024,192]{2,1,0:T(8,128)(2,1)}, f32[1,384]{1,0:T(1,128)}) custom-call(s32[2]{0:T(128)} %lengths_ref.25, s32[1]{0:T(128)} %constant.385.clone.1.which_ref, bf16[3,192,768]{2,1,0:T(8,128)(2,1)} %bitcast.100, bf16[2,1024,256]{2,1,0:T(8,128)(2,1)} %get-tuple-element.153.refs_1_, ...), custom_call_target="tpu_custom_call" | custom-call | flops 1000 | bytes 1000 | tf_op jit(solution)/shard_map/attend_bwd/pallas_call | solution.py:91
  167.6 7.6 %collective-permute-done.24 = bf16[256,768]{1,0:T(8,128)(2,1)} collective-permute-done((bf16[256,768]{1,0:T(8,128)(2,1)}, bf16[256,768]{1,0:T(8,128)(2,1)}, u32[]{:S(2)}, u32[]{:S(2)}) %collective-permute-start.24) | collective-permute-done | bytes 393248 | tf_op jit(solution)/shard_map/ppermute | solution.py:595
  175.2 0.7 add_add_fusion.1
  176.1 1.1 fusion.10
  177.2 1.8 fusion.13
  179.0 1.1 fusion.5
  180.2 1.6 collective-permute-start.27
  182.7 9.2 %project_grads.1 = (bf16[576,384]{1,0:T(8,128)(2,1)}, bf16[584,384]{1,0:T(8,128)(2,1)}, f32[1,384]{1,0:T(1,128)}) custom-call(s32[2]{0:T(128)} %lengths_ref.25, s32[1]{0:T(128)} %constant.384.clone.1.which_ref, bf16[2,1024,768]{2,1,0:T(8,128)(2,1)} %refs_0_.9, bf16[3,1024,192]{2,1,0:T(8,128)(2,1)} %get-tuple-element.212.refs_1_, ...), custom_call_target="tpu_custom_call" | custom-call | flops 1000 | bytes 1000 | tf_op jit(solution)/shard_map/project_grads/pallas_call | solution.py:91
  192.5 1.1 collective-permute-start.29
  193.7 1.0 fusion.14
  194.7 2.6 %collective-permute-start.34 = (bf16[96,768]{1,0:T(8,128)(2,1)S(1)}, bf16[96,768]{1,0:T(8,128)(2,1)S(1)}, u32[]{:S(2)}, u32[]{:S(2)}) collective-permute-start(bf16[96,768]{1,0:T(8,128)(2,1)S(1)} %fusion.14), channel_id=1, source_target_pairs={{0,16},{4,20},{8,24},{12,28},{16,0},{20,4},{24,8},{28,12},{1,17},{... | collective-permute-start | bytes 442376 | tf_op jit(solution)/shard_map/ppermute | solution.py:595
  197.4 1.0 fusion.11
  199.3 10.3 %collective-permute-done.34 = bf16[96,768]{1,0:T(8,128)(2,1)S(1)} collective-permute-done((bf16[96,768]{1,0:T(8,128)(2,1)S(1)}, bf16[96,768]{1,0:T(8,128)(2,1)S(1)}, u32[]{:S(2)}, u32[]{:S(2)}) %collective-permute-start.34) | collective-permute-done | bytes 147488 | tf_op jit(solution)/shard_map/ppermute | solution.py:595
  209.6 1.7 fusion.15
  211.4 1.6 collective-permute-done.33
  212.9 1.1 fusion.12
  214.0 0.6 slice.209
  214.7 0.7 slice.215
  215.4 0.7 slice_reduce_fusion
  216.3 0.7 collective-permute-start.31
  217.0 1.5 fusion.8
  218.5 4.2 %collective-permute-done.31 = bf16[290,384]{1,0:T(8,128)(2,1)S(1)} collective-permute-done((bf16[290,384]{1,0:T(8,128)(2,1)S(1)}, bf16[290,384]{1,0:T(8,128)(2,1)S(1)}, u32[]{:S(2)}, u32[]{:S(2)}) %collective-permute-start.31) | collective-permute-done | bytes 222752 | tf_op jit(solution)/shard_map/ppermute | solution.py:595
  222.9 3.4 %collective-permute-start.32 = (bf16[146,384]{1,0:T(8,128)(2,1)S(1)}, bf16[146,384]{1,0:T(8,128)(2,1)S(1)}, u32[]{:S(2)}, u32[]{:S(2)}) collective-permute-start(bf16[146,384]{1,0:T(8,128)(2,1)S(1)} %pad_maximum_fusion.6), channel_id=1, source_target_pairs={{0,16},{4,20},{8,24},{12,28},{16,0},{20,4},{24,8},{28,12},{1,17},{... | collective-permute-start | bytes 336392 | tf_op jit(solution)/shard_map/ppermute | solution.py:595
  226.3 0.9 pad_maximum_fusion
  227.2 4.4 %collective-permute-done.32 = bf16[146,384]{1,0:T(8,128)(2,1)S(1)} collective-permute-done((bf16[146,384]{1,0:T(8,128)(2,1)S(1)}, bf16[146,384]{1,0:T(8,128)(2,1)S(1)}, u32[]{:S(2)}, u32[]{:S(2)}) %collective-permute-start.32) | collective-permute-done | bytes 112160 | tf_op jit(solution)/shard_map/ppermute | solution.py:595
  231.7 0.7 reshape.190
  232.5 0.7 pad_maximum_fusion.3
  (122 shorter events, 7.5 us)
Async XLA Ops:
  5.6 23.2 %collective-permute-start.2 = (bf16[384,768]{1,0:T(8,128)(2,1)}, bf16[384,768]{1,0:T(8,128)(2,1)S(1)}, u32[]{:S(2)}, u32[]{:S(2)}) collective-permute-start(bf16[384,768]{1,0:T(8,128)(2,1)} %get-tuple-element.131), channel_id=1, source_target_pairs={{0,2},{1,3},{2,0},{3,1},{4,6},{5,7},{6,4},{7,5},{8,10},{9,11},{10,... | collective-permute-start | bytes 1769480 | tf_op jit(solution)/shard_map/ppermute | solution.py:595
  8.6 20.1 %collective-permute-start.1 = (bf16[200,768]{1,0:T(8,128)(2,1)}, bf16[200,768]{1,0:T(8,128)(2,1)S(1)}, u32[]{:S(2)}, u32[]{:S(2)}) collective-permute-start(bf16[200,768]{1,0:T(8,128)(2,1)} %get-tuple-element.130.refs_6_.refs_2_.refs_11_), channel_id=1, source_target_pairs={{0,2},{1,3},{2,0},{3,1},{4,6},{5,7},{6,4},{7,5},{8,10},{9,11},{10,... | collective-permute-start | bytes 921608 | tf_op jit(solution)/shard_map/ppermute | solution.py:595
  8.7 20.0 %collective-permute-start = (bf16[200,768]{1,0:T(8,128)(2,1)}, bf16[200,768]{1,0:T(8,128)(2,1)S(1)}, u32[]{:S(2)}, u32[]{:S(2)}) collective-permute-start(bf16[200,768]{1,0:T(8,128)(2,1)} %get-tuple-element.130.refs_6_.refs_2_.refs_11_), channel_id=1, source_target_pairs={{0,1},{1,0},{2,3},{3,2},{4,5},{5,4},{6,7},{7,6},{8,9},{9,8},{10,11... | collective-permute-start | bytes 921608 | tf_op jit(solution)/shard_map/ppermute | solution.py:595
  8.7 31.2 %copy-start.21 = (bf16[384,768]{1,0:T(8,128)(2,1)S(1)}, bf16[384,768]{1,0:T(8,128)(2,1)}, u32[]{:S(2)}) copy-start(bf16[384,768]{1,0:T(8,128)(2,1)} %get-tuple-element.147) | copy-start | bytes 1769476
  8.7 32.7 %copy-start.14 = (bf16[768]{0:T(1024)(128)(2,1)S(1)}, bf16[768]{0:T(1024)(128)(2,1)}, u32[]{:S(2)}) copy-start(bf16[768]{0:T(1024)(128)(2,1)} %param.21) | copy-start | bytes 4612
  8.7 32.9 %copy-start.15 = (bf16[768]{0:T(1024)(128)(2,1)S(1)}, bf16[768]{0:T(1024)(128)(2,1)}, u32[]{:S(2)}) copy-start(bf16[768]{0:T(1024)(128)(2,1)} %param.22) | copy-start | bytes 4612
  8.7 33.1 %copy-start.16 = (bf16[768]{0:T(1024)(128)(2,1)S(1)}, bf16[768]{0:T(1024)(128)(2,1)}, u32[]{:S(2)}) copy-start(bf16[768]{0:T(1024)(128)(2,1)} %param.23) | copy-start | bytes 4612
  8.8 33.3 %copy-start.17 = (bf16[768]{0:T(1024)(128)(2,1)S(1)}, bf16[768]{0:T(1024)(128)(2,1)}, u32[]{:S(2)}) copy-start(bf16[768]{0:T(1024)(128)(2,1)} %param.27) | copy-start | bytes 4612
  8.8 33.5 %copy-start.18 = (bf16[768]{0:T(1024)(128)(2,1)S(1)}, bf16[768]{0:T(1024)(128)(2,1)}, u32[]{:S(2)}) copy-start(bf16[768]{0:T(1024)(128)(2,1)} %param.28) | copy-start | bytes 4612
  8.8 33.7 %copy-start.19 = (bf16[768]{0:T(1024)(128)(2,1)S(1)}, bf16[768]{0:T(1024)(128)(2,1)}, u32[]{:S(2)}) copy-start(bf16[768]{0:T(1024)(128)(2,1)} %param.29) | copy-start | bytes 4612
  8.8 33.9 %copy-start = (s32[2]{0:T(128)S(1)}, s32[2]{0:T(128)}, u32[]{:S(2)}) copy-start(s32[2]{0:T(128)} %lengths_ref.25) | copy-start | bytes 28
  28.8 11.2 %collective-permute-start.6 = (bf16[200,768]{1,0:T(8,128)(2,1)S(1)}, bf16[200,768]{1,0:T(8,128)(2,1)S(1)}, u32[]{:S(2)}, u32[]{:S(2)}) collective-permute-start(bf16[200,768]{1,0:T(8,128)(2,1)S(1)} %collective-permute-done.1.refs_8_.refs_2_.refs_13_), channel_id=1, source_target_pairs={{0,1},{1,0},{2,3},{3,2},{4,5},{5,4},{6,7},{7,6},{8,9},{9,8},{10,11... | collective-permute-start | bytes 921608 | tf_op jit(solution)/shard_map/ppermute | solution.py:595
  28.8 2.3 collective-permute-start.3
  29.3 8.0 %collective-permute-start.4 = (bf16[2,192,256]{2,1,0:T(8,128)(2,1)}, bf16[2,192,256]{2,1,0:T(8,128)(2,1)S(1)}, u32[]{:S(2)}, u32[]{:S(2)}) collective-permute-start(bf16[2,192,256]{2,1,0:T(8,128)(2,1)} %get-tuple-element.134), channel_id=1, source_target_pairs={{0,2},{1,3},{2,0},{3,1},{4,6},{5,7},{6,4},{7,5},{8,10},{9,11},{10,... | collective-permute-start | bytes 589832 | tf_op jit(solution)/shard_map/ppermute | solution.py:595
  31.0 8.9 %collective-permute-start.5 = (bf16[2,192,256]{2,1,0:T(8,128)(2,1)}, bf16[2,192,256]{2,1,0:T(8,128)(2,1)S(1)}, u32[]{:S(2)}, u32[]{:S(2)}) collective-permute-start(bf16[2,192,256]{2,1,0:T(8,128)(2,1)} %get-tuple-element.135), channel_id=1, source_target_pairs={{0,3},{1,2},{2,1},{3,0},{4,7},{5,6},{6,5},{7,4},{8,11},{9,10},{10,... | collective-permute-start | bytes 589832 | tf_op jit(solution)/shard_map/ppermute | solution.py:595
  40.0 15.7 %collective-permute-start.9 = (bf16[384,768]{1,0:T(8,128)(2,1)S(1)}, bf16[384,768]{1,0:T(8,128)(2,1)S(1)}, u32[]{:S(2)}, u32[]{:S(2)}) collective-permute-start(bf16[384,768]{1,0:T(8,128)(2,1)S(1)} %copy-done.21), channel_id=1, source_target_pairs={{0,2},{1,3},{2,0},{3,1},{4,6},{5,7},{6,4},{7,5},{8,10},{9,11},{10,... | collective-permute-start | bytes 1769480 | tf_op jit(solution)/shard_map/ppermute | solution.py:595
  46.9 10.6 %collective-permute-start.7 = (bf16[512,768]{1,0:T(8,128)(2,1)S(1)}, bf16[512,768]{1,0:T(8,128)(2,1)S(1)}, u32[]{:S(2)}, u32[]{:S(2)}) collective-permute-start(bf16[512,768]{1,0:T(8,128)(2,1)S(1)} %get-tuple-element.145.refs_0_), channel_id=1, source_target_pairs={{0,1},{1,0},{2,3},{3,2},{4,5},{5,4},{6,7},{7,6},{8,9},{9,8},{10,11... | collective-permute-start | bytes 2359304 | tf_op jit(solution)/shard_map/ppermute | solution.py:595
  47.3 17.8 %collective-permute-start.8 = (bf16[384,768]{1,0:T(8,128)(2,1)S(1)}, bf16[384,768]{1,0:T(8,128)(2,1)S(1)}, u32[]{:S(2)}, u32[]{:S(2)}) collective-permute-start(bf16[384,768]{1,0:T(8,128)(2,1)S(1)} %collective-permute-done.2.refs_3_.refs_6_), channel_id=1, source_target_pairs={{0,4},{4,0},{8,12},{12,8},{16,20},{20,16},{24,28},{28,24},{1,5},{5... | collective-permute-start | bytes 1769480 | tf_op jit(solution)/shard_map/ppermute | solution.py:595
  55.7 15.1 %collective-permute-start.10 = (bf16[384,768]{1,0:T(8,128)(2,1)S(1)}, bf16[384,768]{1,0:T(8,128)(2,1)S(1)}, u32[]{:S(2)}, u32[]{:S(2)}) collective-permute-start(bf16[384,768]{1,0:T(8,128)(2,1)S(1)} %collective-permute-done.9.refs_5_.refs_8_), channel_id=1, source_target_pairs={{0,8},{4,12},{8,0},{12,4},{16,24},{20,28},{24,16},{28,20},{1,9},{5... | collective-permute-start | bytes 1769480 | tf_op jit(solution)/shard_map/ppermute | solution.py:595
  77.8 2.4 %collective-permute-start.11 = (bf16[512,768]{1,0:T(8,128)(2,1)S(1)}, bf16[512,768]{1,0:T(8,128)(2,1)S(1)}, u32[]{:S(2)}, u32[]{:S(2)}) collective-permute-start(bf16[512,768]{1,0:T(8,128)(2,1)S(1)} %get-tuple-element.151), channel_id=1, source_target_pairs={{0,1},{1,0},{2,3},{3,2},{4,5},{5,4},{6,7},{7,6},{8,9},{9,8},{10,11... | collective-permute-start | bytes 2359304 | tf_op jit(solution)/shard_map/ppermute | solution.py:595
  84.2 2.4 %collective-permute-start.12 = (bf16[512,768]{1,0:T(8,128)(2,1)S(1)}, bf16[512,768]{1,0:T(8,128)(2,1)S(1)}, u32[]{:S(2)}, u32[]{:S(2)}) collective-permute-start(bf16[512,768]{1,0:T(8,128)(2,1)S(1)} %get-tuple-element.159.refs_0_.refs_2_), channel_id=1, source_target_pairs={{0,1},{1,0},{2,3},{3,2},{4,5},{5,4},{6,7},{7,6},{8,9},{9,8},{10,11... | collective-permute-start | bytes 2359304 | tf_op jit(solution)/shard_map/ppermute | solution.py:595
  96.8 2.4 %collective-permute-start.13 = (bf16[512,768]{1,0:T(8,128)(2,1)S(1)}, bf16[512,768]{1,0:T(8,128)(2,1)S(1)}, u32[]{:S(2)}, u32[]{:S(2)}) collective-permute-start(bf16[512,768]{1,0:T(8,128)(2,1)S(1)} %get-tuple-element.163), channel_id=1, source_target_pairs={{0,1},{1,0},{2,3},{3,2},{4,5},{5,4},{6,7},{7,6},{8,9},{9,8},{10,11... | collective-permute-start | bytes 2359304 | tf_op jit(solution)/shard_map/ppermute | solution.py:595
  106.3 9.2 %collective-permute-start.17 = (bf16[2,200,768]{2,1,0:T(8,128)(2,1)}, bf16[2,200,768]{2,1,0:T(8,128)(2,1)S(1)}, u32[]{:S(2)}, u32[]{:S(2)}) collective-permute-start(bf16[2,200,768]{2,1,0:T(8,128)(2,1)} %get-tuple-element.172), channel_id=1, source_target_pairs={{0,1},{1,0},{2,3},{3,2},{4,5},{5,4},{6,7},{7,6},{8,9},{9,8},{10,11... | collective-permute-start | bytes 1843208 | tf_op jit(solution)/shard_map/ppermute | solution.py:595
  106.5 7.1 %copy-start.24 = (bf16[2,192,256]{2,1,0:T(8,128)(2,1)S(1)}, bf16[2,192,256]{2,1,0:T(8,128)(2,1)}, u32[]{:S(2)}) copy-start(bf16[2,192,256]{2,1,0:T(8,128)(2,1)} %get-tuple-element.167) | copy-start | bytes 589828
  106.5 7.2 %copy-start.23 = (bf16[2,192,256]{2,1,0:T(8,128)(2,1)S(1)}, bf16[2,192,256]{2,1,0:T(8,128)(2,1)}, u32[]{:S(2)}) copy-start(bf16[2,192,256]{2,1,0:T(8,128)(2,1)} %get-tuple-element.168) | copy-start | bytes 589828
  106.5 8.7 %copy-start.22 = (bf16[2,192,256]{2,1,0:T(8,128)(2,1)S(1)}, bf16[2,192,256]{2,1,0:T(8,128)(2,1)}, u32[]{:S(2)}) copy-start(bf16[2,192,256]{2,1,0:T(8,128)(2,1)} %get-tuple-element.169) | copy-start | bytes 589828
  111.9 28.5 %collective-permute-start.19 = (bf16[2,4,96,768]{3,2,1,0:T(8,128)(2,1)}, bf16[2,4,96,768]{3,2,1,0:T(8,128)(2,1)S(1)}, u32[]{:S(2)}, u32[]{:S(2)}) collective-permute-start(bf16[2,4,96,768]{3,2,1,0:T(8,128)(2,1)} %get-tuple-element.190), channel_id=1, source_target_pairs={{0,4},{4,0},{8,12},{12,8},{16,20},{20,16},{24,28},{28,24},{1,5},{5... | collective-permute-start | bytes 3538952 | tf_op jit(solution)/shard_map/ppermute | solution.py:595
  113.6 7.6 %collective-permute-start.14 = (bf16[2,192,256]{2,1,0:T(8,128)(2,1)S(1)}, bf16[2,192,256]{2,1,0:T(8,128)(2,1)S(1)}, u32[]{:S(2)}, u32[]{:S(2)}) collective-permute-start(bf16[2,192,256]{2,1,0:T(8,128)(2,1)S(1)} %copy-done.24), channel_id=1, source_target_pairs={{0,1},{1,0},{2,3},{3,2},{4,5},{5,4},{6,7},{7,6},{8,9},{9,8},{10,11... | collective-permute-start | bytes 589832 | tf_op jit(solution)/shard_map/ppermute | solution.py:595
  113.7 7.7 %collective-permute-start.15 = (bf16[2,192,256]{2,1,0:T(8,128)(2,1)S(1)}, bf16[2,192,256]{2,1,0:T(8,128)(2,1)S(1)}, u32[]{:S(2)}, u32[]{:S(2)}) collective-permute-start(bf16[2,192,256]{2,1,0:T(8,128)(2,1)S(1)} %copy-done.23), channel_id=1, source_target_pairs={{0,2},{1,3},{2,0},{3,1},{4,6},{5,7},{6,4},{7,5},{8,10},{9,11},{10,... | collective-permute-start | bytes 589832 | tf_op jit(solution)/shard_map/ppermute | solution.py:595
  115.2 9.4 %collective-permute-start.16 = (bf16[2,192,256]{2,1,0:T(8,128)(2,1)S(1)}, bf16[2,192,256]{2,1,0:T(8,128)(2,1)S(1)}, u32[]{:S(2)}, u32[]{:S(2)}) collective-permute-start(bf16[2,192,256]{2,1,0:T(8,128)(2,1)S(1)} %copy-done.22), channel_id=1, source_target_pairs={{0,3},{1,2},{2,1},{3,0},{4,7},{5,6},{6,5},{7,4},{8,11},{9,10},{10,... | collective-permute-start | bytes 589832 | tf_op jit(solution)/shard_map/ppermute | solution.py:595
  121.2 5.1 %copy-start.2 = (bf16[2,192,256]{2,1,0:T(8,128)(2,1)}, bf16[2,192,256]{2,1,0:T(8,128)(2,1)S(1)}, u32[]{:S(2)}) copy-start(bf16[2,192,256]{2,1,0:T(8,128)(2,1)S(1)} %collective-permute-done.14.refs_7_) | copy-start | bytes 589828
  121.4 4.9 %copy-start.3 = (bf16[2,192,256]{2,1,0:T(8,128)(2,1)}, bf16[2,192,256]{2,1,0:T(8,128)(2,1)S(1)}, u32[]{:S(2)}) copy-start(bf16[2,192,256]{2,1,0:T(8,128)(2,1)S(1)} %collective-permute-done.15.refs_8_) | copy-start | bytes 589828
  124.7 1.6 copy-start.4
  124.7 19.7 %collective-permute-start.18 = (bf16[496,768]{1,0:T(8,128)(2,1)}, bf16[496,768]{1,0:T(8,128)(2,1)S(1)}, u32[]{:S(2)}, u32[]{:S(2)}) collective-permute-start(bf16[496,768]{1,0:T(8,128)(2,1)} %get-tuple-element.187), channel_id=1, source_target_pairs={{0,8},{4,12},{8,0},{12,4},{16,24},{20,28},{24,16},{28,20},{1,9},{5... | collective-permute-start | bytes 2285576 | tf_op jit(solution)/shard_map/ppermute | solution.py:595
  144.4 3.2 %collective-permute-start.20 = (bf16[2,256,768]{2,1,0:T(8,128)(2,1)}, bf16[2,256,768]{2,1,0:T(8,128)(2,1)}, u32[]{:S(2)}, u32[]{:S(2)}) collective-permute-start(bf16[2,256,768]{2,1,0:T(8,128)(2,1)} %get-tuple-element.191), channel_id=1, source_target_pairs={{0,1},{1,0},{2,3},{3,2},{4,5},{5,4},{6,7},{7,6},{8,9},{9,8},{10,11... | collective-permute-start | bytes 2359304 | tf_op jit(solution)/shard_map/ppermute | solution.py:595
  144.4 2.2 copy-start.10
  145.8 1.8 copy-start.5
  149.4 25.8 %collective-permute-start.22 = (bf16[480,768]{1,0:T(8,128)(2,1)}, bf16[480,768]{1,0:T(8,128)(2,1)}, u32[]{:S(2)}, u32[]{:S(2)}) collective-permute-start(bf16[480,768]{1,0:T(8,128)(2,1)} %get-tuple-element.205), channel_id=1, source_target_pairs={{0,8},{4,12},{8,0},{12,4},{16,24},{20,28},{24,16},{28,20},{1,9},{5... | collective-permute-start | bytes 2211848 | tf_op jit(solution)/shard_map/ppermute | solution.py:595
  151.0 24.2 %collective-permute-start.21 = (bf16[4,96,768]{2,1,0:T(8,128)(2,1)}, bf16[4,96,768]{2,1,0:T(8,128)(2,1)}, u32[]{:S(2)}, u32[]{:S(2)}) collective-permute-start(bf16[4,96,768]{2,1,0:T(8,128)(2,1)} %fusion), channel_id=1, source_target_pairs={{0,2},{1,3},{2,0},{3,1},{4,6},{5,7},{6,4},{7,5},{8,10},{9,11},{10,... | collective-permute-start | bytes 1769480 | tf_op jit(solution)/shard_map/ppermute | solution.py:595
  152.6 15.0 %collective-permute-start.23 = (bf16[256,768]{1,0:T(8,128)(2,1)}, bf16[256,768]{1,0:T(8,128)(2,1)}, u32[]{:S(2)}, u32[]{:S(2)}) collective-permute-start(bf16[256,768]{1,0:T(8,128)(2,1)} %pad_maximum_fusion.1), channel_id=1, source_target_pairs={{0,4},{4,0},{8,12},{12,8},{16,20},{20,16},{24,28},{28,24},{1,5},{5... | collective-permute-start | bytes 1179656 | tf_op jit(solution)/shard_map/ppermute | solution.py:595
  153.1 22.1 %collective-permute-start.24 = (bf16[256,768]{1,0:T(8,128)(2,1)}, bf16[256,768]{1,0:T(8,128)(2,1)}, u32[]{:S(2)}, u32[]{:S(2)}) collective-permute-start(bf16[256,768]{1,0:T(8,128)(2,1)} %fusion.6), channel_id=1, source_target_pairs={{0,2},{1,3},{2,0},{3,1},{4,6},{5,7},{6,4},{7,5},{8,10},{9,11},{10,... | collective-permute-start | bytes 1179656 | tf_op jit(solution)/shard_map/ppermute | solution.py:595
  153.6 22.4 %copy-start.8 = (bf16[480,768]{1,0:T(8,128)(2,1)S(1)}, bf16[480,768]{1,0:T(8,128)(2,1)}, u32[]{:S(2)}) copy-start(bf16[480,768]{1,0:T(8,128)(2,1)} %get-tuple-element.217) | copy-start | bytes 2211844
  153.6 23.6 %copy-start.11 = (bf16[4,96,768]{2,1,0:T(8,128)(2,1)S(1)}, bf16[4,96,768]{2,1,0:T(8,128)(2,1)}, u32[]{:S(2)}) copy-start(bf16[4,96,768]{2,1,0:T(8,128)(2,1)} %get-tuple-element.214) | copy-start | bytes 1769476
  176.0 17.6 %collective-permute-start.25 = (bf16[2,256,768]{2,1,0:T(8,128)(2,1)}, bf16[2,256,768]{2,1,0:T(8,128)(2,1)S(1)}, u32[]{:S(2)}, u32[]{:S(2)}) collective-permute-start(bf16[2,256,768]{2,1,0:T(8,128)(2,1)} %get-tuple-element.211), channel_id=1, source_target_pairs={{0,1},{1,0},{2,3},{3,2},{4,5},{5,4},{6,7},{7,6},{8,9},{9,8},{10,11... | collective-permute-start | bytes 2359304 | tf_op jit(solution)/shard_map/ppermute | solution.py:595
  180.2 12.3 %collective-permute-start.27 = (bf16[256,768]{1,0:T(8,128)(2,1)S(1)}, bf16[256,768]{1,0:T(8,128)(2,1)S(1)}, u32[]{:S(2)}, u32[]{:S(2)}) collective-permute-start(bf16[256,768]{1,0:T(8,128)(2,1)S(1)} %pad_maximum_fusion.2), channel_id=1, source_target_pairs={{0,2},{1,3},{2,0},{3,1},{4,6},{5,7},{6,4},{7,5},{8,10},{9,11},{10,... | collective-permute-start | bytes 1179656 | tf_op jit(solution)/shard_map/ppermute | solution.py:595
  181.8 10.7 %collective-permute-start.28 = (bf16[2,120,768]{2,1,0:T(8,128)(2,1)S(1)}, bf16[2,120,768]{2,1,0:T(8,128)(2,1)S(1)}, u32[]{:S(2)}, u32[]{:S(2)}) collective-permute-start(bf16[2,120,768]{2,1,0:T(8,128)(2,1)S(1)} %fusion.10), channel_id=1, source_target_pairs={{0,4},{4,0},{8,12},{12,8},{16,20},{20,16},{24,28},{28,24},{1,5},{5... | collective-permute-start | bytes 1105928 | tf_op jit(solution)/shard_map/ppermute | solution.py:595
  182.3 9.7 %collective-permute-start.26 = (bf16[2,96,768]{2,1,0:T(8,128)(2,1)}, bf16[2,96,768]{2,1,0:T(8,128)(2,1)S(1)}, u32[]{:S(2)}, u32[]{:S(2)}) collective-permute-start(bf16[2,96,768]{2,1,0:T(8,128)(2,1)} %fusion.13), channel_id=1, source_target_pairs={{0,8},{4,12},{8,0},{12,4},{16,24},{20,28},{24,16},{28,20},{1,9},{5... | collective-permute-start | bytes 884744 | tf_op jit(solution)/shard_map/ppermute | solution.py:595
  182.7 10.8 %copy-start.7 = (bf16[2,256,768]{2,1,0:T(8,128)(2,1)S(1)}, bf16[2,256,768]{2,1,0:T(8,128)(2,1)}, u32[]{:S(2)}) copy-start(bf16[2,256,768]{2,1,0:T(8,128)(2,1)} %get-tuple-element.210) | copy-start | bytes 2359300
  191.9 1.8 copy-start.12
  191.9 5.4 %copy-start.9 = (bf16[480,768]{1,0:T(8,128)(2,1)S(1)}, bf16[480,768]{1,0:T(8,128)(2,1)}, u32[]{:S(2)}) copy-start(bf16[480,768]{1,0:T(8,128)(2,1)} %get-tuple-element.217) | copy-start | bytes 2211844
  192.5 23.6 %collective-permute-start.29 = (bf16[584,384]{1,0:T(8,128)(2,1)}, bf16[584,384]{1,0:T(8,128)(2,1)S(1)}, u32[]{:S(2)}, u32[]{:S(2)}) collective-permute-start(bf16[584,384]{1,0:T(8,128)(2,1)} %get-tuple-element.226), channel_id=1, source_target_pairs={{0,4},{4,0},{8,12},{12,8},{16,20},{20,16},{24,28},{28,24},{1,5},{5... | collective-permute-start | bytes 1345544 | tf_op jit(solution)/shard_map/ppermute | solution.py:595
  194.7 14.9 %collective-permute-start.34 = (bf16[96,768]{1,0:T(8,128)(2,1)S(1)}, bf16[96,768]{1,0:T(8,128)(2,1)S(1)}, u32[]{:S(2)}, u32[]{:S(2)}) collective-permute-start(bf16[96,768]{1,0:T(8,128)(2,1)S(1)} %fusion.14), channel_id=1, source_target_pairs={{0,16},{4,20},{8,24},{12,28},{16,0},{20,4},{24,8},{28,12},{1,17},{... | collective-permute-start | bytes 442376 | tf_op jit(solution)/shard_map/ppermute | solution.py:595
  198.4 14.5 %collective-permute-start.33 = (bf16[136,768]{1,0:T(8,128)(2,1)S(1)}, bf16[136,768]{1,0:T(8,128)(2,1)S(1)}, u32[]{:S(2)}, u32[]{:S(2)}) collective-permute-start(bf16[136,768]{1,0:T(8,128)(2,1)S(1)} %pad_maximum_fusion.5), channel_id=1, source_target_pairs={{0,16},{4,20},{8,24},{12,28},{16,0},{20,4},{24,8},{28,12},{1,17},{... | collective-permute-start | bytes 626696 | tf_op jit(solution)/shard_map/ppermute | solution.py:595
  198.9 17.2 %collective-permute-start.30 = (bf16[256,768]{1,0:T(8,128)(2,1)S(1)}, bf16[256,768]{1,0:T(8,128)(2,1)S(1)}, u32[]{:S(2)}, u32[]{:S(2)}) collective-permute-start(bf16[256,768]{1,0:T(8,128)(2,1)S(1)} %fusion.7), channel_id=1, source_target_pairs={{0,2},{1,3},{2,0},{3,1},{4,6},{5,7},{6,4},{7,5},{8,10},{9,11},{10,... | collective-permute-start | bytes 1179656 | tf_op jit(solution)/shard_map/ppermute | solution.py:595
  211.3 4.8 %copy-start.20 = (f32[1,384]{1,0:T(1,128)S(1)}, f32[1,384]{1,0:T(1,128)}, u32[]{:S(2)}) copy-start(f32[1,384]{1,0:T(1,128)} %get-tuple-element.234) | copy-start | bytes 4612
  211.4 4.8 %copy-start.13 = (bf16[576,384]{1,0:T(8,128)(2,1)S(1)}, bf16[576,384]{1,0:T(8,128)(2,1)}, u32[]{:S(2)}) copy-start(bf16[576,384]{1,0:T(8,128)(2,1)} %get-tuple-element.232) | copy-start | bytes 1327108
  214.0 3.0 %copy-start.1 = (f32[512,768]{1,0:T(8,128)S(1)}, f32[512,768]{1,0:T(8,128)}, u32[]{:S(2)}) copy-start(f32[512,768]{1,0:T(8,128)} %get-tuple-element.209) | copy-start | bytes 4718596
  214.0 3.0 %copy-start.6 = (bf16[2,256,768]{2,1,0:T(8,128)(2,1)S(1)}, bf16[2,256,768]{2,1,0:T(8,128)(2,1)}, u32[]{:S(2)}) copy-start(bf16[2,256,768]{2,1,0:T(8,128)(2,1)} %get-tuple-element.185) | copy-start | bytes 2359300
  216.3 6.5 %collective-permute-start.31 = (bf16[290,384]{1,0:T(8,128)(2,1)S(1)}, bf16[290,384]{1,0:T(8,128)(2,1)S(1)}, u32[]{:S(2)}, u32[]{:S(2)}) collective-permute-start(bf16[290,384]{1,0:T(8,128)(2,1)S(1)} %pad_maximum_fusion.4), channel_id=1, source_target_pairs={{0,8},{4,12},{8,0},{12,4},{16,24},{20,28},{24,16},{28,20},{1,9},{5... | collective-permute-start | bytes 668168 | tf_op jit(solution)/shard_map/ppermute | solution.py:595
  222.9 8.8 %collective-permute-start.32 = (bf16[146,384]{1,0:T(8,128)(2,1)S(1)}, bf16[146,384]{1,0:T(8,128)(2,1)S(1)}, u32[]{:S(2)}, u32[]{:S(2)}) collective-permute-start(bf16[146,384]{1,0:T(8,128)(2,1)S(1)} %pad_maximum_fusion.6), channel_id=1, source_target_pairs={{0,16},{4,20},{8,24},{12,28},{16,0},{20,4},{24,8},{28,12},{1,17},{... | collective-permute-start | bytes 336392 | tf_op jit(solution)/shard_map/ppermute | solution.py:595

commit v2 on v1

--- a/solution.py
+++ b/solution.py
@@ -47,7 +47,7 @@
         self.started = True
 
 
-def call(name, body, info, ins, outs, scratch=(), vmem=58, which=0, **static):
+def call(name, body, info, ins, outs, scratch=(), vmem=58, which=0, cost=1000, **static):
     far_in = [i for i, a in enumerate(ins) if isinstance(a, tuple)]
     pinned = [i for i in far_in if len(ins[i]) == 2]
     far_out = [i for i, o in enumerate(outs) if isinstance(o, list)]
@@ -99,7 +99,7 @@
             scratch_shapes=[*buffers, *scratch, pltpu.SemaphoreType.DMA((max(1, len(far_in) + len(far_out)),))],
         ),
         compiler_params=pltpu.CompilerParams(vmem_limit_bytes=vmem << 20),
-        cost_estimate=pl.CostEstimate(flops=1000, bytes_accessed=1000, transcendentals=0),
+        cost_estimate=pl.CostEstimate(flops=cost, bytes_accessed=1000, transcendentals=0),
         name=name,
     )(info, jnp.full((1,), which, jnp.int32), *[pltpu.with_memory_space_constraint(a, pltpu.HBM) if i in pinned else a for i, a in enumerate(arrays)])
 
@@ -133,11 +133,10 @@
 
 def prepare(info, out_w, bias, up, dn):
     width, d = out_w.shape
-    half = up.shape[0] // 2
-    view = lambda ref, info: ref.at[pl.ds(pl.multiple_of(info[3] * half, half), half)]
-    view2 = lambda ref, info: ref.at[pl.ds(pl.multiple_of(info[4] * half, half), half)]
-    ins = [whole(out_w), bias, (up, ((half, d), view)), (dn, ((half, d), view2))]
-    return call("prepare", prepare_kernel, info, ins, [[SDS((width + 8, d), bf16)]] + [[SDS((half, d), bf16)]] * 2)
+    part = up.shape[0] // 4
+    view = lambda ref, info: ref.at[pl.ds(pl.multiple_of((2 * info[3] + info[4]) * part, part), part)]
+    ins = [whole(out_w), bias, (up, ((part, d), view)), (dn, ((part, d), view))]
+    return call("prepare", prepare_kernel, info, ins, [[SDS((width + 8, d), bf16)]] + [[SDS((part, d), bf16)]] * 2)
 
 
 def head_cols(a, h, extra=()):
@@ -241,6 +240,10 @@
         [Raw(o) for o in far] + [[SDS((batch, width, block), bf16)]] * peers,
         scratch,
     )
+
+
+def nth(at, ref, info):
+    return ref.at[at]
 
 
 def of_sequence(a):
@@ -321,18 +324,18 @@
     ]
     ins = [whole(w_t)] + [of_sequence(a) for a in (q, k, v, lse, c)]
     ins += [(g, ((width, block), lambda ref, info: ref.at[info[5]]), None) for g in gs]
-    return call("attend_bwd", attend_bwd_kernel, info, ins, outs, scratch, which=which)
-
-
-def project_grads_kernel(info, x_in, low0, low1, db0, db1, keep, send, db_ref, dw, pair, *, parts):
-    x = x_in()
+    return call("attend_bwd", attend_bwd_kernel, info, ins, outs, scratch, which=which, cost=10**10)
+
+
+def project_grads_kernel(info, x0, x1, low0, low1, db0, db1, keep, send, db_ref, dw, pair, *, parts):
     lows = (low0(), low1())
+    x = (x0(), x1())
     _, d, width = dw.shape
     step = 256
 
     def chunk(m, carry):
         cols = pl.ds(pl.multiple_of(m * step, step), step)
-        x_t = (x[0, :, cols].T, x[1, :, cols].T)
+        x_t = (x[0][:, cols].T, x[1][:, cols].T)
         for i in range(3):
             dw[i, cols, :] = mm(x_t[0], lows[0][i]) + mm(x_t[1], lows[1][i])
         return carry
@@ -404,8 +407,7 @@
 def feed_kernel(info, low, low2, pack, *rest, width, far):
     if far:
         u_a, u_b, d_a, d_b, p_own, p_sib, act_out, slope_out, own, sib, both, up, dn = rest
-        half = u_a.dst.shape[0]
-        assemble(info[3], up, u_a(), u_b(), half)
+        assemble(info[3], info[4], up, u_a(), u_b(), False)
     else:
         u_in, d_in, act_out, slope_out, own, sib, both = rest
         up = u_in()
@@ -429,7 +431,7 @@
 
     lax.fori_loop(0, 2, side, 0)
     if far:
-        assemble(info[4], dn, d_a(), d_b(), half)
+        assemble(info[3], info[4], dn, d_a(), d_b(), True)
         sib[...] = (p_sib[...] + mm(act[1], dn[...])).astype(bf16)
         own[...] = p_own[...] + mm(act[0], dn[...])
     else:
@@ -438,9 +440,13 @@
         sib[...] = mm(act[1], dn[...])
 
 
-def assemble(bit, dst, a, b, half):
-    dst[pl.ds(pl.multiple_of(bit * half, half), half)] = a[...]
-    dst[pl.ds(pl.multiple_of((1 - bit) * half, half), half)] = b[...]
+def assemble(x, z, dst, a, b, z_first):
+    part = a.shape[0] // 2
+    for src, other in ((a, 0), (b, 1)):
+        for i in range(2):
+            flips = (other, i) if z_first else (i, other)
+            at = 2 * (x ^ flips[0]) + (z ^ flips[1])
+            dst[pl.ds(pl.multiple_of(at * part, part), part)] = src[i * part : (i + 1) * part]
 
 
 def second_norm_kernel(info, cot_in, par, nv_in, own, got, outs, gsec_out, gs_low, small):
@@ -465,7 +471,6 @@
 
 def feed_back_kernel(info, gs, gs2, slope0, slope1, up0, dn0, u_a, u_b, d_a, d_b, gh_out, own, sib, ub, sides, up2, dn2):
     gh = ref(gh_out)
-    half = u_a.dst.shape[0]
     units = up0.dst.shape[1]
     ub[...] = jnp.zeros_like(ub)
     sides[0] = gs[...]
@@ -473,7 +478,7 @@
     step = 256
     for k, slope in enumerate((ref(slope0), ref(slope1))):
         if k:
-            assemble(info[4], dn2, d_a(), d_b(), half)
+            assemble(info[3], info[4], dn2, d_a(), d_b(), True)
             dn = dn2
         else:
             dn = dn0()
@@ -490,7 +495,7 @@
             return lax.fori_loop(0, units // step, chunk, carry)
 
         lax.fori_loop(0, 2, side, 0)
-    assemble(info[3], up2, u_a(), u_b(), half)
+    assemble(info[3], info[4], up2, u_a(), u_b(), False)
     up = up0()
     sib[...] = (mm(gh[0, 1], up[...], NT) + mm(gh[1, 1], up2[...], NT)).astype(bf16)
     own[...] = mm(gh[0, 0], up[...], NT) + mm(gh[1, 0], up2[...], NT)
@@ -649,20 +654,22 @@
     par = jnp.concatenate([out_bias, first_gain, first_shift, down_bias, second_gain, second_shift])
     par = par.reshape(6, d).astype(f32)
     w_t = jnp.transpose(qkv_weight, (1, 2, 0))
-    pack, up_half, dn_half = prepare(info, out_weight, up_bias[None], up_weight, down_weight)
+    pack, u_part, d_part = prepare(info, out_weight, up_bias[None], up_weight, down_weight)
     pack2 = swap(pack, "tensor", 2)
     pack1 = swap(pack, "tensor", 1)
-    u2a = swap(up_half, "tensor", 2)
+    u_part = swap(u_part, "tensor", 2)
+    d_part = swap(d_part, "tensor", 2)
     q, k, v, lse, c, *cs = attend_fwd(info, inputs, w_t, qkv_bias, peers)
     saved = (q, k, v, lse, c)
-    *cs, pack1, pack2, u2a = after(*cs, pack1, pack2, u2a)
+    *cs, pack1, pack2, u_part, d_part = after(*cs, pack1, pack2, u_part, d_part)
     ctx = [cs[0]] + [swap(cs[j], "tensor", j) for j in range(1, peers)]
+    u2a = jnp.concatenate([u_part, swap(u_part, "dp", 1)])
+    d2a = jnp.concatenate([d_part, swap(d_part, "dp", 2)])
+    *ctx, pack2, u2a, d2a = after(*ctx, pack2, u2a, d2a)
     pack3 = swap(pack2, "tensor", 1)
-    *ctx, pack3, dn_half = after(*ctx, pack3, dn_half)
-    d2a = swap(dn_half, "tensor", 2)
     packs = [pack, pack1, pack2, pack3]
-    u2b = swap(u2a, "dp", 1)
-    d2b = swap(d2a, "dp", 2)
+    u2b = swap(u2a, "dp", 2)
+    d2b = swap(d2a, "dp", 1)
     far_ctx = [whole(ctx[0])] + [loose(x) for x in ctx[1:]]
     far_packs = [whole(pack)] + [loose(p) for p in packs[1:]]
     share = (inputs, ((batch, rows, d), lambda ref, info: ref.at[:, pl.ds(pl.multiple_of(info[2] * rows, rows), rows), :]))
@@ -819,7 +826,7 @@
         "project_grads",
         project_grads_kernel,
         info,
-        [whole(inputs), *[whole(a) for a in lows], *biases],
+        [*[(inputs, (inputs.shape[1:], functools.partial(nth, at))) for at in range(batch)], *[whole(a) for a in lows], *biases],
         [[SDS((m, 2 * width), bf16)], [SDS((m + 8, 2 * width), bf16)], SDS((1, 2 * width), f32)],
         [pltpu.VMEM((3, d, width), f32), pltpu.VMEM((2, m, 2 * width), bf16)],
         parts=parts,
@@ -830,25 +837,31 @@
     got, far = after(got, swap(in_sum, "tensor", 2))
     terms_of[1].append(far)
     down_terms = down_kept + [down_more]
-    for i in range(2, bits):
-        down_terms, sent = halve(down_terms, bits - 1 - i, 1 << i, bit_of[i])
-    down_sum = summed(down_terms)
     at = up_y_next.size // d
     small = jnp.concatenate([small[0:6], small[7:8], small[7:8]]) + pair_sum(up_y, at, 8)
-    terms = up_kept + [up_more, up_y[:at].reshape(up_y_next.shape)]
+    up_terms = up_kept + [up_more, up_y[:at].reshape(up_y_next.shape)]
     for i in range(2, bits):
-        terms, sent, more = halve_with(terms, terms[0].ndim - 3, small, "dp", 1 << i, bit_of[i])
-        small = small + more
-    up_sum = summed(terms)
-    mine = small
+        down_terms, sent = halve_sum(down_terms, bits - 1 - i, bit_of[i])
+        down_got = swap(sent, "dp", 1 << i)
+        up_terms, sent = halve_sum(up_terms, bits - 1 - i, bit_of[i])
+        up_got = swap(with_rows(sent, small), "dp", 1 << i)
+        if i == bits - 1:
+            break
+        down_terms, up_terms, small = with_received(down_terms, down_got, up_terms, up_got, sent, small)
     row = 3 * (d // parts) // 2
     at = parts // 2 * row
     shape = ([2] * (bits - 1)) + [row, 2 * width]
     terms = [x.reshape(shape) for x in (w_keep, got[:at])]
     db = db + got[at : at + 1].astype(f32) + got[at + 1 : at + 2].astype(f32)
     for i in range(1, bits):
-        kept, sent, more = halve_with(terms, terms[0].ndim - 3, db, "dp", 1 << i, bit_of[i])
+        kept, rows_sent, more = halve_with(terms, terms[0].ndim - 3, db, "dp", 1 << i, bit_of[i])
+        if i == 1:
+            kept[-1], down_got, up_got = after(kept[-1], down_got, up_got)
         terms, db = kept, db + more
+    down_terms, up_terms, small = with_received(down_terms, down_got, up_terms, up_got, sent, small)
+    down_sum = summed(down_terms)
+    up_sum = summed(up_terms)
+    mine = small
     qkv_sum = summed(terms)
     qkv_sum = jnp.concatenate([qkv_sum[:, :width], qkv_sum[:, width:]], axis=0).reshape(3, -1, width)
     qkv_sum = jnp.transpose(qkv_sum, (1, 0, 2))
@@ -896,6 +909,12 @@
     return kept + [got[:cut].reshape(other.shape)], sent, pair_sum(got, cut, rows.shape[0])
 
 
+def with_received(down_terms, down_got, up_terms, up_got, sent, small):
+    at = sent.size // sent.shape[-1]
+    small = small + pair_sum(up_got, at, small.shape[0])
+    return down_terms + [down_got], up_terms + [up_got[:at].reshape(sent.shape)], small
+
+
 def after(*values):
     return lax.optimization_barrier(values)
 

time: 234 us -> 228 us (0.974)
  waiting for transfers between devices: 67.7 us -> 56 us
  Pallas kernels: 108 us -> 112 us
    ppermute x35 -> x37, waiting for transfers between devices: 67.7 us -> 56 us  [swap(): return lax.ppermute(x, axis, [(i, i ^ bit) for i in range(size)])]
    pallas_call x13, Pallas kernels: 108 us -> 112 us  [call(): pl.pallas_call(kernel, out_shape=[pltpu.HBM(o.shape, o.dtype) if i in far...]
    ppermute x35 -> x37, starting transfers between devices: 32.1 us -> 31.5 us  [swap(): return lax.ppermute(x, axis, [(i, i ^ bit) for i in range(size)])]
  transfers between devices with their start and end apart: 35 -> 37, of which waited for: 18 -> 21; matrix products, arithmetic and copies ran while one was open for 8% -> 6% of each run, Pallas kernels for 33% -> 34%
where the time goes in v2:
time: 228 us; the launch traced here: 227 us
  Pallas kernels  112 us (49%)
  waiting for transfers between devices  56 us (25%)
  starting transfers between devices  31.5 us (14%)
  other arithmetic  18.9 us (8%)
  local copies, waits for them, and re-layouts  6.63 us (3%)
    pallas_call x13, Pallas kernels, call(): pl.pallas_call(kernel, out_shape=[pltpu.HBM(o.shape, o.dtype) if i in far...  112 us
    ppermute x37, waiting for transfers between devices, swap(): return lax.ppermute(x, axis, [(i, i ^ bit) for i in range(size)])  56 us
    ppermute x37, starting transfers between devices, swap(): return lax.ppermute(x, axis, [(i, i ^ bit) for i in range(size)])  31.5 us
  transfers between devices with their start and end apart: 37, of which 21 were waited for; matrix products, arithmetic and copies ran while one was open for 6% of the time, Pallas kernels for 34%

profile of v2, /device:TPU:0, one launch (start us, length us, event | category | flops | bytes accessed | tf_op | source)
XLA Modules:
  0.0 226.7 jit_solution(3211434198441123412)
XLA Ops:
  0.6 1.3 broadcast_in_dim.3.refs_1_
  1.9 3.4 %prepare.1 = (bf16[200,768]{1,0:T(8,128)(2,1)}, bf16[192,768]{1,0:T(8,128)(2,1)}, bf16[192,768]{1,0:T(8,128)(2,1)}) custom-call(s32[2]{0:T(128)} %lengths_ref.25, s32[1]{0:T(128)} %constant.384.clone.1.which_ref, bf16[192,768]{1,0:T(8,128)(2,1)} %refs_0_.6, bf16[1,768]{1,0:T(2,128)(2,1)} %broadcast_in_dim.3.refs_1_, bf16[768,768]{1,0:T(8,128)(2,1)} %refs_4_.3, ...), custom_call_target="tpu_custom_call" | custom-call | flops 1000 | bytes 1000 | tf_op jit(solution)/shard_map/prepare/pallas_call | solution.py:91
  5.3 3.0 %collective-permute-start.1 = (bf16[200,768]{1,0:T(8,128)(2,1)}, bf16[200,768]{1,0:T(8,128)(2,1)S(1)}, u32[]{:S(2)}, u32[]{:S(2)}) collective-permute-start(bf16[200,768]{1,0:T(8,128)(2,1)} %get-tuple-element.135.refs_6_.refs_2_.refs_11_), channel_id=1, source_target_pairs={{0,2},{1,3},{2,0},{3,1},{4,6},{5,7},{6,4},{7,5},{8,10},{9,11},{10,... | collective-permute-start | bytes 921608 | tf_op jit(solution)/shard_map/ppermute | solution.py:600
  8.5 1.9 collective-permute-start.3
  10.4 16.3 %attend_fwd.1 = (bf16[2,1024,256]{2,1,0:T(8,128)(2,1)}, bf16[2,1024,256]{2,1,0:T(8,128)(2,1)}, bf16[2,1024,192]{2,1,0:T(8,128)(2,1)}, f32[2,4,8,256]{3,2,1,0:T(8...) custom-call(s32[2]{0:T(128)} %lengths_ref.25, ...), custom_call_target="tpu_custom_call" | custom-call | flops 1000 | bytes 1000 | tf_op jit(solution)/shard_map/attend_fwd/pallas_call | solution.py:91
  26.8 1.7 collective-permute-done.3
  28.5 1.7 collective-permute-start.7
  30.2 1.6 collective-permute-start.8
  31.8 1.5 collective-permute-start.5
  33.6 3.0 %collective-permute-done.7 = bf16[192,768]{1,0:T(8,128)(2,1)S(1)} collective-permute-done((bf16[192,768]{1,0:T(8,128)(2,1)S(1)}, bf16[192,768]{1,0:T(8,128)(2,1)S(1)}, u32[]{:S(2)}, u32[]{:S(2)}) %collective-permute-start.7) | collective-permute-done | bytes 294944 | tf_op jit(solution)/shard_map/ppermute | solution.py:600
  36.7 1.1 collective-permute-done.8
  37.8 1.8 collective-permute-done.5.refs_4_.refs_9_
  39.7 3.4 %collective-permute-done.6.refs_5_.refs_10_ = bf16[2,192,256]{2,1,0:T(8,128)(2,1)S(1)} collective-permute-done((bf16[2,192,256]{2,1,0:T(8,128)(2,1)}, bf16[2,192,256]{2,1,0:T(8,128)(2,1)S(1)}, u32[]{:S(2)}, u32[]{:S(2)}) %collective-permute-start.6) | collective-permute-done | bytes 196640 | tf_op jit(solution)/shard_map/ppermute | solution.py:600
  44.7 4.1 %first_norm.1 = (f32[512,768]{1,0:T(8,128)S(1)}, f32[512,1]{1,0:T(8,128)S(1)}, bf16[512,768]{1,0:T(8,128)(2,1)S(1)}) custom-call(s32[2]{0:T(128)S(1)} %copy-done, s32[1]{0:T(128)} %constant.384.clone.1.which_ref, bf16[2,1024,768]{2,1,0:T(8,128)(2,1)} %refs_1_.1, f32[6,768]{1,0:T(8,128)S(1)} %reshape.192.refs_1_.refs_0_, ...), custom_call_target="tpu_custom_call" | custom-call | flops 1000 | bytes 1000 | tf_op jit(solution)/shard_map/first_norm/pallas_call | solution.py:91
  49.9 1.3 collective-permute-done.10.refs_1_
  51.2 7.6 %feed.2 = (bf16[2,512,768]{2,1,0:T(8,128)(2,1)S(1)}, bf16[2,512,768]{2,1,0:T(8,128)(2,1)S(1)}, f32[512,768]{1,0:T(8,128)S(1)}, f32[512,768]{1,0:T(8,128)S(1)}) custom-call(s32[2]{0:T(128)S(1)} %copy-done, s32[1]{0:T(128)} %constant.384.clone.1.which_ref, bf16[512,768]{1,0:T(8,128)(2,1)S(1)} %get-tuple-element.152.refs_0_, ...), custom_call_target="tpu_custom_call" | custom-call | flops 1000 | bytes 1000 | tf_op jit(solution)/shard_map/feed/pallas_call | solution.py:91
  58.8 5.8 %collective-permute-done.11.refs_4_.refs_7_ = bf16[384,768]{1,0:T(8,128)(2,1)S(1)} collective-permute-done((bf16[384,768]{1,0:T(8,128)(2,1)S(1)}, bf16[384,768]{1,0:T(8,128)(2,1)S(1)}, u32[]{:S(2)}, u32[]{:S(2)}) %collective-permute-start.11) | collective-permute-done | bytes 589856 | tf_op jit(solution)/shard_map/ppermute | solution.py:600
  64.8 7.0 %feed.3 = (bf16[2,512,768]{2,1,0:T(8,128)(2,1)S(1)}, bf16[2,512,768]{2,1,0:T(8,128)(2,1)S(1)}, f32[512,768]{1,0:T(8,128)S(1)}, bf16[512,768]{1,0:T(8,128)(2,1)S(1)}) custom-call(s32[2]{0:T(128)S(1)} %copy-done, s32[1]{0:T(128)} %constant.384.clone.1.which_ref, bf16[512,768]{1,0:T(8,128)(2,1)S(1)} %get-tuple-element.152.refs_0_, ...), custom_call_target="tpu_custom_call" | custom-call | flops 1000 | bytes 1000 | tf_op jit(solution)/shard_map/feed/pallas_call | solution.py:91
  71.9 2.3 %collective-permute-done.13.refs_4_ = bf16[512,768]{1,0:T(8,128)(2,1)S(1)} collective-permute-done((bf16[512,768]{1,0:T(8,128)(2,1)S(1)}, bf16[512,768]{1,0:T(8,128)(2,1)S(1)}, u32[]{:S(2)}, u32[]{:S(2)}) %collective-permute-start.13) | collective-permute-done | bytes 786464 | tf_op jit(solution)/shard_map/ppermute | solution.py:600
  74.2 4.1 %second_norm.1 = (bf16[2,256,768]{2,1,0:T(8,128)(2,1)}, f32[512,768]{1,0:T(8,128)S(1)}, bf16[512,768]{1,0:T(8,128)(2,1)S(1)}, f32[8,768]{1,0:T(8,128)S(1)}) custom-call(s32[2]{0:T(128)S(1)} %copy-done, s32[1]{0:T(128)} %constant.384.clone.1.which_ref, bf16[2,256,768]{2,1,0:T(8,128)(2,1)} %refs_0_.8, f32[6,768]{1,0:T(8,128)S(1)} %reshape.192.refs_1_.refs_0_, ...), custom_call_target="tpu_custom_call" | custom-call | flops 1000 | bytes 1000 | tf_op jit(solution)/shard_map/second_norm/pallas_call | solution.py:91
  78.5 2.1 collective-permute-done.14.refs_1_.refs_3_
  80.6 10.2 %feed_back.1 = (bf16[2,2,512,768]{3,2,1,0:T(8,128)(2,1)S(1)}, f32[512,768]{1,0:T(8,128)S(1)}, bf16[512,768]{1,0:T(8,128)(2,1)S(1)}, f32[8,768]{1,0:T(8,128)S(1)}) custom-call(s32[2]{0:T(128)S(1)} %copy-done, s32[1]{0:T(128)} %constant.384.clone.1.which_ref, bf16[512,768]{1,0:T(8,128)(2,1)S(1)} %get-tuple-element.166.refs_0_.refs_2_, ...), custom_call_target="tpu_custom_call" | custom-call | flops 1000 | bytes 1000 | tf_op jit(solution)/shard_map/feed_back/pallas_call | solution.py:91
  91.1 2.1 collective-permute-done.15.refs_4_
  93.3 7.1 %first_back.1 = (f32[512,768]{1,0:T(8,128)}, bf16[2,192,256]{2,1,0:T(8,128)(2,1)}, bf16[2,192,256]{2,1,0:T(8,128)(2,1)}, bf16[2,192,256]{2,1,0:T(8,128)(2,1)}, b...) custom-call(s32[2]{0:T(128)S(1)} %copy-done, ...), custom_call_target="tpu_custom_call" | custom-call | flops 1000 | bytes 1000 | tf_op jit(solution)/shard_map/first_back/pallas_call | solution.py:91
  100.6 5.3 %down_grads.1 = (bf16[4,96,768]{2,1,0:T(8,128)(2,1)}, bf16[4,96,768]{2,1,0:T(8,128)(2,1)}, bf16[2,4,96,768]{3,2,1,0:T(8,128)(2,1)}) custom-call(s32[2]{0:T(128)S(1)} %copy-done, s32[1]{0:T(128)} %constant.384.clone.1.which_ref, bf16[2,512,768]{2,1,0:T(8,128)(2,1)S(1)} %get-tuple-element.195.refs_0_, bf16[2,512,768]{2,1,0:T(8,128)(2,1)S(1)} %get-tuple-element.196.refs_1_, ...), custom_call_target="tpu_custom_call" | custom-call | flops 1000 | bytes 1000 | tf_op jit(solution)/shard_map/down_grads/pallas_call | solution.py:91
  106.5 1.7 collective-permute-start.17
  108.3 5.6 %up_grads.1 = (bf16[480,768]{1,0:T(8,128)(2,1)}, bf16[496,768]{1,0:T(8,128)(2,1)}, bf16[480,768]{1,0:T(8,128)(2,1)}, bf16[480,768]{1,0:T(8,128)(2,1)}, f32[8,768]{1,0:T(8,128)S(1)}) custom-call(s32[2]{0:T(128)S(1)} %copy-done, s32[1]{0:T(128)} %constant.384.clone.1.which_ref, bf16[512,768]{1,0:T(8,128)(2,1)S(1)} %get-tuple-element.152.refs_0_, ...), custom_call_target="tpu_custom_call" | custom-call | flops 1000 | bytes 1000 | tf_op jit(solution)/shard_map/up_grads/pallas_call | solution.py:91
  114.2 3.3 %collective-permute-done.18.refs_9_ = bf16[2,192,256]{2,1,0:T(8,128)(2,1)S(1)} collective-permute-done((bf16[2,192,256]{2,1,0:T(8,128)(2,1)S(1)}, bf16[2,192,256]{2,1,0:T(8,128)(2,1)S(1)}, u32[]{:S(2)}, u32[]{:S(2)}) %collective-permute-start.18) | collective-permute-done | bytes 196640 | tf_op jit(solution)/shard_map/ppermute | solution.py:600
  117.5 1.7 collective-permute-start.20
  119.2 16.3 %attend_bwd.2 = (bf16[2,256,768]{2,1,0:T(8,128)(2,1)}, bf16[2,256,768]{2,1,0:T(8,128)(2,1)}, bf16[3,1024,192]{2,1,0:T(8,128)(2,1)}, f32[1,384]{1,0:T(1,128)}) custom-call(s32[2]{0:T(128)} %lengths_ref.25, s32[1]{0:T(128)} %constant.384.clone.1.which_ref, bf16[3,192,768]{2,1,0:T(8,128)(2,1)} %bitcast.109, bf16[2,1024,256]{2,1,0:T(8,128)(2,1)} %get-tuple-element.160.refs_1_, ...), custom_call_target="tpu_custom_call" | custom-call | flops 10000000000 | bytes 1000 | tf_op jit(solution)/shard_map/attend_bwd/pallas_call | solution.py:91
  135.5 1.7 collective-permute-done.20
  137.5 0.8 pad_maximum_fusion.3
  138.3 1.0 fusion
  139.8 1.8 fusion.6
  141.6 1.7 collective-permute-start.25
  143.3 1.5 collective-permute-start.26
  145.3 1.6 collective-permute-start.24
  146.9 16.0 %attend_bwd.3 = (bf16[2,256,768]{2,1,0:T(8,128)(2,1)}, bf16[2,256,768]{2,1,0:T(8,128)(2,1)}, bf16[3,1024,192]{2,1,0:T(8,128)(2,1)}, f32[1,384]{1,0:T(1,128)}) custom-call(s32[2]{0:T(128)} %lengths_ref.25, s32[1]{0:T(128)} %constant.385.clone.1.which_ref, bf16[3,192,768]{2,1,0:T(8,128)(2,1)} %bitcast.110, bf16[2,1024,256]{2,1,0:T(8,128)(2,1)} %get-tuple-element.160.refs_1_, ...), custom_call_target="tpu_custom_call" | custom-call | flops 10000000000 | bytes 1000 | tf_op jit(solution)/shard_map/attend_bwd/pallas_call | solution.py:91
  163.0 4.0 %collective-permute-done.23 = bf16[4,96,768]{2,1,0:T(8,128)(2,1)S(1)} collective-permute-done((bf16[4,96,768]{2,1,0:T(8,128)(2,1)}, bf16[4,96,768]{2,1,0:T(8,128)(2,1)S(1)}, u32[]{:S(2)}, u32[]{:S(2)}) %collective-permute-start.23) | collective-permute-done | bytes 589856 | tf_op jit(solution)/shard_map/ppermute | solution.py:600
  167.0 0.8 add_add_fusion.1
  167.9 0.9 fusion.10
  168.8 0.8 fusion.13
  169.7 1.1 fusion.5
  170.9 1.6 collective-permute-start.29
  173.0 1.6 collective-permute-start.28
  174.6 9.2 %project_grads.1 = (bf16[576,384]{1,0:T(8,128)(2,1)}, bf16[584,384]{1,0:T(8,128)(2,1)}, f32[1,384]{1,0:T(1,128)}) custom-call(s32[2]{0:T(128)} %lengths_ref.25, s32[1]{0:T(128)} %constant.384.clone.1.which_ref, bf16[2,1024,768]{2,1,0:T(8,128)(2,1)} %refs_1_.1, bf16[2,1024,768]{2,1,0:T(8,128)(2,1)} %refs_1_.1, ...), custom_call_target="tpu_custom_call" | custom-call | flops 1000 | bytes 1000 | tf_op jit(solution)/shard_map/project_grads/pallas_call | solution.py:91
  183.8 1.5 collective-permute-start.31
  185.4 1.1 fusion.7
  186.5 1.0 slice.169
  187.6 1.1 fusion.15
  188.6 2.7 %collective-permute-start.34 = (bf16[96,768]{1,0:T(8,128)(2,1)S(1)}, bf16[96,768]{1,0:T(8,128)(2,1)S(1)}, u32[]{:S(2)}, u32[]{:S(2)}) collective-permute-start(bf16[96,768]{1,0:T(8,128)(2,1)S(1)} %fusion.15), channel_id=1, source_target_pairs={{0,16},{4,20},{8,24},{12,28},{16,0},{20,4},{24,8},{28,12},{1,17},{... | collective-permute-start | bytes 442376 | tf_op jit(solution)/shard_map/ppermute | solution.py:600
  191.8 1.2 fusion.12
  193.0 0.7 subtract_convert_fusion
  194.1 1.8 collective-permute-done.31
  196.0 5.4 %collective-permute-done.32 = bf16[256,768]{1,0:T(8,128)(2,1)S(1)} collective-permute-done((bf16[256,768]{1,0:T(8,128)(2,1)S(1)}, bf16[256,768]{1,0:T(8,128)(2,1)S(1)}, u32[]{:S(2)}, u32[]{:S(2)}) %collective-permute-start.32) | collective-permute-done | bytes 393248 | tf_op jit(solution)/shard_map/ppermute | solution.py:600
  202.1 1.5 fusion.8
  203.6 0.9 pad_maximum_fusion
  204.6 7.0 %collective-permute-done.33 = bf16[290,384]{1,0:T(8,128)(2,1)S(1)} collective-permute-done((bf16[290,384]{1,0:T(8,128)(2,1)S(1)}, bf16[290,384]{1,0:T(8,128)(2,1)S(1)}, u32[]{:S(2)}, u32[]{:S(2)}) %collective-permute-start.33) | collective-permute-done | bytes 222752 | tf_op jit(solution)/shard_map/ppermute | solution.py:600
  211.6 1.0 fusion.11
  213.3 0.7 slice.212
  214.0 1.7 fusion.14
  217.2 7.0 %collective-permute-done.36 = bf16[146,384]{1,0:T(8,128)(2,1)S(1)} collective-permute-done((bf16[146,384]{1,0:T(8,128)(2,1)S(1)}, bf16[146,384]{1,0:T(8,128)(2,1)S(1)}, u32[]{:S(2)}, u32[]{:S(2)}) %collective-permute-start.36) | collective-permute-done | bytes 112160 | tf_op jit(solution)/shard_map/ppermute | solution.py:600
  224.9 1.0 fusion.17
  225.9 0.7 pad_maximum_fusion.5
  (138 shorter events, 11.5 us)
Async XLA Ops:
  5.3 23.2 %collective-permute-start.1 = (bf16[200,768]{1,0:T(8,128)(2,1)}, bf16[200,768]{1,0:T(8,128)(2,1)S(1)}, u32[]{:S(2)}, u32[]{:S(2)}) collective-permute-start(bf16[200,768]{1,0:T(8,128)(2,1)} %get-tuple-element.135.refs_6_.refs_2_.refs_11_), channel_id=1, source_target_pairs={{0,2},{1,3},{2,0},{3,1},{4,6},{5,7},{6,4},{7,5},{8,10},{9,11},{10,... | collective-permute-start | bytes 921608 | tf_op jit(solution)/shard_map/ppermute | solution.py:600
  8.3 20.1 %collective-permute-start = (bf16[200,768]{1,0:T(8,128)(2,1)}, bf16[200,768]{1,0:T(8,128)(2,1)S(1)}, u32[]{:S(2)}, u32[]{:S(2)}) collective-permute-start(bf16[200,768]{1,0:T(8,128)(2,1)} %get-tuple-element.135.refs_6_.refs_2_.refs_11_), channel_id=1, source_target_pairs={{0,1},{1,0},{2,3},{3,2},{4,5},{5,4},{6,7},{7,6},{8,9},{9,8},{10,11... | collective-permute-start | bytes 921608 | tf_op jit(solution)/shard_map/ppermute | solution.py:600
  8.3 18.4 %collective-permute-start.2 = (bf16[192,768]{1,0:T(8,128)(2,1)}, bf16[192,768]{1,0:T(8,128)(2,1)S(1)}, u32[]{:S(2)}, u32[]{:S(2)}) collective-permute-start(bf16[192,768]{1,0:T(8,128)(2,1)} %get-tuple-element.136), channel_id=1, source_target_pairs={{0,2},{1,3},{2,0},{3,1},{4,6},{5,7},{6,4},{7,5},{8,10},{9,11},{10,... | collective-permute-start | bytes 884744 | tf_op jit(solution)/shard_map/ppermute | solution.py:600
  8.5 20.0 %collective-permute-start.3 = (bf16[192,768]{1,0:T(8,128)(2,1)}, bf16[192,768]{1,0:T(8,128)(2,1)S(1)}, u32[]{:S(2)}, u32[]{:S(2)}) collective-permute-start(bf16[192,768]{1,0:T(8,128)(2,1)} %get-tuple-element.137), channel_id=1, source_target_pairs={{0,2},{1,3},{2,0},{3,1},{4,6},{5,7},{6,4},{7,5},{8,10},{9,11},{10,... | collective-permute-start | bytes 884744 | tf_op jit(solution)/shard_map/ppermute | solution.py:600
  26.7 16.6 %copy-start.17 = (bf16[768]{0:T(1024)(128)(2,1)S(1)}, bf16[768]{0:T(1024)(128)(2,1)}, u32[]{:S(2)}) copy-start(bf16[768]{0:T(1024)(128)(2,1)} %param.21) | copy-start | bytes 4612
  26.7 16.8 %copy-start.18 = (bf16[768]{0:T(1024)(128)(2,1)S(1)}, bf16[768]{0:T(1024)(128)(2,1)}, u32[]{:S(2)}) copy-start(bf16[768]{0:T(1024)(128)(2,1)} %param.22) | copy-start | bytes 4612
  26.7 17.0 %copy-start.19 = (bf16[768]{0:T(1024)(128)(2,1)S(1)}, bf16[768]{0:T(1024)(128)(2,1)}, u32[]{:S(2)}) copy-start(bf16[768]{0:T(1024)(128)(2,1)} %param.23) | copy-start | bytes 4612
  26.7 17.2 %copy-start.20 = (bf16[768]{0:T(1024)(128)(2,1)S(1)}, bf16[768]{0:T(1024)(128)(2,1)}, u32[]{:S(2)}) copy-start(bf16[768]{0:T(1024)(128)(2,1)} %param.27) | copy-start | bytes 4612
  26.7 17.4 %copy-start.21 = (bf16[768]{0:T(1024)(128)(2,1)S(1)}, bf16[768]{0:T(1024)(128)(2,1)}, u32[]{:S(2)}) copy-start(bf16[768]{0:T(1024)(128)(2,1)} %param.28) | copy-start | bytes 4612
  26.8 17.6 %copy-start.22 = (bf16[768]{0:T(1024)(128)(2,1)S(1)}, bf16[768]{0:T(1024)(128)(2,1)}, u32[]{:S(2)}) copy-start(bf16[768]{0:T(1024)(128)(2,1)} %param.29) | copy-start | bytes 4612
  26.8 17.9 %copy-start = (s32[2]{0:T(128)S(1)}, s32[2]{0:T(128)}, u32[]{:S(2)}) copy-start(s32[2]{0:T(128)} %lengths_ref.25) | copy-start | bytes 28
  28.5 8.2 %collective-permute-start.7 = (bf16[192,768]{1,0:T(8,128)(2,1)S(1)}, bf16[192,768]{1,0:T(8,128)(2,1)S(1)}, u32[]{:S(2)}, u32[]{:S(2)}) collective-permute-start(bf16[192,768]{1,0:T(8,128)(2,1)S(1)} %collective-permute-done.2), channel_id=1, source_target_pairs={{0,4},{4,0},{8,12},{12,8},{16,20},{20,16},{24,28},{28,24},{1,5},{5... | collective-permute-start | bytes 884744 | tf_op jit(solution)/shard_map/ppermute | solution.py:600
  30.2 7.6 %collective-permute-start.8 = (bf16[192,768]{1,0:T(8,128)(2,1)S(1)}, bf16[192,768]{1,0:T(8,128)(2,1)S(1)}, u32[]{:S(2)}, u32[]{:S(2)}) collective-permute-start(bf16[192,768]{1,0:T(8,128)(2,1)S(1)} %collective-permute-done.3), channel_id=1, source_target_pairs={{0,8},{4,12},{8,0},{12,4},{16,24},{20,28},{24,16},{28,20},{1,9},{5... | collective-permute-start | bytes 884744 | tf_op jit(solution)/shard_map/ppermute | solution.py:600
  31.8 6.1 %collective-permute-start.4 = (bf16[2,192,256]{2,1,0:T(8,128)(2,1)}, bf16[2,192,256]{2,1,0:T(8,128)(2,1)S(1)}, u32[]{:S(2)}, u32[]{:S(2)}) collective-permute-start(bf16[2,192,256]{2,1,0:T(8,128)(2,1)} %get-tuple-element.139), channel_id=1, source_target_pairs={{0,1},{1,0},{2,3},{3,2},{4,5},{5,4},{6,7},{7,6},{8,9},{9,8},{10,11... | collective-permute-start | bytes 589832 | tf_op jit(solution)/shard_map/ppermute | solution.py:600
  31.8 7.9 %collective-permute-start.5 = (bf16[2,192,256]{2,1,0:T(8,128)(2,1)}, bf16[2,192,256]{2,1,0:T(8,128)(2,1)S(1)}, u32[]{:S(2)}, u32[]{:S(2)}) collective-permute-start(bf16[2,192,256]{2,1,0:T(8,128)(2,1)} %get-tuple-element.140), channel_id=1, source_target_pairs={{0,2},{1,3},{2,0},{3,1},{4,6},{5,7},{6,4},{7,5},{8,10},{9,11},{10,... | collective-permute-start | bytes 589832 | tf_op jit(solution)/shard_map/ppermute | solution.py:600
  33.3 9.8 %collective-permute-start.6 = (bf16[2,192,256]{2,1,0:T(8,128)(2,1)}, bf16[2,192,256]{2,1,0:T(8,128)(2,1)S(1)}, u32[]{:S(2)}, u32[]{:S(2)}) collective-permute-start(bf16[2,192,256]{2,1,0:T(8,128)(2,1)} %get-tuple-element.141), channel_id=1, source_target_pairs={{0,3},{1,2},{2,1},{3,0},{4,7},{5,6},{6,5},{7,4},{8,11},{9,10},{10,... | collective-permute-start | bytes 589832 | tf_op jit(solution)/shard_map/ppermute | solution.py:600
  43.1 1.6 collective-permute-start.9
  48.8 2.4 %collective-permute-start.10 = (bf16[512,768]{1,0:T(8,128)(2,1)S(1)}, bf16[512,768]{1,0:T(8,128)(2,1)S(1)}, u32[]{:S(2)}, u32[]{:S(2)}) collective-permute-start(bf16[512,768]{1,0:T(8,128)(2,1)S(1)} %get-tuple-element.152.refs_0_), channel_id=1, source_target_pairs={{0,1},{1,0},{2,3},{3,2},{4,5},{5,4},{6,7},{7,6},{8,9},{9,8},{10,11... | collective-permute-start | bytes 2359304 | tf_op jit(solution)/shard_map/ppermute | solution.py:600
  49.1 15.5 %collective-permute-start.11 = (bf16[384,768]{1,0:T(8,128)(2,1)S(1)}, bf16[384,768]{1,0:T(8,128)(2,1)S(1)}, u32[]{:S(2)}, u32[]{:S(2)}) collective-permute-start(bf16[384,768]{1,0:T(8,128)(2,1)S(1)} %pad_maximum_fusion.1.refs_3_.refs_6_), channel_id=1, source_target_pairs={{0,8},{4,12},{8,0},{12,4},{16,24},{20,28},{24,16},{28,20},{1,9},{5... | collective-permute-start | bytes 1769480 | tf_op jit(solution)/shard_map/ppermute | solution.py:600
  49.6 15.3 %collective-permute-start.12 = (bf16[384,768]{1,0:T(8,128)(2,1)S(1)}, bf16[384,768]{1,0:T(8,128)(2,1)S(1)}, u32[]{:S(2)}, u32[]{:S(2)}) collective-permute-start(bf16[384,768]{1,0:T(8,128)(2,1)S(1)} %pad_maximum_fusion.2.refs_5_.refs_8_), channel_id=1, source_target_pairs={{0,4},{4,0},{8,12},{12,8},{16,20},{20,16},{24,28},{28,24},{1,5},{5... | collective-permute-start | bytes 1769480 | tf_op jit(solution)/shard_map/ppermute | solution.py:600
  71.9 2.4 %collective-permute-start.13 = (bf16[512,768]{1,0:T(8,128)(2,1)S(1)}, bf16[512,768]{1,0:T(8,128)(2,1)S(1)}, u32[]{:S(2)}, u32[]{:S(2)}) collective-permute-start(bf16[512,768]{1,0:T(8,128)(2,1)S(1)} %get-tuple-element.158), channel_id=1, source_target_pairs={{0,1},{1,0},{2,3},{3,2},{4,5},{5,4},{6,7},{7,6},{8,9},{9,8},{10,11... | collective-permute-start | bytes 2359304 | tf_op jit(solution)/shard_map/ppermute | solution.py:600
  78.3 2.4 %collective-permute-start.14 = (bf16[512,768]{1,0:T(8,128)(2,1)S(1)}, bf16[512,768]{1,0:T(8,128)(2,1)S(1)}, u32[]{:S(2)}, u32[]{:S(2)}) collective-permute-start(bf16[512,768]{1,0:T(8,128)(2,1)S(1)} %get-tuple-element.166.refs_0_.refs_2_), channel_id=1, source_target_pairs={{0,1},{1,0},{2,3},{3,2},{4,5},{5,4},{6,7},{7,6},{8,9},{9,8},{10,11... | collective-permute-start | bytes 2359304 | tf_op jit(solution)/shard_map/ppermute | solution.py:600
  90.9 2.4 %collective-permute-start.15 = (bf16[512,768]{1,0:T(8,128)(2,1)S(1)}, bf16[512,768]{1,0:T(8,128)(2,1)S(1)}, u32[]{:S(2)}, u32[]{:S(2)}) collective-permute-start(bf16[512,768]{1,0:T(8,128)(2,1)S(1)} %get-tuple-element.170), channel_id=1, source_target_pairs={{0,1},{1,0},{2,3},{3,2},{4,5},{5,4},{6,7},{7,6},{8,9},{9,8},{10,11... | collective-permute-start | bytes 2359304 | tf_op jit(solution)/shard_map/ppermute | solution.py:600
  100.4 7.9 %collective-permute-start.19 = (bf16[2,200,768]{2,1,0:T(8,128)(2,1)}, bf16[2,200,768]{2,1,0:T(8,128)(2,1)S(1)}, u32[]{:S(2)}, u32[]{:S(2)}) collective-permute-start(bf16[2,200,768]{2,1,0:T(8,128)(2,1)} %get-tuple-element.179), channel_id=1, source_target_pairs={{0,1},{1,0},{2,3},{3,2},{4,5},{5,4},{6,7},{7,6},{8,9},{9,8},{10,11... | collective-permute-start | bytes 1843208 | tf_op jit(solution)/shard_map/ppermute | solution.py:600
  100.6 5.8 %copy-start.29 = (bf16[2,192,256]{2,1,0:T(8,128)(2,1)S(1)}, bf16[2,192,256]{2,1,0:T(8,128)(2,1)}, u32[]{:S(2)}) copy-start(bf16[2,192,256]{2,1,0:T(8,128)(2,1)} %get-tuple-element.174) | copy-start | bytes 589828
  100.6 5.9 %copy-start.28 = (bf16[2,192,256]{2,1,0:T(8,128)(2,1)S(1)}, bf16[2,192,256]{2,1,0:T(8,128)(2,1)}, u32[]{:S(2)}) copy-start(bf16[2,192,256]{2,1,0:T(8,128)(2,1)} %get-tuple-element.175) | copy-start | bytes 589828
  100.6 7.6 %copy-start.27 = (bf16[2,192,256]{2,1,0:T(8,128)(2,1)S(1)}, bf16[2,192,256]{2,1,0:T(8,128)(2,1)}, u32[]{:S(2)}) copy-start(bf16[2,192,256]{2,1,0:T(8,128)(2,1)} %get-tuple-element.176) | copy-start | bytes 589828
  105.9 29.6 %collective-permute-start.21 = (bf16[2,4,96,768]{3,2,1,0:T(8,128)(2,1)}, bf16[2,4,96,768]{3,2,1,0:T(8,128)(2,1)S(1)}, u32[]{:S(2)}, u32[]{:S(2)}) collective-permute-start(bf16[2,4,96,768]{3,2,1,0:T(8,128)(2,1)} %get-tuple-element.197), channel_id=1, source_target_pairs={{0,4},{4,0},{8,12},{12,8},{16,20},{20,16},{24,28},{28,24},{1,5},{5... | collective-permute-start | bytes 3538952 | tf_op jit(solution)/shard_map/ppermute | solution.py:600
  106.4 7.5 %collective-permute-start.16 = (bf16[2,192,256]{2,1,0:T(8,128)(2,1)S(1)}, bf16[2,192,256]{2,1,0:T(8,128)(2,1)S(1)}, u32[]{:S(2)}, u32[]{:S(2)}) collective-permute-start(bf16[2,192,256]{2,1,0:T(8,128)(2,1)S(1)} %copy-done.29), channel_id=1, source_target_pairs={{0,1},{1,0},{2,3},{3,2},{4,5},{5,4},{6,7},{7,6},{8,9},{9,8},{10,11... | collective-permute-start | bytes 589832 | tf_op jit(solution)/shard_map/ppermute | solution.py:600
  106.5 7.7 %collective-permute-start.17 = (bf16[2,192,256]{2,1,0:T(8,128)(2,1)S(1)}, bf16[2,192,256]{2,1,0:T(8,128)(2,1)S(1)}, u32[]{:S(2)}, u32[]{:S(2)}) collective-permute-start(bf16[2,192,256]{2,1,0:T(8,128)(2,1)S(1)} %copy-done.28), channel_id=1, source_target_pairs={{0,2},{1,3},{2,0},{3,1},{4,6},{5,7},{6,4},{7,5},{8,10},{9,11},{10,... | collective-permute-start | bytes 589832 | tf_op jit(solution)/shard_map/ppermute | solution.py:600
  108.1 9.3 %collective-permute-start.18 = (bf16[2,192,256]{2,1,0:T(8,128)(2,1)S(1)}, bf16[2,192,256]{2,1,0:T(8,128)(2,1)S(1)}, u32[]{:S(2)}, u32[]{:S(2)}) collective-permute-start(bf16[2,192,256]{2,1,0:T(8,128)(2,1)S(1)} %copy-done.27), channel_id=1, source_target_pairs={{0,3},{1,2},{2,1},{3,0},{4,7},{5,6},{6,5},{7,4},{8,11},{9,10},{10,... | collective-permute-start | bytes 589832 | tf_op jit(solution)/shard_map/ppermute | solution.py:600
  113.9 5.3 %copy-start.24 = (bf16[2,192,256]{2,1,0:T(8,128)(2,1)}, bf16[2,192,256]{2,1,0:T(8,128)(2,1)S(1)}, u32[]{:S(2)}) copy-start(bf16[2,192,256]{2,1,0:T(8,128)(2,1)S(1)} %collective-permute-done.16.refs_7_) | copy-start | bytes 589828
  114.2 5.0 %copy-start.25 = (bf16[2,192,256]{2,1,0:T(8,128)(2,1)}, bf16[2,192,256]{2,1,0:T(8,128)(2,1)S(1)}, u32[]{:S(2)}) copy-start(bf16[2,192,256]{2,1,0:T(8,128)(2,1)S(1)} %collective-permute-done.17.refs_8_) | copy-start | bytes 589828
  117.5 19.7 %collective-permute-start.20 = (bf16[496,768]{1,0:T(8,128)(2,1)}, bf16[496,768]{1,0:T(8,128)(2,1)S(1)}, u32[]{:S(2)}, u32[]{:S(2)}) collective-permute-start(bf16[496,768]{1,0:T(8,128)(2,1)} %get-tuple-element.194), channel_id=1, source_target_pairs={{0,8},{4,12},{8,0},{12,4},{16,24},{20,28},{24,16},{28,20},{1,9},{5... | collective-permute-start | bytes 2285576 | tf_op jit(solution)/shard_map/ppermute | solution.py:600
  137.2 2.6 %collective-permute-start.22 = (bf16[2,256,768]{2,1,0:T(8,128)(2,1)}, bf16[2,256,768]{2,1,0:T(8,128)(2,1)}, u32[]{:S(2)}, u32[]{:S(2)}) collective-permute-start(bf16[2,256,768]{2,1,0:T(8,128)(2,1)} %get-tuple-element.198), channel_id=1, source_target_pairs={{0,1},{1,0},{2,3},{3,2},{4,5},{5,4},{6,7},{7,6},{8,9},{9,8},{10,11... | collective-permute-start | bytes 2359304 | tf_op jit(solution)/shard_map/ppermute | solution.py:600
  137.5 2.3 %copy-start.2 = (bf16[2,256,768]{2,1,0:T(8,128)(2,1)S(1)}, bf16[2,256,768]{2,1,0:T(8,128)(2,1)}, u32[]{:S(2)}) copy-start(bf16[2,256,768]{2,1,0:T(8,128)(2,1)} %get-tuple-element.192) | copy-start | bytes 2359300
  141.6 26.3 %copy-start.5 = (bf16[480,768]{1,0:T(8,128)(2,1)S(1)}, bf16[480,768]{1,0:T(8,128)(2,1)}, u32[]{:S(2)}) copy-start(bf16[480,768]{1,0:T(8,128)(2,1)} %get-tuple-element.224) | copy-start | bytes 2211844
  141.6 27.2 %copy-start.10 = (bf16[4,96,768]{2,1,0:T(8,128)(2,1)S(1)}, bf16[4,96,768]{2,1,0:T(8,128)(2,1)}, u32[]{:S(2)}) copy-start(bf16[4,96,768]{2,1,0:T(8,128)(2,1)} %get-tuple-element.221) | copy-start | bytes 1769476
  141.6 21.3 %collective-permute-start.25 = (bf16[256,768]{1,0:T(8,128)(2,1)}, bf16[256,768]{1,0:T(8,128)(2,1)}, u32[]{:S(2)}, u32[]{:S(2)}) collective-permute-start(bf16[256,768]{1,0:T(8,128)(2,1)} %pad_maximum_fusion.3), channel_id=1, source_target_pairs={{0,4},{4,0},{8,12},{12,8},{16,20},{20,16},{24,28},{28,24},{1,5},{5... | collective-permute-start | bytes 1179656 | tf_op jit(solution)/shard_map/ppermute | solution.py:600
  143.3 19.7 %collective-permute-start.26 = (bf16[256,768]{1,0:T(8,128)(2,1)}, bf16[256,768]{1,0:T(8,128)(2,1)S(1)}, u32[]{:S(2)}, u32[]{:S(2)}) collective-permute-start(bf16[256,768]{1,0:T(8,128)(2,1)} %fusion.6), channel_id=1, source_target_pairs={{0,2},{1,3},{2,0},{3,1},{4,6},{5,7},{6,4},{7,5},{8,10},{9,11},{10,... | collective-permute-start | bytes 1179656 | tf_op jit(solution)/shard_map/ppermute | solution.py:600
  144.8 22.2 %collective-permute-start.23 = (bf16[4,96,768]{2,1,0:T(8,128)(2,1)}, bf16[4,96,768]{2,1,0:T(8,128)(2,1)S(1)}, u32[]{:S(2)}, u32[]{:S(2)}) collective-permute-start(bf16[4,96,768]{2,1,0:T(8,128)(2,1)} %fusion), channel_id=1, source_target_pairs={{0,2},{1,3},{2,0},{3,1},{4,6},{5,7},{6,4},{7,5},{8,10},{9,11},{10,... | collective-permute-start | bytes 1769480 | tf_op jit(solution)/shard_map/ppermute | solution.py:600
  145.3 21.7 %collective-permute-start.24 = (bf16[480,768]{1,0:T(8,128)(2,1)}, bf16[480,768]{1,0:T(8,128)(2,1)S(1)}, u32[]{:S(2)}, u32[]{:S(2)}) collective-permute-start(bf16[480,768]{1,0:T(8,128)(2,1)} %get-tuple-element.212), channel_id=1, source_target_pairs={{0,8},{4,12},{8,0},{12,4},{16,24},{20,28},{24,16},{28,20},{1,9},{5... | collective-permute-start | bytes 2211848 | tf_op jit(solution)/shard_map/ppermute | solution.py:600
  163.0 7.8 %copy-start.15 = (bf16[256,768]{1,0:T(8,128)(2,1)}, bf16[256,768]{1,0:T(8,128)(2,1)S(1)}, u32[]{:S(2)}) copy-start(bf16[256,768]{1,0:T(8,128)(2,1)S(1)} %collective-permute-done.26) | copy-start | bytes 1179652
  167.0 3.8 %copy-start.12 = (bf16[4,96,768]{2,1,0:T(8,128)(2,1)}, bf16[4,96,768]{2,1,0:T(8,128)(2,1)S(1)}, u32[]{:S(2)}) copy-start(bf16[4,96,768]{2,1,0:T(8,128)(2,1)S(1)} %collective-permute-done.23) | copy-start | bytes 1769476
  167.0 2.7 %copy-start.7 = (bf16[480,768]{1,0:T(8,128)(2,1)}, bf16[480,768]{1,0:T(8,128)(2,1)S(1)}, u32[]{:S(2)}) copy-start(bf16[480,768]{1,0:T(8,128)(2,1)S(1)} %collective-permute-done.24) | copy-start | bytes 2211844
  167.8 17.5 %collective-permute-start.27 = (bf16[2,256,768]{2,1,0:T(8,128)(2,1)}, bf16[2,256,768]{2,1,0:T(8,128)(2,1)}, u32[]{:S(2)}, u32[]{:S(2)}) collective-permute-start(bf16[2,256,768]{2,1,0:T(8,128)(2,1)} %get-tuple-element.218), channel_id=1, source_target_pairs={{0,1},{1,0},{2,3},{3,2},{4,5},{5,4},{6,7},{7,6},{8,9},{9,8},{10,11... | collective-permute-start | bytes 2359304 | tf_op jit(solution)/shard_map/ppermute | solution.py:600
  170.9 13.0 %collective-permute-start.29 = (bf16[256,768]{1,0:T(8,128)(2,1)S(1)}, bf16[256,768]{1,0:T(8,128)(2,1)}, u32[]{:S(2)}, u32[]{:S(2)}) collective-permute-start(bf16[256,768]{1,0:T(8,128)(2,1)S(1)} %pad_maximum_fusion.4), channel_id=1, source_target_pairs={{0,2},{1,3},{2,0},{3,1},{4,6},{5,7},{6,4},{7,5},{8,10},{9,11},{10,... | collective-permute-start | bytes 1179656 | tf_op jit(solution)/shard_map/ppermute | solution.py:600
  172.4 11.4 %collective-permute-start.30 = (bf16[2,120,768]{2,1,0:T(8,128)(2,1)}, bf16[2,120,768]{2,1,0:T(8,128)(2,1)}, u32[]{:S(2)}, u32[]{:S(2)}) collective-permute-start(bf16[2,120,768]{2,1,0:T(8,128)(2,1)} %fusion.10), channel_id=1, source_target_pairs={{0,4},{4,0},{8,12},{12,8},{16,20},{20,16},{24,28},{28,24},{1,5},{5... | collective-permute-start | bytes 1105928 | tf_op jit(solution)/shard_map/ppermute | solution.py:600
  173.0 10.8 %collective-permute-start.28 = (bf16[2,96,768]{2,1,0:T(8,128)(2,1)}, bf16[2,96,768]{2,1,0:T(8,128)(2,1)}, u32[]{:S(2)}, u32[]{:S(2)}) collective-permute-start(bf16[2,96,768]{2,1,0:T(8,128)(2,1)} %fusion.13), channel_id=1, source_target_pairs={{0,8},{4,12},{8,0},{12,4},{16,24},{20,28},{24,16},{28,20},{1,9},{5... | collective-permute-start | bytes 884744 | tf_op jit(solution)/shard_map/ppermute | solution.py:600
  174.6 10.8 %copy-start.3 = (bf16[2,256,768]{2,1,0:T(8,128)(2,1)S(1)}, bf16[2,256,768]{2,1,0:T(8,128)(2,1)}, u32[]{:S(2)}) copy-start(bf16[2,256,768]{2,1,0:T(8,128)(2,1)} %get-tuple-element.217) | copy-start | bytes 2359300
  174.6 13.0 %copy-start.11 = (bf16[4,96,768]{2,1,0:T(8,128)(2,1)S(1)}, bf16[4,96,768]{2,1,0:T(8,128)(2,1)}, u32[]{:S(2)}) copy-start(bf16[4,96,768]{2,1,0:T(8,128)(2,1)} %get-tuple-element.221) | copy-start | bytes 1769476
  174.6 13.0 %copy-start.13 = (bf16[4,96,768]{2,1,0:T(8,128)(2,1)S(1)}, bf16[4,96,768]{2,1,0:T(8,128)(2,1)}, u32[]{:S(2)}) copy-start(bf16[4,96,768]{2,1,0:T(8,128)(2,1)} %copy-done.12) | copy-start | bytes 1769476
  183.8 8.0 %copy-start.6 = (bf16[480,768]{1,0:T(8,128)(2,1)S(1)}, bf16[480,768]{1,0:T(8,128)(2,1)}, u32[]{:S(2)}) copy-start(bf16[480,768]{1,0:T(8,128)(2,1)} %get-tuple-element.224) | copy-start | bytes 2211844
  183.8 8.0 %copy-start.8 = (bf16[480,768]{1,0:T(8,128)(2,1)S(1)}, bf16[480,768]{1,0:T(8,128)(2,1)}, u32[]{:S(2)}) copy-start(bf16[480,768]{1,0:T(8,128)(2,1)} %copy-done.7) | copy-start | bytes 2211844
  183.8 12.1 %collective-permute-start.31 = (bf16[584,384]{1,0:T(8,128)(2,1)}, bf16[584,384]{1,0:T(8,128)(2,1)S(1)}, u32[]{:S(2)}, u32[]{:S(2)}) collective-permute-start(bf16[584,384]{1,0:T(8,128)(2,1)} %get-tuple-element.233), channel_id=1, source_target_pairs={{0,4},{4,0},{8,12},{12,8},{16,20},{20,16},{24,28},{28,24},{1,5},{5... | collective-permute-start | bytes 1345544 | tf_op jit(solution)/shard_map/ppermute | solution.py:600
  187.5 13.9 %copy-start.23 = (f32[1,384]{1,0:T(1,128)S(1)}, f32[1,384]{1,0:T(1,128)}, u32[]{:S(2)}) copy-start(f32[1,384]{1,0:T(1,128)} %get-tuple-element.241) | copy-start | bytes 4612
  187.5 13.9 %copy-start.14 = (bf16[576,384]{1,0:T(8,128)(2,1)S(1)}, bf16[576,384]{1,0:T(8,128)(2,1)}, u32[]{:S(2)}) copy-start(bf16[576,384]{1,0:T(8,128)(2,1)} %get-tuple-element.239) | copy-start | bytes 1327108
  188.6 23.0 %collective-permute-start.34 = (bf16[96,768]{1,0:T(8,128)(2,1)S(1)}, bf16[96,768]{1,0:T(8,128)(2,1)S(1)}, u32[]{:S(2)}, u32[]{:S(2)}) collective-permute-start(bf16[96,768]{1,0:T(8,128)(2,1)S(1)} %fusion.15), channel_id=1, source_target_pairs={{0,16},{4,20},{8,24},{12,28},{16,0},{20,4},{24,8},{28,12},{1,17},{... | collective-permute-start | bytes 442376 | tf_op jit(solution)/shard_map/ppermute | solution.py:600
  191.3 10.1 %collective-permute-start.32 = (bf16[256,768]{1,0:T(8,128)(2,1)S(1)}, bf16[256,768]{1,0:T(8,128)(2,1)S(1)}, u32[]{:S(2)}, u32[]{:S(2)}) collective-permute-start(bf16[256,768]{1,0:T(8,128)(2,1)S(1)} %fusion.7), channel_id=1, source_target_pairs={{0,2},{1,3},{2,0},{3,1},{4,6},{5,7},{6,4},{7,5},{8,10},{9,11},{10,... | collective-permute-start | bytes 1179656 | tf_op jit(solution)/shard_map/ppermute | solution.py:600
  191.8 10.3 %copy-start.1 = (f32[512,768]{1,0:T(8,128)S(1)}, f32[512,768]{1,0:T(8,128)}, u32[]{:S(2)}) copy-start(f32[512,768]{1,0:T(8,128)} %get-tuple-element.216) | copy-start | bytes 4718596
  191.8 10.3 %copy-start.16 = (bf16[256,768]{1,0:T(8,128)(2,1)S(1)}, bf16[256,768]{1,0:T(8,128)(2,1)}, u32[]{:S(2)}) copy-start(bf16[256,768]{1,0:T(8,128)(2,1)} %copy-done.15) | copy-start | bytes 1179652
  193.7 17.9 %collective-permute-start.35 = (bf16[136,768]{1,0:T(8,128)(2,1)S(1)}, bf16[136,768]{1,0:T(8,128)(2,1)S(1)}, u32[]{:S(2)}, u32[]{:S(2)}) collective-permute-start(bf16[136,768]{1,0:T(8,128)(2,1)S(1)} %pad_maximum_fusion.7), channel_id=1, source_target_pairs={{0,16},{4,20},{8,24},{12,28},{16,0},{20,4},{24,8},{28,12},{1,17},{... | collective-permute-start | bytes 626696 | tf_op jit(solution)/shard_map/ppermute | solution.py:600
  201.6 10.0 %collective-permute-start.33 = (bf16[290,384]{1,0:T(8,128)(2,1)S(1)}, bf16[290,384]{1,0:T(8,128)(2,1)S(1)}, u32[]{:S(2)}, u32[]{:S(2)}) collective-permute-start(bf16[290,384]{1,0:T(8,128)(2,1)S(1)} %pad_maximum_fusion.6), channel_id=1, source_target_pairs={{0,8},{4,12},{8,0},{12,4},{16,24},{20,28},{24,16},{28,20},{1,9},{5... | collective-permute-start | bytes 668168 | tf_op jit(solution)/shard_map/ppermute | solution.py:600
  215.9 8.3 %collective-permute-start.36 = (bf16[146,384]{1,0:T(8,128)(2,1)S(1)}, bf16[146,384]{1,0:T(8,128)(2,1)S(1)}, u32[]{:S(2)}, u32[]{:S(2)}) collective-permute-start(bf16[146,384]{1,0:T(8,128)(2,1)S(1)} %pad_maximum_fusion.8), channel_id=1, source_target_pairs={{0,16},{4,20},{8,24},{12,28},{16,0},{20,4},{24,8},{28,12},{1,17},{... | collective-permute-start | bytes 336392 | tf_op jit(solution)/shard_map/ppermute | solution.py:600
  (3 other events, 4.6 us)

commit v3 on v2

--- a/solution.py
+++ b/solution.py
@@ -128,7 +128,7 @@
     out_w = out_in()
     width, d = out_w.shape
     pack.src[0:width, :] = out_w[...]
-    pack.src[width : width + 8, :] = jnp.broadcast_to(bias[...], (8, d))
+    pack.src[width : width + 8, :] = jnp.broadcast_to(bias[...].reshape(1, d), (8, d))
 
 
 def prepare(info, out_w, bias, up, dn):
@@ -327,20 +327,14 @@
     return call("attend_bwd", attend_bwd_kernel, info, ins, outs, scratch, which=which, cost=10**10)
 
 
-def project_grads_kernel(info, x0, x1, low0, low1, db0, db1, keep, send, db_ref, dw, pair, *, parts):
-    lows = (low0(), low1())
-    x = (x0(), x1())
+def project_grads_kernel(info, x0, low0, x1, low1, db0, db1, keep, send, db_ref, dw, acc, pair, *, parts):
     _, d, width = dw.shape
-    step = 256
-
-    def chunk(m, carry):
-        cols = pl.ds(pl.multiple_of(m * step, step), step)
-        x_t = (x[0][:, cols].T, x[1][:, cols].T)
-        for i in range(3):
-            dw[i, cols, :] = mm(x_t[0], lows[0][i]) + mm(x_t[1], lows[1][i])
-        return carry
-
-    lax.fori_loop(0, d // step, chunk, 0)
+    x, low = x0(), low0()
+    for i in range(3):
+        acc[i] = mm(low[i].T, x[...])
+    x, low = x1(), low1()
+    for i in range(3):
+        dw[i] = (acc[i] + mm(low[i].T, x[...])).T
     rows = d // parts
     half = 3 * rows // 2
     for b in range(parts):
@@ -384,7 +378,7 @@
 
 
 def first_norm_kernel(info, x_in, par, *rest):
-    nv_ref, r_ref, low = rest[8:]
+    nv_ref, r_ref, low0, low1, low = rest[8:]
     cs, packs = [c() for c in rest[:4]], [p() for p in rest[4:8]]
     x_ref = x_in()
     batch, rows = x_ref.shape[:2]
@@ -398,13 +392,16 @@
         nv, r = norm_parts(total)
         nv_ref[here, :] = nv
         r_ref[here, :] = r
-        low[here, :] = (nv * par[1:2, :] + par[2:3, :]).astype(bf16)
+        low[s] = (nv * par[1:2, :] + par[2:3, :]).astype(bf16)
         return carry
 
     lax.fori_loop(0, batch, one_sequence, 0)
-
-
-def feed_kernel(info, low, low2, pack, *rest, width, far):
+    low0[...] = low[0]
+    low1[...] = low[1]
+
+
+def feed_kernel(info, *rest, width, far):
+    low, (pack, *rest) = rest[:4], rest[4:]
     if far:
         u_a, u_b, d_a, d_b, p_own, p_sib, act_out, slope_out, own, sib, both, up, dn = rest
         assemble(info[3], info[4], up, u_a(), u_b(), False)
@@ -415,8 +412,9 @@
     units = up.shape[1]
     bias = pack()
     step = 256
-    both[0] = low[...]
-    both[1] = low2[...]
+    n = low[0].shape[0]
+    for i, x in enumerate(low):
+        both[i // 2, (i % 2) * n : (i % 2 + 1) * n, :] = x[...]
 
     def side(j, carry):
         def chunk(n, carry):
@@ -555,9 +553,12 @@
     send.start()
 
 
-def up_grads_kernel(
-    info, low, low2, gh_in, okeep, ogot, small, ub, far_keep, far_send, keep, send, sums, scr, *, parts, width
-):
+def up_grads_kernel(info, *rest, parts, width):
+    lows, (gh_in, okeep, ogot, small, ub, far_keep, far_send, keep, send, sums, scr, both_low) = rest[:4], rest[4:]
+    n = lows[0].shape[0]
+    for i, x in enumerate(lows):
+        both_low[i // 2, (i % 2) * n : (i % 2 + 1) * n, :] = x[...]
+    low, low2 = both_low.at[0], both_low.at[1]
     gh = ref(gh_in)
     units = low.shape[1]
     block = units // parts
@@ -654,7 +655,7 @@
     par = jnp.concatenate([out_bias, first_gain, first_shift, down_bias, second_gain, second_shift])
     par = par.reshape(6, d).astype(f32)
     w_t = jnp.transpose(qkv_weight, (1, 2, 0))
-    pack, u_part, d_part = prepare(info, out_weight, up_bias[None], up_weight, down_weight)
+    pack, u_part, d_part = prepare(info, out_weight, up_bias, up_weight, down_weight)
     pack2 = swap(pack, "tensor", 2)
     pack1 = swap(pack, "tensor", 1)
     u_part = swap(u_part, "tensor", 2)
@@ -663,9 +664,11 @@
     saved = (q, k, v, lse, c)
     *cs, pack1, pack2, u_part, d_part = after(*cs, pack1, pack2, u_part, d_part)
     ctx = [cs[0]] + [swap(cs[j], "tensor", j) for j in range(1, peers)]
-    u2a = jnp.concatenate([u_part, swap(u_part, "dp", 1)])
-    d2a = jnp.concatenate([d_part, swap(d_part, "dp", 2)])
-    *ctx, pack2, u2a, d2a = after(*ctx, pack2, u2a, d2a)
+    u_next, d_next = swap(u_part, "dp", 1), swap(d_part, "dp", 2)
+    *ctx, u_next, d_next = after(*ctx, u_next, d_next)
+    u2a = jnp.concatenate([u_part, u_next])
+    d2a = jnp.concatenate([d_part, d_next])
+    pack2, u2a, d2a = after(pack2, u2a, d2a)
     pack3 = swap(pack2, "tensor", 1)
     packs = [pack, pack1, pack2, pack3]
     u2b = swap(u2a, "dp", 2)
@@ -673,15 +676,16 @@
     far_ctx = [whole(ctx[0])] + [loose(x) for x in ctx[1:]]
     far_packs = [whole(pack)] + [loose(p) for p in packs[1:]]
     share = (inputs, ((batch, rows, d), lambda ref, info: ref.at[:, pl.ds(pl.multiple_of(info[2] * rows, rows), rows), :]))
-    nv1, r1, low = call(
+    nv1, r1, *low = call(
         "first_norm",
         first_norm_kernel,
         info,
         [share, par, *far_ctx, *far_packs],
-        [SDS((n, d), f32), SDS((n, 1), f32), SDS((n, d), bf16)],
+        [SDS((n, d), f32), SDS((n, 1), f32), SDS((rows, d), bf16), SDS((rows, d), bf16)],
+        [pltpu.VMEM((batch, rows, d), bf16)],
         vmem=NEAR,
     )
-    low2 = swap(low, "tensor", 1)
+    low2 = [swap(x, "tensor", 1) for x in low]
     pair = SDS((2, n, units), bf16)
     part = SDS((n, d), f32)
     sides = pltpu.VMEM((2, n, d), bf16)
@@ -689,7 +693,7 @@
         "feed",
         feed_kernel,
         info,
-        [low, low2, far_packs[0], whole(up_weight), whole(down_weight)],
+        [*low, *low2, far_packs[0], whole(up_weight), whole(down_weight)],
         [pair, pair, part, part],
         [sides],
         vmem=NEAR,
@@ -702,7 +706,7 @@
         "feed",
         feed_kernel,
         info,
-        [low, low2, far_packs[2], *halves, own, sib],
+        [*low, *low2, far_packs[2], *halves, own, sib],
         [pair, pair, part, SDS((n, d), bf16)],
         [sides, *both],
         vmem=NEAR,
@@ -764,7 +768,7 @@
         "up_grads",
         up_grads_kernel,
         info,
-        [low, low2, gh, whole(okeep), loose(got_o), small1, ub],
+        [*low, *low2, gh, whole(okeep), loose(got_o), small1, ub],
         [
             [SDS((cut, d), bf16)],
             [SDS((cut + 16, d), bf16)],
@@ -772,7 +776,7 @@
             [SDS((cut, d), bf16)],
             SDS((8, d), f32),
         ],
-        [pltpu.VMEM((2, parts // 2, joint, d), bf16)],
+        [pltpu.VMEM((2, parts // 2, joint, d), bf16), sides],
         vmem=NEAR,
         parts=parts,
         width=width,
@@ -822,20 +826,23 @@
     up_y = swap(up_y_rows, "tensor", 2)
     up_more = swap(up_next, "dp", 1)
     m = 3 * d // 4
+    operands = []
+    for s in range(batch):
+        operands += [(inputs, (inputs.shape[1:], functools.partial(nth, s))), whole(lows[s])]
     w_keep, w_send, db = call(
         "project_grads",
         project_grads_kernel,
         info,
-        [*[(inputs, (inputs.shape[1:], functools.partial(nth, at))) for at in range(batch)], *[whole(a) for a in lows], *biases],
+        [*operands, *biases],
         [[SDS((m, 2 * width), bf16)], [SDS((m + 8, 2 * width), bf16)], SDS((1, 2 * width), f32)],
-        [pltpu.VMEM((3, d, width), f32), pltpu.VMEM((2, m, 2 * width), bf16)],
+        [pltpu.VMEM((3, d, width), f32), pltpu.VMEM((3, width, d), f32), pltpu.VMEM((2, m, 2 * width), bf16)],
         parts=parts,
     )
     w_send, down_more, up_y, up_more = after(w_send, down_more, up_y, up_more)
     down_more, up_y, up_more, in_sum = after(down_more, up_y, up_more, in_sum)
     got = swap(w_send, "dp", 1)
-    got, far = after(got, swap(in_sum, "tensor", 2))
-    terms_of[1].append(far)
+    got, in_sum = after(got, in_sum)
+    terms_of[1].append(swap(in_sum, "tensor", 2))
     down_terms = down_kept + [down_more]
     at = up_y_next.size // d
     small = jnp.concatenate([small[0:6], small[7:8], small[7:8]]) + pair_sum(up_y, at, 8)

time: 228 us -> 225 us (0.987)
  waiting for transfers between devices: 56 us -> 48 us
  starting transfers between devices: 31.5 us -> 37.7 us
  Pallas kernels: 112 us -> 107 us
  other arithmetic: 18.9 us -> 22.6 us
    ppermute x37 -> x38, waiting for transfers between devices: 56 us -> 48 us  [swap(): return lax.ppermute(x, axis, [(i, i ^ bit) for i in range(size)])]
    ppermute x37 -> x38, starting transfers between devices: 31.5 us -> 37.7 us  [swap(): return lax.ppermute(x, axis, [(i, i ^ bit) for i in range(size)])]
    pallas_call x13, Pallas kernels: 112 us -> 107 us  [call(): pl.pallas_call(kernel, out_shape=[pltpu.HBM(o.shape, o.dtype) if i in far...]
    unnamed x65 -> x73, local copies, waits for them, and re-layouts: 1.17 us -> 3.58 us
  transfers between devices with their start and end apart: 37 -> 38, of which waited for: 21 -> 18; matrix products, arithmetic and copies ran while one was open for 6% -> 10% of each run, Pallas kernels for 34% -> 33%
where the time goes in v3:
time: 225 us; the launch traced here: 224 us
  Pallas kernels  107 us (48%)
  waiting for transfers between devices  48 us (21%)
  starting transfers between devices  37.7 us (17%)
  other arithmetic  22.6 us (10%)
  local copies, waits for them, and re-layouts  7.83 us (3%)
    pallas_call x13, Pallas kernels, call(): pl.pallas_call(kernel, out_shape=[pltpu.HBM(o.shape, o.dtype) if i in far...  107 us
    ppermute x38, waiting for transfers between devices, swap(): return lax.ppermute(x, axis, [(i, i ^ bit) for i in range(size)])  48 us
    ppermute x38, starting transfers between devices, swap(): return lax.ppermute(x, axis, [(i, i ^ bit) for i in range(size)])  37.7 us
    convert_element_type x4, other arithmetic, halve_sum(): return (kept, summed(other).astype(bf16))  4.65 us
  transfers between devices with their start and end apart: 38, of which 18 were waited for; matrix products, arithmetic and copies ran while one was open for 10% of the time, Pallas kernels for 33%

profile of v3, /device:TPU:0, one launch (start us, length us, event | category | flops | bytes accessed | tf_op | source)
XLA Modules:
  0.0 223.8 jit_solution(11665665164776062759)
XLA Ops:
  0.6 3.4 %prepare.1 = (bf16[200,768]{1,0:T(8,128)(2,1)}, bf16[192,768]{1,0:T(8,128)(2,1)}, bf16[192,768]{1,0:T(8,128)(2,1)}) custom-call(s32[2]{0:T(128)} %lengths_ref.25, s32[1]{0:T(128)} %constant.384.clone.1.which_ref, bf16[192,768]{1,0:T(8,128)(2,1)} %refs_0_.6, bf16[768]{0:T(1024)(128)(2,1)} %refs_1_.1, bf16[768,768]{1,0:T(8,128)(2,1)} %refs_4_.1, ...), custom_call_target="tpu_custom_call" | custom-call | flops 1000 | bytes 1000 | tf_op jit(solution)/shard_map/prepare/pallas_call | solution.py:91
  4.0 3.0 %collective-permute-start.1 = (bf16[200,768]{1,0:T(8,128)(2,1)}, bf16[200,768]{1,0:T(8,128)(2,1)S(1)}, u32[]{:S(2)}, u32[]{:S(2)}) collective-permute-start(bf16[200,768]{1,0:T(8,128)(2,1)} %get-tuple-element.138.refs_6_.refs_4_.refs_11_), channel_id=1, source_target_pairs={{0,2},{1,3},{2,0},{3,1},{4,6},{5,7},{6,4},{7,5},{8,10},{9,11},{10,... | collective-permute-start | bytes 921608 | tf_op jit(solution)/shard_map/ppermute | solution.py:601
  7.2 1.9 collective-permute-start.3
  9.1 16.3 %attend_fwd.1 = (bf16[2,1024,256]{2,1,0:T(8,128)(2,1)}, bf16[2,1024,256]{2,1,0:T(8,128)(2,1)}, bf16[2,1024,192]{2,1,0:T(8,128)(2,1)}, f32[2,4,8,256]{3,2,1,0:T(8...) custom-call(s32[2]{0:T(128)} %lengths_ref.25, ...), custom_call_target="tpu_custom_call" | custom-call | flops 1000 | bytes 1000 | tf_op jit(solution)/shard_map/attend_fwd/pallas_call | solution.py:91
  25.5 1.7 collective-permute-done.3
  27.2 1.7 collective-permute-start.7
  28.9 1.6 collective-permute-start.8
  30.5 1.5 collective-permute-start.5
  32.4 6.0 %collective-permute-done.5.refs_4_.refs_9_ = bf16[2,192,256]{2,1,0:T(8,128)(2,1)S(1)} collective-permute-done((bf16[2,192,256]{2,1,0:T(8,128)(2,1)}, bf16[2,192,256]{2,1,0:T(8,128)(2,1)S(1)}, u32[]{:S(2)}, u32[]{:S(2)}) %collective-permute-start.5) | collective-permute-done | bytes 196640 | tf_op jit(solution)/shard_map/ppermute | solution.py:601
  38.4 3.4 %collective-permute-done.6.refs_5_.refs_10_ = bf16[2,192,256]{2,1,0:T(8,128)(2,1)S(1)} collective-permute-done((bf16[2,192,256]{2,1,0:T(8,128)(2,1)}, bf16[2,192,256]{2,1,0:T(8,128)(2,1)S(1)}, u32[]{:S(2)}, u32[]{:S(2)}) %collective-permute-start.6) | collective-permute-done | bytes 196640 | tf_op jit(solution)/shard_map/ppermute | solution.py:601
  44.8 0.9 copy-done.1
  45.7 0.9 copy-done.4
  46.6 4.2 %first_norm.1 = (f32[512,768]{1,0:T(8,128)S(1)}, f32[512,1]{1,0:T(8,128)S(1)}, bf16[256,768]{1,0:T(8,128)(2,1)S(1)}, bf16[256,768]{1,0:T(8,128)(2,1)S(1)}) custom-call(s32[2]{0:T(128)S(1)} %copy-done.6, s32[1]{0:T(128)} %constant.384.clone.1.which_ref, bf16[2,1024,768]{2,1,0:T(8,128)(2,1)} %refs_2_.5, f32[6,768]{1,0:T(8,128)S(1)} %reshape.192.refs_1_.refs_0_, ...), custom_call_target="tpu_custom_call" | custom-call | flops 1000 | bytes 1000 | tf_op jit(solution)/shard_map/first_norm/pallas_call | solution.py:91
  51.4 1.2 collective-permute-done.10.refs_2_
  53.2 7.6 %feed.2 = (bf16[2,512,768]{2,1,0:T(8,128)(2,1)S(1)}, bf16[2,512,768]{2,1,0:T(8,128)(2,1)S(1)}, f32[512,768]{1,0:T(8,128)S(1)}, f32[512,768]{1,0:T(8,128)S(1)}) custom-call(s32[2]{0:T(128)S(1)} %copy-done.6, s32[1]{0:T(128)} %constant.384.clone.1.which_ref, bf16[256,768]{1,0:T(8,128)(2,1)S(1)} %get-tuple-element.157.refs_0_, ...), custom_call_target="tpu_custom_call" | custom-call | flops 1000 | bytes 1000 | tf_op jit(solution)/shard_map/feed/pallas_call | solution.py:91
  60.8 7.0 %feed.3 = (bf16[2,512,768]{2,1,0:T(8,128)(2,1)S(1)}, bf16[2,512,768]{2,1,0:T(8,128)(2,1)S(1)}, f32[512,768]{1,0:T(8,128)S(1)}, bf16[512,768]{1,0:T(8,128)(2,1)S(1)}) custom-call(s32[2]{0:T(128)S(1)} %copy-done.6, s32[1]{0:T(128)} %constant.384.clone.1.which_ref, bf16[256,768]{1,0:T(8,128)(2,1)S(1)} %get-tuple-element.157.refs_0_, ...), custom_call_target="tpu_custom_call" | custom-call | flops 1000 | bytes 1000 | tf_op jit(solution)/shard_map/feed/pallas_call | solution.py:91
  68.1 2.1 collective-permute-done.14.refs_4_
  70.2 4.1 %second_norm.1 = (bf16[2,256,768]{2,1,0:T(8,128)(2,1)}, f32[512,768]{1,0:T(8,128)S(1)}, bf16[512,768]{1,0:T(8,128)(2,1)S(1)}, f32[8,768]{1,0:T(8,128)S(1)}) custom-call(s32[2]{0:T(128)S(1)} %copy-done.6, s32[1]{0:T(128)} %constant.384.clone.1.which_ref, bf16[2,256,768]{2,1,0:T(8,128)(2,1)} %refs_0_.8, f32[6,768]{1,0:T(8,128)S(1)} %reshape.192.refs_1_.refs_0_, ...), custom_call_target="tpu_custom_call" | custom-call | flops 1000 | bytes 1000 | tf_op jit(solution)/shard_map/second_norm/pallas_call | solution.py:91
  74.5 2.1 collective-permute-done.15.refs_1_.refs_3_
  76.7 10.1 %feed_back.1 = (bf16[2,2,512,768]{3,2,1,0:T(8,128)(2,1)S(1)}, f32[512,768]{1,0:T(8,128)S(1)}, bf16[512,768]{1,0:T(8,128)(2,1)S(1)}, f32[8,768]{1,0:T(8,128)S(1)}) custom-call(s32[2]{0:T(128)S(1)} %copy-done.6, s32[1]{0:T(128)} %constant.384.clone.1.which_ref, bf16[512,768]{1,0:T(8,128)(2,1)S(1)} %get-tuple-element.172.refs_0_.refs_2_, ...), custom_call_target="tpu_custom_call" | custom-call | flops 1000 | bytes 1000 | tf_op jit(solution)/shard_map/feed_back/pallas_call | solution.py:91
  87.0 2.1 collective-permute-done.16.refs_4_
  89.1 7.1 %first_back.1 = (f32[512,768]{1,0:T(8,128)}, bf16[2,192,256]{2,1,0:T(8,128)(2,1)}, bf16[2,192,256]{2,1,0:T(8,128)(2,1)}, bf16[2,192,256]{2,1,0:T(8,128)(2,1)}, b...) custom-call(s32[2]{0:T(128)S(1)} %copy-done.6, ...), custom_call_target="tpu_custom_call" | custom-call | flops 1000 | bytes 1000 | tf_op jit(solution)/shard_map/first_back/pallas_call | solution.py:91
  96.4 5.4 %down_grads.1 = (bf16[4,96,768]{2,1,0:T(8,128)(2,1)}, bf16[4,96,768]{2,1,0:T(8,128)(2,1)}, bf16[2,4,96,768]{3,2,1,0:T(8,128)(2,1)}) custom-call(s32[2]{0:T(128)S(1)} %copy-done.6, s32[1]{0:T(128)} %constant.384.clone.1.which_ref, bf16[2,512,768]{2,1,0:T(8,128)(2,1)S(1)} %get-tuple-element.201.refs_0_, bf16[2,512,768]{2,1,0:T(8,128)(2,1)S(1)} %get-tuple-element.202.refs_1_, ...), custom_call_target="tpu_custom_call" | custom-call | flops 1000 | bytes 1000 | tf_op jit(solution)/shard_map/down_grads/pallas_call | solution.py:91
  101.8 1.8 collective-permute-start.22
  103.7 1.5 collective-permute-start.18
  105.5 5.8 %up_grads.1 = (bf16[480,768]{1,0:T(8,128)(2,1)}, bf16[496,768]{1,0:T(8,128)(2,1)}, bf16[480,768]{1,0:T(8,128)(2,1)}, bf16[480,768]{1,0:T(8,128)(2,1)}, f32[8,768]{1,0:T(8,128)S(1)}) custom-call(s32[2]{0:T(128)S(1)} %copy-done.6, s32[1]{0:T(128)} %constant.384.clone.1.which_ref, bf16[256,768]{1,0:T(8,128)(2,1)S(1)} %get-tuple-element.157.refs_0_, ...), custom_call_target="tpu_custom_call" | custom-call | flops 1000 | bytes 1000 | tf_op jit(solution)/shard_map/up_grads/pallas_call | solution.py:91
  111.4 3.3 %collective-permute-done.19.refs_9_ = bf16[2,192,256]{2,1,0:T(8,128)(2,1)S(1)} collective-permute-done((bf16[2,192,256]{2,1,0:T(8,128)(2,1)S(1)}, bf16[2,192,256]{2,1,0:T(8,128)(2,1)S(1)}, u32[]{:S(2)}, u32[]{:S(2)}) %collective-permute-start.19) | collective-permute-done | bytes 196640 | tf_op jit(solution)/shard_map/ppermute | solution.py:601
  114.7 1.6 collective-permute-start.21
  116.3 13.9 %attend_bwd.2 = (bf16[2,256,768]{2,1,0:T(8,128)(2,1)}, bf16[2,256,768]{2,1,0:T(8,128)(2,1)}, bf16[3,1024,192]{2,1,0:T(8,128)(2,1)}, f32[1,384]{1,0:T(1,128)}) custom-call(s32[2]{0:T(128)} %lengths_ref.25, s32[1]{0:T(128)} %constant.384.clone.1.which_ref, bf16[3,192,768]{2,1,0:T(8,128)(2,1)} %bitcast.109, bf16[2,1024,256]{2,1,0:T(8,128)(2,1)} %get-tuple-element.166.refs_1_, ...), custom_call_target="tpu_custom_call" | custom-call | flops 10000000000 | bytes 1000 | tf_op jit(solution)/shard_map/attend_bwd/pallas_call | solution.py:91
  130.3 4.1 %collective-permute-done.21 = bf16[496,768]{1,0:T(8,128)(2,1)S(1)} collective-permute-done((bf16[496,768]{1,0:T(8,128)(2,1)}, bf16[496,768]{1,0:T(8,128)(2,1)S(1)}, u32[]{:S(2)}, u32[]{:S(2)}) %collective-permute-start.21) | collective-permute-done | bytes 761888 | tf_op jit(solution)/shard_map/ppermute | solution.py:601
  134.7 0.8 pad_maximum_fusion.3
  135.6 1.0 fusion
  137.0 1.9 fusion.6
  139.3 1.7 collective-permute-start.27
  141.3 1.7 collective-permute-start.25
  143.0 13.7 %attend_bwd.3 = (bf16[2,256,768]{2,1,0:T(8,128)(2,1)}, bf16[2,256,768]{2,1,0:T(8,128)(2,1)}, bf16[3,1024,192]{2,1,0:T(8,128)(2,1)}, f32[1,384]{1,0:T(1,128)}) custom-call(s32[2]{0:T(128)} %lengths_ref.25, s32[1]{0:T(128)} %constant.385.clone.1.which_ref, bf16[3,192,768]{2,1,0:T(8,128)(2,1)} %bitcast.110, bf16[2,1024,256]{2,1,0:T(8,128)(2,1)} %get-tuple-element.166.refs_1_, ...), custom_call_target="tpu_custom_call" | custom-call | flops 10000000000 | bytes 1000 | tf_op jit(solution)/shard_map/attend_bwd/pallas_call | solution.py:91
  156.8 6.2 %collective-permute-done.24 = bf16[4,96,768]{2,1,0:T(8,128)(2,1)S(1)} collective-permute-done((bf16[4,96,768]{2,1,0:T(8,128)(2,1)}, bf16[4,96,768]{2,1,0:T(8,128)(2,1)S(1)}, u32[]{:S(2)}, u32[]{:S(2)}) %collective-permute-start.24) | collective-permute-done | bytes 589856 | tf_op jit(solution)/shard_map/ppermute | solution.py:601
  163.0 0.8 add_add_fusion.1
  163.9 0.9 fusion.10
  164.8 0.8 fusion.13
  165.7 1.1 fusion.5
  166.8 1.7 collective-permute-start.30
  168.6 1.5 collective-permute-start.31
  170.1 1.6 collective-permute-start.29
  171.6 7.9 %project_grads.1 = (bf16[576,384]{1,0:T(8,128)(2,1)}, bf16[584,384]{1,0:T(8,128)(2,1)}, f32[1,384]{1,0:T(1,128)}) custom-call(s32[2]{0:T(128)} %lengths_ref.25, s32[1]{0:T(128)} %constant.384.clone.1.which_ref, bf16[2,1024,768]{2,1,0:T(8,128)(2,1)} %refs_2_.5, bf16[3,1024,192]{2,1,0:T(8,128)(2,1)} %get-tuple-element.225.refs_1_, ...), custom_call_target="tpu_custom_call" | custom-call | flops 1000 | bytes 1000 | tf_op jit(solution)/shard_map/project_grads/pallas_call | solution.py:91
  179.6 1.4 collective-permute-start.32
  181.1 1.9 fusion.7
  183.0 1.1 slice.169
  184.1 1.1 fusion.12
  186.6 2.6 %collective-permute-start.36 = (bf16[136,768]{1,0:T(8,128)(2,1)}, bf16[136,768]{1,0:T(8,128)(2,1)}, u32[]{:S(2)}, u32[]{:S(2)}) collective-permute-start(bf16[136,768]{1,0:T(8,128)(2,1)} %pad_maximum_fusion.7), channel_id=1, source_target_pairs={{0,16},{4,20},{8,24},{12,28},{16,0},{20,4},{24,8},{28,12},{1,17},{... | collective-permute-start | bytes 626696 | tf_op jit(solution)/shard_map/ppermute | solution.py:601
  189.2 2.6 %collective-permute-done.32 = bf16[584,384]{1,0:T(8,128)(2,1)S(1)} collective-permute-done((bf16[584,384]{1,0:T(8,128)(2,1)}, bf16[584,384]{1,0:T(8,128)(2,1)S(1)}, u32[]{:S(2)}, u32[]{:S(2)}) %collective-permute-start.32) | collective-permute-done | bytes 448544 | tf_op jit(solution)/shard_map/ppermute | solution.py:601
  192.0 1.3 collective-permute-start.34
  193.2 1.8 fusion.15
  195.0 2.6 %collective-permute-start.35 = (bf16[96,768]{1,0:T(8,128)(2,1)}, bf16[96,768]{1,0:T(8,128)(2,1)}, u32[]{:S(2)}, u32[]{:S(2)}) collective-permute-start(bf16[96,768]{1,0:T(8,128)(2,1)} %fusion.15), channel_id=1, source_target_pairs={{0,16},{4,20},{8,24},{12,28},{16,0},{20,4},{24,8},{28,12},{1,17},{... | collective-permute-start | bytes 442376 | tf_op jit(solution)/shard_map/ppermute | solution.py:601
  197.6 0.9 collective-permute-start.33
  198.5 5.1 %collective-permute-done.34 = bf16[290,384]{1,0:T(8,128)(2,1)S(1)} collective-permute-done((bf16[290,384]{1,0:T(8,128)(2,1)S(1)}, bf16[290,384]{1,0:T(8,128)(2,1)S(1)}, u32[]{:S(2)}, u32[]{:S(2)}) %collective-permute-start.34) | collective-permute-done | bytes 222752 | tf_op jit(solution)/shard_map/ppermute | solution.py:601
  203.6 1.3 collective-permute-done.35
  204.9 1.3 fusion.11
  207.5 1.9 fusion.14
  209.5 0.8 add_add_fusion
  211.2 2.1 collective-permute-start.37
  213.9 5.5 %collective-permute-done.37 = bf16[146,384]{1,0:T(8,128)(2,1)S(1)} collective-permute-done((bf16[146,384]{1,0:T(8,128)(2,1)S(1)}, bf16[146,384]{1,0:T(8,128)(2,1)S(1)}, u32[]{:S(2)}, u32[]{:S(2)}) %collective-permute-start.37) | collective-permute-done | bytes 112160 | tf_op jit(solution)/shard_map/ppermute | solution.py:601
  221.0 1.9 fusion.8
  222.9 0.9 pad_maximum_fusion
  (146 shorter events, 13.8 us)
Async XLA Ops:
  4.0 23.2 %collective-permute-start.1 = (bf16[200,768]{1,0:T(8,128)(2,1)}, bf16[200,768]{1,0:T(8,128)(2,1)S(1)}, u32[]{:S(2)}, u32[]{:S(2)}) collective-permute-start(bf16[200,768]{1,0:T(8,128)(2,1)} %get-tuple-element.138.refs_6_.refs_4_.refs_11_), channel_id=1, source_target_pairs={{0,2},{1,3},{2,0},{3,1},{4,6},{5,7},{6,4},{7,5},{8,10},{9,11},{10,... | collective-permute-start | bytes 921608 | tf_op jit(solution)/shard_map/ppermute | solution.py:601
  7.1 20.1 %collective-permute-start = (bf16[200,768]{1,0:T(8,128)(2,1)}, bf16[200,768]{1,0:T(8,128)(2,1)S(1)}, u32[]{:S(2)}, u32[]{:S(2)}) collective-permute-start(bf16[200,768]{1,0:T(8,128)(2,1)} %get-tuple-element.138.refs_6_.refs_4_.refs_11_), channel_id=1, source_target_pairs={{0,1},{1,0},{2,3},{3,2},{4,5},{5,4},{6,7},{7,6},{8,9},{9,8},{10,11... | collective-permute-start | bytes 921608 | tf_op jit(solution)/shard_map/ppermute | solution.py:601
  7.1 18.4 %collective-permute-start.2 = (bf16[192,768]{1,0:T(8,128)(2,1)}, bf16[192,768]{1,0:T(8,128)(2,1)S(1)}, u32[]{:S(2)}, u32[]{:S(2)}) collective-permute-start(bf16[192,768]{1,0:T(8,128)(2,1)} %get-tuple-element.139), channel_id=1, source_target_pairs={{0,2},{1,3},{2,0},{3,1},{4,6},{5,7},{6,4},{7,5},{8,10},{9,11},{10,... | collective-permute-start | bytes 884744 | tf_op jit(solution)/shard_map/ppermute | solution.py:601
  7.2 20.0 %collective-permute-start.3 = (bf16[192,768]{1,0:T(8,128)(2,1)}, bf16[192,768]{1,0:T(8,128)(2,1)S(1)}, u32[]{:S(2)}, u32[]{:S(2)}) collective-permute-start(bf16[192,768]{1,0:T(8,128)(2,1)} %get-tuple-element.140), channel_id=1, source_target_pairs={{0,2},{1,3},{2,0},{3,1},{4,6},{5,7},{6,4},{7,5},{8,10},{9,11},{10,... | collective-permute-start | bytes 884744 | tf_op jit(solution)/shard_map/ppermute | solution.py:601
  25.4 18.1 %copy-start.21 = (bf16[768]{0:T(1024)(128)(2,1)S(1)}, bf16[768]{0:T(1024)(128)(2,1)}, u32[]{:S(2)}) copy-start(bf16[768]{0:T(1024)(128)(2,1)} %param.21) | copy-start | bytes 4612
  25.4 18.2 %copy-start.22 = (bf16[768]{0:T(1024)(128)(2,1)S(1)}, bf16[768]{0:T(1024)(128)(2,1)}, u32[]{:S(2)}) copy-start(bf16[768]{0:T(1024)(128)(2,1)} %param.22) | copy-start | bytes 4612
  25.5 18.4 %copy-start.23 = (bf16[768]{0:T(1024)(128)(2,1)S(1)}, bf16[768]{0:T(1024)(128)(2,1)}, u32[]{:S(2)}) copy-start(bf16[768]{0:T(1024)(128)(2,1)} %param.23) | copy-start | bytes 4612
  25.5 18.6 %copy-start.24 = (bf16[768]{0:T(1024)(128)(2,1)S(1)}, bf16[768]{0:T(1024)(128)(2,1)}, u32[]{:S(2)}) copy-start(bf16[768]{0:T(1024)(128)(2,1)} %param.27) | copy-start | bytes 4612
  25.5 18.8 %copy-start.25 = (bf16[768]{0:T(1024)(128)(2,1)S(1)}, bf16[768]{0:T(1024)(128)(2,1)}, u32[]{:S(2)}) copy-start(bf16[768]{0:T(1024)(128)(2,1)} %param.28) | copy-start | bytes 4612
  25.5 19.0 %copy-start.26 = (bf16[768]{0:T(1024)(128)(2,1)S(1)}, bf16[768]{0:T(1024)(128)(2,1)}, u32[]{:S(2)}) copy-start(bf16[768]{0:T(1024)(128)(2,1)} %param.29) | copy-start | bytes 4612
  25.5 19.3 %copy-start.6 = (s32[2]{0:T(128)S(1)}, s32[2]{0:T(128)}, u32[]{:S(2)}) copy-start(s32[2]{0:T(128)} %lengths_ref.25) | copy-start | bytes 28
  27.2 14.6 %collective-permute-start.7 = (bf16[192,768]{1,0:T(8,128)(2,1)S(1)}, bf16[192,768]{1,0:T(8,128)(2,1)S(1)}, u32[]{:S(2)}, u32[]{:S(2)}) collective-permute-start(bf16[192,768]{1,0:T(8,128)(2,1)S(1)} %collective-permute-done.2), channel_id=1, source_target_pairs={{0,4},{4,0},{8,12},{12,8},{16,20},{20,16},{24,28},{28,24},{1,5},{5... | collective-permute-start | bytes 884744 | tf_op jit(solution)/shard_map/ppermute | solution.py:601
  28.9 12.9 %collective-permute-start.8 = (bf16[192,768]{1,0:T(8,128)(2,1)S(1)}, bf16[192,768]{1,0:T(8,128)(2,1)S(1)}, u32[]{:S(2)}, u32[]{:S(2)}) collective-permute-start(bf16[192,768]{1,0:T(8,128)(2,1)S(1)} %collective-permute-done.3), channel_id=1, source_target_pairs={{0,8},{4,12},{8,0},{12,4},{16,24},{20,28},{24,16},{28,20},{1,9},{5... | collective-permute-start | bytes 884744 | tf_op jit(solution)/shard_map/ppermute | solution.py:601
  30.5 1.9 collective-permute-start.4
  30.5 7.9 %collective-permute-start.5 = (bf16[2,192,256]{2,1,0:T(8,128)(2,1)}, bf16[2,192,256]{2,1,0:T(8,128)(2,1)S(1)}, u32[]{:S(2)}, u32[]{:S(2)}) collective-permute-start(bf16[2,192,256]{2,1,0:T(8,128)(2,1)} %get-tuple-element.143), channel_id=1, source_target_pairs={{0,2},{1,3},{2,0},{3,1},{4,6},{5,7},{6,4},{7,5},{8,10},{9,11},{10,... | collective-permute-start | bytes 589832 | tf_op jit(solution)/shard_map/ppermute | solution.py:601
  32.0 9.8 %collective-permute-start.6 = (bf16[2,192,256]{2,1,0:T(8,128)(2,1)}, bf16[2,192,256]{2,1,0:T(8,128)(2,1)S(1)}, u32[]{:S(2)}, u32[]{:S(2)}) collective-permute-start(bf16[2,192,256]{2,1,0:T(8,128)(2,1)} %get-tuple-element.144), channel_id=1, source_target_pairs={{0,3},{1,2},{2,1},{3,0},{4,7},{5,6},{6,5},{7,4},{8,11},{9,10},{10,... | collective-permute-start | bytes 589832 | tf_op jit(solution)/shard_map/ppermute | solution.py:601
  42.5 2.2 %collective-permute-start.9 = (bf16[200,768]{1,0:T(8,128)(2,1)S(1)}, bf16[200,768]{1,0:T(8,128)(2,1)S(1)}, u32[]{:S(2)}, u32[]{:S(2)}) collective-permute-start(bf16[200,768]{1,0:T(8,128)(2,1)S(1)} %collective-permute-done.1.refs_8_.refs_4_.refs_13_), channel_id=1, source_target_pairs={{0,1},{1,0},{2,3},{3,2},{4,5},{5,4},{6,7},{7,6},{8,9},{9,8},{10,11... | collective-permute-start | bytes 921608 | tf_op jit(solution)/shard_map/ppermute | solution.py:601
  42.7 18.1 %collective-permute-start.12 = (bf16[384,768]{1,0:T(8,128)(2,1)S(1)}, bf16[384,768]{1,0:T(8,128)(2,1)S(1)}, u32[]{:S(2)}, u32[]{:S(2)}) collective-permute-start(bf16[384,768]{1,0:T(8,128)(2,1)S(1)} %get-tuple-element.159.refs_5_.refs_6_), channel_id=1, source_target_pairs={{0,8},{4,12},{8,0},{12,4},{16,24},{20,28},{24,16},{28,20},{1,9},{5... | collective-permute-start | bytes 1769480 | tf_op jit(solution)/shard_map/ppermute | solution.py:601
  43.2 17.6 %collective-permute-start.13 = (bf16[384,768]{1,0:T(8,128)(2,1)S(1)}, bf16[384,768]{1,0:T(8,128)(2,1)S(1)}, u32[]{:S(2)}, u32[]{:S(2)}) collective-permute-start(bf16[384,768]{1,0:T(8,128)(2,1)S(1)} %get-tuple-element.160.refs_7_.refs_8_), channel_id=1, source_target_pairs={{0,4},{4,0},{8,12},{12,8},{16,20},{20,16},{24,28},{28,24},{1,5},{5... | collective-permute-start | bytes 1769480 | tf_op jit(solution)/shard_map/ppermute | solution.py:601
  50.8 1.8 collective-permute-start.10
  50.9 2.3 %collective-permute-start.11 = (bf16[256,768]{1,0:T(8,128)(2,1)S(1)}, bf16[256,768]{1,0:T(8,128)(2,1)S(1)}, u32[]{:S(2)}, u32[]{:S(2)}) collective-permute-start(bf16[256,768]{1,0:T(8,128)(2,1)S(1)} %get-tuple-element.158.refs_1_), channel_id=1, source_target_pairs={{0,1},{1,0},{2,3},{3,2},{4,5},{5,4},{6,7},{7,6},{8,9},{9,8},{10,11... | collective-permute-start | bytes 1179656 | tf_op jit(solution)/shard_map/ppermute | solution.py:601
  67.9 2.4 %collective-permute-start.14 = (bf16[512,768]{1,0:T(8,128)(2,1)S(1)}, bf16[512,768]{1,0:T(8,128)(2,1)S(1)}, u32[]{:S(2)}, u32[]{:S(2)}) collective-permute-start(bf16[512,768]{1,0:T(8,128)(2,1)S(1)} %get-tuple-element.164), channel_id=1, source_target_pairs={{0,1},{1,0},{2,3},{3,2},{4,5},{5,4},{6,7},{7,6},{8,9},{9,8},{10,11... | collective-permute-start | bytes 2359304 | tf_op jit(solution)/shard_map/ppermute | solution.py:601
  74.3 2.4 %collective-permute-start.15 = (bf16[512,768]{1,0:T(8,128)(2,1)S(1)}, bf16[512,768]{1,0:T(8,128)(2,1)S(1)}, u32[]{:S(2)}, u32[]{:S(2)}) collective-permute-start(bf16[512,768]{1,0:T(8,128)(2,1)S(1)} %get-tuple-element.172.refs_0_.refs_2_), channel_id=1, source_target_pairs={{0,1},{1,0},{2,3},{3,2},{4,5},{5,4},{6,7},{7,6},{8,9},{9,8},{10,11... | collective-permute-start | bytes 2359304 | tf_op jit(solution)/shard_map/ppermute | solution.py:601
  76.7 12.4 %copy-start.2 = (bf16[2,192,256]{2,1,0:T(8,128)(2,1)S(1)}, bf16[2,192,256]{2,1,0:T(8,128)(2,1)}, u32[]{:S(2)}) copy-start(bf16[2,192,256]{2,1,0:T(8,128)(2,1)} %copy-done) | copy-start | bytes 589828
  76.7 12.4 %copy-start.5 = (bf16[2,192,256]{2,1,0:T(8,128)(2,1)S(1)}, bf16[2,192,256]{2,1,0:T(8,128)(2,1)}, u32[]{:S(2)}) copy-start(bf16[2,192,256]{2,1,0:T(8,128)(2,1)} %copy-done.3) | copy-start | bytes 589828
  86.8 2.4 %collective-permute-start.16 = (bf16[512,768]{1,0:T(8,128)(2,1)S(1)}, bf16[512,768]{1,0:T(8,128)(2,1)S(1)}, u32[]{:S(2)}, u32[]{:S(2)}) collective-permute-start(bf16[512,768]{1,0:T(8,128)(2,1)S(1)} %get-tuple-element.176), channel_id=1, source_target_pairs={{0,1},{1,0},{2,3},{3,2},{4,5},{5,4},{6,7},{7,6},{8,9},{9,8},{10,11... | collective-permute-start | bytes 2359304 | tf_op jit(solution)/shard_map/ppermute | solution.py:601
  96.2 9.3 %collective-permute-start.20 = (bf16[2,200,768]{2,1,0:T(8,128)(2,1)}, bf16[2,200,768]{2,1,0:T(8,128)(2,1)S(1)}, u32[]{:S(2)}, u32[]{:S(2)}) collective-permute-start(bf16[2,200,768]{2,1,0:T(8,128)(2,1)} %get-tuple-element.185), channel_id=1, source_target_pairs={{0,1},{1,0},{2,3},{3,2},{4,5},{5,4},{6,7},{7,6},{8,9},{9,8},{10,11... | collective-permute-start | bytes 1843208 | tf_op jit(solution)/shard_map/ppermute | solution.py:601
  96.4 7.2 %copy-start.33 = (bf16[2,192,256]{2,1,0:T(8,128)(2,1)S(1)}, bf16[2,192,256]{2,1,0:T(8,128)(2,1)}, u32[]{:S(2)}) copy-start(bf16[2,192,256]{2,1,0:T(8,128)(2,1)} %get-tuple-element.180) | copy-start | bytes 589828
  96.4 7.2 %copy-start.32 = (bf16[2,192,256]{2,1,0:T(8,128)(2,1)S(1)}, bf16[2,192,256]{2,1,0:T(8,128)(2,1)}, u32[]{:S(2)}) copy-start(bf16[2,192,256]{2,1,0:T(8,128)(2,1)} %get-tuple-element.181) | copy-start | bytes 589828
  96.4 8.8 %copy-start.31 = (bf16[2,192,256]{2,1,0:T(8,128)(2,1)S(1)}, bf16[2,192,256]{2,1,0:T(8,128)(2,1)}, u32[]{:S(2)}) copy-start(bf16[2,192,256]{2,1,0:T(8,128)(2,1)} %get-tuple-element.182) | copy-start | bytes 589828
  101.8 28.5 %collective-permute-start.22 = (bf16[2,4,96,768]{3,2,1,0:T(8,128)(2,1)}, bf16[2,4,96,768]{3,2,1,0:T(8,128)(2,1)S(1)}, u32[]{:S(2)}, u32[]{:S(2)}) collective-permute-start(bf16[2,4,96,768]{3,2,1,0:T(8,128)(2,1)} %get-tuple-element.203), channel_id=1, source_target_pairs={{0,4},{4,0},{8,12},{12,8},{16,20},{20,16},{24,28},{28,24},{1,5},{5... | collective-permute-start | bytes 3538952 | tf_op jit(solution)/shard_map/ppermute | solution.py:601
  103.6 7.6 %collective-permute-start.17 = (bf16[2,192,256]{2,1,0:T(8,128)(2,1)S(1)}, bf16[2,192,256]{2,1,0:T(8,128)(2,1)S(1)}, u32[]{:S(2)}, u32[]{:S(2)}) collective-permute-start(bf16[2,192,256]{2,1,0:T(8,128)(2,1)S(1)} %copy-done.33), channel_id=1, source_target_pairs={{0,1},{1,0},{2,3},{3,2},{4,5},{5,4},{6,7},{7,6},{8,9},{9,8},{10,11... | collective-permute-start | bytes 589832 | tf_op jit(solution)/shard_map/ppermute | solution.py:601
  103.7 7.7 %collective-permute-start.18 = (bf16[2,192,256]{2,1,0:T(8,128)(2,1)S(1)}, bf16[2,192,256]{2,1,0:T(8,128)(2,1)S(1)}, u32[]{:S(2)}, u32[]{:S(2)}) collective-permute-start(bf16[2,192,256]{2,1,0:T(8,128)(2,1)S(1)} %copy-done.32), channel_id=1, source_target_pairs={{0,2},{1,3},{2,0},{3,1},{4,6},{5,7},{6,4},{7,5},{8,10},{9,11},{10,... | collective-permute-start | bytes 589832 | tf_op jit(solution)/shard_map/ppermute | solution.py:601
  105.2 9.5 %collective-permute-start.19 = (bf16[2,192,256]{2,1,0:T(8,128)(2,1)S(1)}, bf16[2,192,256]{2,1,0:T(8,128)(2,1)S(1)}, u32[]{:S(2)}, u32[]{:S(2)}) collective-permute-start(bf16[2,192,256]{2,1,0:T(8,128)(2,1)S(1)} %copy-done.31), channel_id=1, source_target_pairs={{0,3},{1,2},{2,1},{3,0},{4,7},{5,6},{6,5},{7,4},{8,11},{9,10},{10,... | collective-permute-start | bytes 589832 | tf_op jit(solution)/shard_map/ppermute | solution.py:601
  111.2 5.0 %copy-start.28 = (bf16[2,192,256]{2,1,0:T(8,128)(2,1)}, bf16[2,192,256]{2,1,0:T(8,128)(2,1)S(1)}, u32[]{:S(2)}) copy-start(bf16[2,192,256]{2,1,0:T(8,128)(2,1)S(1)} %collective-permute-done.17.refs_7_) | copy-start | bytes 589828
  111.4 4.9 %copy-start.29 = (bf16[2,192,256]{2,1,0:T(8,128)(2,1)}, bf16[2,192,256]{2,1,0:T(8,128)(2,1)S(1)}, u32[]{:S(2)}) copy-start(bf16[2,192,256]{2,1,0:T(8,128)(2,1)S(1)} %collective-permute-done.18.refs_8_) | copy-start | bytes 589828
  114.7 19.7 %collective-permute-start.21 = (bf16[496,768]{1,0:T(8,128)(2,1)}, bf16[496,768]{1,0:T(8,128)(2,1)S(1)}, u32[]{:S(2)}, u32[]{:S(2)}) collective-permute-start(bf16[496,768]{1,0:T(8,128)(2,1)} %get-tuple-element.200), channel_id=1, source_target_pairs={{0,8},{4,12},{8,0},{12,4},{16,24},{20,28},{24,16},{28,20},{1,9},{5... | collective-permute-start | bytes 2285576 | tf_op jit(solution)/shard_map/ppermute | solution.py:601
  130.2 4.3 %copy-start.10 = (bf16[480,768]{1,0:T(8,128)(2,1)S(1)}, bf16[480,768]{1,0:T(8,128)(2,1)}, u32[]{:S(2)}) copy-start(bf16[480,768]{1,0:T(8,128)(2,1)} %get-tuple-element.207) | copy-start | bytes 2211844
  134.4 2.6 %collective-permute-start.23 = (bf16[2,256,768]{2,1,0:T(8,128)(2,1)}, bf16[2,256,768]{2,1,0:T(8,128)(2,1)}, u32[]{:S(2)}, u32[]{:S(2)}) collective-permute-start(bf16[2,256,768]{2,1,0:T(8,128)(2,1)} %get-tuple-element.204), channel_id=1, source_target_pairs={{0,1},{1,0},{2,3},{3,2},{4,5},{5,4},{6,7},{7,6},{8,9},{9,8},{10,11... | collective-permute-start | bytes 2359304 | tf_op jit(solution)/shard_map/ppermute | solution.py:601
  138.9 25.0 %copy-start.11 = (bf16[480,768]{1,0:T(8,128)(2,1)S(1)}, bf16[480,768]{1,0:T(8,128)(2,1)}, u32[]{:S(2)}) copy-start(bf16[480,768]{1,0:T(8,128)(2,1)} %get-tuple-element.230) | copy-start | bytes 2211844
  138.9 25.9 %copy-start.15 = (bf16[4,96,768]{2,1,0:T(8,128)(2,1)S(1)}, bf16[4,96,768]{2,1,0:T(8,128)(2,1)}, u32[]{:S(2)}) copy-start(bf16[4,96,768]{2,1,0:T(8,128)(2,1)} %get-tuple-element.227) | copy-start | bytes 1769476
  138.9 17.9 %collective-permute-start.26 = (bf16[256,768]{1,0:T(8,128)(2,1)}, bf16[256,768]{1,0:T(8,128)(2,1)}, u32[]{:S(2)}, u32[]{:S(2)}) collective-permute-start(bf16[256,768]{1,0:T(8,128)(2,1)} %pad_maximum_fusion.3), channel_id=1, source_target_pairs={{0,4},{4,0},{8,12},{12,8},{16,20},{20,16},{24,28},{28,24},{1,5},{5... | collective-permute-start | bytes 1179656 | tf_op jit(solution)/shard_map/ppermute | solution.py:601
  139.3 17.5 %collective-permute-start.27 = (bf16[256,768]{1,0:T(8,128)(2,1)}, bf16[256,768]{1,0:T(8,128)(2,1)S(1)}, u32[]{:S(2)}, u32[]{:S(2)}) collective-permute-start(bf16[256,768]{1,0:T(8,128)(2,1)} %fusion.6), channel_id=1, source_target_pairs={{0,2},{1,3},{2,0},{3,1},{4,6},{5,7},{6,4},{7,5},{8,10},{9,11},{10,... | collective-permute-start | bytes 1179656 | tf_op jit(solution)/shard_map/ppermute | solution.py:601
  140.9 22.0 %collective-permute-start.24 = (bf16[4,96,768]{2,1,0:T(8,128)(2,1)}, bf16[4,96,768]{2,1,0:T(8,128)(2,1)S(1)}, u32[]{:S(2)}, u32[]{:S(2)}) collective-permute-start(bf16[4,96,768]{2,1,0:T(8,128)(2,1)} %fusion), channel_id=1, source_target_pairs={{0,2},{1,3},{2,0},{3,1},{4,6},{5,7},{6,4},{7,5},{8,10},{9,11},{10,... | collective-permute-start | bytes 1769480 | tf_op jit(solution)/shard_map/ppermute | solution.py:601
  141.3 21.7 %collective-permute-start.25 = (bf16[480,768]{1,0:T(8,128)(2,1)}, bf16[480,768]{1,0:T(8,128)(2,1)S(1)}, u32[]{:S(2)}, u32[]{:S(2)}) collective-permute-start(bf16[480,768]{1,0:T(8,128)(2,1)} %get-tuple-element.218), channel_id=1, source_target_pairs={{0,8},{4,12},{8,0},{12,4},{16,24},{20,28},{24,16},{28,20},{1,9},{5... | collective-permute-start | bytes 2211848 | tf_op jit(solution)/shard_map/ppermute | solution.py:601
  156.8 10.0 %copy-start.19 = (bf16[256,768]{1,0:T(8,128)(2,1)}, bf16[256,768]{1,0:T(8,128)(2,1)S(1)}, u32[]{:S(2)}) copy-start(bf16[256,768]{1,0:T(8,128)(2,1)S(1)} %collective-permute-done.27) | copy-start | bytes 1179652
  163.0 3.8 %copy-start.16 = (bf16[4,96,768]{2,1,0:T(8,128)(2,1)}, bf16[4,96,768]{2,1,0:T(8,128)(2,1)S(1)}, u32[]{:S(2)}) copy-start(bf16[4,96,768]{2,1,0:T(8,128)(2,1)S(1)} %collective-permute-done.24) | copy-start | bytes 1769476
  163.8 17.3 %collective-permute-start.28 = (bf16[2,256,768]{2,1,0:T(8,128)(2,1)}, bf16[2,256,768]{2,1,0:T(8,128)(2,1)}, u32[]{:S(2)}, u32[]{:S(2)}) collective-permute-start(bf16[2,256,768]{2,1,0:T(8,128)(2,1)} %get-tuple-element.224), channel_id=1, source_target_pairs={{0,1},{1,0},{2,3},{3,2},{4,5},{5,4},{6,7},{7,6},{8,9},{9,8},{10,11... | collective-permute-start | bytes 2359304 | tf_op jit(solution)/shard_map/ppermute | solution.py:601
  166.8 12.8 %collective-permute-start.30 = (bf16[256,768]{1,0:T(8,128)(2,1)S(1)}, bf16[256,768]{1,0:T(8,128)(2,1)}, u32[]{:S(2)}, u32[]{:S(2)}) collective-permute-start(bf16[256,768]{1,0:T(8,128)(2,1)S(1)} %pad_maximum_fusion.4), channel_id=1, source_target_pairs={{0,2},{1,3},{2,0},{3,1},{4,6},{5,7},{6,4},{7,5},{8,10},{9,11},{10,... | collective-permute-start | bytes 1179656 | tf_op jit(solution)/shard_map/ppermute | solution.py:601
  168.6 11.0 %collective-permute-start.31 = (bf16[2,120,768]{2,1,0:T(8,128)(2,1)}, bf16[2,120,768]{2,1,0:T(8,128)(2,1)}, u32[]{:S(2)}, u32[]{:S(2)}) collective-permute-start(bf16[2,120,768]{2,1,0:T(8,128)(2,1)} %fusion.10), channel_id=1, source_target_pairs={{0,4},{4,0},{8,12},{12,8},{16,20},{20,16},{24,28},{28,24},{1,5},{5... | collective-permute-start | bytes 1105928 | tf_op jit(solution)/shard_map/ppermute | solution.py:601
  170.1 9.5 %collective-permute-start.29 = (bf16[2,96,768]{2,1,0:T(8,128)(2,1)}, bf16[2,96,768]{2,1,0:T(8,128)(2,1)}, u32[]{:S(2)}, u32[]{:S(2)}) collective-permute-start(bf16[2,96,768]{2,1,0:T(8,128)(2,1)} %fusion.13), channel_id=1, source_target_pairs={{0,8},{4,12},{8,0},{12,4},{16,24},{20,28},{24,16},{28,20},{1,9},{5... | collective-permute-start | bytes 884744 | tf_op jit(solution)/shard_map/ppermute | solution.py:601
  171.6 9.4 %copy-start.9 = (bf16[2,256,768]{2,1,0:T(8,128)(2,1)S(1)}, bf16[2,256,768]{2,1,0:T(8,128)(2,1)}, u32[]{:S(2)}) copy-start(bf16[2,256,768]{2,1,0:T(8,128)(2,1)} %get-tuple-element.223) | copy-start | bytes 2359300
  179.6 4.4 %copy-start.12 = (bf16[480,768]{1,0:T(8,128)(2,1)S(1)}, bf16[480,768]{1,0:T(8,128)(2,1)}, u32[]{:S(2)}) copy-start(bf16[480,768]{1,0:T(8,128)(2,1)} %get-tuple-element.230) | copy-start | bytes 2211844
  179.6 12.1 %collective-permute-start.32 = (bf16[584,384]{1,0:T(8,128)(2,1)}, bf16[584,384]{1,0:T(8,128)(2,1)S(1)}, u32[]{:S(2)}, u32[]{:S(2)}) collective-permute-start(bf16[584,384]{1,0:T(8,128)(2,1)} %get-tuple-element.239), channel_id=1, source_target_pairs={{0,4},{4,0},{8,12},{12,8},{16,20},{20,16},{24,28},{28,24},{1,5},{5... | collective-permute-start | bytes 1345544 | tf_op jit(solution)/shard_map/ppermute | solution.py:601
  183.0 8.8 %copy-start.27 = (f32[1,384]{1,0:T(1,128)S(1)}, f32[1,384]{1,0:T(1,128)}, u32[]{:S(2)}) copy-start(f32[1,384]{1,0:T(1,128)} %get-tuple-element.247) | copy-start | bytes 4612
  183.0 8.9 %copy-start.17 = (bf16[576,384]{1,0:T(8,128)(2,1)S(1)}, bf16[576,384]{1,0:T(8,128)(2,1)}, u32[]{:S(2)}) copy-start(bf16[576,384]{1,0:T(8,128)(2,1)} %get-tuple-element.245) | copy-start | bytes 1327108
  186.6 18.3 %collective-permute-start.36 = (bf16[136,768]{1,0:T(8,128)(2,1)}, bf16[136,768]{1,0:T(8,128)(2,1)}, u32[]{:S(2)}, u32[]{:S(2)}) collective-permute-start(bf16[136,768]{1,0:T(8,128)(2,1)} %pad_maximum_fusion.7), channel_id=1, source_target_pairs={{0,16},{4,20},{8,24},{12,28},{16,0},{20,4},{24,8},{28,12},{1,17},{... | collective-permute-start | bytes 626696 | tf_op jit(solution)/shard_map/ppermute | solution.py:601
  192.0 11.6 %collective-permute-start.34 = (bf16[290,384]{1,0:T(8,128)(2,1)S(1)}, bf16[290,384]{1,0:T(8,128)(2,1)S(1)}, u32[]{:S(2)}, u32[]{:S(2)}) collective-permute-start(bf16[290,384]{1,0:T(8,128)(2,1)S(1)} %pad_maximum_fusion.6), channel_id=1, source_target_pairs={{0,8},{4,12},{8,0},{12,4},{16,24},{20,28},{24,16},{28,20},{1,9},{5... | collective-permute-start | bytes 668168 | tf_op jit(solution)/shard_map/ppermute | solution.py:601
  195.0 9.9 %collective-permute-start.35 = (bf16[96,768]{1,0:T(8,128)(2,1)}, bf16[96,768]{1,0:T(8,128)(2,1)}, u32[]{:S(2)}, u32[]{:S(2)}) collective-permute-start(bf16[96,768]{1,0:T(8,128)(2,1)} %fusion.15), channel_id=1, source_target_pairs={{0,16},{4,20},{8,24},{12,28},{16,0},{20,4},{24,8},{28,12},{1,17},{... | collective-permute-start | bytes 442376 | tf_op jit(solution)/shard_map/ppermute | solution.py:601
  197.6 23.3 %collective-permute-start.33 = (bf16[256,768]{1,0:T(8,128)(2,1)}, bf16[256,768]{1,0:T(8,128)(2,1)}, u32[]{:S(2)}, u32[]{:S(2)}) collective-permute-start(bf16[256,768]{1,0:T(8,128)(2,1)} %fusion.7), channel_id=1, source_target_pairs={{0,2},{1,3},{2,0},{3,1},{4,6},{5,7},{6,4},{7,5},{8,10},{9,11},{10,... | collective-permute-start | bytes 1179656 | tf_op jit(solution)/shard_map/ppermute | solution.py:601
  203.6 3.9 %copy-start.20 = (bf16[290,384]{1,0:T(8,128)(2,1)}, bf16[290,384]{1,0:T(8,128)(2,1)S(1)}, u32[]{:S(2)}) copy-start(bf16[290,384]{1,0:T(8,128)(2,1)S(1)} %collective-permute-done.34) | copy-start | bytes 668164
  204.9 6.2 %copy-start.18 = (bf16[576,384]{1,0:T(8,128)(2,1)S(1)}, bf16[576,384]{1,0:T(8,128)(2,1)}, u32[]{:S(2)}) copy-start(bf16[576,384]{1,0:T(8,128)(2,1)} %get-tuple-element.245) | copy-start | bytes 1327108
  209.5 11.5 %copy-start.7 = (f32[512,768]{1,0:T(8,128)S(1)}, f32[512,768]{1,0:T(8,128)}, u32[]{:S(2)}) copy-start(f32[512,768]{1,0:T(8,128)} %get-tuple-element.222) | copy-start | bytes 4718596
  211.2 8.2 %collective-permute-start.37 = (bf16[146,384]{1,0:T(8,128)(2,1)S(1)}, bf16[146,384]{1,0:T(8,128)(2,1)S(1)}, u32[]{:S(2)}, u32[]{:S(2)}) collective-permute-start(bf16[146,384]{1,0:T(8,128)(2,1)S(1)} %pad_maximum_fusion.8), channel_id=1, source_target_pairs={{0,16},{4,20},{8,24},{12,28},{16,0},{20,4},{24,8},{28,12},{1,17},{... | collective-permute-start | bytes 336392 | tf_op jit(solution)/shard_map/ppermute | solution.py:601
  (8 other events, 13.7 us)

commit v4 on v3

--- a/solution.py
+++ b/solution.py
@@ -36,6 +36,31 @@
         return self.dst
 
 
+class Pieces:
+    def __init__(self, copies, dst):
+        self.copies, self.dst = copies, dst
+        for c in copies:
+            c.start()
+
+    def __call__(self):
+        for c in self.copies:
+            c.wait()
+        self.copies = []
+        return self.dst
+
+
+def pieces(info, a, b, dst, sem, z_first):
+    part = a.shape[0] // 2
+    copies = []
+    for src, other in ((a, 0), (b, 1)):
+        for i in range(2):
+            flips = (other, i) if z_first else (i, other)
+            at = 2 * (info[3] ^ flips[0]) + (info[4] ^ flips[1])
+            rows = pl.ds(pl.multiple_of(at * part, part), part)
+            copies.append(pltpu.make_async_copy(src.at[pl.ds(i * part, part)], dst.at[rows], sem.at[len(copies)]))
+    return Pieces(copies, dst)
+
+
 class Flush:
     def __init__(self, src, dst, sem):
         self.src, self.copy = src, pltpu.make_async_copy(src, dst, sem)
@@ -53,7 +78,8 @@
     far_out = [i for i, o in enumerate(outs) if isinstance(o, list)]
     raw_in = [i for i, a in enumerate(ins) if isinstance(a, Raw)]
     raw_out = [i for i, o in enumerate(outs) if isinstance(o, Raw)]
-    pinned += raw_in
+    pinned += [i for i in raw_in if ins[i].pinned]
+    any_in = far_in + raw_in
     arrays = [a[0] if isinstance(a, tuple) else a.value if isinstance(a, Raw) else a for a in ins]
     shapes = [o[0] if isinstance(o, list) else o.value if isinstance(o, Raw) else o for o in outs]
     picked = [a[1] if isinstance(a, tuple) else None for a in ins]
@@ -94,7 +120,7 @@
         grid_spec=pltpu.PrefetchScalarGridSpec(
             num_scalar_prefetch=2,
             grid=(1,),
-            in_specs=[hbm if i in pinned else pl.BlockSpec(memory_space=pl.ANY) if i in far_in else VM for i in range(n_in)],
+            in_specs=[hbm if i in pinned else pl.BlockSpec(memory_space=pl.ANY) if i in any_in else VM for i in range(n_in)],
             out_specs=[hbm if i in far_out + raw_out else VM for i in range(n_out)],
             scratch_shapes=[*buffers, *scratch, pltpu.SemaphoreType.DMA((max(1, len(far_in) + len(far_out)),))],
         ),
@@ -105,8 +131,8 @@
 
 
 class Raw:
-    def __init__(self, value):
-        self.value = value
+    def __init__(self, value, pinned=True):
+        self.value, self.pinned = value, pinned
 
 
 def ref(x):
@@ -324,7 +350,7 @@
     ]
     ins = [whole(w_t)] + [of_sequence(a) for a in (q, k, v, lse, c)]
     ins += [(g, ((width, block), lambda ref, info: ref.at[info[5]]), None) for g in gs]
-    return call("attend_bwd", attend_bwd_kernel, info, ins, outs, scratch, which=which, cost=10**10)
+    return call("attend_bwd", attend_bwd_kernel, info, ins, outs, scratch, which=which, cost=2 * 10**10)
 
 
 def project_grads_kernel(info, x0, low0, x1, low1, db0, db1, keep, send, db_ref, dw, acc, pair, *, parts):
@@ -354,7 +380,10 @@
 
 
 def gelu_parts(h):
-    t = 1.0 / (1.0 + (0.3275911 * 0.7071067811865476) * jnp.abs(h))
+    den = 1.0 + (0.3275911 * 0.7071067811865476) * jnp.abs(h)
+    t = pl.reciprocal(den, approx=True)
+    t = t * (2.0 - den * t)
+    t = t * (2.0 - den * t)
     poly = t * (0.127414796 + t * (-0.142248368 + t * (0.7107068705 + t * (-0.7265760135 + t * 0.5307027145))))
     bell = jnp.exp2((-0.5 * 1.4426950408889634) * (h * h))
     tail = poly * bell
@@ -403,8 +432,10 @@
 def feed_kernel(info, *rest, width, far):
     low, (pack, *rest) = rest[:4], rest[4:]
     if far:
-        u_a, u_b, d_a, d_b, p_own, p_sib, act_out, slope_out, own, sib, both, up, dn = rest
-        assemble(info[3], info[4], up, u_a(), u_b(), False)
+        u_a, u_b, d_a, d_b, p_own, p_sib, act_out, slope_out, own, sib, both, up, dn, sem = rest
+        up = pieces(info, u_a, u_b, up, sem.at[0], False)
+        dn = pieces(info, d_a, d_b, dn, sem.at[1], True)
+        up = up()
     else:
         u_in, d_in, act_out, slope_out, own, sib, both = rest
         up = u_in()
@@ -429,22 +460,13 @@
 
     lax.fori_loop(0, 2, side, 0)
     if far:
-        assemble(info[3], info[4], dn, d_a(), d_b(), True)
+        dn = dn()
         sib[...] = (p_sib[...] + mm(act[1], dn[...])).astype(bf16)
         own[...] = p_own[...] + mm(act[0], dn[...])
     else:
         dn = d_in()
         own[...] = mm(act[0], dn[...])
         sib[...] = mm(act[1], dn[...])
-
-
-def assemble(x, z, dst, a, b, z_first):
-    part = a.shape[0] // 2
-    for src, other in ((a, 0), (b, 1)):
-        for i in range(2):
-            flips = (other, i) if z_first else (i, other)
-            at = 2 * (x ^ flips[0]) + (z ^ flips[1])
-            dst[pl.ds(pl.multiple_of(at * part, part), part)] = src[i * part : (i + 1) * part]
 
 
 def second_norm_kernel(info, cot_in, par, nv_in, own, got, outs, gsec_out, gs_low, small):
@@ -467,17 +489,18 @@
     small[...] = jnp.concatenate([*sums, jnp.zeros((5, d), f32)], axis=0)
 
 
-def feed_back_kernel(info, gs, gs2, slope0, slope1, up0, dn0, u_a, u_b, d_a, d_b, gh_out, own, sib, ub, sides, up2, dn2):
+def feed_back_kernel(info, gs, gs2, slope0, slope1, up0, dn0, u_a, u_b, d_a, d_b, gh_out, own, sib, ub, sides, up2, dn2, sem):
     gh = ref(gh_out)
     units = up0.dst.shape[1]
+    dn2 = pieces(info, d_a, d_b, dn2, sem.at[1], True)
+    up2 = pieces(info, u_a, u_b, up2, sem.at[0], False)
     ub[...] = jnp.zeros_like(ub)
     sides[0] = gs[...]
     sides[1] = gs2[...]
     step = 256
     for k, slope in enumerate((ref(slope0), ref(slope1))):
         if k:
-            assemble(info[3], info[4], dn2, d_a(), d_b(), True)
-            dn = dn2
+            dn = dn2()
         else:
             dn = dn0()
 
@@ -493,7 +516,7 @@
             return lax.fori_loop(0, units // step, chunk, carry)
 
         lax.fori_loop(0, 2, side, 0)
-    assemble(info[3], info[4], up2, u_a(), u_b(), False)
+    up2 = up2()
     up = up0()
     sib[...] = (mm(gh[0, 1], up[...], NT) + mm(gh[1, 1], up2[...], NT)).astype(bf16)
     own[...] = mm(gh[0, 0], up[...], NT) + mm(gh[1, 0], up2[...], NT)
@@ -700,8 +723,8 @@
         width=width,
         far=False,
     )
-    halves = [loose(x) for x in (u2a, u2b, d2a, d2b)]
-    both = [pltpu.VMEM((d, units), bf16), pltpu.VMEM((units, d), bf16)]
+    halves = [Raw(x, False) for x in (u2a, u2b, d2a, d2b)]
+    both = [pltpu.VMEM((d, units), bf16), pltpu.VMEM((units, d), bf16), pltpu.SemaphoreType.DMA((2, 4))]
     act1, slope1, own, sib = call(
         "feed",
         feed_kernel,
@@ -860,10 +883,14 @@
     shape = ([2] * (bits - 1)) + [row, 2 * width]
     terms = [x.reshape(shape) for x in (w_keep, got[:at])]
     db = db + got[at : at + 1].astype(f32) + got[at + 1 : at + 2].astype(f32)
+    input_grad = jnp.stack([
+        (summed(x) + gfi[s * rows : (s + 1) * rows]).astype(bf16)
+        for s, x in enumerate(terms_of)
+    ])
     for i in range(1, bits):
         kept, rows_sent, more = halve_with(terms, terms[0].ndim - 3, db, "dp", 1 << i, bit_of[i])
-        if i == 1:
-            kept[-1], down_got, up_got = after(kept[-1], down_got, up_got)
+        if i == bits - 1:
+            _, down_got, up_got = after(rows_sent, down_got, up_got)
         terms, db = kept, db + more
     down_terms, up_terms, small = with_received(down_terms, down_got, up_terms, up_got, sent, small)
     down_sum = summed(down_terms)
@@ -873,13 +900,9 @@
     qkv_sum = jnp.concatenate([qkv_sum[:, :width], qkv_sum[:, width:]], axis=0).reshape(3, -1, width)
     qkv_sum = jnp.transpose(qkv_sum, (1, 0, 2))
     db = db.reshape(2, width)
-    input_list = [
-        (summed(x) + gfi[s * rows : (s + 1) * rows]).astype(bf16)
-        for s, x in enumerate(terms_of)
-    ]
     return (
         outputs,
-        jnp.stack(input_list, 0),
+        input_grad,
         qkv_sum,
         db,
         up_sum[block:],

time: 225 us -> 217 us (0.964)
  other arithmetic: 22.6 us -> 15.1 us
  Pallas kernels: 107 us -> 110 us
    pallas_call x13, Pallas kernels: 107 us -> 110 us  [call(): pl.pallas_call(kernel, out_shape=[pltpu.HBM(o.shape, o.dtype) if i in far...]
  transfers between devices with their start and end apart: 38 -> 38, of which waited for: 18 -> 16; matrix products, arithmetic and copies ran while one was open for 10% -> 7% of each run, Pallas kernels for 33% -> 36%
where the time goes in v4:
time: 217 us; the launch traced here: 216 us
  Pallas kernels  110 us (51%)
  waiting for transfers between devices  45.9 us (21%)
  starting transfers between devices  36.2 us (17%)
  other arithmetic  15.1 us (7%)
  local copies, waits for them, and re-layouts  7.79 us (4%)
    pallas_call x13, Pallas kernels, call(): pl.pallas_call(kernel, out_shape=[pltpu.HBM(o.shape, o.dtype) if i in far...  110 us
    ppermute x38, waiting for transfers between devices, swap(): return lax.ppermute(x, axis, [(i, i ^ bit) for i in range(size)])  45.9 us
    ppermute x38, starting transfers between devices, swap(): return lax.ppermute(x, axis, [(i, i ^ bit) for i in range(size)])  36.2 us
  transfers between devices with their start and end apart: 38, of which 16 were waited for; matrix products, arithmetic and copies ran while one was open for 7% of the time, Pallas kernels for 36%

profile of v4, /device:TPU:0, one launch (start us, length us, event | category | flops | bytes accessed | tf_op | source)
XLA Modules:
  0.0 216.4 jit_solution(14060707263271042156)
XLA Ops:
  0.6 3.4 %prepare.1 = (bf16[200,768]{1,0:T(8,128)(2,1)}, bf16[192,768]{1,0:T(8,128)(2,1)}, bf16[192,768]{1,0:T(8,128)(2,1)}) custom-call(s32[2]{0:T(128)} %lengths_ref.25, s32[1]{0:T(128)} %constant.384.clone.1.which_ref, bf16[192,768]{1,0:T(8,128)(2,1)} %refs_0_.6, bf16[768]{0:T(1024)(128)(2,1)} %refs_1_.1, bf16[768,768]{1,0:T(8,128)(2,1)} %refs_4_.1, ...), custom_call_target="tpu_custom_call" | custom-call | flops 1000 | bytes 1000 | tf_op jit(solution)/shard_map/prepare/pallas_call | solution.py:117
  4.0 3.0 %collective-permute-start.1 = (bf16[200,768]{1,0:T(8,128)(2,1)}, bf16[200,768]{1,0:T(8,128)(2,1)S(1)}, u32[]{:S(2)}, u32[]{:S(2)}) collective-permute-start(bf16[200,768]{1,0:T(8,128)(2,1)} %get-tuple-element.137.refs_6_.refs_4_.refs_11_), channel_id=1, source_target_pairs={{0,2},{1,3},{2,0},{3,1},{4,6},{5,7},{6,4},{7,5},{8,10},{9,11},{10,... | collective-permute-start | bytes 921608 | tf_op jit(solution)/shard_map/ppermute | solution.py:624
  7.2 1.9 collective-permute-start.3
  9.1 16.3 %attend_fwd.1 = (bf16[2,1024,256]{2,1,0:T(8,128)(2,1)}, bf16[2,1024,256]{2,1,0:T(8,128)(2,1)}, bf16[2,1024,192]{2,1,0:T(8,128)(2,1)}, f32[2,4,8,256]{3,2,1,0:T(8...) custom-call(s32[2]{0:T(128)} %lengths_ref.25, ...), custom_call_target="tpu_custom_call" | custom-call | flops 1000 | bytes 1000 | tf_op jit(solution)/shard_map/attend_fwd/pallas_call | solution.py:117
  25.5 1.7 collective-permute-done.3
  27.2 1.7 collective-permute-start.7
  28.9 1.6 collective-permute-start.8
  30.5 1.5 collective-permute-start.5
  32.4 6.0 %collective-permute-done.5.refs_4_.refs_9_ = bf16[2,192,256]{2,1,0:T(8,128)(2,1)S(1)} collective-permute-done((bf16[2,192,256]{2,1,0:T(8,128)(2,1)}, bf16[2,192,256]{2,1,0:T(8,128)(2,1)S(1)}, u32[]{:S(2)}, u32[]{:S(2)}) %collective-permute-start.5) | collective-permute-done | bytes 196640 | tf_op jit(solution)/shard_map/ppermute | solution.py:624
  38.4 3.4 %collective-permute-done.6.refs_5_.refs_10_ = bf16[2,192,256]{2,1,0:T(8,128)(2,1)S(1)} collective-permute-done((bf16[2,192,256]{2,1,0:T(8,128)(2,1)}, bf16[2,192,256]{2,1,0:T(8,128)(2,1)S(1)}, u32[]{:S(2)}, u32[]{:S(2)}) %collective-permute-start.6) | collective-permute-done | bytes 196640 | tf_op jit(solution)/shard_map/ppermute | solution.py:624
  44.8 0.9 copy-done.1
  45.7 0.9 copy-done.4
  46.6 4.2 %first_norm.1 = (f32[512,768]{1,0:T(8,128)S(1)}, f32[512,1]{1,0:T(8,128)S(1)}, bf16[256,768]{1,0:T(8,128)(2,1)S(1)}, bf16[256,768]{1,0:T(8,128)(2,1)S(1)}) custom-call(s32[2]{0:T(128)S(1)} %copy-done.6, s32[1]{0:T(128)} %constant.384.clone.1.which_ref, bf16[2,1024,768]{2,1,0:T(8,128)(2,1)} %refs_2_.5, f32[6,768]{1,0:T(8,128)S(1)} %reshape.192.refs_1_.refs_0_, ...), custom_call_target="tpu_custom_call" | custom-call | flops 1000 | bytes 1000 | tf_op jit(solution)/shard_map/first_norm/pallas_call | solution.py:117
  51.4 1.2 collective-permute-done.10.refs_2_
  53.2 8.4 %feed.2 = (bf16[2,512,768]{2,1,0:T(8,128)(2,1)S(1)}, bf16[2,512,768]{2,1,0:T(8,128)(2,1)S(1)}, f32[512,768]{1,0:T(8,128)S(1)}, f32[512,768]{1,0:T(8,128)S(1)}) custom-call(s32[2]{0:T(128)S(1)} %copy-done.6, s32[1]{0:T(128)} %constant.384.clone.1.which_ref, bf16[256,768]{1,0:T(8,128)(2,1)S(1)} %get-tuple-element.156.refs_0_, ...), custom_call_target="tpu_custom_call" | custom-call | flops 1000 | bytes 1000 | tf_op jit(solution)/shard_map/feed/pallas_call | solution.py:117
  61.5 7.7 %feed.3 = (bf16[2,512,768]{2,1,0:T(8,128)(2,1)S(1)}, bf16[2,512,768]{2,1,0:T(8,128)(2,1)S(1)}, f32[512,768]{1,0:T(8,128)S(1)}, bf16[512,768]{1,0:T(8,128)(2,1)S(1)}) custom-call(s32[2]{0:T(128)S(1)} %copy-done.6, s32[1]{0:T(128)} %constant.384.clone.1.which_ref, bf16[256,768]{1,0:T(8,128)(2,1)S(1)} %get-tuple-element.156.refs_0_, ...), custom_call_target="tpu_custom_call" | custom-call | flops 1000 | bytes 1000 | tf_op jit(solution)/shard_map/feed/pallas_call | solution.py:117
  69.4 2.1 collective-permute-done.14.refs_4_
  71.6 4.1 %second_norm.1 = (bf16[2,256,768]{2,1,0:T(8,128)(2,1)}, f32[512,768]{1,0:T(8,128)S(1)}, bf16[512,768]{1,0:T(8,128)(2,1)S(1)}, f32[8,768]{1,0:T(8,128)S(1)}) custom-call(s32[2]{0:T(128)S(1)} %copy-done.6, s32[1]{0:T(128)} %constant.384.clone.1.which_ref, bf16[2,256,768]{2,1,0:T(8,128)(2,1)} %refs_0_.8, f32[6,768]{1,0:T(8,128)S(1)} %reshape.192.refs_1_.refs_0_, ...), custom_call_target="tpu_custom_call" | custom-call | flops 1000 | bytes 1000 | tf_op jit(solution)/shard_map/second_norm/pallas_call | solution.py:117
  75.9 2.1 collective-permute-done.15.refs_1_.refs_3_
  78.0 10.0 %feed_back.1 = (bf16[2,2,512,768]{3,2,1,0:T(8,128)(2,1)S(1)}, f32[512,768]{1,0:T(8,128)S(1)}, bf16[512,768]{1,0:T(8,128)(2,1)S(1)}, f32[8,768]{1,0:T(8,128)S(1)}) custom-call(s32[2]{0:T(128)S(1)} %copy-done.6, s32[1]{0:T(128)} %constant.384.clone.1.which_ref, bf16[512,768]{1,0:T(8,128)(2,1)S(1)} %get-tuple-element.171.refs_0_.refs_2_, ...), custom_call_target="tpu_custom_call" | custom-call | flops 1000 | bytes 1000 | tf_op jit(solution)/shard_map/feed_back/pallas_call | solution.py:117
  88.2 2.1 collective-permute-done.16.refs_4_
  90.3 7.1 %first_back.1 = (f32[512,768]{1,0:T(8,128)}, bf16[2,192,256]{2,1,0:T(8,128)(2,1)}, bf16[2,192,256]{2,1,0:T(8,128)(2,1)}, bf16[2,192,256]{2,1,0:T(8,128)(2,1)}, b...) custom-call(s32[2]{0:T(128)S(1)} %copy-done.6, ...), custom_call_target="tpu_custom_call" | custom-call | flops 1000 | bytes 1000 | tf_op jit(solution)/shard_map/first_back/pallas_call | solution.py:117
  98.0 1.7 collective-permute-start.18
  99.8 5.4 %down_grads.1 = (bf16[4,96,768]{2,1,0:T(8,128)(2,1)}, bf16[4,96,768]{2,1,0:T(8,128)(2,1)}, bf16[2,4,96,768]{3,2,1,0:T(8,128)(2,1)}) custom-call(s32[2]{0:T(128)S(1)} %copy-done.6, s32[1]{0:T(128)} %constant.384.clone.1.which_ref, bf16[2,512,768]{2,1,0:T(8,128)(2,1)S(1)} %get-tuple-element.200.refs_0_, bf16[2,512,768]{2,1,0:T(8,128)(2,1)S(1)} %get-tuple-element.201.refs_1_, ...), custom_call_target="tpu_custom_call" | custom-call | flops 1000 | bytes 1000 | tf_op jit(solution)/shard_map/down_grads/pallas_call | solution.py:117
  105.1 1.6 collective-permute-start.22
  106.7 5.8 %up_grads.1 = (bf16[480,768]{1,0:T(8,128)(2,1)}, bf16[496,768]{1,0:T(8,128)(2,1)}, bf16[480,768]{1,0:T(8,128)(2,1)}, bf16[480,768]{1,0:T(8,128)(2,1)}, f32[8,768]{1,0:T(8,128)S(1)}) custom-call(s32[2]{0:T(128)S(1)} %copy-done.6, s32[1]{0:T(128)} %constant.384.clone.1.which_ref, bf16[256,768]{1,0:T(8,128)(2,1)S(1)} %get-tuple-element.156.refs_0_, ...), custom_call_target="tpu_custom_call" | custom-call | flops 1000 | bytes 1000 | tf_op jit(solution)/shard_map/up_grads/pallas_call | solution.py:117
  112.5 1.6 collective-permute-start.21
  114.2 13.9 %attend_bwd.2 = (bf16[2,256,768]{2,1,0:T(8,128)(2,1)}, bf16[2,256,768]{2,1,0:T(8,128)(2,1)}, bf16[3,1024,192]{2,1,0:T(8,128)(2,1)}, f32[1,384]{1,0:T(1,128)}) custom-call(s32[2]{0:T(128)} %lengths_ref.25, s32[1]{0:T(128)} %constant.384.clone.1.which_ref, bf16[3,192,768]{2,1,0:T(8,128)(2,1)} %bitcast.109, bf16[2,1024,256]{2,1,0:T(8,128)(2,1)} %get-tuple-element.165.refs_1_, ...), custom_call_target="tpu_custom_call" | custom-call | flops 20000000000 | bytes 1000 | tf_op jit(solution)/shard_map/attend_bwd/pallas_call | solution.py:117
  128.1 5.6 %collective-permute-done.22 = bf16[2,4,96,768]{3,2,1,0:T(8,128)(2,1)S(1)} collective-permute-done((bf16[2,4,96,768]{3,2,1,0:T(8,128)(2,1)}, bf16[2,4,96,768]{3,2,1,0:T(8,128)(2,1)S(1)}, u32[]{:S(2)}, u32[]{:S(2)}) %collective-permute-start.22) | collective-permute-done | bytes 1179680 | tf_op jit(solution)/shard_map/ppermute | solution.py:624
  134.1 0.8 pad_maximum_fusion.3
  134.9 1.0 fusion
  136.3 1.8 fusion.6
  138.2 1.7 collective-permute-start.26
  139.9 1.5 collective-permute-start.27
  141.9 1.6 collective-permute-start.25
  143.5 16.0 %attend_bwd.3 = (bf16[2,256,768]{2,1,0:T(8,128)(2,1)}, bf16[2,256,768]{2,1,0:T(8,128)(2,1)}, bf16[3,1024,192]{2,1,0:T(8,128)(2,1)}, f32[1,384]{1,0:T(1,128)}) custom-call(s32[2]{0:T(128)} %lengths_ref.25, s32[1]{0:T(128)} %constant.385.clone.1.which_ref, bf16[3,192,768]{2,1,0:T(8,128)(2,1)} %bitcast.110, bf16[2,1024,256]{2,1,0:T(8,128)(2,1)} %get-tuple-element.165.refs_1_, ...), custom_call_target="tpu_custom_call" | custom-call | flops 20000000000 | bytes 1000 | tf_op jit(solution)/shard_map/attend_bwd/pallas_call | solution.py:117
  159.6 4.1 %collective-permute-done.24 = bf16[4,96,768]{2,1,0:T(8,128)(2,1)S(1)} collective-permute-done((bf16[4,96,768]{2,1,0:T(8,128)(2,1)}, bf16[4,96,768]{2,1,0:T(8,128)(2,1)S(1)}, u32[]{:S(2)}, u32[]{:S(2)}) %collective-permute-start.24) | collective-permute-done | bytes 589856 | tf_op jit(solution)/shard_map/ppermute | solution.py:624
  163.8 0.8 fusion.10
  164.6 0.8 fusion.13
  165.6 0.8 pad_maximum_fusion.4
  166.4 1.5 collective-permute-start.30
  168.4 1.6 collective-permute-start.29
  170.0 8.0 %project_grads.1 = (bf16[576,384]{1,0:T(8,128)(2,1)}, bf16[584,384]{1,0:T(8,128)(2,1)}, f32[1,384]{1,0:T(1,128)}) custom-call(s32[2]{0:T(128)} %lengths_ref.25, s32[1]{0:T(128)} %constant.384.clone.1.which_ref, bf16[2,1024,768]{2,1,0:T(8,128)(2,1)} %refs_2_.5, bf16[3,1024,192]{2,1,0:T(8,128)(2,1)} %get-tuple-element.224.refs_1_, ...), custom_call_target="tpu_custom_call" | custom-call | flops 1000 | bytes 1000 | tf_op jit(solution)/shard_map/project_grads/pallas_call | solution.py:117
  178.0 0.8 collective-permute-done.31
  178.8 0.8 collective-permute-start.32
  179.6 0.9 fusion.7
  180.5 1.0 slice.176
  181.5 1.1 fusion.15
  182.6 2.6 %collective-permute-start.36 = (bf16[96,768]{1,0:T(8,128)(2,1)S(1)}, bf16[96,768]{1,0:T(8,128)(2,1)S(1)}, u32[]{:S(2)}, u32[]{:S(2)}) collective-permute-start(bf16[96,768]{1,0:T(8,128)(2,1)S(1)} %fusion.15), channel_id=1, source_target_pairs={{0,16},{4,20},{8,24},{12,28},{16,0},{20,4},{24,8},{28,12},{1,17},{... | collective-permute-start | bytes 442376 | tf_op jit(solution)/shard_map/ppermute | solution.py:624
  185.3 0.7 subtract_convert_fusion
  186.0 4.7 %collective-permute-done.32 = bf16[584,384]{1,0:T(8,128)(2,1)S(1)} collective-permute-done((bf16[584,384]{1,0:T(8,128)(2,1)}, bf16[584,384]{1,0:T(8,128)(2,1)S(1)}, u32[]{:S(2)}, u32[]{:S(2)}) %collective-permute-start.32) | collective-permute-done | bytes 448544 | tf_op jit(solution)/shard_map/ppermute | solution.py:624
  190.9 1.6 collective-permute-start.34
  192.7 2.6 %collective-permute-start.37 = (bf16[136,768]{1,0:T(8,128)(2,1)S(1)}, bf16[136,768]{1,0:T(8,128)(2,1)S(1)}, u32[]{:S(2)}, u32[]{:S(2)}) collective-permute-start(bf16[136,768]{1,0:T(8,128)(2,1)S(1)} %pad_maximum_fusion.7), channel_id=1, source_target_pairs={{0,16},{4,20},{8,24},{12,28},{16,0},{20,4},{24,8},{28,12},{1,17},{... | collective-permute-start | bytes 626696 | tf_op jit(solution)/shard_map/ppermute | solution.py:624
  195.3 1.1 collective-permute-start.33
  196.4 4.9 %collective-permute-done.34 = bf16[290,384]{1,0:T(8,128)(2,1)S(1)} collective-permute-done((bf16[290,384]{1,0:T(8,128)(2,1)S(1)}, bf16[290,384]{1,0:T(8,128)(2,1)S(1)}, u32[]{:S(2)}, u32[]{:S(2)}) %collective-permute-start.34) | collective-permute-done | bytes 222752 | tf_op jit(solution)/shard_map/ppermute | solution.py:624
  201.5 2.1 collective-permute-done.37
  204.4 0.7 slice.212
  205.6 1.8 fusion.14
  207.3 0.7 slice_reduce_fusion
  208.0 4.0 %collective-permute-done.35 = bf16[146,384]{1,0:T(8,128)(2,1)S(1)} collective-permute-done((bf16[146,384]{1,0:T(8,128)(2,1)S(1)}, bf16[146,384]{1,0:T(8,128)(2,1)S(1)}, u32[]{:S(2)}, u32[]{:S(2)}) %collective-permute-start.35) | collective-permute-done | bytes 112160 | tf_op jit(solution)/shard_map/ppermute | solution.py:624
  212.1 0.7 reshape.190
  212.8 0.7 pad_maximum_fusion.5
  213.6 1.9 fusion.8
  215.5 0.9 pad_maximum_fusion
  (146 shorter events, 9.7 us)
Async XLA Ops:
  4.0 23.2 %collective-permute-start.1 = (bf16[200,768]{1,0:T(8,128)(2,1)}, bf16[200,768]{1,0:T(8,128)(2,1)S(1)}, u32[]{:S(2)}, u32[]{:S(2)}) collective-permute-start(bf16[200,768]{1,0:T(8,128)(2,1)} %get-tuple-element.137.refs_6_.refs_4_.refs_11_), channel_id=1, source_target_pairs={{0,2},{1,3},{2,0},{3,1},{4,6},{5,7},{6,4},{7,5},{8,10},{9,11},{10,... | collective-permute-start | bytes 921608 | tf_op jit(solution)/shard_map/ppermute | solution.py:624
  7.1 20.1 %collective-permute-start = (bf16[200,768]{1,0:T(8,128)(2,1)}, bf16[200,768]{1,0:T(8,128)(2,1)S(1)}, u32[]{:S(2)}, u32[]{:S(2)}) collective-permute-start(bf16[200,768]{1,0:T(8,128)(2,1)} %get-tuple-element.137.refs_6_.refs_4_.refs_11_), channel_id=1, source_target_pairs={{0,1},{1,0},{2,3},{3,2},{4,5},{5,4},{6,7},{7,6},{8,9},{9,8},{10,11... | collective-permute-start | bytes 921608 | tf_op jit(solution)/shard_map/ppermute | solution.py:624
  7.1 18.4 %collective-permute-start.2 = (bf16[192,768]{1,0:T(8,128)(2,1)}, bf16[192,768]{1,0:T(8,128)(2,1)S(1)}, u32[]{:S(2)}, u32[]{:S(2)}) collective-permute-start(bf16[192,768]{1,0:T(8,128)(2,1)} %get-tuple-element.138), channel_id=1, source_target_pairs={{0,2},{1,3},{2,0},{3,1},{4,6},{5,7},{6,4},{7,5},{8,10},{9,11},{10,... | collective-permute-start | bytes 884744 | tf_op jit(solution)/shard_map/ppermute | solution.py:624
  7.2 20.0 %collective-permute-start.3 = (bf16[192,768]{1,0:T(8,128)(2,1)}, bf16[192,768]{1,0:T(8,128)(2,1)S(1)}, u32[]{:S(2)}, u32[]{:S(2)}) collective-permute-start(bf16[192,768]{1,0:T(8,128)(2,1)} %get-tuple-element.139), channel_id=1, source_target_pairs={{0,2},{1,3},{2,0},{3,1},{4,6},{5,7},{6,4},{7,5},{8,10},{9,11},{10,... | collective-permute-start | bytes 884744 | tf_op jit(solution)/shard_map/ppermute | solution.py:624
  25.4 18.1 %copy-start.24 = (bf16[768]{0:T(1024)(128)(2,1)S(1)}, bf16[768]{0:T(1024)(128)(2,1)}, u32[]{:S(2)}) copy-start(bf16[768]{0:T(1024)(128)(2,1)} %param.21) | copy-start | bytes 4612
  25.4 18.2 %copy-start.25 = (bf16[768]{0:T(1024)(128)(2,1)S(1)}, bf16[768]{0:T(1024)(128)(2,1)}, u32[]{:S(2)}) copy-start(bf16[768]{0:T(1024)(128)(2,1)} %param.22) | copy-start | bytes 4612
  25.5 18.4 %copy-start.26 = (bf16[768]{0:T(1024)(128)(2,1)S(1)}, bf16[768]{0:T(1024)(128)(2,1)}, u32[]{:S(2)}) copy-start(bf16[768]{0:T(1024)(128)(2,1)} %param.23) | copy-start | bytes 4612
  25.5 18.6 %copy-start.27 = (bf16[768]{0:T(1024)(128)(2,1)S(1)}, bf16[768]{0:T(1024)(128)(2,1)}, u32[]{:S(2)}) copy-start(bf16[768]{0:T(1024)(128)(2,1)} %param.27) | copy-start | bytes 4612
  25.5 18.8 %copy-start.28 = (bf16[768]{0:T(1024)(128)(2,1)S(1)}, bf16[768]{0:T(1024)(128)(2,1)}, u32[]{:S(2)}) copy-start(bf16[768]{0:T(1024)(128)(2,1)} %param.28) | copy-start | bytes 4612
  25.5 19.0 %copy-start.29 = (bf16[768]{0:T(1024)(128)(2,1)S(1)}, bf16[768]{0:T(1024)(128)(2,1)}, u32[]{:S(2)}) copy-start(bf16[768]{0:T(1024)(128)(2,1)} %param.29) | copy-start | bytes 4612
  25.5 19.3 %copy-start.6 = (s32[2]{0:T(128)S(1)}, s32[2]{0:T(128)}, u32[]{:S(2)}) copy-start(s32[2]{0:T(128)} %lengths_ref.25) | copy-start | bytes 28
  27.2 14.6 %collective-permute-start.7 = (bf16[192,768]{1,0:T(8,128)(2,1)S(1)}, bf16[192,768]{1,0:T(8,128)(2,1)S(1)}, u32[]{:S(2)}, u32[]{:S(2)}) collective-permute-start(bf16[192,768]{1,0:T(8,128)(2,1)S(1)} %collective-permute-done.2), channel_id=1, source_target_pairs={{0,4},{4,0},{8,12},{12,8},{16,20},{20,16},{24,28},{28,24},{1,5},{5... | collective-permute-start | bytes 884744 | tf_op jit(solution)/shard_map/ppermute | solution.py:624
  28.9 12.9 %collective-permute-start.8 = (bf16[192,768]{1,0:T(8,128)(2,1)S(1)}, bf16[192,768]{1,0:T(8,128)(2,1)S(1)}, u32[]{:S(2)}, u32[]{:S(2)}) collective-permute-start(bf16[192,768]{1,0:T(8,128)(2,1)S(1)} %collective-permute-done.3), channel_id=1, source_target_pairs={{0,8},{4,12},{8,0},{12,4},{16,24},{20,28},{24,16},{28,20},{1,9},{5... | collective-permute-start | bytes 884744 | tf_op jit(solution)/shard_map/ppermute | solution.py:624
  30.5 1.9 collective-permute-start.4
  30.5 7.9 %collective-permute-start.5 = (bf16[2,192,256]{2,1,0:T(8,128)(2,1)}, bf16[2,192,256]{2,1,0:T(8,128)(2,1)S(1)}, u32[]{:S(2)}, u32[]{:S(2)}) collective-permute-start(bf16[2,192,256]{2,1,0:T(8,128)(2,1)} %get-tuple-element.142), channel_id=1, source_target_pairs={{0,2},{1,3},{2,0},{3,1},{4,6},{5,7},{6,4},{7,5},{8,10},{9,11},{10,... | collective-permute-start | bytes 589832 | tf_op jit(solution)/shard_map/ppermute | solution.py:624
  32.0 9.8 %collective-permute-start.6 = (bf16[2,192,256]{2,1,0:T(8,128)(2,1)}, bf16[2,192,256]{2,1,0:T(8,128)(2,1)S(1)}, u32[]{:S(2)}, u32[]{:S(2)}) collective-permute-start(bf16[2,192,256]{2,1,0:T(8,128)(2,1)} %get-tuple-element.143), channel_id=1, source_target_pairs={{0,3},{1,2},{2,1},{3,0},{4,7},{5,6},{6,5},{7,4},{8,11},{9,10},{10,... | collective-permute-start | bytes 589832 | tf_op jit(solution)/shard_map/ppermute | solution.py:624
  38.4 3.5 %copy-start = (bf16[2,192,256]{2,1,0:T(8,128)(2,1)}, bf16[2,192,256]{2,1,0:T(8,128)(2,1)S(1)}, u32[]{:S(2)}) copy-start(bf16[2,192,256]{2,1,0:T(8,128)(2,1)S(1)} %collective-permute-done.5.refs_4_.refs_9_) | copy-start | bytes 589828
  42.5 2.2 %collective-permute-start.9 = (bf16[200,768]{1,0:T(8,128)(2,1)S(1)}, bf16[200,768]{1,0:T(8,128)(2,1)S(1)}, u32[]{:S(2)}, u32[]{:S(2)}) collective-permute-start(bf16[200,768]{1,0:T(8,128)(2,1)S(1)} %collective-permute-done.1.refs_8_.refs_4_.refs_13_), channel_id=1, source_target_pairs={{0,1},{1,0},{2,3},{3,2},{4,5},{5,4},{6,7},{7,6},{8,9},{9,8},{10,11... | collective-permute-start | bytes 921608 | tf_op jit(solution)/shard_map/ppermute | solution.py:624
  42.7 18.8 %collective-permute-start.12 = (bf16[384,768]{1,0:T(8,128)(2,1)S(1)}, bf16[384,768]{1,0:T(8,128)(2,1)S(1)}, u32[]{:S(2)}, u32[]{:S(2)}) collective-permute-start(bf16[384,768]{1,0:T(8,128)(2,1)S(1)} %get-tuple-element.158.refs_5_.refs_6_), channel_id=1, source_target_pairs={{0,8},{4,12},{8,0},{12,4},{16,24},{20,28},{24,16},{28,20},{1,9},{5... | collective-permute-start | bytes 1769480 | tf_op jit(solution)/shard_map/ppermute | solution.py:624
  43.2 18.4 %collective-permute-start.13 = (bf16[384,768]{1,0:T(8,128)(2,1)S(1)}, bf16[384,768]{1,0:T(8,128)(2,1)S(1)}, u32[]{:S(2)}, u32[]{:S(2)}) collective-permute-start(bf16[384,768]{1,0:T(8,128)(2,1)S(1)} %get-tuple-element.159.refs_7_.refs_8_), channel_id=1, source_target_pairs={{0,4},{4,0},{8,12},{12,8},{16,20},{20,16},{24,28},{28,24},{1,5},{5... | collective-permute-start | bytes 1769480 | tf_op jit(solution)/shard_map/ppermute | solution.py:624
  50.8 1.8 collective-permute-start.10
  50.9 2.3 %collective-permute-start.11 = (bf16[256,768]{1,0:T(8,128)(2,1)S(1)}, bf16[256,768]{1,0:T(8,128)(2,1)S(1)}, u32[]{:S(2)}, u32[]{:S(2)}) collective-permute-start(bf16[256,768]{1,0:T(8,128)(2,1)S(1)} %get-tuple-element.157.refs_1_), channel_id=1, source_target_pairs={{0,1},{1,0},{2,3},{3,2},{4,5},{5,4},{6,7},{7,6},{8,9},{9,8},{10,11... | collective-permute-start | bytes 1179656 | tf_op jit(solution)/shard_map/ppermute | solution.py:624
  69.2 2.4 %collective-permute-start.14 = (bf16[512,768]{1,0:T(8,128)(2,1)S(1)}, bf16[512,768]{1,0:T(8,128)(2,1)S(1)}, u32[]{:S(2)}, u32[]{:S(2)}) collective-permute-start(bf16[512,768]{1,0:T(8,128)(2,1)S(1)} %get-tuple-element.163), channel_id=1, source_target_pairs={{0,1},{1,0},{2,3},{3,2},{4,5},{5,4},{6,7},{7,6},{8,9},{9,8},{10,11... | collective-permute-start | bytes 2359304 | tf_op jit(solution)/shard_map/ppermute | solution.py:624
  75.7 2.4 %collective-permute-start.15 = (bf16[512,768]{1,0:T(8,128)(2,1)S(1)}, bf16[512,768]{1,0:T(8,128)(2,1)S(1)}, u32[]{:S(2)}, u32[]{:S(2)}) collective-permute-start(bf16[512,768]{1,0:T(8,128)(2,1)S(1)} %get-tuple-element.171.refs_0_.refs_2_), channel_id=1, source_target_pairs={{0,1},{1,0},{2,3},{3,2},{4,5},{5,4},{6,7},{7,6},{8,9},{9,8},{10,11... | collective-permute-start | bytes 2359304 | tf_op jit(solution)/shard_map/ppermute | solution.py:624
  78.0 12.3 %copy-start.2 = (bf16[2,192,256]{2,1,0:T(8,128)(2,1)S(1)}, bf16[2,192,256]{2,1,0:T(8,128)(2,1)}, u32[]{:S(2)}) copy-start(bf16[2,192,256]{2,1,0:T(8,128)(2,1)} %copy-done) | copy-start | bytes 589828
  78.0 12.3 %copy-start.5 = (bf16[2,192,256]{2,1,0:T(8,128)(2,1)S(1)}, bf16[2,192,256]{2,1,0:T(8,128)(2,1)}, u32[]{:S(2)}) copy-start(bf16[2,192,256]{2,1,0:T(8,128)(2,1)} %copy-done.3) | copy-start | bytes 589828
  88.0 2.4 %collective-permute-start.16 = (bf16[512,768]{1,0:T(8,128)(2,1)S(1)}, bf16[512,768]{1,0:T(8,128)(2,1)S(1)}, u32[]{:S(2)}, u32[]{:S(2)}) collective-permute-start(bf16[512,768]{1,0:T(8,128)(2,1)S(1)} %get-tuple-element.175), channel_id=1, source_target_pairs={{0,1},{1,0},{2,3},{3,2},{4,5},{5,4},{6,7},{7,6},{8,9},{9,8},{10,11... | collective-permute-start | bytes 2359304 | tf_op jit(solution)/shard_map/ppermute | solution.py:624
  97.4 9.3 %collective-permute-start.20 = (bf16[2,200,768]{2,1,0:T(8,128)(2,1)}, bf16[2,200,768]{2,1,0:T(8,128)(2,1)S(1)}, u32[]{:S(2)}, u32[]{:S(2)}) collective-permute-start(bf16[2,200,768]{2,1,0:T(8,128)(2,1)} %get-tuple-element.184), channel_id=1, source_target_pairs={{0,1},{1,0},{2,3},{3,2},{4,5},{5,4},{6,7},{7,6},{8,9},{9,8},{10,11... | collective-permute-start | bytes 1843208 | tf_op jit(solution)/shard_map/ppermute | solution.py:624
  97.6 14.8 %collective-permute-start.17 = (bf16[2,192,256]{2,1,0:T(8,128)(2,1)}, bf16[2,192,256]{2,1,0:T(8,128)(2,1)S(1)}, u32[]{:S(2)}, u32[]{:S(2)}) collective-permute-start(bf16[2,192,256]{2,1,0:T(8,128)(2,1)} %get-tuple-element.179), channel_id=1, source_target_pairs={{0,1},{1,0},{2,3},{3,2},{4,5},{5,4},{6,7},{7,6},{8,9},{9,8},{10,11... | collective-permute-start | bytes 589832 | tf_op jit(solution)/shard_map/ppermute | solution.py:624
  98.0 14.5 %collective-permute-start.18 = (bf16[2,192,256]{2,1,0:T(8,128)(2,1)}, bf16[2,192,256]{2,1,0:T(8,128)(2,1)S(1)}, u32[]{:S(2)}, u32[]{:S(2)}) collective-permute-start(bf16[2,192,256]{2,1,0:T(8,128)(2,1)} %get-tuple-element.180), channel_id=1, source_target_pairs={{0,2},{1,3},{2,0},{3,1},{4,6},{5,7},{6,4},{7,5},{8,10},{9,11},{10,... | collective-permute-start | bytes 589832 | tf_op jit(solution)/shard_map/ppermute | solution.py:624
  99.8 12.8 %collective-permute-start.19 = (bf16[2,192,256]{2,1,0:T(8,128)(2,1)}, bf16[2,192,256]{2,1,0:T(8,128)(2,1)S(1)}, u32[]{:S(2)}, u32[]{:S(2)}) collective-permute-start(bf16[2,192,256]{2,1,0:T(8,128)(2,1)} %get-tuple-element.181), channel_id=1, source_target_pairs={{0,3},{1,2},{2,1},{3,0},{4,7},{5,6},{6,5},{7,4},{8,11},{9,10},{10,... | collective-permute-start | bytes 589832 | tf_op jit(solution)/shard_map/ppermute | solution.py:624
  105.1 28.6 %collective-permute-start.22 = (bf16[2,4,96,768]{3,2,1,0:T(8,128)(2,1)}, bf16[2,4,96,768]{3,2,1,0:T(8,128)(2,1)S(1)}, u32[]{:S(2)}, u32[]{:S(2)}) collective-permute-start(bf16[2,4,96,768]{3,2,1,0:T(8,128)(2,1)} %get-tuple-element.202), channel_id=1, source_target_pairs={{0,4},{4,0},{8,12},{12,8},{16,20},{20,16},{24,28},{28,24},{1,5},{5... | collective-permute-start | bytes 3538952 | tf_op jit(solution)/shard_map/ppermute | solution.py:624
  112.5 21.2 %collective-permute-start.21 = (bf16[496,768]{1,0:T(8,128)(2,1)}, bf16[496,768]{1,0:T(8,128)(2,1)S(1)}, u32[]{:S(2)}, u32[]{:S(2)}) collective-permute-start(bf16[496,768]{1,0:T(8,128)(2,1)} %get-tuple-element.199), channel_id=1, source_target_pairs={{0,8},{4,12},{8,0},{12,4},{16,24},{20,28},{24,16},{28,20},{1,9},{5... | collective-permute-start | bytes 2285576 | tf_op jit(solution)/shard_map/ppermute | solution.py:624
  128.1 5.7 %copy-start.11 = (bf16[480,768]{1,0:T(8,128)(2,1)S(1)}, bf16[480,768]{1,0:T(8,128)(2,1)}, u32[]{:S(2)}) copy-start(bf16[480,768]{1,0:T(8,128)(2,1)} %get-tuple-element.206) | copy-start | bytes 2211844
  133.7 2.6 %collective-permute-start.23 = (bf16[2,256,768]{2,1,0:T(8,128)(2,1)}, bf16[2,256,768]{2,1,0:T(8,128)(2,1)}, u32[]{:S(2)}, u32[]{:S(2)}) collective-permute-start(bf16[2,256,768]{2,1,0:T(8,128)(2,1)} %get-tuple-element.203), channel_id=1, source_target_pairs={{0,1},{1,0},{2,3},{3,2},{4,5},{5,4},{6,7},{7,6},{8,9},{9,8},{10,11... | collective-permute-start | bytes 2359304 | tf_op jit(solution)/shard_map/ppermute | solution.py:624
  134.0 2.3 %copy-start.8 = (bf16[2,256,768]{2,1,0:T(8,128)(2,1)S(1)}, bf16[2,256,768]{2,1,0:T(8,128)(2,1)}, u32[]{:S(2)}) copy-start(bf16[2,256,768]{2,1,0:T(8,128)(2,1)} %get-tuple-element.197) | copy-start | bytes 2359300
  138.2 25.6 %copy-start.12 = (bf16[480,768]{1,0:T(8,128)(2,1)S(1)}, bf16[480,768]{1,0:T(8,128)(2,1)}, u32[]{:S(2)}) copy-start(bf16[480,768]{1,0:T(8,128)(2,1)} %get-tuple-element.229) | copy-start | bytes 2211844
  138.2 26.4 %copy-start.17 = (bf16[4,96,768]{2,1,0:T(8,128)(2,1)S(1)}, bf16[4,96,768]{2,1,0:T(8,128)(2,1)}, u32[]{:S(2)}) copy-start(bf16[4,96,768]{2,1,0:T(8,128)(2,1)} %get-tuple-element.226) | copy-start | bytes 1769476
  138.2 21.3 %collective-permute-start.26 = (bf16[256,768]{1,0:T(8,128)(2,1)}, bf16[256,768]{1,0:T(8,128)(2,1)S(1)}, u32[]{:S(2)}, u32[]{:S(2)}) collective-permute-start(bf16[256,768]{1,0:T(8,128)(2,1)} %pad_maximum_fusion.3), channel_id=1, source_target_pairs={{0,4},{4,0},{8,12},{12,8},{16,20},{20,16},{24,28},{28,24},{1,5},{5... | collective-permute-start | bytes 1179656 | tf_op jit(solution)/shard_map/ppermute | solution.py:624
  139.9 19.7 %collective-permute-start.27 = (bf16[256,768]{1,0:T(8,128)(2,1)}, bf16[256,768]{1,0:T(8,128)(2,1)}, u32[]{:S(2)}, u32[]{:S(2)}) collective-permute-start(bf16[256,768]{1,0:T(8,128)(2,1)} %fusion.6), channel_id=1, source_target_pairs={{0,2},{1,3},{2,0},{3,1},{4,6},{5,7},{6,4},{7,5},{8,10},{9,11},{10,... | collective-permute-start | bytes 1179656 | tf_op jit(solution)/shard_map/ppermute | solution.py:624
  141.4 22.2 %collective-permute-start.24 = (bf16[4,96,768]{2,1,0:T(8,128)(2,1)}, bf16[4,96,768]{2,1,0:T(8,128)(2,1)S(1)}, u32[]{:S(2)}, u32[]{:S(2)}) collective-permute-start(bf16[4,96,768]{2,1,0:T(8,128)(2,1)} %fusion), channel_id=1, source_target_pairs={{0,2},{1,3},{2,0},{3,1},{4,6},{5,7},{6,4},{7,5},{8,10},{9,11},{10,... | collective-permute-start | bytes 1769480 | tf_op jit(solution)/shard_map/ppermute | solution.py:624
  141.9 21.7 %collective-permute-start.25 = (bf16[480,768]{1,0:T(8,128)(2,1)}, bf16[480,768]{1,0:T(8,128)(2,1)S(1)}, u32[]{:S(2)}, u32[]{:S(2)}) collective-permute-start(bf16[480,768]{1,0:T(8,128)(2,1)} %get-tuple-element.217), channel_id=1, source_target_pairs={{0,8},{4,12},{8,0},{12,4},{16,24},{20,28},{24,16},{28,20},{1,9},{5... | collective-permute-start | bytes 2211848 | tf_op jit(solution)/shard_map/ppermute | solution.py:624
  159.5 4.1 %copy-start.22 = (bf16[256,768]{1,0:T(8,128)(2,1)}, bf16[256,768]{1,0:T(8,128)(2,1)S(1)}, u32[]{:S(2)}) copy-start(bf16[256,768]{1,0:T(8,128)(2,1)S(1)} %collective-permute-done.26) | copy-start | bytes 1179652
  163.6 2.0 copy-start.19
  163.6 1.9 copy-start.14
  163.7 15.9 %collective-permute-start.28 = (bf16[2,256,768]{2,1,0:T(8,128)(2,1)}, bf16[2,256,768]{2,1,0:T(8,128)(2,1)S(1)}, u32[]{:S(2)}, u32[]{:S(2)}) collective-permute-start(bf16[2,256,768]{2,1,0:T(8,128)(2,1)} %get-tuple-element.223), channel_id=1, source_target_pairs={{0,1},{1,0},{2,3},{3,2},{4,5},{5,4},{6,7},{7,6},{8,9},{9,8},{10,11... | collective-permute-start | bytes 2359304 | tf_op jit(solution)/shard_map/ppermute | solution.py:624
  166.4 12.4 %collective-permute-start.30 = (bf16[256,768]{1,0:T(8,128)(2,1)}, bf16[256,768]{1,0:T(8,128)(2,1)}, u32[]{:S(2)}, u32[]{:S(2)}) collective-permute-start(bf16[256,768]{1,0:T(8,128)(2,1)} %pad_maximum_fusion.4), channel_id=1, source_target_pairs={{0,2},{1,3},{2,0},{3,1},{4,6},{5,7},{6,4},{7,5},{8,10},{9,11},{10,... | collective-permute-start | bytes 1179656 | tf_op jit(solution)/shard_map/ppermute | solution.py:624
  167.9 10.9 %collective-permute-start.31 = (bf16[2,120,768]{2,1,0:T(8,128)(2,1)}, bf16[2,120,768]{2,1,0:T(8,128)(2,1)S(1)}, u32[]{:S(2)}, u32[]{:S(2)}) collective-permute-start(bf16[2,120,768]{2,1,0:T(8,128)(2,1)} %fusion.10), channel_id=1, source_target_pairs={{0,4},{4,0},{8,12},{12,8},{16,20},{20,16},{24,28},{28,24},{1,5},{5... | collective-permute-start | bytes 1105928 | tf_op jit(solution)/shard_map/ppermute | solution.py:624
  168.4 9.6 %collective-permute-start.29 = (bf16[2,96,768]{2,1,0:T(8,128)(2,1)}, bf16[2,96,768]{2,1,0:T(8,128)(2,1)}, u32[]{:S(2)}, u32[]{:S(2)}) collective-permute-start(bf16[2,96,768]{2,1,0:T(8,128)(2,1)} %fusion.13), channel_id=1, source_target_pairs={{0,8},{4,12},{8,0},{12,4},{16,24},{20,28},{24,16},{28,20},{1,9},{5... | collective-permute-start | bytes 884744 | tf_op jit(solution)/shard_map/ppermute | solution.py:624
  170.0 9.6 %copy-start.9 = (bf16[2,256,768]{2,1,0:T(8,128)(2,1)S(1)}, bf16[2,256,768]{2,1,0:T(8,128)(2,1)}, u32[]{:S(2)}) copy-start(bf16[2,256,768]{2,1,0:T(8,128)(2,1)} %get-tuple-element.222) | copy-start | bytes 2359300
  178.0 3.5 %copy-start.18 = (bf16[4,96,768]{2,1,0:T(8,128)(2,1)S(1)}, bf16[4,96,768]{2,1,0:T(8,128)(2,1)}, u32[]{:S(2)}) copy-start(bf16[4,96,768]{2,1,0:T(8,128)(2,1)} %get-tuple-element.226) | copy-start | bytes 1769476
  178.0 3.5 %copy-start.20 = (bf16[4,96,768]{2,1,0:T(8,128)(2,1)S(1)}, bf16[4,96,768]{2,1,0:T(8,128)(2,1)}, u32[]{:S(2)}) copy-start(bf16[4,96,768]{2,1,0:T(8,128)(2,1)} %copy-done.19) | copy-start | bytes 1769476
  178.8 11.9 %collective-permute-start.32 = (bf16[584,384]{1,0:T(8,128)(2,1)}, bf16[584,384]{1,0:T(8,128)(2,1)S(1)}, u32[]{:S(2)}, u32[]{:S(2)}) collective-permute-start(bf16[584,384]{1,0:T(8,128)(2,1)} %get-tuple-element.238), channel_id=1, source_target_pairs={{0,4},{4,0},{8,12},{12,8},{16,20},{20,16},{24,28},{28,24},{1,5},{5... | collective-permute-start | bytes 1345544 | tf_op jit(solution)/shard_map/ppermute | solution.py:624
  179.6 24.8 %copy-start.10 = (bf16[2,256,768]{2,1,0:T(8,128)(2,1)}, bf16[2,256,768]{2,1,0:T(8,128)(2,1)S(1)}, u32[]{:S(2)}) copy-start(bf16[2,256,768]{2,1,0:T(8,128)(2,1)S(1)} %collective-permute-done.28) | copy-start | bytes 2359300
  179.6 11.1 %copy-start.30 = (f32[1,384]{1,0:T(1,128)S(1)}, f32[1,384]{1,0:T(1,128)}, u32[]{:S(2)}) copy-start(f32[1,384]{1,0:T(1,128)} %get-tuple-element.246) | copy-start | bytes 4612
  179.6 11.2 %copy-start.21 = (bf16[576,384]{1,0:T(8,128)(2,1)S(1)}, bf16[576,384]{1,0:T(8,128)(2,1)}, u32[]{:S(2)}) copy-start(bf16[576,384]{1,0:T(8,128)(2,1)} %get-tuple-element.244) | copy-start | bytes 1327108
  181.5 11.0 %copy-start.13 = (bf16[480,768]{1,0:T(8,128)(2,1)S(1)}, bf16[480,768]{1,0:T(8,128)(2,1)}, u32[]{:S(2)}) copy-start(bf16[480,768]{1,0:T(8,128)(2,1)} %get-tuple-element.229) | copy-start | bytes 2211844
  181.5 11.0 %copy-start.15 = (bf16[480,768]{1,0:T(8,128)(2,1)S(1)}, bf16[480,768]{1,0:T(8,128)(2,1)}, u32[]{:S(2)}) copy-start(bf16[480,768]{1,0:T(8,128)(2,1)} %copy-done.14) | copy-start | bytes 2211844
  182.6 18.9 %collective-permute-start.36 = (bf16[96,768]{1,0:T(8,128)(2,1)S(1)}, bf16[96,768]{1,0:T(8,128)(2,1)S(1)}, u32[]{:S(2)}, u32[]{:S(2)}) collective-permute-start(bf16[96,768]{1,0:T(8,128)(2,1)S(1)} %fusion.15), channel_id=1, source_target_pairs={{0,16},{4,20},{8,24},{12,28},{16,0},{20,4},{24,8},{28,12},{1,17},{... | collective-permute-start | bytes 442376 | tf_op jit(solution)/shard_map/ppermute | solution.py:624
  190.9 10.5 %collective-permute-start.34 = (bf16[290,384]{1,0:T(8,128)(2,1)S(1)}, bf16[290,384]{1,0:T(8,128)(2,1)S(1)}, u32[]{:S(2)}, u32[]{:S(2)}) collective-permute-start(bf16[290,384]{1,0:T(8,128)(2,1)S(1)} %pad_maximum_fusion.6), channel_id=1, source_target_pairs={{0,8},{4,12},{8,0},{12,4},{16,24},{20,28},{24,16},{28,20},{1,9},{5... | collective-permute-start | bytes 668168 | tf_op jit(solution)/shard_map/ppermute | solution.py:624
  192.7 10.9 %collective-permute-start.37 = (bf16[136,768]{1,0:T(8,128)(2,1)S(1)}, bf16[136,768]{1,0:T(8,128)(2,1)S(1)}, u32[]{:S(2)}, u32[]{:S(2)}) collective-permute-start(bf16[136,768]{1,0:T(8,128)(2,1)S(1)} %pad_maximum_fusion.7), channel_id=1, source_target_pairs={{0,16},{4,20},{8,24},{12,28},{16,0},{20,4},{24,8},{28,12},{1,17},{... | collective-permute-start | bytes 626696 | tf_op jit(solution)/shard_map/ppermute | solution.py:624
  195.3 18.2 %collective-permute-start.33 = (bf16[256,768]{1,0:T(8,128)(2,1)}, bf16[256,768]{1,0:T(8,128)(2,1)}, u32[]{:S(2)}, u32[]{:S(2)}) collective-permute-start(bf16[256,768]{1,0:T(8,128)(2,1)} %fusion.7), channel_id=1, source_target_pairs={{0,2},{1,3},{2,0},{3,1},{4,6},{5,7},{6,4},{7,5},{8,10},{9,11},{10,... | collective-permute-start | bytes 1179656 | tf_op jit(solution)/shard_map/ppermute | solution.py:624
  205.1 8.5 %copy-start.7 = (f32[512,768]{1,0:T(8,128)S(1)}, f32[512,768]{1,0:T(8,128)}, u32[]{:S(2)}) copy-start(f32[512,768]{1,0:T(8,128)} %get-tuple-element.221) | copy-start | bytes 4718596
  205.1 6.9 %collective-permute-start.35 = (bf16[146,384]{1,0:T(8,128)(2,1)S(1)}, bf16[146,384]{1,0:T(8,128)(2,1)S(1)}, u32[]{:S(2)}, u32[]{:S(2)}) collective-permute-start(bf16[146,384]{1,0:T(8,128)(2,1)S(1)} %pad_maximum_fusion.8), channel_id=1, source_target_pairs={{0,16},{4,20},{8,24},{12,28},{16,0},{20,4},{24,8},{28,12},{1,17},{... | collective-permute-start | bytes 336392 | tf_op jit(solution)/shard_map/ppermute | solution.py:624
  (8 other events, 10.5 us)

commit v5 on v4

--- a/solution.py
+++ b/solution.py
@@ -380,10 +380,7 @@
 
 
 def gelu_parts(h):
-    den = 1.0 + (0.3275911 * 0.7071067811865476) * jnp.abs(h)
-    t = pl.reciprocal(den, approx=True)
-    t = t * (2.0 - den * t)
-    t = t * (2.0 - den * t)
+    t = 1.0 / (1.0 + (0.3275911 * 0.7071067811865476) * jnp.abs(h))
     poly = t * (0.127414796 + t * (-0.142248368 + t * (0.7107068705 + t * (-0.7265760135 + t * 0.5307027145))))
     bell = jnp.exp2((-0.5 * 1.4426950408889634) * (h * h))
     tail = poly * bell
@@ -402,11 +399,16 @@
     return r * (gu - jnp.mean(gu, axis=1, keepdims=True) - nv * jnp.mean(gu * nv, axis=1, keepdims=True))
 
 
+def rows_of(vectors):
+    return jnp.concatenate([v[...].reshape(1, -1).astype(f32) for v in vectors], axis=0)
+
+
 def rowsum(v):
     return jnp.sum(v, axis=0, keepdims=True)
 
 
-def first_norm_kernel(info, x_in, par, *rest):
+def first_norm_kernel(info, x_in, *rest):
+    par, rest = rows_of(rest[:6]), rest[6:]
     nv_ref, r_ref, low0, low1, low = rest[8:]
     cs, packs = [c() for c in rest[:4]], [p() for p in rest[4:8]]
     x_ref = x_in()
@@ -469,7 +471,8 @@
         sib[...] = mm(act[1], dn[...])
 
 
-def second_norm_kernel(info, cot_in, par, nv_in, own, got, outs, gsec_out, gs_low, small):
+def second_norm_kernel(info, cot_in, *rest):
+    par, (nv_in, own, got, outs, gsec_out, gs_low, small) = rows_of(rest[:6]), rest[6:]
     cot, nv_ref, gsec = cot_in(), ref(nv_in), ref(gsec_out)
     batch, rows, d = cot.shape
 
@@ -522,7 +525,8 @@
     own[...] = mm(gh[0, 0], up[...], NT) + mm(gh[1, 0], up2[...], NT)
 
 
-def first_back_kernel(info, par, nv_in, r_ref, own, got, gsec_in, small2, *rest):
+def first_back_kernel(info, *rest):
+    par, (nv_in, r_ref, own, got, gsec_in, small2, *rest) = rows_of(rest[:6]), rest[6:]
     cs, packs = [c() for c in rest[:4]], rest[4:8]
     gfi, g0, g1, g2, g3, okeep, osend, small, ga_low = rest[8:]
     nv_ref, gsec = ref(nv_in), ref(gsec_in)
@@ -675,8 +679,7 @@
     dp = lax.axis_index("dp")
     bit_of = [(dp >> i) & 1 for i in range(bits)]
     info = lengths
-    par = jnp.concatenate([out_bias, first_gain, first_shift, down_bias, second_gain, second_shift])
-    par = par.reshape(6, d).astype(f32)
+    par = [out_bias, first_gain, first_shift, down_bias, second_gain, second_shift]
     w_t = jnp.transpose(qkv_weight, (1, 2, 0))
     pack, u_part, d_part = prepare(info, out_weight, up_bias, up_weight, down_weight)
     pack2 = swap(pack, "tensor", 2)
@@ -703,7 +706,7 @@
         "first_norm",
         first_norm_kernel,
         info,
-        [share, par, *far_ctx, *far_packs],
+        [share, *par, *far_ctx, *far_packs],
         [SDS((n, d), f32), SDS((n, 1), f32), SDS((rows, d), bf16), SDS((rows, d), bf16)],
         [pltpu.VMEM((batch, rows, d), bf16)],
         vmem=NEAR,
@@ -741,7 +744,7 @@
         "second_norm",
         second_norm_kernel,
         info,
-        [whole(cotangent), par, nv1, own, got],
+        [whole(cotangent), *par, nv1, own, got],
         [[SDS((batch, rows, d), bf16)], part, SDS((n, d), bf16), SDS((8, d), f32)],
         vmem=NEAR,
     )
@@ -773,7 +776,7 @@
         "first_back",
         first_back_kernel,
         info,
-        [par, nv1, r1, own, got, gsec, small2, *far_ctx, *far_packs],
+        [*par, nv1, r1, own, got, gsec, small2, *far_ctx, *far_packs],
         [
             [part],
             *[[SDS((batch, width, rows), bf16)]] * 4,
@@ -807,18 +810,17 @@
     *gctx, up_far_send = after(*gctx, up_far_send)
     up_far_got = swap(up_far_send, "dp", 2)
     *gctx, up_far_keep = after(*gctx, up_far_keep)
-    lows, biases, terms_of = [], [], []
+    lows, biases, keeps = [], [], []
     for s in range(batch):
         keep, send, low_grads, db = attend_bwd(s, info, w_t, *saved, gctx, d)
         biases.append(db)
         if s == 0:
             send, up_far_got, down_got = after(send, up_far_got, down_got)
         else:
-            send, low_grads, down_y, up_got, up_more, far = after(send, low_grads, down_y, up_got, up_more, far)
-            terms_of[0].append(far)
+            send, low_grads, down_y, up_got, up_more, near = after(send, low_grads, down_y, up_got, up_more, near)
+            keeps.append(near)
+        keeps.append(keep)
         near = swap(send, "tensor", 1)
-        in_sum = summed([keep[1], near[1]]).astype(bf16)
-        terms_of.append([keep[0], near[0]])
         if s == 0:
             lows.append(low_grads)
             down_sum = summed([down_far_keep, down_got[0]]).astype(bf16)
@@ -827,12 +829,12 @@
             terms = [x.reshape(shape) for x in (up_far_keep, up_far_got[:cut])]
             up_far_kept, up_far_next = halve_sum(terms, bits - 2, bit_of[0])
             up_far_rows = with_rows(up_far_next, small)
-            tied = after(down_sum, up_far_rows, in_sum, up_send, *gctx)
-            (down_sum, up_far_rows, in_sum, up_send), gctx = tied[:4], tied[4:]
+            tied = after(down_sum, up_far_rows, up_send, *gctx)
+            (down_sum, up_far_rows, up_send), gctx = tied[:3], tied[3:]
             down_y = swap(down_sum, "tensor", 2)
             up_got = swap(up_send, "dp", 2)
             up_more = swap(up_far_rows, "dp", 1)
-            far = swap(in_sum, "tensor", 2)
+    keeps.append(near)
     shape = ([2] * (bits - 1)) + [block, d]
     down_terms = [x.reshape(shape) for x in (down_keep, down_got[1], down_y)]
     down_kept, down_next = halve_sum(down_terms, bits - 2, bit_of[1])
@@ -862,10 +864,12 @@
         parts=parts,
     )
     w_send, down_more, up_y, up_more = after(w_send, down_more, up_y, up_more)
-    down_more, up_y, up_more, in_sum = after(down_more, up_y, up_more, in_sum)
+    keep0, near0, keep1, near1 = keeps
+    in_sums = [summed([k[1], x[1]]).astype(bf16) for k, x in ((keep0, near0), (keep1, near1))]
+    down_more, up_y, up_more, *in_sums = after(down_more, up_y, up_more, *in_sums)
     got = swap(w_send, "dp", 1)
-    got, in_sum = after(got, in_sum)
-    terms_of[1].append(swap(in_sum, "tensor", 2))
+    got, *in_sums = after(got, *in_sums)
+    far = [swap(x, "tensor", 2) for x in in_sums]
     down_terms = down_kept + [down_more]
     at = up_y_next.size // d
     small = jnp.concatenate([small[0:6], small[7:8], small[7:8]]) + pair_sum(up_y, at, 8)
@@ -883,10 +887,6 @@
     shape = ([2] * (bits - 1)) + [row, 2 * width]
     terms = [x.reshape(shape) for x in (w_keep, got[:at])]
     db = db + got[at : at + 1].astype(f32) + got[at + 1 : at + 2].astype(f32)
-    input_grad = jnp.stack([
-        (summed(x) + gfi[s * rows : (s + 1) * rows]).astype(bf16)
-        for s, x in enumerate(terms_of)
-    ])
     for i in range(1, bits):
         kept, rows_sent, more = halve_with(terms, terms[0].ndim - 3, db, "dp", 1 << i, bit_of[i])
         if i == bits - 1:
@@ -896,6 +896,10 @@
     down_sum = summed(down_terms)
     up_sum = summed(up_terms)
     mine = small
+    input_grad = jnp.stack([
+        (summed([k[0], x[0], y]) + gfi[s * rows : (s + 1) * rows]).astype(bf16)
+        for s, (k, x, y) in enumerate(((keep0, near0, far[0]), (keep1, near1, far[1])))
+    ])
     qkv_sum = summed(terms)
     qkv_sum = jnp.concatenate([qkv_sum[:, :width], qkv_sum[:, width:]], axis=0).reshape(3, -1, width)
     qkv_sum = jnp.transpose(qkv_sum, (1, 0, 2))

time: 217 us -> 221 us (1.018)
  local copies, waits for them, and re-layouts: 7.79 us -> 11.6 us
  starting transfers between devices: 36.2 us -> 32.8 us
  other arithmetic: 15.1 us -> 18.2 us
  Pallas kernels: 110 us -> 107 us
  waiting for transfers between devices: 45.9 us -> 48.6 us
    unnamed x73 -> x56, local copies, waits for them, and re-layouts: 3.59 us -> 7.57 us
    ppermute x38, starting transfers between devices: 36.2 us -> 32.8 us  [swap(): return lax.ppermute(x, axis, [(i, i ^ bit) for i in range(size)])]
    convert_element_type x4, other arithmetic: 2.88 us -> 5.92 us  [halve_sum(): return (kept, summed(other).astype(bf16))]
    ppermute x38, waiting for transfers between devices: 45.9 us -> 48.6 us  [swap(): return lax.ppermute(x, axis, [(i, i ^ bit) for i in range(size)])]
    pallas_call x13, Pallas kernels: 110 us -> 107 us  [call(): pl.pallas_call(kernel, out_shape=[pltpu.HBM(o.shape, o.dtype) if i in far...]
  transfers between devices with their start and end apart: 38 -> 38, of which waited for: 16 -> 16; matrix products, arithmetic and copies ran while one was open for 7% -> 8% of each run, Pallas kernels for 36% -> 35%
where the time goes in v5:
time: 221 us; the launch traced here: 220 us
  Pallas kernels  107 us (48%)
  waiting for transfers between devices  48.6 us (22%)
  starting transfers between devices  32.8 us (15%)
  other arithmetic  18.2 us (8%)
  local copies, waits for them, and re-layouts  11.6 us (5%)
    pallas_call x13, Pallas kernels, call(): pl.pallas_call(kernel, out_shape=[pltpu.HBM(o.shape, o.dtype) if i in far...  107 us
    ppermute x38, waiting for transfers between devices, swap(): return lax.ppermute(x, axis, [(i, i ^ bit) for i in range(size)])  48.6 us
    ppermute x38, starting transfers between devices, swap(): return lax.ppermute(x, axis, [(i, i ^ bit) for i in range(size)])  32.8 us
    unnamed x56, local copies, waits for them, and re-layouts  7.57 us
    convert_element_type x4, other arithmetic, halve_sum(): return (kept, summed(other).astype(bf16))  5.92 us
  transfers between devices with their start and end apart: 38, of which 16 were waited for; matrix products, arithmetic and copies ran while one was open for 8% of the time, Pallas kernels for 35%

profile of v5, /device:TPU:0, one launch (start us, length us, event | category | flops | bytes accessed | tf_op | source)
XLA Modules:
  0.0 219.9 jit_solution(447808058872411496)
XLA Ops:
  0.6 3.4 %prepare.1 = (bf16[200,768]{1,0:T(8,128)(2,1)}, bf16[192,768]{1,0:T(8,128)(2,1)}, bf16[192,768]{1,0:T(8,128)(2,1)}) custom-call(s32[2]{0:T(128)} %lengths_ref.25, s32[1]{0:T(128)} %constant.384.clone.1.which_ref, bf16[192,768]{1,0:T(8,128)(2,1)} %refs_0_.7, bf16[768]{0:T(1024)(128)(2,1)} %refs_1_.4, bf16[768,768]{1,0:T(8,128)(2,1)} %refs_4_.6, ...), custom_call_target="tpu_custom_call" | custom-call | flops 1000 | bytes 1000 | tf_op jit(solution)/shard_map/prepare/pallas_call | solution.py:117
  4.6 2.6 %collective-permute-start.1 = (bf16[200,768]{1,0:T(8,128)(2,1)}, bf16[200,768]{1,0:T(8,128)(2,1)S(1)}, u32[]{:S(2)}, u32[]{:S(2)}) collective-permute-start(bf16[200,768]{1,0:T(8,128)(2,1)} %get-tuple-element.138.refs_11_.refs_4_.refs_16_), channel_id=1, source_target_pairs={{0,2},{1,3},{2,0},{3,1},{4,6},{5,7},{6,4},{7,5},{8,10},{9,11},{10,... | collective-permute-start | bytes 921608 | tf_op jit(solution)/shard_map/ppermute | solution.py:628
  7.2 1.9 collective-permute-start.3
  9.2 16.3 %attend_fwd.1 = (bf16[2,1024,256]{2,1,0:T(8,128)(2,1)}, bf16[2,1024,256]{2,1,0:T(8,128)(2,1)}, bf16[2,1024,192]{2,1,0:T(8,128)(2,1)}, f32[2,4,8,256]{3,2,1,0:T(8...) custom-call(s32[2]{0:T(128)} %lengths_ref.25, ...), custom_call_target="tpu_custom_call" | custom-call | flops 1000 | bytes 1000 | tf_op jit(solution)/shard_map/attend_fwd/pallas_call | solution.py:117
  25.6 2.3 %collective-permute-done.3 = bf16[192,768]{1,0:T(8,128)(2,1)S(1)} collective-permute-done((bf16[192,768]{1,0:T(8,128)(2,1)}, bf16[192,768]{1,0:T(8,128)(2,1)S(1)}, u32[]{:S(2)}, u32[]{:S(2)}) %collective-permute-start.3) | collective-permute-done | bytes 294944 | tf_op jit(solution)/shard_map/ppermute | solution.py:628
  27.9 1.7 collective-permute-start.7
  29.6 1.6 collective-permute-start.8
  31.2 1.5 collective-permute-start.5
  33.0 6.0 %collective-permute-done.5.refs_9_.refs_14_ = bf16[2,192,256]{2,1,0:T(8,128)(2,1)S(1)} collective-permute-done((bf16[2,192,256]{2,1,0:T(8,128)(2,1)}, bf16[2,192,256]{2,1,0:T(8,128)(2,1)S(1)}, u32[]{:S(2)}, u32[]{:S(2)}) %collective-permute-start.5) | collective-permute-done | bytes 196640 | tf_op jit(solution)/shard_map/ppermute | solution.py:628
  39.1 3.4 %collective-permute-done.6.refs_10_.refs_15_ = bf16[2,192,256]{2,1,0:T(8,128)(2,1)S(1)} collective-permute-done((bf16[2,192,256]{2,1,0:T(8,128)(2,1)}, bf16[2,192,256]{2,1,0:T(8,128)(2,1)S(1)}, u32[]{:S(2)}, u32[]{:S(2)}) %collective-permute-start.6) | collective-permute-done | bytes 196640 | tf_op jit(solution)/shard_map/ppermute | solution.py:628
  44.3 4.2 %first_norm.1 = (f32[512,768]{1,0:T(8,128)S(1)}, f32[512,1]{1,0:T(8,128)S(1)}, bf16[256,768]{1,0:T(8,128)(2,1)S(1)}, bf16[256,768]{1,0:T(8,128)(2,1)S(1)}) custom-call(s32[2]{0:T(128)S(1)} %copy-done.6, s32[1]{0:T(128)} %constant.384.clone.1.which_ref, bf16[2,1024,768]{2,1,0:T(8,128)(2,1)} %refs_2_.11, bf16[768]{0:T(1024)(128)(2,1)S(1)} %copy-done.7, ...), custom_call_target="tpu_custom_call" | custom-call | flops 1000 | bytes 1000 | tf_op jit(solution)/shard_map/first_norm/pallas_call | solution.py:117
  49.1 1.2 collective-permute-done.10.refs_2_
  50.9 7.6 %feed.2 = (bf16[2,512,768]{2,1,0:T(8,128)(2,1)S(1)}, bf16[2,512,768]{2,1,0:T(8,128)(2,1)S(1)}, f32[512,768]{1,0:T(8,128)S(1)}, f32[512,768]{1,0:T(8,128)S(1)}) custom-call(s32[2]{0:T(128)S(1)} %copy-done.6, s32[1]{0:T(128)} %constant.384.clone.1.which_ref, bf16[256,768]{1,0:T(8,128)(2,1)S(1)} %get-tuple-element.157.refs_0_, ...), custom_call_target="tpu_custom_call" | custom-call | flops 1000 | bytes 1000 | tf_op jit(solution)/shard_map/feed/pallas_call | solution.py:117
  58.6 6.9 %feed.3 = (bf16[2,512,768]{2,1,0:T(8,128)(2,1)S(1)}, bf16[2,512,768]{2,1,0:T(8,128)(2,1)S(1)}, f32[512,768]{1,0:T(8,128)S(1)}, bf16[512,768]{1,0:T(8,128)(2,1)S(1)}) custom-call(s32[2]{0:T(128)S(1)} %copy-done.6, s32[1]{0:T(128)} %constant.384.clone.1.which_ref, bf16[256,768]{1,0:T(8,128)(2,1)S(1)} %get-tuple-element.157.refs_0_, ...), custom_call_target="tpu_custom_call" | custom-call | flops 1000 | bytes 1000 | tf_op jit(solution)/shard_map/feed/pallas_call | solution.py:117
  65.5 1.2 copy-done.4
  67.0 2.1 collective-permute-done.14.refs_9_
  69.1 4.0 %second_norm.1 = (bf16[2,256,768]{2,1,0:T(8,128)(2,1)}, f32[512,768]{1,0:T(8,128)S(1)}, bf16[512,768]{1,0:T(8,128)(2,1)S(1)}, f32[8,768]{1,0:T(8,128)S(1)}) custom-call(s32[2]{0:T(128)S(1)} %copy-done.6, s32[1]{0:T(128)} %constant.384.clone.1.which_ref, bf16[2,256,768]{2,1,0:T(8,128)(2,1)} %refs_0_.9, bf16[768]{0:T(1024)(128)(2,1)S(1)} %copy-done.7, ...), custom_call_target="tpu_custom_call" | custom-call | flops 1000 | bytes 1000 | tf_op jit(solution)/shard_map/second_norm/pallas_call | solution.py:117
  73.4 2.1 collective-permute-done.15.refs_1_.refs_3_
  75.5 10.1 %feed_back.1 = (bf16[2,2,512,768]{3,2,1,0:T(8,128)(2,1)S(1)}, f32[512,768]{1,0:T(8,128)S(1)}, bf16[512,768]{1,0:T(8,128)(2,1)S(1)}, f32[8,768]{1,0:T(8,128)S(1)}) custom-call(s32[2]{0:T(128)S(1)} %copy-done.6, s32[1]{0:T(128)} %constant.384.clone.1.which_ref, bf16[512,768]{1,0:T(8,128)(2,1)S(1)} %get-tuple-element.172.refs_0_.refs_2_, ...), custom_call_target="tpu_custom_call" | custom-call | flops 1000 | bytes 1000 | tf_op jit(solution)/shard_map/feed_back/pallas_call | solution.py:117
  85.6 1.6 copy-done
  87.4 2.1 collective-permute-done.16.refs_9_
  89.5 6.9 %first_back.1 = (f32[512,768]{1,0:T(8,128)}, bf16[2,192,256]{2,1,0:T(8,128)(2,1)}, bf16[2,192,256]{2,1,0:T(8,128)(2,1)}, bf16[2,192,256]{2,1,0:T(8,128)(2,1)}, b...) custom-call(s32[2]{0:T(128)S(1)} %copy-done.6, ...), custom_call_target="tpu_custom_call" | custom-call | flops 1000 | bytes 1000 | tf_op jit(solution)/shard_map/first_back/pallas_call | solution.py:117
  97.0 1.5 collective-permute-start.18
  98.5 1.4 copy-done.3
  100.0 1.4 copy-done.5
  101.4 5.4 %down_grads.1 = (bf16[4,96,768]{2,1,0:T(8,128)(2,1)}, bf16[4,96,768]{2,1,0:T(8,128)(2,1)}, bf16[2,4,96,768]{3,2,1,0:T(8,128)(2,1)}) custom-call(s32[2]{0:T(128)S(1)} %copy-done.6, s32[1]{0:T(128)} %constant.384.clone.1.which_ref, bf16[2,512,768]{2,1,0:T(8,128)(2,1)S(1)} %copy-done.3, bf16[2,512,768]{2,1,0:T(8,128)(2,1)S(1)} %copy-done.5, ...), custom_call_target="tpu_custom_call" | custom-call | flops 1000 | bytes 1000 | tf_op jit(solution)/shard_map/down_grads/pallas_call | solution.py:117
  106.8 1.1 collective-permute-start.22
  107.9 6.8 %up_grads.1 = (bf16[480,768]{1,0:T(8,128)(2,1)}, bf16[496,768]{1,0:T(8,128)(2,1)}, bf16[480,768]{1,0:T(8,128)(2,1)}, bf16[480,768]{1,0:T(8,128)(2,1)}, f32[8,768]{1,0:T(8,128)S(1)}) custom-call(s32[2]{0:T(128)S(1)} %copy-done.6, s32[1]{0:T(128)} %constant.384.clone.1.which_ref, bf16[256,768]{1,0:T(8,128)(2,1)S(1)} %get-tuple-element.157.refs_0_, ...), custom_call_target="tpu_custom_call" | custom-call | flops 1000 | bytes 1000 | tf_op jit(solution)/shard_map/up_grads/pallas_call | solution.py:117
  114.7 1.6 collective-permute-start.21
  116.4 14.0 %attend_bwd.2 = (bf16[2,256,768]{2,1,0:T(8,128)(2,1)}, bf16[2,256,768]{2,1,0:T(8,128)(2,1)}, bf16[3,1024,192]{2,1,0:T(8,128)(2,1)}, f32[1,384]{1,0:T(1,128)}) custom-call(s32[2]{0:T(128)} %lengths_ref.25, s32[1]{0:T(128)} %constant.384.clone.1.which_ref, bf16[3,192,768]{2,1,0:T(8,128)(2,1)} %bitcast.109, bf16[2,1024,256]{2,1,0:T(8,128)(2,1)} %get-tuple-element.166.refs_1_, ...), custom_call_target="tpu_custom_call" | custom-call | flops 20000000000 | bytes 1000 | tf_op jit(solution)/shard_map/attend_bwd/pallas_call | solution.py:117
  130.5 5.1 %collective-permute-done.22 = bf16[2,4,96,768]{3,2,1,0:T(8,128)(2,1)S(1)} collective-permute-done((bf16[2,4,96,768]{3,2,1,0:T(8,128)(2,1)}, bf16[2,4,96,768]{3,2,1,0:T(8,128)(2,1)S(1)}, u32[]{:S(2)}, u32[]{:S(2)}) %collective-permute-start.22) | collective-permute-done | bytes 1179680 | tf_op jit(solution)/shard_map/ppermute | solution.py:628
  135.8 0.9 copy-done.18
  136.9 0.8 pad_maximum_fusion.3
  137.7 1.6 collective-permute-start.24
  139.3 1.5 collective-permute-start.23
  140.8 1.1 collective-permute-start.25
  141.9 13.8 %attend_bwd.3 = (bf16[2,256,768]{2,1,0:T(8,128)(2,1)}, bf16[2,256,768]{2,1,0:T(8,128)(2,1)}, bf16[3,1024,192]{2,1,0:T(8,128)(2,1)}, f32[1,384]{1,0:T(1,128)}) custom-call(s32[2]{0:T(128)} %lengths_ref.25, s32[1]{0:T(128)} %constant.385.clone.1.which_ref, bf16[3,192,768]{2,1,0:T(8,128)(2,1)} %bitcast.110, bf16[2,1024,256]{2,1,0:T(8,128)(2,1)} %get-tuple-element.166.refs_1_, ...), custom_call_target="tpu_custom_call" | custom-call | flops 20000000000 | bytes 1000 | tf_op jit(solution)/shard_map/attend_bwd/pallas_call | solution.py:117
  156.1 0.9 copy-done.20
  157.2 0.7 add_add_fusion.1
  157.9 2.0 fusion.10
  159.9 1.8 fusion.13
  161.7 1.1 fusion.5
  162.9 1.5 collective-permute-start.28
  164.4 1.0 collective-permute-start.29
  165.4 1.8 collective-permute-start.27
  167.2 8.0 %project_grads.1 = (bf16[576,384]{1,0:T(8,128)(2,1)}, bf16[584,384]{1,0:T(8,128)(2,1)}, f32[1,384]{1,0:T(1,128)}) custom-call(s32[2]{0:T(128)} %lengths_ref.25, s32[1]{0:T(128)} %constant.384.clone.1.which_ref, bf16[2,1024,768]{2,1,0:T(8,128)(2,1)} %refs_2_.11, bf16[3,1024,192]{2,1,0:T(8,128)(2,1)} %get-tuple-element.221.refs_1_, ...), custom_call_target="tpu_custom_call" | custom-call | flops 1000 | bytes 1000 | tf_op jit(solution)/shard_map/project_grads/pallas_call | solution.py:117
  175.2 0.9 fusion.6
  176.1 1.1 collective-permute-start.30
  177.2 1.0 fusion.7
  178.2 1.1 slice.176
  179.3 1.1 fusion.11
  180.4 0.7 subtract_convert_fusion
  181.1 6.9 %collective-permute-done.30 = bf16[584,384]{1,0:T(8,128)(2,1)S(1)} collective-permute-done((bf16[584,384]{1,0:T(8,128)(2,1)}, bf16[584,384]{1,0:T(8,128)(2,1)S(1)}, u32[]{:S(2)}, u32[]{:S(2)}) %collective-permute-start.30) | collective-permute-done | bytes 448544 | tf_op jit(solution)/shard_map/ppermute | solution.py:628
  188.8 3.0 %collective-permute-start.37 = (bf16[136,768]{1,0:T(8,128)(2,1)S(1)}, bf16[136,768]{1,0:T(8,128)(2,1)S(1)}, u32[]{:S(2)}, u32[]{:S(2)}) collective-permute-start(bf16[136,768]{1,0:T(8,128)(2,1)S(1)} %pad_maximum_fusion.7), channel_id=1, source_target_pairs={{0,16},{4,20},{8,24},{12,28},{16,0},{20,4},{24,8},{28,12},{1,17},{... | collective-permute-start | bytes 626696 | tf_op jit(solution)/shard_map/ppermute | solution.py:628
  191.7 1.1 fusion.15
  192.9 1.4 collective-permute-start.32
  195.0 4.3 %collective-permute-done.34 = bf16[290,384]{1,0:T(8,128)(2,1)S(1)} collective-permute-done((bf16[290,384]{1,0:T(8,128)(2,1)S(1)}, bf16[290,384]{1,0:T(8,128)(2,1)S(1)}, u32[]{:S(2)}, u32[]{:S(2)}) %collective-permute-start.34) | collective-permute-done | bytes 222752 | tf_op jit(solution)/shard_map/ppermute | solution.py:628
  199.4 6.9 %collective-permute-done.36 = bf16[96,768]{1,0:T(8,128)(2,1)S(1)} collective-permute-done((bf16[96,768]{1,0:T(8,128)(2,1)S(1)}, bf16[96,768]{1,0:T(8,128)(2,1)S(1)}, u32[]{:S(2)}, u32[]{:S(2)}) %collective-permute-start.36) | collective-permute-done | bytes 147488 | tf_op jit(solution)/shard_map/ppermute | solution.py:628
  206.3 1.0 fusion.12
  208.7 1.8 fusion.14
  211.2 4.4 %collective-permute-done.35 = bf16[146,384]{1,0:T(8,128)(2,1)S(1)} collective-permute-done((bf16[146,384]{1,0:T(8,128)(2,1)S(1)}, bf16[146,384]{1,0:T(8,128)(2,1)S(1)}, u32[]{:S(2)}, u32[]{:S(2)}) %collective-permute-start.35) | collective-permute-done | bytes 112160 | tf_op jit(solution)/shard_map/ppermute | solution.py:628
  216.5 0.7 pad_maximum_fusion.5
  217.2 1.7 fusion.8
  218.9 0.9 pad_maximum_fusion
  (126 shorter events, 10.8 us)
Async XLA Ops:
  4.0 23.8 %collective-permute-start = (bf16[200,768]{1,0:T(8,128)(2,1)}, bf16[200,768]{1,0:T(8,128)(2,1)S(1)}, u32[]{:S(2)}, u32[]{:S(2)}) collective-permute-start(bf16[200,768]{1,0:T(8,128)(2,1)} %get-tuple-element.138.refs_11_.refs_4_.refs_16_), channel_id=1, source_target_pairs={{0,1},{1,0},{2,3},{3,2},{4,5},{5,4},{6,7},{7,6},{8,9},{9,8},{10,11... | collective-permute-start | bytes 921608 | tf_op jit(solution)/shard_map/ppermute | solution.py:628
  4.6 23.3 %collective-permute-start.1 = (bf16[200,768]{1,0:T(8,128)(2,1)}, bf16[200,768]{1,0:T(8,128)(2,1)S(1)}, u32[]{:S(2)}, u32[]{:S(2)}) collective-permute-start(bf16[200,768]{1,0:T(8,128)(2,1)} %get-tuple-element.138.refs_11_.refs_4_.refs_16_), channel_id=1, source_target_pairs={{0,2},{1,3},{2,0},{3,1},{4,6},{5,7},{6,4},{7,5},{8,10},{9,11},{10,... | collective-permute-start | bytes 921608 | tf_op jit(solution)/shard_map/ppermute | solution.py:628
  7.2 18.4 %collective-permute-start.2 = (bf16[192,768]{1,0:T(8,128)(2,1)}, bf16[192,768]{1,0:T(8,128)(2,1)S(1)}, u32[]{:S(2)}, u32[]{:S(2)}) collective-permute-start(bf16[192,768]{1,0:T(8,128)(2,1)} %get-tuple-element.139), channel_id=1, source_target_pairs={{0,2},{1,3},{2,0},{3,1},{4,6},{5,7},{6,4},{7,5},{8,10},{9,11},{10,... | collective-permute-start | bytes 884744 | tf_op jit(solution)/shard_map/ppermute | solution.py:628
  7.2 20.6 %collective-permute-start.3 = (bf16[192,768]{1,0:T(8,128)(2,1)}, bf16[192,768]{1,0:T(8,128)(2,1)S(1)}, u32[]{:S(2)}, u32[]{:S(2)}) collective-permute-start(bf16[192,768]{1,0:T(8,128)(2,1)} %get-tuple-element.140), channel_id=1, source_target_pairs={{0,2},{1,3},{2,0},{3,1},{4,6},{5,7},{6,4},{7,5},{8,10},{9,11},{10,... | collective-permute-start | bytes 884744 | tf_op jit(solution)/shard_map/ppermute | solution.py:628
  25.5 18.8 %copy-start.6 = (s32[2]{0:T(128)S(1)}, s32[2]{0:T(128)}, u32[]{:S(2)}) copy-start(s32[2]{0:T(128)} %lengths_ref.25) | copy-start | bytes 28
  25.5 18.8 %copy-start.7 = (bf16[768]{0:T(1024)(128)(2,1)S(1)}, bf16[768]{0:T(1024)(128)(2,1)}, u32[]{:S(2)}) copy-start(bf16[768]{0:T(1024)(128)(2,1)} %refs_0_.10) | copy-start | bytes 4612
  25.5 18.8 %copy-start.8 = (bf16[768]{0:T(1024)(128)(2,1)S(1)}, bf16[768]{0:T(1024)(128)(2,1)}, u32[]{:S(2)}) copy-start(bf16[768]{0:T(1024)(128)(2,1)} %refs_1_.7) | copy-start | bytes 4612
  25.5 18.8 %copy-start.9 = (bf16[768]{0:T(1024)(128)(2,1)S(1)}, bf16[768]{0:T(1024)(128)(2,1)}, u32[]{:S(2)}) copy-start(bf16[768]{0:T(1024)(128)(2,1)} %refs_2_.10) | copy-start | bytes 4612
  25.5 18.8 %copy-start.10 = (bf16[768]{0:T(1024)(128)(2,1)S(1)}, bf16[768]{0:T(1024)(128)(2,1)}, u32[]{:S(2)}) copy-start(bf16[768]{0:T(1024)(128)(2,1)} %refs_3_.7) | copy-start | bytes 4612
  25.6 18.8 %copy-start.11 = (bf16[768]{0:T(1024)(128)(2,1)S(1)}, bf16[768]{0:T(1024)(128)(2,1)}, u32[]{:S(2)}) copy-start(bf16[768]{0:T(1024)(128)(2,1)} %refs_4_.7) | copy-start | bytes 4612
  25.6 18.8 %copy-start.12 = (bf16[768]{0:T(1024)(128)(2,1)S(1)}, bf16[768]{0:T(1024)(128)(2,1)}, u32[]{:S(2)}) copy-start(bf16[768]{0:T(1024)(128)(2,1)} %refs_5_.9) | copy-start | bytes 4612
  27.9 14.7 %collective-permute-start.7 = (bf16[192,768]{1,0:T(8,128)(2,1)S(1)}, bf16[192,768]{1,0:T(8,128)(2,1)S(1)}, u32[]{:S(2)}, u32[]{:S(2)}) collective-permute-start(bf16[192,768]{1,0:T(8,128)(2,1)S(1)} %collective-permute-done.2), channel_id=1, source_target_pairs={{0,4},{4,0},{8,12},{12,8},{16,20},{20,16},{24,28},{28,24},{1,5},{5... | collective-permute-start | bytes 884744 | tf_op jit(solution)/shard_map/ppermute | solution.py:628
  29.6 12.9 %collective-permute-start.8 = (bf16[192,768]{1,0:T(8,128)(2,1)S(1)}, bf16[192,768]{1,0:T(8,128)(2,1)S(1)}, u32[]{:S(2)}, u32[]{:S(2)}) collective-permute-start(bf16[192,768]{1,0:T(8,128)(2,1)S(1)} %collective-permute-done.3), channel_id=1, source_target_pairs={{0,8},{4,12},{8,0},{12,4},{16,24},{20,28},{24,16},{28,20},{1,9},{5... | collective-permute-start | bytes 884744 | tf_op jit(solution)/shard_map/ppermute | solution.py:628
  31.2 1.9 collective-permute-start.4
  31.2 7.9 %collective-permute-start.5 = (bf16[2,192,256]{2,1,0:T(8,128)(2,1)}, bf16[2,192,256]{2,1,0:T(8,128)(2,1)S(1)}, u32[]{:S(2)}, u32[]{:S(2)}) collective-permute-start(bf16[2,192,256]{2,1,0:T(8,128)(2,1)} %get-tuple-element.143), channel_id=1, source_target_pairs={{0,2},{1,3},{2,0},{3,1},{4,6},{5,7},{6,4},{7,5},{8,10},{9,11},{10,... | collective-permute-start | bytes 589832 | tf_op jit(solution)/shard_map/ppermute | solution.py:628
  32.7 9.8 %collective-permute-start.6 = (bf16[2,192,256]{2,1,0:T(8,128)(2,1)}, bf16[2,192,256]{2,1,0:T(8,128)(2,1)S(1)}, u32[]{:S(2)}, u32[]{:S(2)}) collective-permute-start(bf16[2,192,256]{2,1,0:T(8,128)(2,1)} %get-tuple-element.144), channel_id=1, source_target_pairs={{0,3},{1,2},{2,1},{3,0},{4,7},{5,6},{6,5},{7,4},{8,11},{9,10},{10,... | collective-permute-start | bytes 589832 | tf_op jit(solution)/shard_map/ppermute | solution.py:628
  42.6 1.7 collective-permute-start.9
  42.9 15.6 %collective-permute-start.12 = (bf16[384,768]{1,0:T(8,128)(2,1)S(1)}, bf16[384,768]{1,0:T(8,128)(2,1)S(1)}, u32[]{:S(2)}, u32[]{:S(2)}) collective-permute-start(bf16[384,768]{1,0:T(8,128)(2,1)S(1)} %get-tuple-element.159.refs_5_.refs_6_), channel_id=1, source_target_pairs={{0,8},{4,12},{8,0},{12,4},{16,24},{20,28},{24,16},{28,20},{1,9},{5... | collective-permute-start | bytes 1769480 | tf_op jit(solution)/shard_map/ppermute | solution.py:628
  43.4 15.3 %collective-permute-start.13 = (bf16[384,768]{1,0:T(8,128)(2,1)S(1)}, bf16[384,768]{1,0:T(8,128)(2,1)S(1)}, u32[]{:S(2)}, u32[]{:S(2)}) collective-permute-start(bf16[384,768]{1,0:T(8,128)(2,1)S(1)} %get-tuple-element.160.refs_7_.refs_8_), channel_id=1, source_target_pairs={{0,4},{4,0},{8,12},{12,8},{16,20},{20,16},{24,28},{28,24},{1,5},{5... | collective-permute-start | bytes 1769480 | tf_op jit(solution)/shard_map/ppermute | solution.py:628
  48.5 1.8 collective-permute-start.10
  48.8 2.1 collective-permute-start.11
  58.5 7.0 %copy-start.2 = (bf16[2,512,768]{2,1,0:T(8,128)(2,1)}, bf16[2,512,768]{2,1,0:T(8,128)(2,1)S(1)}, u32[]{:S(2)}) copy-start(bf16[2,512,768]{2,1,0:T(8,128)(2,1)S(1)} %get-tuple-element.199.refs_0_) | copy-start | bytes 4718596
  65.5 1.2 copy-start.4
  66.8 2.3 %collective-permute-start.14 = (bf16[512,768]{1,0:T(8,128)(2,1)S(1)}, bf16[512,768]{1,0:T(8,128)(2,1)S(1)}, u32[]{:S(2)}, u32[]{:S(2)}) collective-permute-start(bf16[512,768]{1,0:T(8,128)(2,1)S(1)} %get-tuple-element.164), channel_id=1, source_target_pairs={{0,1},{1,0},{2,3},{3,2},{4,5},{5,4},{6,7},{7,6},{8,9},{9,8},{10,11... | collective-permute-start | bytes 2359304 | tf_op jit(solution)/shard_map/ppermute | solution.py:628
  73.1 2.4 %collective-permute-start.15 = (bf16[512,768]{1,0:T(8,128)(2,1)S(1)}, bf16[512,768]{1,0:T(8,128)(2,1)S(1)}, u32[]{:S(2)}, u32[]{:S(2)}) collective-permute-start(bf16[512,768]{1,0:T(8,128)(2,1)S(1)} %get-tuple-element.172.refs_0_.refs_2_), channel_id=1, source_target_pairs={{0,1},{1,0},{2,3},{3,2},{4,5},{5,4},{6,7},{7,6},{8,9},{9,8},{10,11... | collective-permute-start | bytes 2359304 | tf_op jit(solution)/shard_map/ppermute | solution.py:628
  85.6 1.6 copy-start
  87.2 2.3 %collective-permute-start.16 = (bf16[512,768]{1,0:T(8,128)(2,1)S(1)}, bf16[512,768]{1,0:T(8,128)(2,1)S(1)}, u32[]{:S(2)}, u32[]{:S(2)}) collective-permute-start(bf16[512,768]{1,0:T(8,128)(2,1)S(1)} %get-tuple-element.176), channel_id=1, source_target_pairs={{0,1},{1,0},{2,3},{3,2},{4,5},{5,4},{6,7},{7,6},{8,9},{9,8},{10,11... | collective-permute-start | bytes 2359304 | tf_op jit(solution)/shard_map/ppermute | solution.py:628
  96.4 11.5 %collective-permute-start.20 = (bf16[2,200,768]{2,1,0:T(8,128)(2,1)}, bf16[2,200,768]{2,1,0:T(8,128)(2,1)}, u32[]{:S(2)}, u32[]{:S(2)}) collective-permute-start(bf16[2,200,768]{2,1,0:T(8,128)(2,1)} %get-tuple-element.185), channel_id=1, source_target_pairs={{0,1},{1,0},{2,3},{3,2},{4,5},{5,4},{6,7},{7,6},{8,9},{9,8},{10,11... | collective-permute-start | bytes 1843208 | tf_op jit(solution)/shard_map/ppermute | solution.py:628
  96.7 18.1 %collective-permute-start.17 = (bf16[2,192,256]{2,1,0:T(8,128)(2,1)}, bf16[2,192,256]{2,1,0:T(8,128)(2,1)S(1)}, u32[]{:S(2)}, u32[]{:S(2)}) collective-permute-start(bf16[2,192,256]{2,1,0:T(8,128)(2,1)} %get-tuple-element.180), channel_id=1, source_target_pairs={{0,1},{1,0},{2,3},{3,2},{4,5},{5,4},{6,7},{7,6},{8,9},{9,8},{10,11... | collective-permute-start | bytes 589832 | tf_op jit(solution)/shard_map/ppermute | solution.py:628
  97.0 17.7 %collective-permute-start.18 = (bf16[2,192,256]{2,1,0:T(8,128)(2,1)}, bf16[2,192,256]{2,1,0:T(8,128)(2,1)}, u32[]{:S(2)}, u32[]{:S(2)}) collective-permute-start(bf16[2,192,256]{2,1,0:T(8,128)(2,1)} %get-tuple-element.181), channel_id=1, source_target_pairs={{0,2},{1,3},{2,0},{3,1},{4,6},{5,7},{6,4},{7,5},{8,10},{9,11},{10,... | collective-permute-start | bytes 589832 | tf_op jit(solution)/shard_map/ppermute | solution.py:628
  98.5 16.2 %collective-permute-start.19 = (bf16[2,192,256]{2,1,0:T(8,128)(2,1)}, bf16[2,192,256]{2,1,0:T(8,128)(2,1)}, u32[]{:S(2)}, u32[]{:S(2)}) collective-permute-start(bf16[2,192,256]{2,1,0:T(8,128)(2,1)} %get-tuple-element.182), channel_id=1, source_target_pairs={{0,3},{1,2},{2,1},{3,0},{4,7},{5,6},{6,5},{7,4},{8,11},{9,10},{10,... | collective-permute-start | bytes 589832 | tf_op jit(solution)/shard_map/ppermute | solution.py:628
  98.5 1.4 copy-start.3
  100.0 1.4 copy-start.5
  101.4 6.6 %copy-start.1 = (bf16[2,2,512,768]{3,2,1,0:T(8,128)(2,1)S(1)}, bf16[2,2,512,768]{3,2,1,0:T(8,128)(2,1)}, u32[]{:S(2)}) copy-start(bf16[2,2,512,768]{3,2,1,0:T(8,128)(2,1)} %copy-done) | copy-start | bytes 9437188
  106.8 28.7 %collective-permute-start.22 = (bf16[2,4,96,768]{3,2,1,0:T(8,128)(2,1)}, bf16[2,4,96,768]{3,2,1,0:T(8,128)(2,1)S(1)}, u32[]{:S(2)}, u32[]{:S(2)}) collective-permute-start(bf16[2,4,96,768]{3,2,1,0:T(8,128)(2,1)} %get-tuple-element.204), channel_id=1, source_target_pairs={{0,4},{4,0},{8,12},{12,8},{16,20},{20,16},{24,28},{28,24},{1,5},{5... | collective-permute-start | bytes 3538952 | tf_op jit(solution)/shard_map/ppermute | solution.py:628
  114.7 1.7 copy-start.27
  114.7 20.8 %collective-permute-start.21 = (bf16[496,768]{1,0:T(8,128)(2,1)}, bf16[496,768]{1,0:T(8,128)(2,1)S(1)}, u32[]{:S(2)}, u32[]{:S(2)}) collective-permute-start(bf16[496,768]{1,0:T(8,128)(2,1)} %get-tuple-element.203), channel_id=1, source_target_pairs={{0,8},{4,12},{8,0},{12,4},{16,24},{20,28},{24,16},{28,20},{1,9},{5... | collective-permute-start | bytes 2285576 | tf_op jit(solution)/shard_map/ppermute | solution.py:628
  130.4 5.2 %copy-start.22 = (bf16[4,96,768]{2,1,0:T(8,128)(2,1)S(1)}, bf16[4,96,768]{2,1,0:T(8,128)(2,1)}, u32[]{:S(2)}) copy-start(bf16[4,96,768]{2,1,0:T(8,128)(2,1)} %get-tuple-element.201) | copy-start | bytes 1769476
  137.7 18.4 %collective-permute-start.24 = (bf16[480,768]{1,0:T(8,128)(2,1)}, bf16[480,768]{1,0:T(8,128)(2,1)S(1)}, u32[]{:S(2)}, u32[]{:S(2)}) collective-permute-start(bf16[480,768]{1,0:T(8,128)(2,1)} %get-tuple-element.217), channel_id=1, source_target_pairs={{0,8},{4,12},{8,0},{12,4},{16,24},{20,28},{24,16},{28,20},{1,9},{5... | collective-permute-start | bytes 2211848 | tf_op jit(solution)/shard_map/ppermute | solution.py:628
  139.3 16.5 %collective-permute-start.23 = (bf16[4,96,768]{2,1,0:T(8,128)(2,1)S(1)}, bf16[4,96,768]{2,1,0:T(8,128)(2,1)}, u32[]{:S(2)}, u32[]{:S(2)}) collective-permute-start(bf16[4,96,768]{2,1,0:T(8,128)(2,1)S(1)} %fusion), channel_id=1, source_target_pairs={{0,2},{1,3},{2,0},{3,1},{4,6},{5,7},{6,4},{7,5},{8,10},{9,11},{10,... | collective-permute-start | bytes 1769480 | tf_op jit(solution)/shard_map/ppermute | solution.py:628
  140.8 14.9 %collective-permute-start.25 = (bf16[256,768]{1,0:T(8,128)(2,1)}, bf16[256,768]{1,0:T(8,128)(2,1)}, u32[]{:S(2)}, u32[]{:S(2)}) collective-permute-start(bf16[256,768]{1,0:T(8,128)(2,1)} %pad_maximum_fusion.3), channel_id=1, source_target_pairs={{0,4},{4,0},{8,12},{12,8},{16,20},{20,16},{24,28},{28,24},{1,5},{5... | collective-permute-start | bytes 1179656 | tf_op jit(solution)/shard_map/ppermute | solution.py:628
  141.9 14.3 %collective-permute-start.26 = (bf16[2,256,768]{2,1,0:T(8,128)(2,1)}, bf16[2,256,768]{2,1,0:T(8,128)(2,1)S(1)}, u32[]{:S(2)}, u32[]{:S(2)}) collective-permute-start(bf16[2,256,768]{2,1,0:T(8,128)(2,1)} %get-tuple-element.219), channel_id=1, source_target_pairs={{0,1},{1,0},{2,3},{3,2},{4,5},{5,4},{6,7},{7,6},{8,9},{9,8},{10,11... | collective-permute-start | bytes 2359304 | tf_op jit(solution)/shard_map/ppermute | solution.py:628
  155.6 4.3 %copy-start.23 = (bf16[4,96,768]{2,1,0:T(8,128)(2,1)S(1)}, bf16[4,96,768]{2,1,0:T(8,128)(2,1)}, u32[]{:S(2)}) copy-start(bf16[4,96,768]{2,1,0:T(8,128)(2,1)} %get-tuple-element.223) | copy-start | bytes 1769476
  156.1 19.0 %copy-start.15 = (bf16[2,256,768]{2,1,0:T(8,128)(2,1)}, bf16[2,256,768]{2,1,0:T(8,128)(2,1)S(1)}, u32[]{:S(2)}) copy-start(bf16[2,256,768]{2,1,0:T(8,128)(2,1)S(1)} %collective-permute-done.26) | copy-start | bytes 2359300
  157.0 20.2 %collective-permute-start.31 = (bf16[2,256,768]{2,1,0:T(8,128)(2,1)}, bf16[2,256,768]{2,1,0:T(8,128)(2,1)S(1)}, u32[]{:S(2)}, u32[]{:S(2)}) collective-permute-start(bf16[2,256,768]{2,1,0:T(8,128)(2,1)} %get-tuple-element.240), channel_id=1, source_target_pairs={{0,1},{1,0},{2,3},{3,2},{4,5},{5,4},{6,7},{7,6},{8,9},{9,8},{10,11... | collective-permute-start | bytes 2359304 | tf_op jit(solution)/shard_map/ppermute | solution.py:628
  162.9 13.2 %collective-permute-start.28 = (bf16[256,768]{1,0:T(8,128)(2,1)S(1)}, bf16[256,768]{1,0:T(8,128)(2,1)}, u32[]{:S(2)}, u32[]{:S(2)}) collective-permute-start(bf16[256,768]{1,0:T(8,128)(2,1)S(1)} %pad_maximum_fusion.4), channel_id=1, source_target_pairs={{0,2},{1,3},{2,0},{3,1},{4,6},{5,7},{6,4},{7,5},{8,10},{9,11},{10,... | collective-permute-start | bytes 1179656 | tf_op jit(solution)/shard_map/ppermute | solution.py:628
  164.4 11.7 %collective-permute-start.29 = (bf16[2,120,768]{2,1,0:T(8,128)(2,1)}, bf16[2,120,768]{2,1,0:T(8,128)(2,1)}, u32[]{:S(2)}, u32[]{:S(2)}) collective-permute-start(bf16[2,120,768]{2,1,0:T(8,128)(2,1)} %fusion.10), channel_id=1, source_target_pairs={{0,4},{4,0},{8,12},{12,8},{16,20},{20,16},{24,28},{28,24},{1,5},{5... | collective-permute-start | bytes 1105928 | tf_op jit(solution)/shard_map/ppermute | solution.py:628
  165.4 10.7 %collective-permute-start.27 = (bf16[2,96,768]{2,1,0:T(8,128)(2,1)}, bf16[2,96,768]{2,1,0:T(8,128)(2,1)}, u32[]{:S(2)}, u32[]{:S(2)}) collective-permute-start(bf16[2,96,768]{2,1,0:T(8,128)(2,1)} %fusion.13), channel_id=1, source_target_pairs={{0,8},{4,12},{8,0},{12,4},{16,24},{20,28},{24,16},{28,20},{1,9},{5... | collective-permute-start | bytes 884744 | tf_op jit(solution)/shard_map/ppermute | solution.py:628
  167.2 8.0 %copy-start.14 = (bf16[2,256,768]{2,1,0:T(8,128)(2,1)S(1)}, bf16[2,256,768]{2,1,0:T(8,128)(2,1)}, u32[]{:S(2)}) copy-start(bf16[2,256,768]{2,1,0:T(8,128)(2,1)} %get-tuple-element.198) | copy-start | bytes 2359300
  167.2 10.0 %copy-start.16 = (bf16[2,256,768]{2,1,0:T(8,128)(2,1)S(1)}, bf16[2,256,768]{2,1,0:T(8,128)(2,1)}, u32[]{:S(2)}) copy-start(bf16[2,256,768]{2,1,0:T(8,128)(2,1)} %get-tuple-element.239) | copy-start | bytes 2359300
  175.1 4.1 %copy-start.19 = (bf16[480,768]{1,0:T(8,128)(2,1)S(1)}, bf16[480,768]{1,0:T(8,128)(2,1)}, u32[]{:S(2)}) copy-start(bf16[480,768]{1,0:T(8,128)(2,1)} %get-tuple-element.226) | copy-start | bytes 2211844
  175.2 4.1 %copy-start.21 = (bf16[480,768]{1,0:T(8,128)(2,1)S(1)}, bf16[480,768]{1,0:T(8,128)(2,1)}, u32[]{:S(2)}) copy-start(bf16[480,768]{1,0:T(8,128)(2,1)} %copy-done.20) | copy-start | bytes 2211844
  176.1 11.9 %collective-permute-start.30 = (bf16[584,384]{1,0:T(8,128)(2,1)}, bf16[584,384]{1,0:T(8,128)(2,1)S(1)}, u32[]{:S(2)}, u32[]{:S(2)}) collective-permute-start(bf16[584,384]{1,0:T(8,128)(2,1)} %get-tuple-element.235), channel_id=1, source_target_pairs={{0,4},{4,0},{8,12},{12,8},{16,20},{20,16},{24,28},{28,24},{1,5},{5... | collective-permute-start | bytes 1345544 | tf_op jit(solution)/shard_map/ppermute | solution.py:628
  177.2 10.9 %copy-start.17 = (bf16[2,256,768]{2,1,0:T(8,128)(2,1)}, bf16[2,256,768]{2,1,0:T(8,128)(2,1)S(1)}, u32[]{:S(2)}) copy-start(bf16[2,256,768]{2,1,0:T(8,128)(2,1)S(1)} %collective-permute-done.31) | copy-start | bytes 2359300
  178.2 9.9 %copy-start.26 = (f32[1,384]{1,0:T(1,128)S(1)}, f32[1,384]{1,0:T(1,128)}, u32[]{:S(2)}) copy-start(f32[1,384]{1,0:T(1,128)} %get-tuple-element.248) | copy-start | bytes 4612
  178.2 9.9 %copy-start.25 = (bf16[576,384]{1,0:T(8,128)(2,1)S(1)}, bf16[576,384]{1,0:T(8,128)(2,1)}, u32[]{:S(2)}) copy-start(bf16[576,384]{1,0:T(8,128)(2,1)} %get-tuple-element.246) | copy-start | bytes 1327108
  179.3 12.5 %copy-start.24 = (bf16[4,96,768]{2,1,0:T(8,128)(2,1)S(1)}, bf16[4,96,768]{2,1,0:T(8,128)(2,1)}, u32[]{:S(2)}) copy-start(bf16[4,96,768]{2,1,0:T(8,128)(2,1)} %get-tuple-element.223) | copy-start | bytes 1769476
  188.2 11.1 %collective-permute-start.34 = (bf16[290,384]{1,0:T(8,128)(2,1)S(1)}, bf16[290,384]{1,0:T(8,128)(2,1)S(1)}, u32[]{:S(2)}, u32[]{:S(2)}) collective-permute-start(bf16[290,384]{1,0:T(8,128)(2,1)S(1)} %pad_maximum_fusion.6), channel_id=1, source_target_pairs={{0,8},{4,12},{8,0},{12,4},{16,24},{20,28},{24,16},{28,20},{1,9},{5... | collective-permute-start | bytes 668168 | tf_op jit(solution)/shard_map/ppermute | solution.py:628
  188.8 17.6 %collective-permute-start.37 = (bf16[136,768]{1,0:T(8,128)(2,1)S(1)}, bf16[136,768]{1,0:T(8,128)(2,1)S(1)}, u32[]{:S(2)}, u32[]{:S(2)}) collective-permute-start(bf16[136,768]{1,0:T(8,128)(2,1)S(1)} %pad_maximum_fusion.7), channel_id=1, source_target_pairs={{0,16},{4,20},{8,24},{12,28},{16,0},{20,4},{24,8},{28,12},{1,17},{... | collective-permute-start | bytes 626696 | tf_op jit(solution)/shard_map/ppermute | solution.py:628
  192.8 13.5 %collective-permute-start.36 = (bf16[96,768]{1,0:T(8,128)(2,1)S(1)}, bf16[96,768]{1,0:T(8,128)(2,1)S(1)}, u32[]{:S(2)}, u32[]{:S(2)}) collective-permute-start(bf16[96,768]{1,0:T(8,128)(2,1)S(1)} %fusion.15), channel_id=1, source_target_pairs={{0,16},{4,20},{8,24},{12,28},{16,0},{20,4},{24,8},{28,12},{1,17},{... | collective-permute-start | bytes 442376 | tf_op jit(solution)/shard_map/ppermute | solution.py:628
  192.9 24.3 %collective-permute-start.32 = (bf16[256,768]{1,0:T(8,128)(2,1)}, bf16[256,768]{1,0:T(8,128)(2,1)S(1)}, u32[]{:S(2)}, u32[]{:S(2)}) collective-permute-start(bf16[256,768]{1,0:T(8,128)(2,1)} %fusion.6), channel_id=1, source_target_pairs={{0,2},{1,3},{2,0},{3,1},{4,6},{5,7},{6,4},{7,5},{8,10},{9,11},{10,... | collective-permute-start | bytes 1179656 | tf_op jit(solution)/shard_map/ppermute | solution.py:628
  194.3 22.9 %collective-permute-start.33 = (bf16[256,768]{1,0:T(8,128)(2,1)}, bf16[256,768]{1,0:T(8,128)(2,1)}, u32[]{:S(2)}, u32[]{:S(2)}) collective-permute-start(bf16[256,768]{1,0:T(8,128)(2,1)} %fusion.7), channel_id=1, source_target_pairs={{0,2},{1,3},{2,0},{3,1},{4,6},{5,7},{6,4},{7,5},{8,10},{9,11},{10,... | collective-permute-start | bytes 1179656 | tf_op jit(solution)/shard_map/ppermute | solution.py:628
  208.1 9.1 %copy-start.13 = (f32[512,768]{1,0:T(8,128)S(1)}, f32[512,768]{1,0:T(8,128)}, u32[]{:S(2)}) copy-start(f32[512,768]{1,0:T(8,128)} %get-tuple-element.244) | copy-start | bytes 4718596
  208.7 6.9 %collective-permute-start.35 = (bf16[146,384]{1,0:T(8,128)(2,1)S(1)}, bf16[146,384]{1,0:T(8,128)(2,1)S(1)}, u32[]{:S(2)}, u32[]{:S(2)}) collective-permute-start(bf16[146,384]{1,0:T(8,128)(2,1)S(1)} %pad_maximum_fusion.8), channel_id=1, source_target_pairs={{0,16},{4,20},{8,24},{12,28},{16,0},{20,4},{24,8},{28,12},{1,17},{... | collective-permute-start | bytes 336392 | tf_op jit(solution)/shard_map/ppermute | solution.py:628
  (2 other events, 2.0 us)

commit v6 on v5

--- a/solution.py
+++ b/solution.py
@@ -866,10 +866,11 @@
     w_send, down_more, up_y, up_more = after(w_send, down_more, up_y, up_more)
     keep0, near0, keep1, near1 = keeps
     in_sums = [summed([k[1], x[1]]).astype(bf16) for k, x in ((keep0, near0), (keep1, near1))]
-    down_more, up_y, up_more, *in_sums = after(down_more, up_y, up_more, *in_sums)
+    down_more, up_y, up_more, in_sums[1] = after(down_more, up_y, up_more, in_sums[1])
     got = swap(w_send, "dp", 1)
-    got, *in_sums = after(got, *in_sums)
+    in_sums[0], _ = after(in_sums[0], w_send)
     far = [swap(x, "tensor", 2) for x in in_sums]
+    got, far[0] = after(got, far[0])
     down_terms = down_kept + [down_more]
     at = up_y_next.size // d
     small = jnp.concatenate([small[0:6], small[7:8], small[7:8]]) + pair_sum(up_y, at, 8)
@@ -878,7 +879,10 @@
         down_terms, sent = halve_sum(down_terms, bits - 1 - i, bit_of[i])
         down_got = swap(sent, "dp", 1 << i)
         up_terms, sent = halve_sum(up_terms, bits - 1 - i, bit_of[i])
-        up_got = swap(with_rows(sent, small), "dp", 1 << i)
+        up_rows = with_rows(sent, small)
+        if i == 2:
+            got, down_got, up_rows = after(got, down_got, up_rows)
+        up_got = swap(up_rows, "dp", 1 << i)
         if i == bits - 1:
             break
         down_terms, up_terms, small = with_received(down_terms, down_got, up_terms, up_got, sent, small)

time: 221 us -> 215 us (0.973)
  waiting for transfers between devices: 48.6 us -> 41.8 us
  starting transfers between devices: 32.8 us -> 36.2 us
    ppermute x38, waiting for transfers between devices: 48.6 us -> 41.8 us  [swap(): return lax.ppermute(x, axis, [(i, i ^ bit) for i in range(size)])]
    ppermute x38, starting transfers between devices: 32.8 us -> 36.2 us  [swap(): return lax.ppermute(x, axis, [(i, i ^ bit) for i in range(size)])]
    pallas_call x13, Pallas kernels: 107 us -> 105 us  [call(): pl.pallas_call(kernel, out_shape=[pltpu.HBM(o.shape, o.dtype) if i in far...]
  transfers between devices with their start and end apart: 38 -> 38, of which waited for: 16 -> 18; matrix products, arithmetic and copies ran while one was open for 8% -> 9% of each run, Pallas kernels for 35% -> 34%
where the time goes in v6:
time: 215 us; the launch traced here: 214 us
  Pallas kernels  105 us (49%)
  waiting for transfers between devices  41.8 us (19%)
  starting transfers between devices  36.2 us (17%)
  other arithmetic  19.4 us (9%)
  local copies, waits for them, and re-layouts  10.1 us (5%)
    pallas_call x13, Pallas kernels, call(): pl.pallas_call(kernel, out_shape=[pltpu.HBM(o.shape, o.dtype) if i in far...  105 us
    ppermute x38, waiting for transfers between devices, swap(): return lax.ppermute(x, axis, [(i, i ^ bit) for i in range(size)])  41.8 us
    ppermute x38, starting transfers between devices, swap(): return lax.ppermute(x, axis, [(i, i ^ bit) for i in range(size)])  36.2 us
    unnamed x56, local copies, waits for them, and re-layouts  7.15 us
    convert_element_type x4, other arithmetic, halve_sum(): return (kept, summed(other).astype(bf16))  5.34 us
  transfers between devices with their start and end apart: 38, of which 18 were waited for; matrix products, arithmetic and copies ran while one was open for 9% of the time, Pallas kernels for 34%

profile of v6, /device:TPU:0, one launch (start us, length us, event | category | flops | bytes accessed | tf_op | source)
XLA Modules:
  0.0 213.7 jit_solution(3541864893699187031)
XLA Ops:
  0.6 3.4 %prepare.1 = (bf16[200,768]{1,0:T(8,128)(2,1)}, bf16[192,768]{1,0:T(8,128)(2,1)}, bf16[192,768]{1,0:T(8,128)(2,1)}) custom-call(s32[2]{0:T(128)} %lengths_ref.25, s32[1]{0:T(128)} %constant.384.clone.1.which_ref, bf16[192,768]{1,0:T(8,128)(2,1)} %refs_0_.7, bf16[768]{0:T(1024)(128)(2,1)} %refs_1_.4, bf16[768,768]{1,0:T(8,128)(2,1)} %refs_4_.6, ...), custom_call_target="tpu_custom_call" | custom-call | flops 1000 | bytes 1000 | tf_op jit(solution)/shard_map/prepare/pallas_call | solution.py:117
  4.5 2.6 %collective-permute-start.1 = (bf16[200,768]{1,0:T(8,128)(2,1)}, bf16[200,768]{1,0:T(8,128)(2,1)S(1)}, u32[]{:S(2)}, u32[]{:S(2)}) collective-permute-start(bf16[200,768]{1,0:T(8,128)(2,1)} %get-tuple-element.140.refs_11_.refs_4_.refs_16_), channel_id=1, source_target_pairs={{0,2},{1,3},{2,0},{3,1},{4,6},{5,7},{6,4},{7,5},{8,10},{9,11},{10,... | collective-permute-start | bytes 921608 | tf_op jit(solution)/shard_map/ppermute | solution.py:628
  7.2 1.9 collective-permute-start.3
  9.2 16.3 %attend_fwd.1 = (bf16[2,1024,256]{2,1,0:T(8,128)(2,1)}, bf16[2,1024,256]{2,1,0:T(8,128)(2,1)}, bf16[2,1024,192]{2,1,0:T(8,128)(2,1)}, f32[2,4,8,256]{3,2,1,0:T(8...) custom-call(s32[2]{0:T(128)} %lengths_ref.25, ...), custom_call_target="tpu_custom_call" | custom-call | flops 1000 | bytes 1000 | tf_op jit(solution)/shard_map/attend_fwd/pallas_call | solution.py:117
  25.6 2.3 %collective-permute-done.3 = bf16[192,768]{1,0:T(8,128)(2,1)S(1)} collective-permute-done((bf16[192,768]{1,0:T(8,128)(2,1)}, bf16[192,768]{1,0:T(8,128)(2,1)S(1)}, u32[]{:S(2)}, u32[]{:S(2)}) %collective-permute-start.3) | collective-permute-done | bytes 294944 | tf_op jit(solution)/shard_map/ppermute | solution.py:628
  27.9 1.7 collective-permute-start.7
  29.6 1.6 collective-permute-start.8
  31.2 1.5 collective-permute-start.5
  33.0 6.0 %collective-permute-done.5.refs_9_.refs_14_ = bf16[2,192,256]{2,1,0:T(8,128)(2,1)S(1)} collective-permute-done((bf16[2,192,256]{2,1,0:T(8,128)(2,1)}, bf16[2,192,256]{2,1,0:T(8,128)(2,1)S(1)}, u32[]{:S(2)}, u32[]{:S(2)}) %collective-permute-start.5) | collective-permute-done | bytes 196640 | tf_op jit(solution)/shard_map/ppermute | solution.py:628
  39.1 3.4 %collective-permute-done.6.refs_10_.refs_15_ = bf16[2,192,256]{2,1,0:T(8,128)(2,1)S(1)} collective-permute-done((bf16[2,192,256]{2,1,0:T(8,128)(2,1)}, bf16[2,192,256]{2,1,0:T(8,128)(2,1)S(1)}, u32[]{:S(2)}, u32[]{:S(2)}) %collective-permute-start.6) | collective-permute-done | bytes 196640 | tf_op jit(solution)/shard_map/ppermute | solution.py:628
  44.3 4.2 %first_norm.1 = (f32[512,768]{1,0:T(8,128)S(1)}, f32[512,1]{1,0:T(8,128)S(1)}, bf16[256,768]{1,0:T(8,128)(2,1)S(1)}, bf16[256,768]{1,0:T(8,128)(2,1)S(1)}) custom-call(s32[2]{0:T(128)S(1)} %copy-done.6, s32[1]{0:T(128)} %constant.384.clone.1.which_ref, bf16[2,1024,768]{2,1,0:T(8,128)(2,1)} %refs_2_.11, bf16[768]{0:T(1024)(128)(2,1)S(1)} %copy-done.7, ...), custom_call_target="tpu_custom_call" | custom-call | flops 1000 | bytes 1000 | tf_op jit(solution)/shard_map/first_norm/pallas_call | solution.py:117
  49.1 1.2 collective-permute-done.10.refs_2_
  50.9 7.6 %feed.2 = (bf16[2,512,768]{2,1,0:T(8,128)(2,1)S(1)}, bf16[2,512,768]{2,1,0:T(8,128)(2,1)S(1)}, f32[512,768]{1,0:T(8,128)S(1)}, f32[512,768]{1,0:T(8,128)S(1)}) custom-call(s32[2]{0:T(128)S(1)} %copy-done.6, s32[1]{0:T(128)} %constant.384.clone.1.which_ref, bf16[256,768]{1,0:T(8,128)(2,1)S(1)} %get-tuple-element.159.refs_0_, ...), custom_call_target="tpu_custom_call" | custom-call | flops 1000 | bytes 1000 | tf_op jit(solution)/shard_map/feed/pallas_call | solution.py:117
  58.6 6.9 %feed.3 = (bf16[2,512,768]{2,1,0:T(8,128)(2,1)S(1)}, bf16[2,512,768]{2,1,0:T(8,128)(2,1)S(1)}, f32[512,768]{1,0:T(8,128)S(1)}, bf16[512,768]{1,0:T(8,128)(2,1)S(1)}) custom-call(s32[2]{0:T(128)S(1)} %copy-done.6, s32[1]{0:T(128)} %constant.384.clone.1.which_ref, bf16[256,768]{1,0:T(8,128)(2,1)S(1)} %get-tuple-element.159.refs_0_, ...), custom_call_target="tpu_custom_call" | custom-call | flops 1000 | bytes 1000 | tf_op jit(solution)/shard_map/feed/pallas_call | solution.py:117
  65.5 1.2 copy-done.4
  66.9 2.1 collective-permute-done.14.refs_9_
  69.0 4.0 %second_norm.1 = (bf16[2,256,768]{2,1,0:T(8,128)(2,1)}, f32[512,768]{1,0:T(8,128)S(1)}, bf16[512,768]{1,0:T(8,128)(2,1)S(1)}, f32[8,768]{1,0:T(8,128)S(1)}) custom-call(s32[2]{0:T(128)S(1)} %copy-done.6, s32[1]{0:T(128)} %constant.384.clone.1.which_ref, bf16[2,256,768]{2,1,0:T(8,128)(2,1)} %refs_0_.9, bf16[768]{0:T(1024)(128)(2,1)S(1)} %copy-done.7, ...), custom_call_target="tpu_custom_call" | custom-call | flops 1000 | bytes 1000 | tf_op jit(solution)/shard_map/second_norm/pallas_call | solution.py:117
  73.3 2.1 collective-permute-done.15.refs_1_.refs_3_
  75.4 10.1 %feed_back.1 = (bf16[2,2,512,768]{3,2,1,0:T(8,128)(2,1)S(1)}, f32[512,768]{1,0:T(8,128)S(1)}, bf16[512,768]{1,0:T(8,128)(2,1)S(1)}, f32[8,768]{1,0:T(8,128)S(1)}) custom-call(s32[2]{0:T(128)S(1)} %copy-done.6, s32[1]{0:T(128)} %constant.384.clone.1.which_ref, bf16[512,768]{1,0:T(8,128)(2,1)S(1)} %get-tuple-element.174.refs_0_.refs_2_, ...), custom_call_target="tpu_custom_call" | custom-call | flops 1000 | bytes 1000 | tf_op jit(solution)/shard_map/feed_back/pallas_call | solution.py:117
  85.5 1.7 copy-done
  87.4 2.1 collective-permute-done.16.refs_9_
  89.5 6.9 %first_back.1 = (f32[512,768]{1,0:T(8,128)}, bf16[2,192,256]{2,1,0:T(8,128)(2,1)}, bf16[2,192,256]{2,1,0:T(8,128)(2,1)}, bf16[2,192,256]{2,1,0:T(8,128)(2,1)}, b...) custom-call(s32[2]{0:T(128)S(1)} %copy-done.6, ...), custom_call_target="tpu_custom_call" | custom-call | flops 1000 | bytes 1000 | tf_op jit(solution)/shard_map/first_back/pallas_call | solution.py:117
  97.0 1.5 collective-permute-start.18
  98.6 1.4 copy-done.3
  100.0 1.4 copy-done.5
  101.4 5.4 %down_grads.1 = (bf16[4,96,768]{2,1,0:T(8,128)(2,1)}, bf16[4,96,768]{2,1,0:T(8,128)(2,1)}, bf16[2,4,96,768]{3,2,1,0:T(8,128)(2,1)}) custom-call(s32[2]{0:T(128)S(1)} %copy-done.6, s32[1]{0:T(128)} %constant.384.clone.1.which_ref, bf16[2,512,768]{2,1,0:T(8,128)(2,1)S(1)} %copy-done.3, bf16[2,512,768]{2,1,0:T(8,128)(2,1)S(1)} %copy-done.5, ...), custom_call_target="tpu_custom_call" | custom-call | flops 1000 | bytes 1000 | tf_op jit(solution)/shard_map/down_grads/pallas_call | solution.py:117
  106.8 1.1 collective-permute-start.22
  107.9 6.7 %up_grads.1 = (bf16[480,768]{1,0:T(8,128)(2,1)}, bf16[496,768]{1,0:T(8,128)(2,1)}, bf16[480,768]{1,0:T(8,128)(2,1)}, bf16[480,768]{1,0:T(8,128)(2,1)}, f32[8,768]{1,0:T(8,128)S(1)}) custom-call(s32[2]{0:T(128)S(1)} %copy-done.6, s32[1]{0:T(128)} %constant.384.clone.1.which_ref, bf16[256,768]{1,0:T(8,128)(2,1)S(1)} %get-tuple-element.159.refs_0_, ...), custom_call_target="tpu_custom_call" | custom-call | flops 1000 | bytes 1000 | tf_op jit(solution)/shard_map/up_grads/pallas_call | solution.py:117
  114.7 1.6 collective-permute-start.21
  116.3 11.7 %attend_bwd.2 = (bf16[2,256,768]{2,1,0:T(8,128)(2,1)}, bf16[2,256,768]{2,1,0:T(8,128)(2,1)}, bf16[3,1024,192]{2,1,0:T(8,128)(2,1)}, f32[1,384]{1,0:T(1,128)}) custom-call(s32[2]{0:T(128)} %lengths_ref.25, s32[1]{0:T(128)} %constant.384.clone.1.which_ref, bf16[3,192,768]{2,1,0:T(8,128)(2,1)} %bitcast.109, bf16[2,1024,256]{2,1,0:T(8,128)(2,1)} %get-tuple-element.168.refs_1_, ...), custom_call_target="tpu_custom_call" | custom-call | flops 20000000000 | bytes 1000 | tf_op jit(solution)/shard_map/attend_bwd/pallas_call | solution.py:117
  128.0 7.5 %collective-permute-done.22 = bf16[2,4,96,768]{3,2,1,0:T(8,128)(2,1)S(1)} collective-permute-done((bf16[2,4,96,768]{3,2,1,0:T(8,128)(2,1)}, bf16[2,4,96,768]{3,2,1,0:T(8,128)(2,1)S(1)}, u32[]{:S(2)}, u32[]{:S(2)}) %collective-permute-start.22) | collective-permute-done | bytes 1179680 | tf_op jit(solution)/shard_map/ppermute | solution.py:628
  135.8 0.9 copy-done.17
  136.9 0.8 pad_maximum_fusion.3
  137.6 1.6 collective-permute-start.24
  139.2 1.5 collective-permute-start.23
  140.7 1.1 collective-permute-start.25
  141.8 13.7 %attend_bwd.3 = (bf16[2,256,768]{2,1,0:T(8,128)(2,1)}, bf16[2,256,768]{2,1,0:T(8,128)(2,1)}, bf16[3,1024,192]{2,1,0:T(8,128)(2,1)}, f32[1,384]{1,0:T(1,128)}) custom-call(s32[2]{0:T(128)} %lengths_ref.25, s32[1]{0:T(128)} %constant.385.clone.1.which_ref, bf16[3,192,768]{2,1,0:T(8,128)(2,1)} %bitcast.110, bf16[2,1024,256]{2,1,0:T(8,128)(2,1)} %get-tuple-element.168.refs_1_, ...), custom_call_target="tpu_custom_call" | custom-call | flops 20000000000 | bytes 1000 | tf_op jit(solution)/shard_map/attend_bwd/pallas_call | solution.py:117
  157.0 1.9 fusion.10
  158.8 1.1 fusion.13
  159.9 1.1 fusion.5
  161.1 1.6 collective-permute-start.28
  162.6 2.3 %collective-permute-start.29 = (bf16[2,120,768]{2,1,0:T(8,128)(2,1)}, bf16[2,120,768]{2,1,0:T(8,128)(2,1)}, u32[]{:S(2)}, u32[]{:S(2)}) collective-permute-start(bf16[2,120,768]{2,1,0:T(8,128)(2,1)} %fusion.10), channel_id=1, source_target_pairs={{0,4},{4,0},{8,12},{12,8},{16,20},{20,16},{24,28},{28,24},{1,5},{5... | collective-permute-start | bytes 1105928 | tf_op jit(solution)/shard_map/ppermute | solution.py:628
  165.4 7.9 %project_grads.1 = (bf16[576,384]{1,0:T(8,128)(2,1)}, bf16[584,384]{1,0:T(8,128)(2,1)}, f32[1,384]{1,0:T(1,128)}) custom-call(s32[2]{0:T(128)} %lengths_ref.25, s32[1]{0:T(128)} %constant.384.clone.1.which_ref, bf16[2,1024,768]{2,1,0:T(8,128)(2,1)} %refs_2_.11, bf16[3,1024,192]{2,1,0:T(8,128)(2,1)} %get-tuple-element.223.refs_1_, ...), custom_call_target="tpu_custom_call" | custom-call | flops 1000 | bytes 1000 | tf_op jit(solution)/shard_map/project_grads/pallas_call | solution.py:117
  173.7 1.7 collective-permute-start.30
  175.5 1.5 collective-permute-start.31
  177.0 1.9 fusion.7
  178.9 1.2 fusion.15
  180.1 2.6 %collective-permute-start.34 = (bf16[96,768]{1,0:T(8,128)(2,1)S(1)}, bf16[96,768]{1,0:T(8,128)(2,1)S(1)}, u32[]{:S(2)}, u32[]{:S(2)}) collective-permute-start(bf16[96,768]{1,0:T(8,128)(2,1)S(1)} %fusion.15), channel_id=1, source_target_pairs={{0,16},{4,20},{8,24},{12,28},{16,0},{20,4},{24,8},{28,12},{1,17},{... | collective-permute-start | bytes 442376 | tf_op jit(solution)/shard_map/ppermute | solution.py:628
  182.8 1.2 fusion.12
  184.7 0.8 collective-permute-done.31
  185.5 2.8 %collective-permute-done.34 = bf16[96,768]{1,0:T(8,128)(2,1)S(1)} collective-permute-done((bf16[96,768]{1,0:T(8,128)(2,1)S(1)}, bf16[96,768]{1,0:T(8,128)(2,1)S(1)}, u32[]{:S(2)}, u32[]{:S(2)}) %collective-permute-start.34) | collective-permute-done | bytes 147488 | tf_op jit(solution)/shard_map/ppermute | solution.py:628
  189.2 0.8 collective-permute-start.33
  190.0 3.4 %collective-permute-start.37 = (bf16[136,768]{1,0:T(8,128)(2,1)}, bf16[136,768]{1,0:T(8,128)(2,1)S(1)}, u32[]{:S(2)}, u32[]{:S(2)}) collective-permute-start(bf16[136,768]{1,0:T(8,128)(2,1)} %pad_maximum_fusion.7), channel_id=1, source_target_pairs={{0,16},{4,20},{8,24},{12,28},{16,0},{20,4},{24,8},{28,12},{1,17},{... | collective-permute-start | bytes 626696 | tf_op jit(solution)/shard_map/ppermute | solution.py:628
  193.3 5.8 %collective-permute-done.35 = bf16[290,384]{1,0:T(8,128)(2,1)S(1)} collective-permute-done((bf16[290,384]{1,0:T(8,128)(2,1)S(1)}, bf16[290,384]{1,0:T(8,128)(2,1)S(1)}, u32[]{:S(2)}, u32[]{:S(2)}) %collective-permute-start.35) | collective-permute-done | bytes 222752 | tf_op jit(solution)/shard_map/ppermute | solution.py:628
  199.2 1.0 fusion.16
  200.3 2.0 collective-permute-done.37
  202.2 1.2 fusion.11
  203.5 0.7 slice.210
  205.5 1.9 fusion.14
  207.4 1.4 fusion.8
  208.8 0.9 pad_maximum_fusion
  209.8 1.5 collective-permute-done.36
  211.9 1.0 fusion.17
  213.0 0.7 pad_maximum_fusion.5
  (126 shorter events, 11.6 us)
Async XLA Ops:
  4.0 23.8 %collective-permute-start = (bf16[200,768]{1,0:T(8,128)(2,1)}, bf16[200,768]{1,0:T(8,128)(2,1)S(1)}, u32[]{:S(2)}, u32[]{:S(2)}) collective-permute-start(bf16[200,768]{1,0:T(8,128)(2,1)} %get-tuple-element.140.refs_11_.refs_4_.refs_16_), channel_id=1, source_target_pairs={{0,1},{1,0},{2,3},{3,2},{4,5},{5,4},{6,7},{7,6},{8,9},{9,8},{10,11... | collective-permute-start | bytes 921608 | tf_op jit(solution)/shard_map/ppermute | solution.py:628
  4.5 23.3 %collective-permute-start.1 = (bf16[200,768]{1,0:T(8,128)(2,1)}, bf16[200,768]{1,0:T(8,128)(2,1)S(1)}, u32[]{:S(2)}, u32[]{:S(2)}) collective-permute-start(bf16[200,768]{1,0:T(8,128)(2,1)} %get-tuple-element.140.refs_11_.refs_4_.refs_16_), channel_id=1, source_target_pairs={{0,2},{1,3},{2,0},{3,1},{4,6},{5,7},{6,4},{7,5},{8,10},{9,11},{10,... | collective-permute-start | bytes 921608 | tf_op jit(solution)/shard_map/ppermute | solution.py:628
  7.1 18.4 %collective-permute-start.2 = (bf16[192,768]{1,0:T(8,128)(2,1)}, bf16[192,768]{1,0:T(8,128)(2,1)S(1)}, u32[]{:S(2)}, u32[]{:S(2)}) collective-permute-start(bf16[192,768]{1,0:T(8,128)(2,1)} %get-tuple-element.141), channel_id=1, source_target_pairs={{0,2},{1,3},{2,0},{3,1},{4,6},{5,7},{6,4},{7,5},{8,10},{9,11},{10,... | collective-permute-start | bytes 884744 | tf_op jit(solution)/shard_map/ppermute | solution.py:628
  7.2 20.6 %collective-permute-start.3 = (bf16[192,768]{1,0:T(8,128)(2,1)}, bf16[192,768]{1,0:T(8,128)(2,1)S(1)}, u32[]{:S(2)}, u32[]{:S(2)}) collective-permute-start(bf16[192,768]{1,0:T(8,128)(2,1)} %get-tuple-element.142), channel_id=1, source_target_pairs={{0,2},{1,3},{2,0},{3,1},{4,6},{5,7},{6,4},{7,5},{8,10},{9,11},{10,... | collective-permute-start | bytes 884744 | tf_op jit(solution)/shard_map/ppermute | solution.py:628
  25.5 18.8 %copy-start.6 = (s32[2]{0:T(128)S(1)}, s32[2]{0:T(128)}, u32[]{:S(2)}) copy-start(s32[2]{0:T(128)} %lengths_ref.25) | copy-start | bytes 28
  25.5 18.8 %copy-start.7 = (bf16[768]{0:T(1024)(128)(2,1)S(1)}, bf16[768]{0:T(1024)(128)(2,1)}, u32[]{:S(2)}) copy-start(bf16[768]{0:T(1024)(128)(2,1)} %refs_0_.10) | copy-start | bytes 4612
  25.5 18.8 %copy-start.8 = (bf16[768]{0:T(1024)(128)(2,1)S(1)}, bf16[768]{0:T(1024)(128)(2,1)}, u32[]{:S(2)}) copy-start(bf16[768]{0:T(1024)(128)(2,1)} %refs_1_.7) | copy-start | bytes 4612
  25.5 18.8 %copy-start.9 = (bf16[768]{0:T(1024)(128)(2,1)S(1)}, bf16[768]{0:T(1024)(128)(2,1)}, u32[]{:S(2)}) copy-start(bf16[768]{0:T(1024)(128)(2,1)} %refs_2_.10) | copy-start | bytes 4612
  25.5 18.8 %copy-start.10 = (bf16[768]{0:T(1024)(128)(2,1)S(1)}, bf16[768]{0:T(1024)(128)(2,1)}, u32[]{:S(2)}) copy-start(bf16[768]{0:T(1024)(128)(2,1)} %refs_3_.7) | copy-start | bytes 4612
  25.5 18.8 %copy-start.11 = (bf16[768]{0:T(1024)(128)(2,1)S(1)}, bf16[768]{0:T(1024)(128)(2,1)}, u32[]{:S(2)}) copy-start(bf16[768]{0:T(1024)(128)(2,1)} %refs_4_.7) | copy-start | bytes 4612
  25.6 18.8 %copy-start.12 = (bf16[768]{0:T(1024)(128)(2,1)S(1)}, bf16[768]{0:T(1024)(128)(2,1)}, u32[]{:S(2)}) copy-start(bf16[768]{0:T(1024)(128)(2,1)} %refs_5_.9) | copy-start | bytes 4612
  27.9 14.7 %collective-permute-start.7 = (bf16[192,768]{1,0:T(8,128)(2,1)S(1)}, bf16[192,768]{1,0:T(8,128)(2,1)S(1)}, u32[]{:S(2)}, u32[]{:S(2)}) collective-permute-start(bf16[192,768]{1,0:T(8,128)(2,1)S(1)} %collective-permute-done.2), channel_id=1, source_target_pairs={{0,4},{4,0},{8,12},{12,8},{16,20},{20,16},{24,28},{28,24},{1,5},{5... | collective-permute-start | bytes 884744 | tf_op jit(solution)/shard_map/ppermute | solution.py:628
  29.6 12.9 %collective-permute-start.8 = (bf16[192,768]{1,0:T(8,128)(2,1)S(1)}, bf16[192,768]{1,0:T(8,128)(2,1)S(1)}, u32[]{:S(2)}, u32[]{:S(2)}) collective-permute-start(bf16[192,768]{1,0:T(8,128)(2,1)S(1)} %collective-permute-done.3), channel_id=1, source_target_pairs={{0,8},{4,12},{8,0},{12,4},{16,24},{20,28},{24,16},{28,20},{1,9},{5... | collective-permute-start | bytes 884744 | tf_op jit(solution)/shard_map/ppermute | solution.py:628
  31.2 1.9 collective-permute-start.4
  31.2 7.9 %collective-permute-start.5 = (bf16[2,192,256]{2,1,0:T(8,128)(2,1)}, bf16[2,192,256]{2,1,0:T(8,128)(2,1)S(1)}, u32[]{:S(2)}, u32[]{:S(2)}) collective-permute-start(bf16[2,192,256]{2,1,0:T(8,128)(2,1)} %get-tuple-element.145), channel_id=1, source_target_pairs={{0,2},{1,3},{2,0},{3,1},{4,6},{5,7},{6,4},{7,5},{8,10},{9,11},{10,... | collective-permute-start | bytes 589832 | tf_op jit(solution)/shard_map/ppermute | solution.py:628
  32.7 9.8 %collective-permute-start.6 = (bf16[2,192,256]{2,1,0:T(8,128)(2,1)}, bf16[2,192,256]{2,1,0:T(8,128)(2,1)S(1)}, u32[]{:S(2)}, u32[]{:S(2)}) collective-permute-start(bf16[2,192,256]{2,1,0:T(8,128)(2,1)} %get-tuple-element.146), channel_id=1, source_target_pairs={{0,3},{1,2},{2,1},{3,0},{4,7},{5,6},{6,5},{7,4},{8,11},{9,10},{10,... | collective-permute-start | bytes 589832 | tf_op jit(solution)/shard_map/ppermute | solution.py:628
  42.6 1.7 collective-permute-start.9
  42.9 15.6 %collective-permute-start.12 = (bf16[384,768]{1,0:T(8,128)(2,1)S(1)}, bf16[384,768]{1,0:T(8,128)(2,1)S(1)}, u32[]{:S(2)}, u32[]{:S(2)}) collective-permute-start(bf16[384,768]{1,0:T(8,128)(2,1)S(1)} %get-tuple-element.161.refs_5_.refs_6_), channel_id=1, source_target_pairs={{0,8},{4,12},{8,0},{12,4},{16,24},{20,28},{24,16},{28,20},{1,9},{5... | collective-permute-start | bytes 1769480 | tf_op jit(solution)/shard_map/ppermute | solution.py:628
  43.3 15.3 %collective-permute-start.13 = (bf16[384,768]{1,0:T(8,128)(2,1)S(1)}, bf16[384,768]{1,0:T(8,128)(2,1)S(1)}, u32[]{:S(2)}, u32[]{:S(2)}) collective-permute-start(bf16[384,768]{1,0:T(8,128)(2,1)S(1)} %get-tuple-element.162.refs_7_.refs_8_), channel_id=1, source_target_pairs={{0,4},{4,0},{8,12},{12,8},{16,20},{20,16},{24,28},{28,24},{1,5},{5... | collective-permute-start | bytes 1769480 | tf_op jit(solution)/shard_map/ppermute | solution.py:628
  48.5 1.8 collective-permute-start.10
  48.8 2.1 collective-permute-start.11
  58.5 7.0 %copy-start.2 = (bf16[2,512,768]{2,1,0:T(8,128)(2,1)}, bf16[2,512,768]{2,1,0:T(8,128)(2,1)S(1)}, u32[]{:S(2)}) copy-start(bf16[2,512,768]{2,1,0:T(8,128)(2,1)S(1)} %get-tuple-element.201.refs_0_) | copy-start | bytes 4718596
  65.5 1.2 copy-start.4
  66.7 2.3 %collective-permute-start.14 = (bf16[512,768]{1,0:T(8,128)(2,1)S(1)}, bf16[512,768]{1,0:T(8,128)(2,1)S(1)}, u32[]{:S(2)}, u32[]{:S(2)}) collective-permute-start(bf16[512,768]{1,0:T(8,128)(2,1)S(1)} %get-tuple-element.166), channel_id=1, source_target_pairs={{0,1},{1,0},{2,3},{3,2},{4,5},{5,4},{6,7},{7,6},{8,9},{9,8},{10,11... | collective-permute-start | bytes 2359304 | tf_op jit(solution)/shard_map/ppermute | solution.py:628
  73.0 2.4 %collective-permute-start.15 = (bf16[512,768]{1,0:T(8,128)(2,1)S(1)}, bf16[512,768]{1,0:T(8,128)(2,1)S(1)}, u32[]{:S(2)}, u32[]{:S(2)}) collective-permute-start(bf16[512,768]{1,0:T(8,128)(2,1)S(1)} %get-tuple-element.174.refs_0_.refs_2_), channel_id=1, source_target_pairs={{0,1},{1,0},{2,3},{3,2},{4,5},{5,4},{6,7},{7,6},{8,9},{9,8},{10,11... | collective-permute-start | bytes 2359304 | tf_op jit(solution)/shard_map/ppermute | solution.py:628
  85.5 1.7 copy-start
  87.3 2.3 %collective-permute-start.16 = (bf16[512,768]{1,0:T(8,128)(2,1)S(1)}, bf16[512,768]{1,0:T(8,128)(2,1)S(1)}, u32[]{:S(2)}, u32[]{:S(2)}) collective-permute-start(bf16[512,768]{1,0:T(8,128)(2,1)S(1)} %get-tuple-element.178), channel_id=1, source_target_pairs={{0,1},{1,0},{2,3},{3,2},{4,5},{5,4},{6,7},{7,6},{8,9},{9,8},{10,11... | collective-permute-start | bytes 2359304 | tf_op jit(solution)/shard_map/ppermute | solution.py:628
  96.4 11.5 %collective-permute-start.20 = (bf16[2,200,768]{2,1,0:T(8,128)(2,1)}, bf16[2,200,768]{2,1,0:T(8,128)(2,1)}, u32[]{:S(2)}, u32[]{:S(2)}) collective-permute-start(bf16[2,200,768]{2,1,0:T(8,128)(2,1)} %get-tuple-element.187), channel_id=1, source_target_pairs={{0,1},{1,0},{2,3},{3,2},{4,5},{5,4},{6,7},{7,6},{8,9},{9,8},{10,11... | collective-permute-start | bytes 1843208 | tf_op jit(solution)/shard_map/ppermute | solution.py:628
  96.7 18.0 %collective-permute-start.17 = (bf16[2,192,256]{2,1,0:T(8,128)(2,1)}, bf16[2,192,256]{2,1,0:T(8,128)(2,1)S(1)}, u32[]{:S(2)}, u32[]{:S(2)}) collective-permute-start(bf16[2,192,256]{2,1,0:T(8,128)(2,1)} %get-tuple-element.182), channel_id=1, source_target_pairs={{0,1},{1,0},{2,3},{3,2},{4,5},{5,4},{6,7},{7,6},{8,9},{9,8},{10,11... | collective-permute-start | bytes 589832 | tf_op jit(solution)/shard_map/ppermute | solution.py:628
  97.0 17.6 %collective-permute-start.18 = (bf16[2,192,256]{2,1,0:T(8,128)(2,1)}, bf16[2,192,256]{2,1,0:T(8,128)(2,1)}, u32[]{:S(2)}, u32[]{:S(2)}) collective-permute-start(bf16[2,192,256]{2,1,0:T(8,128)(2,1)} %get-tuple-element.183), channel_id=1, source_target_pairs={{0,2},{1,3},{2,0},{3,1},{4,6},{5,7},{6,4},{7,5},{8,10},{9,11},{10,... | collective-permute-start | bytes 589832 | tf_op jit(solution)/shard_map/ppermute | solution.py:628
  98.6 16.1 %collective-permute-start.19 = (bf16[2,192,256]{2,1,0:T(8,128)(2,1)}, bf16[2,192,256]{2,1,0:T(8,128)(2,1)}, u32[]{:S(2)}, u32[]{:S(2)}) collective-permute-start(bf16[2,192,256]{2,1,0:T(8,128)(2,1)} %get-tuple-element.184), channel_id=1, source_target_pairs={{0,3},{1,2},{2,1},{3,0},{4,7},{5,6},{6,5},{7,4},{8,11},{9,10},{10,... | collective-permute-start | bytes 589832 | tf_op jit(solution)/shard_map/ppermute | solution.py:628
  98.6 1.4 copy-start.3
  100.0 1.4 copy-start.5
  101.4 6.5 %copy-start.1 = (bf16[2,2,512,768]{3,2,1,0:T(8,128)(2,1)S(1)}, bf16[2,2,512,768]{3,2,1,0:T(8,128)(2,1)}, u32[]{:S(2)}) copy-start(bf16[2,2,512,768]{3,2,1,0:T(8,128)(2,1)} %copy-done) | copy-start | bytes 9437188
  106.8 28.7 %collective-permute-start.22 = (bf16[2,4,96,768]{3,2,1,0:T(8,128)(2,1)}, bf16[2,4,96,768]{3,2,1,0:T(8,128)(2,1)S(1)}, u32[]{:S(2)}, u32[]{:S(2)}) collective-permute-start(bf16[2,4,96,768]{3,2,1,0:T(8,128)(2,1)} %get-tuple-element.206), channel_id=1, source_target_pairs={{0,4},{4,0},{8,12},{12,8},{16,20},{20,16},{24,28},{28,24},{1,5},{5... | collective-permute-start | bytes 3538952 | tf_op jit(solution)/shard_map/ppermute | solution.py:628
  114.7 1.7 copy-start.27
  114.7 20.9 %collective-permute-start.21 = (bf16[496,768]{1,0:T(8,128)(2,1)}, bf16[496,768]{1,0:T(8,128)(2,1)S(1)}, u32[]{:S(2)}, u32[]{:S(2)}) collective-permute-start(bf16[496,768]{1,0:T(8,128)(2,1)} %get-tuple-element.205), channel_id=1, source_target_pairs={{0,8},{4,12},{8,0},{12,4},{16,24},{20,28},{24,16},{28,20},{1,9},{5... | collective-permute-start | bytes 2285576 | tf_op jit(solution)/shard_map/ppermute | solution.py:628
  128.0 7.6 %copy-start.19 = (bf16[4,96,768]{2,1,0:T(8,128)(2,1)S(1)}, bf16[4,96,768]{2,1,0:T(8,128)(2,1)}, u32[]{:S(2)}) copy-start(bf16[4,96,768]{2,1,0:T(8,128)(2,1)} %get-tuple-element.203) | copy-start | bytes 1769476
  137.6 19.3 %copy-start.18 = (bf16[480,768]{1,0:T(8,128)(2,1)S(1)}, bf16[480,768]{1,0:T(8,128)(2,1)}, u32[]{:S(2)}) copy-start(bf16[480,768]{1,0:T(8,128)(2,1)} %get-tuple-element.228) | copy-start | bytes 2211844
  137.6 18.5 %collective-permute-start.24 = (bf16[480,768]{1,0:T(8,128)(2,1)}, bf16[480,768]{1,0:T(8,128)(2,1)}, u32[]{:S(2)}, u32[]{:S(2)}) collective-permute-start(bf16[480,768]{1,0:T(8,128)(2,1)} %get-tuple-element.219), channel_id=1, source_target_pairs={{0,8},{4,12},{8,0},{12,4},{16,24},{20,28},{24,16},{28,20},{1,9},{5... | collective-permute-start | bytes 2211848 | tf_op jit(solution)/shard_map/ppermute | solution.py:628
  139.2 16.4 %collective-permute-start.23 = (bf16[4,96,768]{2,1,0:T(8,128)(2,1)S(1)}, bf16[4,96,768]{2,1,0:T(8,128)(2,1)}, u32[]{:S(2)}, u32[]{:S(2)}) collective-permute-start(bf16[4,96,768]{2,1,0:T(8,128)(2,1)S(1)} %fusion), channel_id=1, source_target_pairs={{0,2},{1,3},{2,0},{3,1},{4,6},{5,7},{6,4},{7,5},{8,10},{9,11},{10,... | collective-permute-start | bytes 1769480 | tf_op jit(solution)/shard_map/ppermute | solution.py:628
  140.7 14.8 %collective-permute-start.25 = (bf16[256,768]{1,0:T(8,128)(2,1)}, bf16[256,768]{1,0:T(8,128)(2,1)}, u32[]{:S(2)}, u32[]{:S(2)}) collective-permute-start(bf16[256,768]{1,0:T(8,128)(2,1)} %pad_maximum_fusion.3), channel_id=1, source_target_pairs={{0,4},{4,0},{8,12},{12,8},{16,20},{20,16},{24,28},{28,24},{1,5},{5... | collective-permute-start | bytes 1179656 | tf_op jit(solution)/shard_map/ppermute | solution.py:628
  141.8 14.4 %collective-permute-start.26 = (bf16[2,256,768]{2,1,0:T(8,128)(2,1)}, bf16[2,256,768]{2,1,0:T(8,128)(2,1)S(1)}, u32[]{:S(2)}, u32[]{:S(2)}) collective-permute-start(bf16[2,256,768]{2,1,0:T(8,128)(2,1)} %get-tuple-element.221), channel_id=1, source_target_pairs={{0,1},{1,0},{2,3},{3,2},{4,5},{5,4},{6,7},{7,6},{8,9},{9,8},{10,11... | collective-permute-start | bytes 2359304 | tf_op jit(solution)/shard_map/ppermute | solution.py:628
  155.5 3.3 %copy-start.20 = (bf16[4,96,768]{2,1,0:T(8,128)(2,1)S(1)}, bf16[4,96,768]{2,1,0:T(8,128)(2,1)}, u32[]{:S(2)}) copy-start(bf16[4,96,768]{2,1,0:T(8,128)(2,1)} %get-tuple-element.225) | copy-start | bytes 1769476
  156.2 20.9 %collective-permute-start.32 = (bf16[2,256,768]{2,1,0:T(8,128)(2,1)}, bf16[2,256,768]{2,1,0:T(8,128)(2,1)}, u32[]{:S(2)}, u32[]{:S(2)}) collective-permute-start(bf16[2,256,768]{2,1,0:T(8,128)(2,1)} %get-tuple-element.242), channel_id=1, source_target_pairs={{0,1},{1,0},{2,3},{3,2},{4,5},{5,4},{6,7},{7,6},{8,9},{9,8},{10,11... | collective-permute-start | bytes 2359304 | tf_op jit(solution)/shard_map/ppermute | solution.py:628
  161.1 12.6 %collective-permute-start.28 = (bf16[256,768]{1,0:T(8,128)(2,1)S(1)}, bf16[256,768]{1,0:T(8,128)(2,1)S(1)}, u32[]{:S(2)}, u32[]{:S(2)}) collective-permute-start(bf16[256,768]{1,0:T(8,128)(2,1)S(1)} %pad_maximum_fusion.4), channel_id=1, source_target_pairs={{0,2},{1,3},{2,0},{3,1},{4,6},{5,7},{6,4},{7,5},{8,10},{9,11},{10,... | collective-permute-start | bytes 1179656 | tf_op jit(solution)/shard_map/ppermute | solution.py:628
  162.6 11.1 %collective-permute-start.29 = (bf16[2,120,768]{2,1,0:T(8,128)(2,1)}, bf16[2,120,768]{2,1,0:T(8,128)(2,1)}, u32[]{:S(2)}, u32[]{:S(2)}) collective-permute-start(bf16[2,120,768]{2,1,0:T(8,128)(2,1)} %fusion.10), channel_id=1, source_target_pairs={{0,4},{4,0},{8,12},{12,8},{16,20},{20,16},{24,28},{28,24},{1,5},{5... | collective-permute-start | bytes 1105928 | tf_op jit(solution)/shard_map/ppermute | solution.py:628
  164.9 8.5 %collective-permute-start.27 = (bf16[2,96,768]{2,1,0:T(8,128)(2,1)S(1)}, bf16[2,96,768]{2,1,0:T(8,128)(2,1)}, u32[]{:S(2)}, u32[]{:S(2)}) collective-permute-start(bf16[2,96,768]{2,1,0:T(8,128)(2,1)S(1)} %fusion.13), channel_id=1, source_target_pairs={{0,8},{4,12},{8,0},{12,4},{16,24},{20,28},{24,16},{28,20},{1,9},{5... | collective-permute-start | bytes 884744 | tf_op jit(solution)/shard_map/ppermute | solution.py:628
  165.4 8.0 %copy-start.14 = (bf16[2,256,768]{2,1,0:T(8,128)(2,1)S(1)}, bf16[2,256,768]{2,1,0:T(8,128)(2,1)}, u32[]{:S(2)}) copy-start(bf16[2,256,768]{2,1,0:T(8,128)(2,1)} %get-tuple-element.200) | copy-start | bytes 2359300
  165.4 11.6 %copy-start.15 = (bf16[2,256,768]{2,1,0:T(8,128)(2,1)S(1)}, bf16[2,256,768]{2,1,0:T(8,128)(2,1)}, u32[]{:S(2)}) copy-start(bf16[2,256,768]{2,1,0:T(8,128)(2,1)} %get-tuple-element.241) | copy-start | bytes 2359300
  173.7 11.8 %collective-permute-start.30 = (bf16[584,384]{1,0:T(8,128)(2,1)}, bf16[584,384]{1,0:T(8,128)(2,1)S(1)}, u32[]{:S(2)}, u32[]{:S(2)}) collective-permute-start(bf16[584,384]{1,0:T(8,128)(2,1)} %get-tuple-element.237), channel_id=1, source_target_pairs={{0,4},{4,0},{8,12},{12,8},{16,20},{20,16},{24,28},{28,24},{1,5},{5... | collective-permute-start | bytes 1345544 | tf_op jit(solution)/shard_map/ppermute | solution.py:628
  175.5 10.0 %collective-permute-start.31 = (bf16[256,768]{1,0:T(8,128)(2,1)S(1)}, bf16[256,768]{1,0:T(8,128)(2,1)S(1)}, u32[]{:S(2)}, u32[]{:S(2)}) collective-permute-start(bf16[256,768]{1,0:T(8,128)(2,1)S(1)} %fusion.6), channel_id=1, source_target_pairs={{0,2},{1,3},{2,0},{3,1},{4,6},{5,7},{6,4},{7,5},{8,10},{9,11},{10,... | collective-permute-start | bytes 1179656 | tf_op jit(solution)/shard_map/ppermute | solution.py:628
  178.9 9.4 %copy-start.26 = (f32[1,384]{1,0:T(1,128)S(1)}, f32[1,384]{1,0:T(1,128)}, u32[]{:S(2)}) copy-start(f32[1,384]{1,0:T(1,128)} %get-tuple-element.253) | copy-start | bytes 4612
  178.9 9.5 %copy-start.21 = (bf16[576,384]{1,0:T(8,128)(2,1)S(1)}, bf16[576,384]{1,0:T(8,128)(2,1)}, u32[]{:S(2)}) copy-start(bf16[576,384]{1,0:T(8,128)(2,1)} %get-tuple-element.247) | copy-start | bytes 1327108
  180.1 8.2 %collective-permute-start.34 = (bf16[96,768]{1,0:T(8,128)(2,1)S(1)}, bf16[96,768]{1,0:T(8,128)(2,1)S(1)}, u32[]{:S(2)}, u32[]{:S(2)}) collective-permute-start(bf16[96,768]{1,0:T(8,128)(2,1)S(1)} %fusion.15), channel_id=1, source_target_pairs={{0,16},{4,20},{8,24},{12,28},{16,0},{20,4},{24,8},{28,12},{1,17},{... | collective-permute-start | bytes 442376 | tf_op jit(solution)/shard_map/ppermute | solution.py:628
  185.5 3.0 %copy-start.22 = (bf16[256,768]{1,0:T(8,128)(2,1)}, bf16[256,768]{1,0:T(8,128)(2,1)S(1)}, u32[]{:S(2)}) copy-start(bf16[256,768]{1,0:T(8,128)(2,1)S(1)} %collective-permute-done.31) | copy-start | bytes 1179652
  188.9 10.2 %collective-permute-start.35 = (bf16[290,384]{1,0:T(8,128)(2,1)S(1)}, bf16[290,384]{1,0:T(8,128)(2,1)S(1)}, u32[]{:S(2)}, u32[]{:S(2)}) collective-permute-start(bf16[290,384]{1,0:T(8,128)(2,1)S(1)} %pad_maximum_fusion.6), channel_id=1, source_target_pairs={{0,8},{4,12},{8,0},{12,4},{16,24},{20,28},{24,16},{28,20},{1,9},{5... | collective-permute-start | bytes 668168 | tf_op jit(solution)/shard_map/ppermute | solution.py:628
  189.2 18.2 %collective-permute-start.33 = (bf16[256,768]{1,0:T(8,128)(2,1)}, bf16[256,768]{1,0:T(8,128)(2,1)S(1)}, u32[]{:S(2)}, u32[]{:S(2)}) collective-permute-start(bf16[256,768]{1,0:T(8,128)(2,1)} %fusion.7), channel_id=1, source_target_pairs={{0,2},{1,3},{2,0},{3,1},{4,6},{5,7},{6,4},{7,5},{8,10},{9,11},{10,... | collective-permute-start | bytes 1179656 | tf_op jit(solution)/shard_map/ppermute | solution.py:628
  190.0 12.3 %collective-permute-start.37 = (bf16[136,768]{1,0:T(8,128)(2,1)}, bf16[136,768]{1,0:T(8,128)(2,1)S(1)}, u32[]{:S(2)}, u32[]{:S(2)}) collective-permute-start(bf16[136,768]{1,0:T(8,128)(2,1)} %pad_maximum_fusion.7), channel_id=1, source_target_pairs={{0,16},{4,20},{8,24},{12,28},{16,0},{20,4},{24,8},{28,12},{1,17},{... | collective-permute-start | bytes 626696 | tf_op jit(solution)/shard_map/ppermute | solution.py:628
  199.2 6.3 %copy-start.25 = (bf16[96,768]{1,0:T(8,128)(2,1)S(1)}, bf16[96,768]{1,0:T(8,128)(2,1)}, u32[]{:S(2)}) copy-start(bf16[96,768]{1,0:T(8,128)(2,1)} %copy-done.24) | copy-start | bytes 442372
  200.2 7.1 %copy-start.13 = (f32[512,768]{1,0:T(8,128)S(1)}, f32[512,768]{1,0:T(8,128)}, u32[]{:S(2)}) copy-start(f32[512,768]{1,0:T(8,128)} %get-tuple-element.240) | copy-start | bytes 4718596
  200.2 7.1 %copy-start.16 = (bf16[2,256,768]{2,1,0:T(8,128)(2,1)S(1)}, bf16[2,256,768]{2,1,0:T(8,128)(2,1)}, u32[]{:S(2)}) copy-start(bf16[2,256,768]{2,1,0:T(8,128)(2,1)} %get-tuple-element.241) | copy-start | bytes 2359300
  200.2 7.1 %copy-start.23 = (bf16[256,768]{1,0:T(8,128)(2,1)S(1)}, bf16[256,768]{1,0:T(8,128)(2,1)}, u32[]{:S(2)}) copy-start(bf16[256,768]{1,0:T(8,128)(2,1)} %copy-done.22) | copy-start | bytes 1179652
  204.8 6.4 %collective-permute-start.36 = (bf16[146,384]{1,0:T(8,128)(2,1)S(1)}, bf16[146,384]{1,0:T(8,128)(2,1)S(1)}, u32[]{:S(2)}, u32[]{:S(2)}) collective-permute-start(bf16[146,384]{1,0:T(8,128)(2,1)S(1)} %pad_maximum_fusion.8), channel_id=1, source_target_pairs={{0,16},{4,20},{8,24},{12,28},{16,0},{20,4},{24,8},{28,12},{1,17},{... | collective-permute-start | bytes 336392 | tf_op jit(solution)/shard_map/ppermute | solution.py:628
  (2 other events, 1.8 us)

commit v7 on v6

--- a/solution.py
+++ b/solution.py
@@ -447,28 +447,28 @@
     step = 256
     n = low[0].shape[0]
     for i, x in enumerate(low):
-        both[i // 2, (i % 2) * n : (i % 2 + 1) * n, :] = x[...]
-
-    def side(j, carry):
-        def chunk(n, carry):
-            cols = pl.ds(pl.multiple_of(n * step, step), step)
-            hidden = mm(both[j], up[:, cols]) + bias[width : width + 1, cols].astype(f32)
-            a, g = gelu_parts(hidden)
-            act[j, :, cols] = a.astype(bf16)
-            slope[j, :, cols] = g.astype(bf16)
-            return carry
-
-        return lax.fori_loop(0, units // step, chunk, carry)
-
-    lax.fori_loop(0, 2, side, 0)
+        both[i * n : (i + 1) * n, :] = x[...]
+    n = 2 * n
+
+    def chunk(m, carry):
+        cols = pl.ds(pl.multiple_of(m * step, step), step)
+        hidden = mm(both[...], up[:, cols]) + bias[width : width + 1, cols].astype(f32)
+        a, g = gelu_parts(hidden)
+        act[:, cols] = a.astype(bf16)
+        slope[:, cols] = g.astype(bf16)
+        return carry
+
+    lax.fori_loop(0, units // step, chunk, 0)
     if far:
         dn = dn()
-        sib[...] = (p_sib[...] + mm(act[1], dn[...])).astype(bf16)
-        own[...] = p_own[...] + mm(act[0], dn[...])
+        total = mm(act[...], dn[...])
+        sib[...] = (p_sib[...] + total[n:]).astype(bf16)
+        own[...] = p_own[...] + total[:n]
     else:
         dn = d_in()
-        own[...] = mm(act[0], dn[...])
-        sib[...] = mm(act[1], dn[...])
+        total = mm(act[...], dn[...])
+        own[...] = total[:n]
+        sib[...] = total[n:]
 
 
 def second_norm_kernel(info, cot_in, *rest):
@@ -498,8 +498,9 @@
     dn2 = pieces(info, d_a, d_b, dn2, sem.at[1], True)
     up2 = pieces(info, u_a, u_b, up2, sem.at[0], False)
     ub[...] = jnp.zeros_like(ub)
-    sides[0] = gs[...]
-    sides[1] = gs2[...]
+    n = gs.shape[0]
+    sides[0:n, :] = gs[...]
+    sides[n : 2 * n, :] = gs2[...]
     step = 256
     for k, slope in enumerate((ref(slope0), ref(slope1))):
         if k:
@@ -507,22 +508,20 @@
         else:
             dn = dn0()
 
-        def side(j, carry):
-            def chunk(n, carry):
-                cols = pl.ds(pl.multiple_of(n * step, step), step)
-                ga = mm(sides[j], dn[cols, :], NT)
-                h = (ga * slope[j, :, cols].astype(f32)).astype(bf16)
-                gh[k, j, :, cols] = h
-                ub[k : k + 1, cols] += rowsum(h.astype(f32))
-                return carry
-
-            return lax.fori_loop(0, units // step, chunk, carry)
-
-        lax.fori_loop(0, 2, side, 0)
+        def chunk(m, carry):
+            cols = pl.ds(pl.multiple_of(m * step, step), step)
+            ga = mm(sides[...], dn[cols, :], NT)
+            h = (ga * slope[:, cols].astype(f32)).astype(bf16)
+            gh[k, :, cols] = h
+            ub[k : k + 1, cols] += rowsum(h.astype(f32))
+            return carry
+
+        lax.fori_loop(0, units // step, chunk, 0)
     up2 = up2()
     up = up0()
-    sib[...] = (mm(gh[0, 1], up[...], NT) + mm(gh[1, 1], up2[...], NT)).astype(bf16)
-    own[...] = mm(gh[0, 0], up[...], NT) + mm(gh[1, 0], up2[...], NT)
+    total = mm(gh[0], up[...], NT) + mm(gh[1], up2[...], NT)
+    sib[...] = total[n:].astype(bf16)
+    own[...] = total[:n]
 
 
 def first_back_kernel(info, *rest):
@@ -560,16 +559,18 @@
     osend.src[1, width : width + 8, :] = (both - high.astype(f32)).astype(bf16)
 
 
-def down_grads_kernel(info, act0, act1, gs, gs2, far_keep, keep, send, scr, *, parts):
-    units = act0.shape[2]
+def down_grads_kernel(info, act0, act1, gs, gs2, far_keep, keep, send, scr, sides, *, parts):
+    units = act0.shape[1]
+    n = gs.shape[0]
+    sides[0:n, :] = gs[...]
+    sides[n : 2 * n, :] = gs2[...]
     block = units // parts
     step = 384
     for k, (act, mine) in enumerate(((act1, far_keep), (act0, keep))):
 
         def chunk(m, carry):
             cols = pl.ds(pl.multiple_of(m * step, step), step)
-            total = mm(act[0, :, cols], gs[...], TN) + mm(act[1, :, cols], gs2[...], TN)
-            total = total.astype(bf16)
+            total = mm(act[:, cols], sides[...], TN).astype(bf16)
             for i in range(step // block):
                 scr[(i & 1) ^ info[3], m * (step // block // 2) + (i >> 1)] = total[i * block : (i + 1) * block]
             return carry
@@ -584,10 +585,9 @@
     lows, (gh_in, okeep, ogot, small, ub, far_keep, far_send, keep, send, sums, scr, both_low) = rest[:4], rest[4:]
     n = lows[0].shape[0]
     for i, x in enumerate(lows):
-        both_low[i // 2, (i % 2) * n : (i % 2 + 1) * n, :] = x[...]
-    low, low2 = both_low.at[0], both_low.at[1]
+        both_low[i * n : (i + 1) * n, :] = x[...]
     gh = ref(gh_in)
-    units = low.shape[1]
+    units = both_low.shape[1]
     block = units // parts
     extra = width // parts
     joint = block + extra
@@ -604,8 +604,7 @@
 
         def chunk(m, carry):
             cols = pl.ds(pl.multiple_of(m * step, step), step)
-            total = mm(low[:, cols], gh[k, 0], TN) + mm(low2[:, cols], gh[k, 1], TN)
-            total = total.astype(bf16)
+            total = mm(both_low[:, cols], gh[k], TN).astype(bf16)
             for i in range(step // block):
                 at = (m * (step // block // 4) + (i >> 2)) * 2 + (i & 1)
                 scr[((i >> 1) & 1) ^ info[4], at, 0:block, :] = total[i * block : (i + 1) * block]
@@ -712,9 +711,9 @@
         vmem=NEAR,
     )
     low2 = [swap(x, "tensor", 1) for x in low]
-    pair = SDS((2, n, units), bf16)
+    pair = SDS((2 * n, units), bf16)
     part = SDS((n, d), f32)
-    sides = pltpu.VMEM((2, n, d), bf16)
+    sides = pltpu.VMEM((2 * n, d), bf16)
     act0, slope0, own, sib = call(
         "feed",
         feed_kernel,
@@ -754,7 +753,7 @@
         feed_back_kernel,
         info,
         [gs_low, gs_low2, slope0, slope1, whole(up_weight), whole(down_weight), *halves],
-        [SDS((2, 2, n, units), bf16), part, SDS((n, d), bf16), SDS((8, d), f32)],
+        [SDS((2, 2 * n, units), bf16), part, SDS((n, d), bf16), SDS((8, d), f32)],
         [sides, *both],
         vmem=NEAR,
     )
@@ -767,7 +766,7 @@
         info,
         [act0, act1, gs_low, gs_low2],
         [[SDS(half_shape, bf16)], [SDS(half_shape, bf16)], [SDS((2, *half_shape), bf16)]],
-        [pltpu.VMEM((2, *half_shape), bf16)],
+        [pltpu.VMEM((2, *half_shape), bf16), sides],
         vmem=NEAR,
         parts=parts,
     )

time: 215 us -> 212 us (0.986)
  starting transfers between devices: 36.2 us -> 33.8 us
    ppermute x38, starting transfers between devices: 36.2 us -> 33.8 us  [swap(): return lax.ppermute(x, axis, [(i, i ^ bit) for i in range(size)])]
  transfers between devices with their start and end apart: 38 -> 38, of which waited for: 18 -> 20; matrix products, arithmetic and copies ran while one was open for 9% -> 9% of each run, Pallas kernels for 34% -> 36%
where the time goes in v7:
time: 212 us
  Pallas kernels  105 us (50%)
  waiting for transfers between devices  41.9 us (20%)
  starting transfers between devices  33.8 us (16%)
  other arithmetic  19.4 us (9%)
  local copies, waits for them, and re-layouts  10.1 us (5%)
    pallas_call x13, Pallas kernels, call(): pl.pallas_call(kernel, out_shape=[pltpu.HBM(o.shape, o.dtype) if i in far...  105 us
    ppermute x38, waiting for transfers between devices, swap(): return lax.ppermute(x, axis, [(i, i ^ bit) for i in range(size)])  41.9 us
    ppermute x38, starting transfers between devices, swap(): return lax.ppermute(x, axis, [(i, i ^ bit) for i in range(size)])  33.8 us
    unnamed x56, local copies, waits for them, and re-layouts  7.15 us
    convert_element_type x4, other arithmetic, halve_sum(): return (kept, summed(other).astype(bf16))  5.34 us
  transfers between devices with their start and end apart: 38, of which 20 were waited for; matrix products, arithmetic and copies ran while one was open for 9% of the time, Pallas kernels for 36%

profile of v7, /device:TPU:0, one launch (start us, length us, event | category | flops | bytes accessed | tf_op | source)
XLA Modules:
  0.0 211.5 jit_solution(8190206788773571713)
XLA Ops:
  0.6 3.4 %prepare.1 = (bf16[200,768]{1,0:T(8,128)(2,1)}, bf16[192,768]{1,0:T(8,128)(2,1)}, bf16[192,768]{1,0:T(8,128)(2,1)}) custom-call(s32[2]{0:T(128)} %lengths_ref.25, s32[1]{0:T(128)} %constant.384.clone.1.which_ref, bf16[192,768]{1,0:T(8,128)(2,1)} %refs_0_.7, bf16[768]{0:T(1024)(128)(2,1)} %refs_1_.4, bf16[768,768]{1,0:T(8,128)(2,1)} %refs_4_.6, ...), custom_call_target="tpu_custom_call" | custom-call | flops 1000 | bytes 1000 | tf_op jit(solution)/shard_map/prepare/pallas_call | solution.py:117
  4.5 2.6 %collective-permute-start.1 = (bf16[200,768]{1,0:T(8,128)(2,1)}, bf16[200,768]{1,0:T(8,128)(2,1)S(1)}, u32[]{:S(2)}, u32[]{:S(2)}) collective-permute-start(bf16[200,768]{1,0:T(8,128)(2,1)} %get-tuple-element.140.refs_11_.refs_4_.refs_16_), channel_id=1, source_target_pairs={{0,2},{1,3},{2,0},{3,1},{4,6},{5,7},{6,4},{7,5},{8,10},{9,11},{10,... | collective-permute-start | bytes 921608 | tf_op jit(solution)/shard_map/ppermute | solution.py:627
  7.2 1.9 collective-permute-start.3
  9.2 16.3 %attend_fwd.1 = (bf16[2,1024,256]{2,1,0:T(8,128)(2,1)}, bf16[2,1024,256]{2,1,0:T(8,128)(2,1)}, bf16[2,1024,192]{2,1,0:T(8,128)(2,1)}, f32[2,4,8,256]{3,2,1,0:T(8...) custom-call(s32[2]{0:T(128)} %lengths_ref.25, ...), custom_call_target="tpu_custom_call" | custom-call | flops 1000 | bytes 1000 | tf_op jit(solution)/shard_map/attend_fwd/pallas_call | solution.py:117
  25.6 2.3 %collective-permute-done.3 = bf16[192,768]{1,0:T(8,128)(2,1)S(1)} collective-permute-done((bf16[192,768]{1,0:T(8,128)(2,1)}, bf16[192,768]{1,0:T(8,128)(2,1)S(1)}, u32[]{:S(2)}, u32[]{:S(2)}) %collective-permute-start.3) | collective-permute-done | bytes 294944 | tf_op jit(solution)/shard_map/ppermute | solution.py:627
  27.9 1.7 collective-permute-start.7
  29.6 1.6 collective-permute-start.8
  31.2 1.5 collective-permute-start.5
  33.0 6.0 %collective-permute-done.5.refs_9_.refs_14_ = bf16[2,192,256]{2,1,0:T(8,128)(2,1)S(1)} collective-permute-done((bf16[2,192,256]{2,1,0:T(8,128)(2,1)}, bf16[2,192,256]{2,1,0:T(8,128)(2,1)S(1)}, u32[]{:S(2)}, u32[]{:S(2)}) %collective-permute-start.5) | collective-permute-done | bytes 196640 | tf_op jit(solution)/shard_map/ppermute | solution.py:627
  39.1 3.4 %collective-permute-done.6.refs_10_.refs_15_ = bf16[2,192,256]{2,1,0:T(8,128)(2,1)S(1)} collective-permute-done((bf16[2,192,256]{2,1,0:T(8,128)(2,1)}, bf16[2,192,256]{2,1,0:T(8,128)(2,1)S(1)}, u32[]{:S(2)}, u32[]{:S(2)}) %collective-permute-start.6) | collective-permute-done | bytes 196640 | tf_op jit(solution)/shard_map/ppermute | solution.py:627
  44.3 4.2 %first_norm.1 = (f32[512,768]{1,0:T(8,128)S(1)}, f32[512,1]{1,0:T(8,128)S(1)}, bf16[256,768]{1,0:T(8,128)(2,1)S(1)}, bf16[256,768]{1,0:T(8,128)(2,1)S(1)}) custom-call(s32[2]{0:T(128)S(1)} %copy-done.6, s32[1]{0:T(128)} %constant.384.clone.1.which_ref, bf16[2,1024,768]{2,1,0:T(8,128)(2,1)} %refs_2_.11, bf16[768]{0:T(1024)(128)(2,1)S(1)} %copy-done.7, ...), custom_call_target="tpu_custom_call" | custom-call | flops 1000 | bytes 1000 | tf_op jit(solution)/shard_map/first_norm/pallas_call | solution.py:117
  49.1 1.2 collective-permute-done.10.refs_2_
  50.9 7.2 %feed.2 = (bf16[1024,768]{1,0:T(8,128)(2,1)S(1)}, bf16[1024,768]{1,0:T(8,128)(2,1)S(1)}, f32[512,768]{1,0:T(8,128)S(1)}, f32[512,768]{1,0:T(8,128)S(1)}) custom-call(s32[2]{0:T(128)S(1)} %copy-done.6, s32[1]{0:T(128)} %constant.384.clone.1.which_ref, bf16[256,768]{1,0:T(8,128)(2,1)S(1)} %get-tuple-element.159.refs_0_, ...), custom_call_target="tpu_custom_call" | custom-call | flops 1000 | bytes 1000 | tf_op jit(solution)/shard_map/feed/pallas_call | solution.py:117
  58.6 6.5 %feed.3 = (bf16[1024,768]{1,0:T(8,128)(2,1)S(1)}, bf16[1024,768]{1,0:T(8,128)(2,1)S(1)}, f32[512,768]{1,0:T(8,128)S(1)}, bf16[512,768]{1,0:T(8,128)(2,1)S(1)}) custom-call(s32[2]{0:T(128)S(1)} %copy-done.6, s32[1]{0:T(128)} %constant.384.clone.1.which_ref, bf16[256,768]{1,0:T(8,128)(2,1)S(1)} %get-tuple-element.159.refs_0_, ...), custom_call_target="tpu_custom_call" | custom-call | flops 1000 | bytes 1000 | tf_op jit(solution)/shard_map/feed/pallas_call | solution.py:117
  65.1 1.2 copy-done.4
  66.2 2.3 %collective-permute-done.14.refs_9_ = bf16[512,768]{1,0:T(8,128)(2,1)S(1)} collective-permute-done((bf16[512,768]{1,0:T(8,128)(2,1)S(1)}, bf16[512,768]{1,0:T(8,128)(2,1)S(1)}, u32[]{:S(2)}, u32[]{:S(2)}) %collective-permute-start.14) | collective-permute-done | bytes 786464 | tf_op jit(solution)/shard_map/ppermute | solution.py:627
  68.5 4.0 %second_norm.1 = (bf16[2,256,768]{2,1,0:T(8,128)(2,1)}, f32[512,768]{1,0:T(8,128)S(1)}, bf16[512,768]{1,0:T(8,128)(2,1)S(1)}, f32[8,768]{1,0:T(8,128)S(1)}) custom-call(s32[2]{0:T(128)S(1)} %copy-done.6, s32[1]{0:T(128)} %constant.384.clone.1.which_ref, bf16[2,256,768]{2,1,0:T(8,128)(2,1)} %refs_0_.9, bf16[768]{0:T(1024)(128)(2,1)S(1)} %copy-done.7, ...), custom_call_target="tpu_custom_call" | custom-call | flops 1000 | bytes 1000 | tf_op jit(solution)/shard_map/second_norm/pallas_call | solution.py:117
  72.8 2.1 %collective-permute-done.15.refs_1_.refs_3_ = bf16[512,768]{1,0:T(8,128)(2,1)S(1)} collective-permute-done((bf16[512,768]{1,0:T(8,128)(2,1)S(1)}, bf16[512,768]{1,0:T(8,128)(2,1)S(1)}, u32[]{:S(2)}, u32[]{:S(2)}) %collective-permute-start.15) | collective-permute-done | bytes 786464 | tf_op jit(solution)/shard_map/ppermute | solution.py:627
  74.9 8.7 %feed_back.1 = (bf16[2,1024,768]{2,1,0:T(8,128)(2,1)S(1)}, f32[512,768]{1,0:T(8,128)S(1)}, bf16[512,768]{1,0:T(8,128)(2,1)S(1)}, f32[8,768]{1,0:T(8,128)S(1)}) custom-call(s32[2]{0:T(128)S(1)} %copy-done.6, s32[1]{0:T(128)} %constant.384.clone.1.which_ref, bf16[512,768]{1,0:T(8,128)(2,1)S(1)} %get-tuple-element.174.refs_0_.refs_2_, ...), custom_call_target="tpu_custom_call" | custom-call | flops 1000 | bytes 1000 | tf_op jit(solution)/shard_map/feed_back/pallas_call | solution.py:117
  83.6 1.7 copy-done
  85.5 2.2 %collective-permute-done.16.refs_9_ = bf16[512,768]{1,0:T(8,128)(2,1)S(1)} collective-permute-done((bf16[512,768]{1,0:T(8,128)(2,1)S(1)}, bf16[512,768]{1,0:T(8,128)(2,1)S(1)}, u32[]{:S(2)}, u32[]{:S(2)}) %collective-permute-start.16) | collective-permute-done | bytes 786464 | tf_op jit(solution)/shard_map/ppermute | solution.py:627
  87.6 6.9 %first_back.1 = (f32[512,768]{1,0:T(8,128)}, bf16[2,192,256]{2,1,0:T(8,128)(2,1)}, bf16[2,192,256]{2,1,0:T(8,128)(2,1)}, bf16[2,192,256]{2,1,0:T(8,128)(2,1)}, b...) custom-call(s32[2]{0:T(128)S(1)} %copy-done.6, ...), custom_call_target="tpu_custom_call" | custom-call | flops 1000 | bytes 1000 | tf_op jit(solution)/shard_map/first_back/pallas_call | solution.py:117
  95.1 1.5 collective-permute-start.18
  96.6 1.4 copy-done.3
  98.0 1.4 copy-done.5
  99.4 5.5 %down_grads.1 = (bf16[4,96,768]{2,1,0:T(8,128)(2,1)}, bf16[4,96,768]{2,1,0:T(8,128)(2,1)}, bf16[2,4,96,768]{3,2,1,0:T(8,128)(2,1)}) custom-call(s32[2]{0:T(128)S(1)} %copy-done.6, s32[1]{0:T(128)} %constant.384.clone.1.which_ref, bf16[1024,768]{1,0:T(8,128)(2,1)S(1)} %copy-done.3, bf16[1024,768]{1,0:T(8,128)(2,1)S(1)} %copy-done.5, ...), custom_call_target="tpu_custom_call" | custom-call | flops 1000 | bytes 1000 | tf_op jit(solution)/shard_map/down_grads/pallas_call | solution.py:117
  105.7 6.8 %up_grads.1 = (bf16[480,768]{1,0:T(8,128)(2,1)}, bf16[496,768]{1,0:T(8,128)(2,1)}, bf16[480,768]{1,0:T(8,128)(2,1)}, bf16[480,768]{1,0:T(8,128)(2,1)}, f32[8,768]{1,0:T(8,128)S(1)}) custom-call(s32[2]{0:T(128)S(1)} %copy-done.6, s32[1]{0:T(128)} %constant.384.clone.1.which_ref, bf16[256,768]{1,0:T(8,128)(2,1)S(1)} %get-tuple-element.159.refs_0_, ...), custom_call_target="tpu_custom_call" | custom-call | flops 1000 | bytes 1000 | tf_op jit(solution)/shard_map/up_grads/pallas_call | solution.py:117
  112.5 1.6 collective-permute-start.21
  114.2 14.0 %attend_bwd.2 = (bf16[2,256,768]{2,1,0:T(8,128)(2,1)}, bf16[2,256,768]{2,1,0:T(8,128)(2,1)}, bf16[3,1024,192]{2,1,0:T(8,128)(2,1)}, f32[1,384]{1,0:T(1,128)}) custom-call(s32[2]{0:T(128)} %lengths_ref.25, s32[1]{0:T(128)} %constant.384.clone.1.which_ref, bf16[3,192,768]{2,1,0:T(8,128)(2,1)} %bitcast.109, bf16[2,1024,256]{2,1,0:T(8,128)(2,1)} %get-tuple-element.168.refs_1_, ...), custom_call_target="tpu_custom_call" | custom-call | flops 20000000000 | bytes 1000 | tf_op jit(solution)/shard_map/attend_bwd/pallas_call | solution.py:117
  128.1 5.6 %collective-permute-done.22 = bf16[2,4,96,768]{3,2,1,0:T(8,128)(2,1)S(1)} collective-permute-done((bf16[2,4,96,768]{3,2,1,0:T(8,128)(2,1)}, bf16[2,4,96,768]{3,2,1,0:T(8,128)(2,1)S(1)}, u32[]{:S(2)}, u32[]{:S(2)}) %collective-permute-start.22) | collective-permute-done | bytes 1179680 | tf_op jit(solution)/shard_map/ppermute | solution.py:627
  134.0 0.9 copy-done.17
  135.1 0.8 pad_maximum_fusion.3
  135.8 1.6 collective-permute-start.24
  137.4 1.5 collective-permute-start.23
  139.6 13.7 %attend_bwd.3 = (bf16[2,256,768]{2,1,0:T(8,128)(2,1)}, bf16[2,256,768]{2,1,0:T(8,128)(2,1)}, bf16[3,1024,192]{2,1,0:T(8,128)(2,1)}, f32[1,384]{1,0:T(1,128)}) custom-call(s32[2]{0:T(128)} %lengths_ref.25, s32[1]{0:T(128)} %constant.385.clone.1.which_ref, bf16[3,192,768]{2,1,0:T(8,128)(2,1)} %bitcast.110, bf16[2,1024,256]{2,1,0:T(8,128)(2,1)} %get-tuple-element.168.refs_1_, ...), custom_call_target="tpu_custom_call" | custom-call | flops 20000000000 | bytes 1000 | tf_op jit(solution)/shard_map/attend_bwd/pallas_call | solution.py:117
  153.4 1.0 collective-permute-done.24
  154.4 0.7 add_add_fusion.1
  155.2 1.9 fusion.10
  157.0 1.1 fusion.13
  158.1 1.1 fusion.5
  159.3 1.5 collective-permute-start.28
  161.4 1.6 collective-permute-start.27
  163.0 7.9 %project_grads.1 = (bf16[576,384]{1,0:T(8,128)(2,1)}, bf16[584,384]{1,0:T(8,128)(2,1)}, f32[1,384]{1,0:T(1,128)}) custom-call(s32[2]{0:T(128)} %lengths_ref.25, s32[1]{0:T(128)} %constant.384.clone.1.which_ref, bf16[2,1024,768]{2,1,0:T(8,128)(2,1)} %refs_2_.11, bf16[3,1024,192]{2,1,0:T(8,128)(2,1)} %get-tuple-element.223.refs_1_, ...), custom_call_target="tpu_custom_call" | custom-call | flops 1000 | bytes 1000 | tf_op jit(solution)/shard_map/project_grads/pallas_call | solution.py:117
  171.1 0.8 collective-permute-done.29
  172.6 1.3 collective-permute-start.31
  173.9 1.9 fusion.7
  175.8 1.2 fusion.15
  177.0 2.9 %collective-permute-start.34 = (bf16[96,768]{1,0:T(8,128)(2,1)S(1)}, bf16[96,768]{1,0:T(8,128)(2,1)S(1)}, u32[]{:S(2)}, u32[]{:S(2)}) collective-permute-start(bf16[96,768]{1,0:T(8,128)(2,1)S(1)} %fusion.15), channel_id=1, source_target_pairs={{0,16},{4,20},{8,24},{12,28},{16,0},{20,4},{24,8},{28,12},{1,17},{... | collective-permute-start | bytes 442376 | tf_op jit(solution)/shard_map/ppermute | solution.py:627
  179.9 1.2 fusion.12
  181.8 1.2 collective-permute-done.31
  183.7 1.9 collective-permute-done.34
  186.9 0.8 collective-permute-start.33
  187.7 3.4 %collective-permute-start.37 = (bf16[136,768]{1,0:T(8,128)(2,1)}, bf16[136,768]{1,0:T(8,128)(2,1)S(1)}, u32[]{:S(2)}, u32[]{:S(2)}) collective-permute-start(bf16[136,768]{1,0:T(8,128)(2,1)} %pad_maximum_fusion.7), channel_id=1, source_target_pairs={{0,16},{4,20},{8,24},{12,28},{16,0},{20,4},{24,8},{28,12},{1,17},{... | collective-permute-start | bytes 626696 | tf_op jit(solution)/shard_map/ppermute | solution.py:627
  191.1 5.4 %collective-permute-done.35 = bf16[290,384]{1,0:T(8,128)(2,1)S(1)} collective-permute-done((bf16[290,384]{1,0:T(8,128)(2,1)S(1)}, bf16[290,384]{1,0:T(8,128)(2,1)S(1)}, u32[]{:S(2)}, u32[]{:S(2)}) %collective-permute-start.35) | collective-permute-done | bytes 222752 | tf_op jit(solution)/shard_map/ppermute | solution.py:627
  196.6 1.0 fusion.16
  197.6 2.4 %collective-permute-done.37 = bf16[136,768]{1,0:T(8,128)(2,1)S(1)} collective-permute-done((bf16[136,768]{1,0:T(8,128)(2,1)}, bf16[136,768]{1,0:T(8,128)(2,1)S(1)}, u32[]{:S(2)}, u32[]{:S(2)}) %collective-permute-start.37) | collective-permute-done | bytes 208928 | tf_op jit(solution)/shard_map/ppermute | solution.py:627
  200.0 1.2 fusion.11
  201.2 0.7 slice.210
  203.3 1.9 fusion.14
  205.1 1.4 fusion.8
  206.6 0.9 pad_maximum_fusion
  207.5 1.5 collective-permute-done.36
  209.7 1.0 fusion.17
  210.8 0.7 pad_maximum_fusion.5
  (126 shorter events, 13.5 us)
Async XLA Ops:
  4.0 23.8 %collective-permute-start = (bf16[200,768]{1,0:T(8,128)(2,1)}, bf16[200,768]{1,0:T(8,128)(2,1)S(1)}, u32[]{:S(2)}, u32[]{:S(2)}) collective-permute-start(bf16[200,768]{1,0:T(8,128)(2,1)} %get-tuple-element.140.refs_11_.refs_4_.refs_16_), channel_id=1, source_target_pairs={{0,1},{1,0},{2,3},{3,2},{4,5},{5,4},{6,7},{7,6},{8,9},{9,8},{10,11... | collective-permute-start | bytes 921608 | tf_op jit(solution)/shard_map/ppermute | solution.py:627
  4.5 23.3 %collective-permute-start.1 = (bf16[200,768]{1,0:T(8,128)(2,1)}, bf16[200,768]{1,0:T(8,128)(2,1)S(1)}, u32[]{:S(2)}, u32[]{:S(2)}) collective-permute-start(bf16[200,768]{1,0:T(8,128)(2,1)} %get-tuple-element.140.refs_11_.refs_4_.refs_16_), channel_id=1, source_target_pairs={{0,2},{1,3},{2,0},{3,1},{4,6},{5,7},{6,4},{7,5},{8,10},{9,11},{10,... | collective-permute-start | bytes 921608 | tf_op jit(solution)/shard_map/ppermute | solution.py:627
  7.1 18.4 %collective-permute-start.2 = (bf16[192,768]{1,0:T(8,128)(2,1)}, bf16[192,768]{1,0:T(8,128)(2,1)S(1)}, u32[]{:S(2)}, u32[]{:S(2)}) collective-permute-start(bf16[192,768]{1,0:T(8,128)(2,1)} %get-tuple-element.141), channel_id=1, source_target_pairs={{0,2},{1,3},{2,0},{3,1},{4,6},{5,7},{6,4},{7,5},{8,10},{9,11},{10,... | collective-permute-start | bytes 884744 | tf_op jit(solution)/shard_map/ppermute | solution.py:627
  7.2 20.6 %collective-permute-start.3 = (bf16[192,768]{1,0:T(8,128)(2,1)}, bf16[192,768]{1,0:T(8,128)(2,1)S(1)}, u32[]{:S(2)}, u32[]{:S(2)}) collective-permute-start(bf16[192,768]{1,0:T(8,128)(2,1)} %get-tuple-element.142), channel_id=1, source_target_pairs={{0,2},{1,3},{2,0},{3,1},{4,6},{5,7},{6,4},{7,5},{8,10},{9,11},{10,... | collective-permute-start | bytes 884744 | tf_op jit(solution)/shard_map/ppermute | solution.py:627
  25.5 18.8 %copy-start.6 = (s32[2]{0:T(128)S(1)}, s32[2]{0:T(128)}, u32[]{:S(2)}) copy-start(s32[2]{0:T(128)} %lengths_ref.25) | copy-start | bytes 28
  25.5 18.8 %copy-start.7 = (bf16[768]{0:T(1024)(128)(2,1)S(1)}, bf16[768]{0:T(1024)(128)(2,1)}, u32[]{:S(2)}) copy-start(bf16[768]{0:T(1024)(128)(2,1)} %refs_0_.10) | copy-start | bytes 4612
  25.5 18.8 %copy-start.8 = (bf16[768]{0:T(1024)(128)(2,1)S(1)}, bf16[768]{0:T(1024)(128)(2,1)}, u32[]{:S(2)}) copy-start(bf16[768]{0:T(1024)(128)(2,1)} %refs_1_.7) | copy-start | bytes 4612
  25.5 18.8 %copy-start.9 = (bf16[768]{0:T(1024)(128)(2,1)S(1)}, bf16[768]{0:T(1024)(128)(2,1)}, u32[]{:S(2)}) copy-start(bf16[768]{0:T(1024)(128)(2,1)} %refs_2_.10) | copy-start | bytes 4612
  25.5 18.8 %copy-start.10 = (bf16[768]{0:T(1024)(128)(2,1)S(1)}, bf16[768]{0:T(1024)(128)(2,1)}, u32[]{:S(2)}) copy-start(bf16[768]{0:T(1024)(128)(2,1)} %refs_3_.7) | copy-start | bytes 4612
  25.5 18.8 %copy-start.11 = (bf16[768]{0:T(1024)(128)(2,1)S(1)}, bf16[768]{0:T(1024)(128)(2,1)}, u32[]{:S(2)}) copy-start(bf16[768]{0:T(1024)(128)(2,1)} %refs_4_.7) | copy-start | bytes 4612
  25.6 18.8 %copy-start.12 = (bf16[768]{0:T(1024)(128)(2,1)S(1)}, bf16[768]{0:T(1024)(128)(2,1)}, u32[]{:S(2)}) copy-start(bf16[768]{0:T(1024)(128)(2,1)} %refs_5_.9) | copy-start | bytes 4612
  27.9 14.7 %collective-permute-start.7 = (bf16[192,768]{1,0:T(8,128)(2,1)S(1)}, bf16[192,768]{1,0:T(8,128)(2,1)S(1)}, u32[]{:S(2)}, u32[]{:S(2)}) collective-permute-start(bf16[192,768]{1,0:T(8,128)(2,1)S(1)} %collective-permute-done.2), channel_id=1, source_target_pairs={{0,4},{4,0},{8,12},{12,8},{16,20},{20,16},{24,28},{28,24},{1,5},{5... | collective-permute-start | bytes 884744 | tf_op jit(solution)/shard_map/ppermute | solution.py:627
  29.6 12.9 %collective-permute-start.8 = (bf16[192,768]{1,0:T(8,128)(2,1)S(1)}, bf16[192,768]{1,0:T(8,128)(2,1)S(1)}, u32[]{:S(2)}, u32[]{:S(2)}) collective-permute-start(bf16[192,768]{1,0:T(8,128)(2,1)S(1)} %collective-permute-done.3), channel_id=1, source_target_pairs={{0,8},{4,12},{8,0},{12,4},{16,24},{20,28},{24,16},{28,20},{1,9},{5... | collective-permute-start | bytes 884744 | tf_op jit(solution)/shard_map/ppermute | solution.py:627
  31.2 1.9 collective-permute-start.4
  31.2 7.9 %collective-permute-start.5 = (bf16[2,192,256]{2,1,0:T(8,128)(2,1)}, bf16[2,192,256]{2,1,0:T(8,128)(2,1)S(1)}, u32[]{:S(2)}, u32[]{:S(2)}) collective-permute-start(bf16[2,192,256]{2,1,0:T(8,128)(2,1)} %get-tuple-element.145), channel_id=1, source_target_pairs={{0,2},{1,3},{2,0},{3,1},{4,6},{5,7},{6,4},{7,5},{8,10},{9,11},{10,... | collective-permute-start | bytes 589832 | tf_op jit(solution)/shard_map/ppermute | solution.py:627
  32.7 9.8 %collective-permute-start.6 = (bf16[2,192,256]{2,1,0:T(8,128)(2,1)}, bf16[2,192,256]{2,1,0:T(8,128)(2,1)S(1)}, u32[]{:S(2)}, u32[]{:S(2)}) collective-permute-start(bf16[2,192,256]{2,1,0:T(8,128)(2,1)} %get-tuple-element.146), channel_id=1, source_target_pairs={{0,3},{1,2},{2,1},{3,0},{4,7},{5,6},{6,5},{7,4},{8,11},{9,10},{10,... | collective-permute-start | bytes 589832 | tf_op jit(solution)/shard_map/ppermute | solution.py:627
  42.6 1.7 collective-permute-start.9
  42.9 15.5 %collective-permute-start.12 = (bf16[384,768]{1,0:T(8,128)(2,1)S(1)}, bf16[384,768]{1,0:T(8,128)(2,1)S(1)}, u32[]{:S(2)}, u32[]{:S(2)}) collective-permute-start(bf16[384,768]{1,0:T(8,128)(2,1)S(1)} %get-tuple-element.161.refs_5_.refs_6_), channel_id=1, source_target_pairs={{0,8},{4,12},{8,0},{12,4},{16,24},{20,28},{24,16},{28,20},{1,9},{5... | collective-permute-start | bytes 1769480 | tf_op jit(solution)/shard_map/ppermute | solution.py:627
  43.3 15.3 %collective-permute-start.13 = (bf16[384,768]{1,0:T(8,128)(2,1)S(1)}, bf16[384,768]{1,0:T(8,128)(2,1)S(1)}, u32[]{:S(2)}, u32[]{:S(2)}) collective-permute-start(bf16[384,768]{1,0:T(8,128)(2,1)S(1)} %get-tuple-element.162.refs_7_.refs_8_), channel_id=1, source_target_pairs={{0,4},{4,0},{8,12},{12,8},{16,20},{20,16},{24,28},{28,24},{1,5},{5... | collective-permute-start | bytes 1769480 | tf_op jit(solution)/shard_map/ppermute | solution.py:627
  48.5 1.8 collective-permute-start.10
  48.8 2.1 collective-permute-start.11
  58.1 7.0 %copy-start.2 = (bf16[1024,768]{1,0:T(8,128)(2,1)}, bf16[1024,768]{1,0:T(8,128)(2,1)S(1)}, u32[]{:S(2)}) copy-start(bf16[1024,768]{1,0:T(8,128)(2,1)S(1)} %get-tuple-element.201.refs_0_) | copy-start | bytes 4718596
  65.1 1.2 copy-start.4
  66.2 2.3 %collective-permute-start.14 = (bf16[512,768]{1,0:T(8,128)(2,1)S(1)}, bf16[512,768]{1,0:T(8,128)(2,1)S(1)}, u32[]{:S(2)}, u32[]{:S(2)}) collective-permute-start(bf16[512,768]{1,0:T(8,128)(2,1)S(1)} %get-tuple-element.166), channel_id=1, source_target_pairs={{0,1},{1,0},{2,3},{3,2},{4,5},{5,4},{6,7},{7,6},{8,9},{9,8},{10,11... | collective-permute-start | bytes 2359304 | tf_op jit(solution)/shard_map/ppermute | solution.py:627
  72.6 2.4 %collective-permute-start.15 = (bf16[512,768]{1,0:T(8,128)(2,1)S(1)}, bf16[512,768]{1,0:T(8,128)(2,1)S(1)}, u32[]{:S(2)}, u32[]{:S(2)}) collective-permute-start(bf16[512,768]{1,0:T(8,128)(2,1)S(1)} %get-tuple-element.174.refs_0_.refs_2_), channel_id=1, source_target_pairs={{0,1},{1,0},{2,3},{3,2},{4,5},{5,4},{6,7},{7,6},{8,9},{9,8},{10,11... | collective-permute-start | bytes 2359304 | tf_op jit(solution)/shard_map/ppermute | solution.py:627
  83.6 1.7 copy-start
  85.3 2.3 %collective-permute-start.16 = (bf16[512,768]{1,0:T(8,128)(2,1)S(1)}, bf16[512,768]{1,0:T(8,128)(2,1)S(1)}, u32[]{:S(2)}, u32[]{:S(2)}) collective-permute-start(bf16[512,768]{1,0:T(8,128)(2,1)S(1)} %get-tuple-element.178), channel_id=1, source_target_pairs={{0,1},{1,0},{2,3},{3,2},{4,5},{5,4},{6,7},{7,6},{8,9},{9,8},{10,11... | collective-permute-start | bytes 2359304 | tf_op jit(solution)/shard_map/ppermute | solution.py:627
  94.5 11.1 %collective-permute-start.20 = (bf16[2,200,768]{2,1,0:T(8,128)(2,1)}, bf16[2,200,768]{2,1,0:T(8,128)(2,1)}, u32[]{:S(2)}, u32[]{:S(2)}) collective-permute-start(bf16[2,200,768]{2,1,0:T(8,128)(2,1)} %get-tuple-element.187), channel_id=1, source_target_pairs={{0,1},{1,0},{2,3},{3,2},{4,5},{5,4},{6,7},{7,6},{8,9},{9,8},{10,11... | collective-permute-start | bytes 1843208 | tf_op jit(solution)/shard_map/ppermute | solution.py:627
  94.7 17.7 %collective-permute-start.17 = (bf16[2,192,256]{2,1,0:T(8,128)(2,1)}, bf16[2,192,256]{2,1,0:T(8,128)(2,1)S(1)}, u32[]{:S(2)}, u32[]{:S(2)}) collective-permute-start(bf16[2,192,256]{2,1,0:T(8,128)(2,1)} %get-tuple-element.182), channel_id=1, source_target_pairs={{0,1},{1,0},{2,3},{3,2},{4,5},{5,4},{6,7},{7,6},{8,9},{9,8},{10,11... | collective-permute-start | bytes 589832 | tf_op jit(solution)/shard_map/ppermute | solution.py:627
  95.1 17.4 %collective-permute-start.18 = (bf16[2,192,256]{2,1,0:T(8,128)(2,1)}, bf16[2,192,256]{2,1,0:T(8,128)(2,1)}, u32[]{:S(2)}, u32[]{:S(2)}) collective-permute-start(bf16[2,192,256]{2,1,0:T(8,128)(2,1)} %get-tuple-element.183), channel_id=1, source_target_pairs={{0,2},{1,3},{2,0},{3,1},{4,6},{5,7},{6,4},{7,5},{8,10},{9,11},{10,... | collective-permute-start | bytes 589832 | tf_op jit(solution)/shard_map/ppermute | solution.py:627
  96.6 15.9 %collective-permute-start.19 = (bf16[2,192,256]{2,1,0:T(8,128)(2,1)}, bf16[2,192,256]{2,1,0:T(8,128)(2,1)}, u32[]{:S(2)}, u32[]{:S(2)}) collective-permute-start(bf16[2,192,256]{2,1,0:T(8,128)(2,1)} %get-tuple-element.184), channel_id=1, source_target_pairs={{0,3},{1,2},{2,1},{3,0},{4,7},{5,6},{6,5},{7,4},{8,11},{9,10},{10,... | collective-permute-start | bytes 589832 | tf_op jit(solution)/shard_map/ppermute | solution.py:627
  96.6 1.4 copy-start.3
  98.0 1.4 copy-start.5
  99.4 6.2 %copy-start.1 = (bf16[2,1024,768]{2,1,0:T(8,128)(2,1)S(1)}, bf16[2,1024,768]{2,1,0:T(8,128)(2,1)}, u32[]{:S(2)}) copy-start(bf16[2,1024,768]{2,1,0:T(8,128)(2,1)} %copy-done) | copy-start | bytes 9437188
  105.0 28.8 %collective-permute-start.22 = (bf16[2,4,96,768]{3,2,1,0:T(8,128)(2,1)}, bf16[2,4,96,768]{3,2,1,0:T(8,128)(2,1)S(1)}, u32[]{:S(2)}, u32[]{:S(2)}) collective-permute-start(bf16[2,4,96,768]{3,2,1,0:T(8,128)(2,1)} %get-tuple-element.206), channel_id=1, source_target_pairs={{0,4},{4,0},{8,12},{12,8},{16,20},{20,16},{24,28},{28,24},{1,5},{5... | collective-permute-start | bytes 3538952 | tf_op jit(solution)/shard_map/ppermute | solution.py:627
  112.5 1.7 copy-start.27
  112.5 21.2 %collective-permute-start.21 = (bf16[496,768]{1,0:T(8,128)(2,1)}, bf16[496,768]{1,0:T(8,128)(2,1)S(1)}, u32[]{:S(2)}, u32[]{:S(2)}) collective-permute-start(bf16[496,768]{1,0:T(8,128)(2,1)} %get-tuple-element.205), channel_id=1, source_target_pairs={{0,8},{4,12},{8,0},{12,4},{16,24},{20,28},{24,16},{28,20},{1,9},{5... | collective-permute-start | bytes 2285576 | tf_op jit(solution)/shard_map/ppermute | solution.py:627
  128.1 5.7 %copy-start.19 = (bf16[4,96,768]{2,1,0:T(8,128)(2,1)S(1)}, bf16[4,96,768]{2,1,0:T(8,128)(2,1)}, u32[]{:S(2)}) copy-start(bf16[4,96,768]{2,1,0:T(8,128)(2,1)} %get-tuple-element.203) | copy-start | bytes 1769476
  135.8 19.3 %copy-start.18 = (bf16[480,768]{1,0:T(8,128)(2,1)S(1)}, bf16[480,768]{1,0:T(8,128)(2,1)}, u32[]{:S(2)}) copy-start(bf16[480,768]{1,0:T(8,128)(2,1)} %get-tuple-element.228) | copy-start | bytes 2211844
  135.8 18.6 %collective-permute-start.24 = (bf16[480,768]{1,0:T(8,128)(2,1)}, bf16[480,768]{1,0:T(8,128)(2,1)}, u32[]{:S(2)}, u32[]{:S(2)}) collective-permute-start(bf16[480,768]{1,0:T(8,128)(2,1)} %get-tuple-element.219), channel_id=1, source_target_pairs={{0,8},{4,12},{8,0},{12,4},{16,24},{20,28},{24,16},{28,20},{1,9},{5... | collective-permute-start | bytes 2211848 | tf_op jit(solution)/shard_map/ppermute | solution.py:627
  137.4 15.9 %collective-permute-start.23 = (bf16[4,96,768]{2,1,0:T(8,128)(2,1)S(1)}, bf16[4,96,768]{2,1,0:T(8,128)(2,1)}, u32[]{:S(2)}, u32[]{:S(2)}) collective-permute-start(bf16[4,96,768]{2,1,0:T(8,128)(2,1)S(1)} %fusion), channel_id=1, source_target_pairs={{0,2},{1,3},{2,0},{3,1},{4,6},{5,7},{6,4},{7,5},{8,10},{9,11},{10,... | collective-permute-start | bytes 1769480 | tf_op jit(solution)/shard_map/ppermute | solution.py:627
  138.9 14.4 %collective-permute-start.25 = (bf16[256,768]{1,0:T(8,128)(2,1)}, bf16[256,768]{1,0:T(8,128)(2,1)}, u32[]{:S(2)}, u32[]{:S(2)}) collective-permute-start(bf16[256,768]{1,0:T(8,128)(2,1)} %pad_maximum_fusion.3), channel_id=1, source_target_pairs={{0,4},{4,0},{8,12},{12,8},{16,20},{20,16},{24,28},{28,24},{1,5},{5... | collective-permute-start | bytes 1179656 | tf_op jit(solution)/shard_map/ppermute | solution.py:627
  139.5 14.8 %collective-permute-start.26 = (bf16[2,256,768]{2,1,0:T(8,128)(2,1)}, bf16[2,256,768]{2,1,0:T(8,128)(2,1)S(1)}, u32[]{:S(2)}, u32[]{:S(2)}) collective-permute-start(bf16[2,256,768]{2,1,0:T(8,128)(2,1)} %get-tuple-element.221), channel_id=1, source_target_pairs={{0,1},{1,0},{2,3},{3,2},{4,5},{5,4},{6,7},{7,6},{8,9},{9,8},{10,11... | collective-permute-start | bytes 2359304 | tf_op jit(solution)/shard_map/ppermute | solution.py:627
  153.3 3.8 %copy-start.20 = (bf16[4,96,768]{2,1,0:T(8,128)(2,1)S(1)}, bf16[4,96,768]{2,1,0:T(8,128)(2,1)}, u32[]{:S(2)}) copy-start(bf16[4,96,768]{2,1,0:T(8,128)(2,1)} %get-tuple-element.225) | copy-start | bytes 1769476
  154.4 19.5 %collective-permute-start.32 = (bf16[2,256,768]{2,1,0:T(8,128)(2,1)}, bf16[2,256,768]{2,1,0:T(8,128)(2,1)}, u32[]{:S(2)}, u32[]{:S(2)}) collective-permute-start(bf16[2,256,768]{2,1,0:T(8,128)(2,1)} %get-tuple-element.242), channel_id=1, source_target_pairs={{0,1},{1,0},{2,3},{3,2},{4,5},{5,4},{6,7},{7,6},{8,9},{9,8},{10,11... | collective-permute-start | bytes 2359304 | tf_op jit(solution)/shard_map/ppermute | solution.py:627
  159.3 12.6 %collective-permute-start.28 = (bf16[256,768]{1,0:T(8,128)(2,1)S(1)}, bf16[256,768]{1,0:T(8,128)(2,1)S(1)}, u32[]{:S(2)}, u32[]{:S(2)}) collective-permute-start(bf16[256,768]{1,0:T(8,128)(2,1)S(1)} %pad_maximum_fusion.4), channel_id=1, source_target_pairs={{0,2},{1,3},{2,0},{3,1},{4,6},{5,7},{6,4},{7,5},{8,10},{9,11},{10,... | collective-permute-start | bytes 1179656 | tf_op jit(solution)/shard_map/ppermute | solution.py:627
  160.8 11.0 %collective-permute-start.29 = (bf16[2,120,768]{2,1,0:T(8,128)(2,1)}, bf16[2,120,768]{2,1,0:T(8,128)(2,1)}, u32[]{:S(2)}, u32[]{:S(2)}) collective-permute-start(bf16[2,120,768]{2,1,0:T(8,128)(2,1)} %fusion.10), channel_id=1, source_target_pairs={{0,4},{4,0},{8,12},{12,8},{16,20},{20,16},{24,28},{28,24},{1,5},{5... | collective-permute-start | bytes 1105928 | tf_op jit(solution)/shard_map/ppermute | solution.py:627
  161.4 9.6 %collective-permute-start.27 = (bf16[2,96,768]{2,1,0:T(8,128)(2,1)S(1)}, bf16[2,96,768]{2,1,0:T(8,128)(2,1)}, u32[]{:S(2)}, u32[]{:S(2)}) collective-permute-start(bf16[2,96,768]{2,1,0:T(8,128)(2,1)S(1)} %fusion.13), channel_id=1, source_target_pairs={{0,8},{4,12},{8,0},{12,4},{16,24},{20,28},{24,16},{28,20},{1,9},{5... | collective-permute-start | bytes 884744 | tf_op jit(solution)/shard_map/ppermute | solution.py:627
  163.0 8.0 %copy-start.14 = (bf16[2,256,768]{2,1,0:T(8,128)(2,1)S(1)}, bf16[2,256,768]{2,1,0:T(8,128)(2,1)}, u32[]{:S(2)}) copy-start(bf16[2,256,768]{2,1,0:T(8,128)(2,1)} %get-tuple-element.200) | copy-start | bytes 2359300
  163.0 10.9 %copy-start.15 = (bf16[2,256,768]{2,1,0:T(8,128)(2,1)S(1)}, bf16[2,256,768]{2,1,0:T(8,128)(2,1)}, u32[]{:S(2)}) copy-start(bf16[2,256,768]{2,1,0:T(8,128)(2,1)} %get-tuple-element.241) | copy-start | bytes 2359300
  171.9 11.8 %collective-permute-start.30 = (bf16[584,384]{1,0:T(8,128)(2,1)}, bf16[584,384]{1,0:T(8,128)(2,1)S(1)}, u32[]{:S(2)}, u32[]{:S(2)}) collective-permute-start(bf16[584,384]{1,0:T(8,128)(2,1)} %get-tuple-element.237), channel_id=1, source_target_pairs={{0,4},{4,0},{8,12},{12,8},{16,20},{20,16},{24,28},{28,24},{1,5},{5... | collective-permute-start | bytes 1345544 | tf_op jit(solution)/shard_map/ppermute | solution.py:627
  172.6 10.4 %collective-permute-start.31 = (bf16[256,768]{1,0:T(8,128)(2,1)S(1)}, bf16[256,768]{1,0:T(8,128)(2,1)S(1)}, u32[]{:S(2)}, u32[]{:S(2)}) collective-permute-start(bf16[256,768]{1,0:T(8,128)(2,1)S(1)} %fusion.6), channel_id=1, source_target_pairs={{0,2},{1,3},{2,0},{3,1},{4,6},{5,7},{6,4},{7,5},{8,10},{9,11},{10,... | collective-permute-start | bytes 1179656 | tf_op jit(solution)/shard_map/ppermute | solution.py:627
  175.8 9.9 %copy-start.26 = (f32[1,384]{1,0:T(1,128)S(1)}, f32[1,384]{1,0:T(1,128)}, u32[]{:S(2)}) copy-start(f32[1,384]{1,0:T(1,128)} %get-tuple-element.253) | copy-start | bytes 4612
  175.8 9.9 %copy-start.21 = (bf16[576,384]{1,0:T(8,128)(2,1)S(1)}, bf16[576,384]{1,0:T(8,128)(2,1)}, u32[]{:S(2)}) copy-start(bf16[576,384]{1,0:T(8,128)(2,1)} %get-tuple-element.247) | copy-start | bytes 1327108
  177.0 8.6 %collective-permute-start.34 = (bf16[96,768]{1,0:T(8,128)(2,1)S(1)}, bf16[96,768]{1,0:T(8,128)(2,1)S(1)}, u32[]{:S(2)}, u32[]{:S(2)}) collective-permute-start(bf16[96,768]{1,0:T(8,128)(2,1)S(1)} %fusion.15), channel_id=1, source_target_pairs={{0,16},{4,20},{8,24},{12,28},{16,0},{20,4},{24,8},{28,12},{1,17},{... | collective-permute-start | bytes 442376 | tf_op jit(solution)/shard_map/ppermute | solution.py:627
  183.0 2.9 %copy-start.22 = (bf16[256,768]{1,0:T(8,128)(2,1)}, bf16[256,768]{1,0:T(8,128)(2,1)S(1)}, u32[]{:S(2)}) copy-start(bf16[256,768]{1,0:T(8,128)(2,1)S(1)} %collective-permute-done.31) | copy-start | bytes 1179652
  186.3 10.2 %collective-permute-start.35 = (bf16[290,384]{1,0:T(8,128)(2,1)S(1)}, bf16[290,384]{1,0:T(8,128)(2,1)S(1)}, u32[]{:S(2)}, u32[]{:S(2)}) collective-permute-start(bf16[290,384]{1,0:T(8,128)(2,1)S(1)} %pad_maximum_fusion.6), channel_id=1, source_target_pairs={{0,8},{4,12},{8,0},{12,4},{16,24},{20,28},{24,16},{28,20},{1,9},{5... | collective-permute-start | bytes 668168 | tf_op jit(solution)/shard_map/ppermute | solution.py:627
  186.9 18.2 %collective-permute-start.33 = (bf16[256,768]{1,0:T(8,128)(2,1)}, bf16[256,768]{1,0:T(8,128)(2,1)S(1)}, u32[]{:S(2)}, u32[]{:S(2)}) collective-permute-start(bf16[256,768]{1,0:T(8,128)(2,1)} %fusion.7), channel_id=1, source_target_pairs={{0,2},{1,3},{2,0},{3,1},{4,6},{5,7},{6,4},{7,5},{8,10},{9,11},{10,... | collective-permute-start | bytes 1179656 | tf_op jit(solution)/shard_map/ppermute | solution.py:627
  187.7 12.3 %collective-permute-start.37 = (bf16[136,768]{1,0:T(8,128)(2,1)}, bf16[136,768]{1,0:T(8,128)(2,1)S(1)}, u32[]{:S(2)}, u32[]{:S(2)}) collective-permute-start(bf16[136,768]{1,0:T(8,128)(2,1)} %pad_maximum_fusion.7), channel_id=1, source_target_pairs={{0,16},{4,20},{8,24},{12,28},{16,0},{20,4},{24,8},{28,12},{1,17},{... | collective-permute-start | bytes 626696 | tf_op jit(solution)/shard_map/ppermute | solution.py:627
  196.5 6.8 %copy-start.25 = (bf16[96,768]{1,0:T(8,128)(2,1)S(1)}, bf16[96,768]{1,0:T(8,128)(2,1)}, u32[]{:S(2)}) copy-start(bf16[96,768]{1,0:T(8,128)(2,1)} %copy-done.24) | copy-start | bytes 442372
  197.6 7.6 %copy-start.13 = (f32[512,768]{1,0:T(8,128)S(1)}, f32[512,768]{1,0:T(8,128)}, u32[]{:S(2)}) copy-start(f32[512,768]{1,0:T(8,128)} %get-tuple-element.240) | copy-start | bytes 4718596
  197.6 7.5 %copy-start.16 = (bf16[2,256,768]{2,1,0:T(8,128)(2,1)S(1)}, bf16[2,256,768]{2,1,0:T(8,128)(2,1)}, u32[]{:S(2)}) copy-start(bf16[2,256,768]{2,1,0:T(8,128)(2,1)} %get-tuple-element.241) | copy-start | bytes 2359300
  197.6 7.5 %copy-start.23 = (bf16[256,768]{1,0:T(8,128)(2,1)S(1)}, bf16[256,768]{1,0:T(8,128)(2,1)}, u32[]{:S(2)}) copy-start(bf16[256,768]{1,0:T(8,128)(2,1)} %copy-done.22) | copy-start | bytes 1179652
  202.6 6.4 %collective-permute-start.36 = (bf16[146,384]{1,0:T(8,128)(2,1)S(1)}, bf16[146,384]{1,0:T(8,128)(2,1)S(1)}, u32[]{:S(2)}, u32[]{:S(2)}) collective-permute-start(bf16[146,384]{1,0:T(8,128)(2,1)S(1)} %pad_maximum_fusion.8), channel_id=1, source_target_pairs={{0,16},{4,20},{8,24},{12,28},{16,0},{20,4},{24,8},{28,12},{1,17},{... | collective-permute-start | bytes 336392 | tf_op jit(solution)/shard_map/ppermute | solution.py:627
  (2 other events, 1.8 us)

commit v8 on v7

--- a/solution.py
+++ b/solution.py
@@ -771,6 +771,7 @@
         parts=parts,
     )
     down_got = swap(down_send, "dp", 1)
+    got, down_far_keep = after(got, down_far_keep)
     gfi, g0, g1, g2, g3, okeep, osend, small1 = call(
         "first_back",
         first_back_kernel,

time: 212 us -> 205 us (0.967)
  local copies, waits for them, and re-layouts: 10.1 us -> 6.29 us
  waiting for transfers between devices: 41.9 us -> 39.4 us
    unnamed x56 -> x48, local copies, waits for them, and re-layouts: 7.15 us -> 3.32 us
    ppermute x38, waiting for transfers between devices: 41.9 us -> 39.4 us  [swap(): return lax.ppermute(x, axis, [(i, i ^ bit) for i in range(size)])]
  transfers between devices with their start and end apart: 38 -> 38, of which waited for: 20 -> 21; matrix products, arithmetic and copies ran while one was open for 9% -> 9% of each run, Pallas kernels for 36% -> 36%
where the time goes in v8:
time: 205 us
  Pallas kernels  104 us (51%)
  waiting for transfers between devices  39.4 us (19%)
  starting transfers between devices  34.1 us (17%)
  other arithmetic  19.4 us (9%)
  local copies, waits for them, and re-layouts  6.29 us (3%)
    pallas_call x13, Pallas kernels, call(): pl.pallas_call(kernel, out_shape=[pltpu.HBM(o.shape, o.dtype) if i in far...  104 us
    ppermute x38, waiting for transfers between devices, swap(): return lax.ppermute(x, axis, [(i, i ^ bit) for i in range(size)])  39.4 us
    ppermute x38, starting transfers between devices, swap(): return lax.ppermute(x, axis, [(i, i ^ bit) for i in range(size)])  34.1 us
    convert_element_type x4, other arithmetic, halve_sum(): return (kept, summed(other).astype(bf16))  5.32 us
    add x4, other arithmetic, summed(): return sum((p.astype(f32) for p in parts))  4.22 us
  transfers between devices with their start and end apart: 38, of which 21 were waited for; matrix products, arithmetic and copies ran while one was open for 9% of the time, Pallas kernels for 36%

profile of v8, /device:TPU:0, one launch (start us, length us, event | category | flops | bytes accessed | tf_op | source)
XLA Modules:
  0.0 204.6 jit_solution(841028437382521937)
XLA Ops:
  0.6 3.4 %prepare.1 = (bf16[200,768]{1,0:T(8,128)(2,1)}, bf16[192,768]{1,0:T(8,128)(2,1)}, bf16[192,768]{1,0:T(8,128)(2,1)}) custom-call(s32[2]{0:T(128)} %lengths_ref.25, s32[1]{0:T(128)} %constant.384.clone.1.which_ref, bf16[192,768]{1,0:T(8,128)(2,1)} %refs_0_.7, bf16[768]{0:T(1024)(128)(2,1)} %refs_1_.4, bf16[768,768]{1,0:T(8,128)(2,1)} %refs_4_.6, ...), custom_call_target="tpu_custom_call" | custom-call | flops 1000 | bytes 1000 | tf_op jit(solution)/shard_map/prepare/pallas_call | solution.py:117
  4.6 2.6 %collective-permute-start.1 = (bf16[200,768]{1,0:T(8,128)(2,1)}, bf16[200,768]{1,0:T(8,128)(2,1)S(1)}, u32[]{:S(2)}, u32[]{:S(2)}) collective-permute-start(bf16[200,768]{1,0:T(8,128)(2,1)} %get-tuple-element.142.refs_11_.refs_4_.refs_16_), channel_id=1, source_target_pairs={{0,2},{1,3},{2,0},{3,1},{4,6},{5,7},{6,4},{7,5},{8,10},{9,11},{10,... | collective-permute-start | bytes 921608 | tf_op jit(solution)/shard_map/ppermute | solution.py:627
  7.2 1.9 collective-permute-start.3
  9.2 16.3 %attend_fwd.1 = (bf16[2,1024,256]{2,1,0:T(8,128)(2,1)}, bf16[2,1024,256]{2,1,0:T(8,128)(2,1)}, bf16[2,1024,192]{2,1,0:T(8,128)(2,1)}, f32[2,4,8,256]{3,2,1,0:T(8...) custom-call(s32[2]{0:T(128)} %lengths_ref.25, ...), custom_call_target="tpu_custom_call" | custom-call | flops 1000 | bytes 1000 | tf_op jit(solution)/shard_map/attend_fwd/pallas_call | solution.py:117
  25.6 2.3 %collective-permute-done.3 = bf16[192,768]{1,0:T(8,128)(2,1)S(1)} collective-permute-done((bf16[192,768]{1,0:T(8,128)(2,1)}, bf16[192,768]{1,0:T(8,128)(2,1)S(1)}, u32[]{:S(2)}, u32[]{:S(2)}) %collective-permute-start.3) | collective-permute-done | bytes 294944 | tf_op jit(solution)/shard_map/ppermute | solution.py:627
  27.9 1.7 collective-permute-start.7
  29.6 1.6 collective-permute-start.8
  31.2 1.5 collective-permute-start.5
  33.0 6.0 %collective-permute-done.5.refs_9_.refs_14_ = bf16[2,192,256]{2,1,0:T(8,128)(2,1)S(1)} collective-permute-done((bf16[2,192,256]{2,1,0:T(8,128)(2,1)}, bf16[2,192,256]{2,1,0:T(8,128)(2,1)S(1)}, u32[]{:S(2)}, u32[]{:S(2)}) %collective-permute-start.5) | collective-permute-done | bytes 196640 | tf_op jit(solution)/shard_map/ppermute | solution.py:627
  39.1 3.4 %collective-permute-done.6.refs_10_.refs_15_ = bf16[2,192,256]{2,1,0:T(8,128)(2,1)S(1)} collective-permute-done((bf16[2,192,256]{2,1,0:T(8,128)(2,1)}, bf16[2,192,256]{2,1,0:T(8,128)(2,1)S(1)}, u32[]{:S(2)}, u32[]{:S(2)}) %collective-permute-start.6) | collective-permute-done | bytes 196640 | tf_op jit(solution)/shard_map/ppermute | solution.py:627
  44.3 4.2 %first_norm.1 = (f32[512,768]{1,0:T(8,128)S(1)}, f32[512,1]{1,0:T(8,128)S(1)}, bf16[256,768]{1,0:T(8,128)(2,1)S(1)}, bf16[256,768]{1,0:T(8,128)(2,1)S(1)}) custom-call(s32[2]{0:T(128)S(1)} %copy-done.2, s32[1]{0:T(128)} %constant.384.clone.1.which_ref, bf16[2,1024,768]{2,1,0:T(8,128)(2,1)} %refs_2_.11, bf16[768]{0:T(1024)(128)(2,1)S(1)} %copy-done.3, ...), custom_call_target="tpu_custom_call" | custom-call | flops 1000 | bytes 1000 | tf_op jit(solution)/shard_map/first_norm/pallas_call | solution.py:117
  49.1 1.2 collective-permute-done.10.refs_2_
  50.9 7.2 %feed.2 = (bf16[1024,768]{1,0:T(8,128)(2,1)S(1)}, bf16[1024,768]{1,0:T(8,128)(2,1)S(1)}, f32[512,768]{1,0:T(8,128)S(1)}, f32[512,768]{1,0:T(8,128)S(1)}) custom-call(s32[2]{0:T(128)S(1)} %copy-done.2, s32[1]{0:T(128)} %constant.384.clone.1.which_ref, bf16[256,768]{1,0:T(8,128)(2,1)S(1)} %get-tuple-element.161.refs_0_, ...), custom_call_target="tpu_custom_call" | custom-call | flops 1000 | bytes 1000 | tf_op jit(solution)/shard_map/feed/pallas_call | solution.py:117
  58.6 6.5 %feed.3 = (bf16[1024,768]{1,0:T(8,128)(2,1)S(1)}, bf16[1024,768]{1,0:T(8,128)(2,1)S(1)}, f32[512,768]{1,0:T(8,128)S(1)}, bf16[512,768]{1,0:T(8,128)(2,1)S(1)}) custom-call(s32[2]{0:T(128)S(1)} %copy-done.2, s32[1]{0:T(128)} %constant.384.clone.1.which_ref, bf16[256,768]{1,0:T(8,128)(2,1)S(1)} %get-tuple-element.161.refs_0_, ...), custom_call_target="tpu_custom_call" | custom-call | flops 1000 | bytes 1000 | tf_op jit(solution)/shard_map/feed/pallas_call | solution.py:117
  65.2 2.3 %collective-permute-done.14.refs_9_ = bf16[512,768]{1,0:T(8,128)(2,1)S(1)} collective-permute-done((bf16[512,768]{1,0:T(8,128)(2,1)S(1)}, bf16[512,768]{1,0:T(8,128)(2,1)S(1)}, u32[]{:S(2)}, u32[]{:S(2)}) %collective-permute-start.14) | collective-permute-done | bytes 786464 | tf_op jit(solution)/shard_map/ppermute | solution.py:627
  67.4 4.0 %second_norm.1 = (bf16[2,256,768]{2,1,0:T(8,128)(2,1)}, f32[512,768]{1,0:T(8,128)S(1)}, bf16[512,768]{1,0:T(8,128)(2,1)S(1)}, f32[8,768]{1,0:T(8,128)S(1)}) custom-call(s32[2]{0:T(128)S(1)} %copy-done.2, s32[1]{0:T(128)} %constant.384.clone.1.which_ref, bf16[2,256,768]{2,1,0:T(8,128)(2,1)} %refs_0_.9, bf16[768]{0:T(1024)(128)(2,1)S(1)} %copy-done.3, ...), custom_call_target="tpu_custom_call" | custom-call | flops 1000 | bytes 1000 | tf_op jit(solution)/shard_map/second_norm/pallas_call | solution.py:117
  71.7 2.1 %collective-permute-done.15.refs_1_.refs_3_ = bf16[512,768]{1,0:T(8,128)(2,1)S(1)} collective-permute-done((bf16[512,768]{1,0:T(8,128)(2,1)S(1)}, bf16[512,768]{1,0:T(8,128)(2,1)S(1)}, u32[]{:S(2)}, u32[]{:S(2)}) %collective-permute-start.15) | collective-permute-done | bytes 786464 | tf_op jit(solution)/shard_map/ppermute | solution.py:627
  73.8 8.7 %feed_back.1 = (bf16[2,1024,768]{2,1,0:T(8,128)(2,1)S(1)}, f32[512,768]{1,0:T(8,128)S(1)}, bf16[512,768]{1,0:T(8,128)(2,1)S(1)}, f32[8,768]{1,0:T(8,128)S(1)}) custom-call(s32[2]{0:T(128)S(1)} %copy-done.2, s32[1]{0:T(128)} %constant.384.clone.1.which_ref, bf16[512,768]{1,0:T(8,128)(2,1)S(1)} %get-tuple-element.176.refs_0_.refs_2_, ...), custom_call_target="tpu_custom_call" | custom-call | flops 1000 | bytes 1000 | tf_op jit(solution)/shard_map/feed_back/pallas_call | solution.py:117
  82.7 5.5 %down_grads.1 = (bf16[4,96,768]{2,1,0:T(8,128)(2,1)}, bf16[4,96,768]{2,1,0:T(8,128)(2,1)}, bf16[2,4,96,768]{3,2,1,0:T(8,128)(2,1)}) custom-call(s32[2]{0:T(128)S(1)} %copy-done.2, s32[1]{0:T(128)} %constant.384.clone.1.which_ref, bf16[1024,768]{1,0:T(8,128)(2,1)S(1)} %get-tuple-element.181.refs_0_, bf16[1024,768]{1,0:T(8,128)(2,1)S(1)} %get-tuple-element.182.refs_1_, ...), custom_call_target="tpu_custom_call" | custom-call | flops 1000 | bytes 1000 | tf_op jit(solution)/shard_map/down_grads/pallas_call | solution.py:117
  88.3 6.9 %first_back.1 = (f32[512,768]{1,0:T(8,128)}, bf16[2,192,256]{2,1,0:T(8,128)(2,1)}, bf16[2,192,256]{2,1,0:T(8,128)(2,1)}, bf16[2,192,256]{2,1,0:T(8,128)(2,1)}, b...) custom-call(s32[2]{0:T(128)S(1)} %copy-done.2, ...), custom_call_target="tpu_custom_call" | custom-call | flops 1000 | bytes 1000 | tf_op jit(solution)/shard_map/first_back/pallas_call | solution.py:117
  95.8 1.5 collective-permute-start.18
  98.1 1.9 copy-done.1
  100.0 5.8 %up_grads.1 = (bf16[480,768]{1,0:T(8,128)(2,1)}, bf16[496,768]{1,0:T(8,128)(2,1)}, bf16[480,768]{1,0:T(8,128)(2,1)}, bf16[480,768]{1,0:T(8,128)(2,1)}, f32[8,768]{1,0:T(8,128)S(1)}) custom-call(s32[2]{0:T(128)S(1)} %copy-done.2, s32[1]{0:T(128)} %constant.384.clone.1.which_ref, bf16[256,768]{1,0:T(8,128)(2,1)S(1)} %get-tuple-element.161.refs_0_, ...), custom_call_target="tpu_custom_call" | custom-call | flops 1000 | bytes 1000 | tf_op jit(solution)/shard_map/up_grads/pallas_call | solution.py:117
  105.8 1.1 collective-permute-done.19.refs_9_
  106.9 1.6 collective-permute-start.21
  108.5 13.9 %attend_bwd.2 = (bf16[2,256,768]{2,1,0:T(8,128)(2,1)}, bf16[2,256,768]{2,1,0:T(8,128)(2,1)}, bf16[3,1024,192]{2,1,0:T(8,128)(2,1)}, f32[1,384]{1,0:T(1,128)}) custom-call(s32[2]{0:T(128)} %lengths_ref.25, s32[1]{0:T(128)} %constant.384.clone.1.which_ref, bf16[3,192,768]{2,1,0:T(8,128)(2,1)} %bitcast.109, bf16[2,1024,256]{2,1,0:T(8,128)(2,1)} %get-tuple-element.170.refs_1_, ...), custom_call_target="tpu_custom_call" | custom-call | flops 20000000000 | bytes 1000 | tf_op jit(solution)/shard_map/attend_bwd/pallas_call | solution.py:117
  122.5 3.4 %collective-permute-done.22 = bf16[2,4,96,768]{3,2,1,0:T(8,128)(2,1)S(1)} collective-permute-done((bf16[2,4,96,768]{3,2,1,0:T(8,128)(2,1)S(1)}, bf16[2,4,96,768]{3,2,1,0:T(8,128)(2,1)S(1)}, u32[]{:S(2)}, u32[]{:S(2)}) %collective-permute-start.22) | collective-permute-done | bytes 1179680 | tf_op jit(solution)/shard_map/ppermute | solution.py:627
  125.8 0.8 collective-permute-done.21
  126.9 0.9 copy-done.13
  127.9 0.8 pad_maximum_fusion.3
  128.7 1.6 collective-permute-start.24
  130.3 1.5 collective-permute-start.23
  132.4 13.7 %attend_bwd.3 = (bf16[2,256,768]{2,1,0:T(8,128)(2,1)}, bf16[2,256,768]{2,1,0:T(8,128)(2,1)}, bf16[3,1024,192]{2,1,0:T(8,128)(2,1)}, f32[1,384]{1,0:T(1,128)}) custom-call(s32[2]{0:T(128)} %lengths_ref.25, s32[1]{0:T(128)} %constant.385.clone.1.which_ref, bf16[3,192,768]{2,1,0:T(8,128)(2,1)} %bitcast.110, bf16[2,1024,256]{2,1,0:T(8,128)(2,1)} %get-tuple-element.170.refs_1_, ...), custom_call_target="tpu_custom_call" | custom-call | flops 20000000000 | bytes 1000 | tf_op jit(solution)/shard_map/attend_bwd/pallas_call | solution.py:117
  146.2 1.0 collective-permute-done.24
  147.3 0.7 add_add_fusion.1
  148.0 1.8 fusion.10
  149.9 1.1 fusion.13
  151.0 1.1 fusion.5
  152.1 1.6 collective-permute-start.28
  154.3 1.6 collective-permute-start.27
  155.9 8.0 %project_grads.1 = (bf16[576,384]{1,0:T(8,128)(2,1)}, bf16[584,384]{1,0:T(8,128)(2,1)}, f32[1,384]{1,0:T(1,128)}) custom-call(s32[2]{0:T(128)} %lengths_ref.25, s32[1]{0:T(128)} %constant.384.clone.1.which_ref, bf16[2,1024,768]{2,1,0:T(8,128)(2,1)} %refs_2_.11, bf16[3,1024,192]{2,1,0:T(8,128)(2,1)} %get-tuple-element.227.refs_1_, ...), custom_call_target="tpu_custom_call" | custom-call | flops 1000 | bytes 1000 | tf_op jit(solution)/shard_map/project_grads/pallas_call | solution.py:117
  164.0 0.7 collective-permute-done.29
  164.8 0.8 collective-permute-start.30
  165.5 1.3 collective-permute-start.31
  166.8 1.9 fusion.7
  168.7 1.2 fusion.15
  169.9 2.7 %collective-permute-start.34 = (bf16[96,768]{1,0:T(8,128)(2,1)S(1)}, bf16[96,768]{1,0:T(8,128)(2,1)S(1)}, u32[]{:S(2)}, u32[]{:S(2)}) collective-permute-start(bf16[96,768]{1,0:T(8,128)(2,1)S(1)} %fusion.15), channel_id=1, source_target_pairs={{0,16},{4,20},{8,24},{12,28},{16,0},{20,4},{24,8},{28,12},{1,17},{... | collective-permute-start | bytes 442376 | tf_op jit(solution)/shard_map/ppermute | solution.py:627
  172.6 1.2 fusion.12
  173.8 0.7 pad_maximum_fusion.7
  174.5 1.4 collective-permute-done.31
  176.6 1.8 collective-permute-done.34
  179.6 1.1 collective-permute-start.33
  180.7 3.4 %collective-permute-start.37 = (bf16[136,768]{1,0:T(8,128)(2,1)}, bf16[136,768]{1,0:T(8,128)(2,1)S(1)}, u32[]{:S(2)}, u32[]{:S(2)}) collective-permute-start(bf16[136,768]{1,0:T(8,128)(2,1)} %pad_maximum_fusion.7), channel_id=1, source_target_pairs={{0,16},{4,20},{8,24},{12,28},{16,0},{20,4},{24,8},{28,12},{1,17},{... | collective-permute-start | bytes 626696 | tf_op jit(solution)/shard_map/ppermute | solution.py:627
  184.1 5.6 %collective-permute-done.35 = bf16[290,384]{1,0:T(8,128)(2,1)S(1)} collective-permute-done((bf16[290,384]{1,0:T(8,128)(2,1)S(1)}, bf16[290,384]{1,0:T(8,128)(2,1)S(1)}, u32[]{:S(2)}, u32[]{:S(2)}) %collective-permute-start.35) | collective-permute-done | bytes 222752 | tf_op jit(solution)/shard_map/ppermute | solution.py:627
  189.7 1.0 fusion.16
  190.8 2.3 %collective-permute-done.37 = bf16[136,768]{1,0:T(8,128)(2,1)S(1)} collective-permute-done((bf16[136,768]{1,0:T(8,128)(2,1)}, bf16[136,768]{1,0:T(8,128)(2,1)S(1)}, u32[]{:S(2)}, u32[]{:S(2)}) %collective-permute-start.37) | collective-permute-done | bytes 208928 | tf_op jit(solution)/shard_map/ppermute | solution.py:627
  193.1 1.2 fusion.11
  194.3 0.7 slice.210
  196.3 1.9 fusion.14
  198.2 1.4 fusion.8
  199.6 0.9 pad_maximum_fusion
  200.6 1.5 collective-permute-done.36
  202.8 1.0 fusion.17
  203.8 0.7 pad_maximum_fusion.5
  (118 shorter events, 12.1 us)
Async XLA Ops:
  4.0 23.8 %collective-permute-start = (bf16[200,768]{1,0:T(8,128)(2,1)}, bf16[200,768]{1,0:T(8,128)(2,1)S(1)}, u32[]{:S(2)}, u32[]{:S(2)}) collective-permute-start(bf16[200,768]{1,0:T(8,128)(2,1)} %get-tuple-element.142.refs_11_.refs_4_.refs_16_), channel_id=1, source_target_pairs={{0,1},{1,0},{2,3},{3,2},{4,5},{5,4},{6,7},{7,6},{8,9},{9,8},{10,11... | collective-permute-start | bytes 921608 | tf_op jit(solution)/shard_map/ppermute | solution.py:627
  4.6 23.3 %collective-permute-start.1 = (bf16[200,768]{1,0:T(8,128)(2,1)}, bf16[200,768]{1,0:T(8,128)(2,1)S(1)}, u32[]{:S(2)}, u32[]{:S(2)}) collective-permute-start(bf16[200,768]{1,0:T(8,128)(2,1)} %get-tuple-element.142.refs_11_.refs_4_.refs_16_), channel_id=1, source_target_pairs={{0,2},{1,3},{2,0},{3,1},{4,6},{5,7},{6,4},{7,5},{8,10},{9,11},{10,... | collective-permute-start | bytes 921608 | tf_op jit(solution)/shard_map/ppermute | solution.py:627
  7.1 18.4 %collective-permute-start.2 = (bf16[192,768]{1,0:T(8,128)(2,1)}, bf16[192,768]{1,0:T(8,128)(2,1)S(1)}, u32[]{:S(2)}, u32[]{:S(2)}) collective-permute-start(bf16[192,768]{1,0:T(8,128)(2,1)} %get-tuple-element.143), channel_id=1, source_target_pairs={{0,2},{1,3},{2,0},{3,1},{4,6},{5,7},{6,4},{7,5},{8,10},{9,11},{10,... | collective-permute-start | bytes 884744 | tf_op jit(solution)/shard_map/ppermute | solution.py:627
  7.2 20.6 %collective-permute-start.3 = (bf16[192,768]{1,0:T(8,128)(2,1)}, bf16[192,768]{1,0:T(8,128)(2,1)S(1)}, u32[]{:S(2)}, u32[]{:S(2)}) collective-permute-start(bf16[192,768]{1,0:T(8,128)(2,1)} %get-tuple-element.144), channel_id=1, source_target_pairs={{0,2},{1,3},{2,0},{3,1},{4,6},{5,7},{6,4},{7,5},{8,10},{9,11},{10,... | collective-permute-start | bytes 884744 | tf_op jit(solution)/shard_map/ppermute | solution.py:627
  25.5 18.8 %copy-start.2 = (s32[2]{0:T(128)S(1)}, s32[2]{0:T(128)}, u32[]{:S(2)}) copy-start(s32[2]{0:T(128)} %lengths_ref.25) | copy-start | bytes 28
  25.5 18.8 %copy-start.3 = (bf16[768]{0:T(1024)(128)(2,1)S(1)}, bf16[768]{0:T(1024)(128)(2,1)}, u32[]{:S(2)}) copy-start(bf16[768]{0:T(1024)(128)(2,1)} %refs_0_.10) | copy-start | bytes 4612
  25.5 18.8 %copy-start.4 = (bf16[768]{0:T(1024)(128)(2,1)S(1)}, bf16[768]{0:T(1024)(128)(2,1)}, u32[]{:S(2)}) copy-start(bf16[768]{0:T(1024)(128)(2,1)} %refs_1_.7) | copy-start | bytes 4612
  25.5 18.8 %copy-start.5 = (bf16[768]{0:T(1024)(128)(2,1)S(1)}, bf16[768]{0:T(1024)(128)(2,1)}, u32[]{:S(2)}) copy-start(bf16[768]{0:T(1024)(128)(2,1)} %refs_2_.10) | copy-start | bytes 4612
  25.6 18.8 %copy-start.6 = (bf16[768]{0:T(1024)(128)(2,1)S(1)}, bf16[768]{0:T(1024)(128)(2,1)}, u32[]{:S(2)}) copy-start(bf16[768]{0:T(1024)(128)(2,1)} %refs_3_.7) | copy-start | bytes 4612
  25.6 18.8 %copy-start.7 = (bf16[768]{0:T(1024)(128)(2,1)S(1)}, bf16[768]{0:T(1024)(128)(2,1)}, u32[]{:S(2)}) copy-start(bf16[768]{0:T(1024)(128)(2,1)} %refs_4_.7) | copy-start | bytes 4612
  25.6 18.8 %copy-start.8 = (bf16[768]{0:T(1024)(128)(2,1)S(1)}, bf16[768]{0:T(1024)(128)(2,1)}, u32[]{:S(2)}) copy-start(bf16[768]{0:T(1024)(128)(2,1)} %refs_5_.9) | copy-start | bytes 4612
  27.9 14.7 %collective-permute-start.7 = (bf16[192,768]{1,0:T(8,128)(2,1)S(1)}, bf16[192,768]{1,0:T(8,128)(2,1)S(1)}, u32[]{:S(2)}, u32[]{:S(2)}) collective-permute-start(bf16[192,768]{1,0:T(8,128)(2,1)S(1)} %collective-permute-done.2), channel_id=1, source_target_pairs={{0,4},{4,0},{8,12},{12,8},{16,20},{20,16},{24,28},{28,24},{1,5},{5... | collective-permute-start | bytes 884744 | tf_op jit(solution)/shard_map/ppermute | solution.py:627
  29.6 12.9 %collective-permute-start.8 = (bf16[192,768]{1,0:T(8,128)(2,1)S(1)}, bf16[192,768]{1,0:T(8,128)(2,1)S(1)}, u32[]{:S(2)}, u32[]{:S(2)}) collective-permute-start(bf16[192,768]{1,0:T(8,128)(2,1)S(1)} %collective-permute-done.3), channel_id=1, source_target_pairs={{0,8},{4,12},{8,0},{12,4},{16,24},{20,28},{24,16},{28,20},{1,9},{5... | collective-permute-start | bytes 884744 | tf_op jit(solution)/shard_map/ppermute | solution.py:627
  31.2 1.9 collective-permute-start.4
  31.2 7.9 %collective-permute-start.5 = (bf16[2,192,256]{2,1,0:T(8,128)(2,1)}, bf16[2,192,256]{2,1,0:T(8,128)(2,1)S(1)}, u32[]{:S(2)}, u32[]{:S(2)}) collective-permute-start(bf16[2,192,256]{2,1,0:T(8,128)(2,1)} %get-tuple-element.147), channel_id=1, source_target_pairs={{0,2},{1,3},{2,0},{3,1},{4,6},{5,7},{6,4},{7,5},{8,10},{9,11},{10,... | collective-permute-start | bytes 589832 | tf_op jit(solution)/shard_map/ppermute | solution.py:627
  32.7 9.8 %collective-permute-start.6 = (bf16[2,192,256]{2,1,0:T(8,128)(2,1)}, bf16[2,192,256]{2,1,0:T(8,128)(2,1)S(1)}, u32[]{:S(2)}, u32[]{:S(2)}) collective-permute-start(bf16[2,192,256]{2,1,0:T(8,128)(2,1)} %get-tuple-element.148), channel_id=1, source_target_pairs={{0,3},{1,2},{2,1},{3,0},{4,7},{5,6},{6,5},{7,4},{8,11},{9,10},{10,... | collective-permute-start | bytes 589832 | tf_op jit(solution)/shard_map/ppermute | solution.py:627
  42.6 1.7 collective-permute-start.9
  42.9 15.5 %collective-permute-start.12 = (bf16[384,768]{1,0:T(8,128)(2,1)S(1)}, bf16[384,768]{1,0:T(8,128)(2,1)S(1)}, u32[]{:S(2)}, u32[]{:S(2)}) collective-permute-start(bf16[384,768]{1,0:T(8,128)(2,1)S(1)} %get-tuple-element.163.refs_5_.refs_6_), channel_id=1, source_target_pairs={{0,8},{4,12},{8,0},{12,4},{16,24},{20,28},{24,16},{28,20},{1,9},{5... | collective-permute-start | bytes 1769480 | tf_op jit(solution)/shard_map/ppermute | solution.py:627
  43.3 15.3 %collective-permute-start.13 = (bf16[384,768]{1,0:T(8,128)(2,1)S(1)}, bf16[384,768]{1,0:T(8,128)(2,1)S(1)}, u32[]{:S(2)}, u32[]{:S(2)}) collective-permute-start(bf16[384,768]{1,0:T(8,128)(2,1)S(1)} %get-tuple-element.164.refs_7_.refs_8_), channel_id=1, source_target_pairs={{0,4},{4,0},{8,12},{12,8},{16,20},{20,16},{24,28},{28,24},{1,5},{5... | collective-permute-start | bytes 1769480 | tf_op jit(solution)/shard_map/ppermute | solution.py:627
  48.5 1.8 collective-permute-start.10
  48.8 2.1 %collective-permute-start.11 = (bf16[256,768]{1,0:T(8,128)(2,1)S(1)}, bf16[256,768]{1,0:T(8,128)(2,1)S(1)}, u32[]{:S(2)}, u32[]{:S(2)}) collective-permute-start(bf16[256,768]{1,0:T(8,128)(2,1)S(1)} %get-tuple-element.162.refs_1_), channel_id=1, source_target_pairs={{0,1},{1,0},{2,3},{3,2},{4,5},{5,4},{6,7},{7,6},{8,9},{9,8},{10,11... | collective-permute-start | bytes 1179656 | tf_op jit(solution)/shard_map/ppermute | solution.py:627
  65.1 2.4 %collective-permute-start.14 = (bf16[512,768]{1,0:T(8,128)(2,1)S(1)}, bf16[512,768]{1,0:T(8,128)(2,1)S(1)}, u32[]{:S(2)}, u32[]{:S(2)}) collective-permute-start(bf16[512,768]{1,0:T(8,128)(2,1)S(1)} %get-tuple-element.168), channel_id=1, source_target_pairs={{0,1},{1,0},{2,3},{3,2},{4,5},{5,4},{6,7},{7,6},{8,9},{9,8},{10,11... | collective-permute-start | bytes 2359304 | tf_op jit(solution)/shard_map/ppermute | solution.py:627
  71.5 2.4 %collective-permute-start.15 = (bf16[512,768]{1,0:T(8,128)(2,1)S(1)}, bf16[512,768]{1,0:T(8,128)(2,1)S(1)}, u32[]{:S(2)}, u32[]{:S(2)}) collective-permute-start(bf16[512,768]{1,0:T(8,128)(2,1)S(1)} %get-tuple-element.176.refs_0_.refs_2_), channel_id=1, source_target_pairs={{0,1},{1,0},{2,3},{3,2},{4,5},{5,4},{6,7},{7,6},{8,9},{9,8},{10,11... | collective-permute-start | bytes 2359304 | tf_op jit(solution)/shard_map/ppermute | solution.py:627
  82.5 5.8 %copy-start = (bf16[2,1024,768]{2,1,0:T(8,128)(2,1)}, bf16[2,1024,768]{2,1,0:T(8,128)(2,1)S(1)}, u32[]{:S(2)}) copy-start(bf16[2,1024,768]{2,1,0:T(8,128)(2,1)S(1)} %get-tuple-element.191.refs_4_) | copy-start | bytes 9437188
  82.5 5.8 %collective-permute-start.16 = (bf16[512,768]{1,0:T(8,128)(2,1)S(1)}, bf16[512,768]{1,0:T(8,128)(2,1)S(1)}, u32[]{:S(2)}, u32[]{:S(2)}) collective-permute-start(bf16[512,768]{1,0:T(8,128)(2,1)S(1)} %get-tuple-element.180), channel_id=1, source_target_pairs={{0,1},{1,0},{2,3},{3,2},{4,5},{5,4},{6,7},{7,6},{8,9},{9,8},{10,11... | collective-permute-start | bytes 2359304 | tf_op jit(solution)/shard_map/ppermute | solution.py:627
  88.3 9.2 %copy-start.23 = (bf16[2,4,96,768]{3,2,1,0:T(8,128)(2,1)S(1)}, bf16[2,4,96,768]{3,2,1,0:T(8,128)(2,1)}, u32[]{:S(2)}) copy-start(bf16[2,4,96,768]{3,2,1,0:T(8,128)(2,1)} %get-tuple-element.210) | copy-start | bytes 3538948
  95.2 2.9 %collective-permute-start.20 = (bf16[2,200,768]{2,1,0:T(8,128)(2,1)}, bf16[2,200,768]{2,1,0:T(8,128)(2,1)S(1)}, u32[]{:S(2)}, u32[]{:S(2)}) collective-permute-start(bf16[2,200,768]{2,1,0:T(8,128)(2,1)} %get-tuple-element.193), channel_id=1, source_target_pairs={{0,1},{1,0},{2,3},{3,2},{4,5},{5,4},{6,7},{7,6},{8,9},{9,8},{10,11... | collective-permute-start | bytes 1843208 | tf_op jit(solution)/shard_map/ppermute | solution.py:627
  95.6 10.2 %collective-permute-start.17 = (bf16[2,192,256]{2,1,0:T(8,128)(2,1)}, bf16[2,192,256]{2,1,0:T(8,128)(2,1)}, u32[]{:S(2)}, u32[]{:S(2)}) collective-permute-start(bf16[2,192,256]{2,1,0:T(8,128)(2,1)} %get-tuple-element.188), channel_id=1, source_target_pairs={{0,1},{1,0},{2,3},{3,2},{4,5},{5,4},{6,7},{7,6},{8,9},{9,8},{10,11... | collective-permute-start | bytes 589832 | tf_op jit(solution)/shard_map/ppermute | solution.py:627
  95.8 10.0 %collective-permute-start.18 = (bf16[2,192,256]{2,1,0:T(8,128)(2,1)}, bf16[2,192,256]{2,1,0:T(8,128)(2,1)}, u32[]{:S(2)}, u32[]{:S(2)}) collective-permute-start(bf16[2,192,256]{2,1,0:T(8,128)(2,1)} %get-tuple-element.189), channel_id=1, source_target_pairs={{0,2},{1,3},{2,0},{3,1},{4,6},{5,7},{6,4},{7,5},{8,10},{9,11},{10,... | collective-permute-start | bytes 589832 | tf_op jit(solution)/shard_map/ppermute | solution.py:627
  97.3 9.6 %collective-permute-start.19 = (bf16[2,192,256]{2,1,0:T(8,128)(2,1)}, bf16[2,192,256]{2,1,0:T(8,128)(2,1)}, u32[]{:S(2)}, u32[]{:S(2)}) collective-permute-start(bf16[2,192,256]{2,1,0:T(8,128)(2,1)} %get-tuple-element.190), channel_id=1, source_target_pairs={{0,3},{1,2},{2,1},{3,0},{4,7},{5,6},{6,5},{7,4},{8,11},{9,10},{10,... | collective-permute-start | bytes 589832 | tf_op jit(solution)/shard_map/ppermute | solution.py:627
  97.5 28.3 %collective-permute-start.22 = (bf16[2,4,96,768]{3,2,1,0:T(8,128)(2,1)S(1)}, bf16[2,4,96,768]{3,2,1,0:T(8,128)(2,1)S(1)}, u32[]{:S(2)}, u32[]{:S(2)}) collective-permute-start(bf16[2,4,96,768]{3,2,1,0:T(8,128)(2,1)S(1)} %copy-done.23), channel_id=1, source_target_pairs={{0,4},{4,0},{8,12},{12,8},{16,20},{20,16},{24,28},{28,24},{1,5},{5... | collective-permute-start | bytes 3538952 | tf_op jit(solution)/shard_map/ppermute | solution.py:627
  98.1 1.9 copy-start.1
  106.9 19.7 %collective-permute-start.21 = (bf16[496,768]{1,0:T(8,128)(2,1)}, bf16[496,768]{1,0:T(8,128)(2,1)S(1)}, u32[]{:S(2)}, u32[]{:S(2)}) collective-permute-start(bf16[496,768]{1,0:T(8,128)(2,1)} %get-tuple-element.209), channel_id=1, source_target_pairs={{0,8},{4,12},{8,0},{12,4},{16,24},{20,28},{24,16},{28,20},{1,9},{5... | collective-permute-start | bytes 2285576 | tf_op jit(solution)/shard_map/ppermute | solution.py:627
  122.4 4.3 %copy-start.15 = (bf16[4,96,768]{2,1,0:T(8,128)(2,1)S(1)}, bf16[4,96,768]{2,1,0:T(8,128)(2,1)}, u32[]{:S(2)}) copy-start(bf16[4,96,768]{2,1,0:T(8,128)(2,1)} %get-tuple-element.207) | copy-start | bytes 1769476
  126.6 1.1 copy-start.13
  128.7 19.3 %copy-start.14 = (bf16[480,768]{1,0:T(8,128)(2,1)S(1)}, bf16[480,768]{1,0:T(8,128)(2,1)}, u32[]{:S(2)}) copy-start(bf16[480,768]{1,0:T(8,128)(2,1)} %get-tuple-element.232) | copy-start | bytes 2211844
  128.7 18.5 %collective-permute-start.24 = (bf16[480,768]{1,0:T(8,128)(2,1)}, bf16[480,768]{1,0:T(8,128)(2,1)}, u32[]{:S(2)}, u32[]{:S(2)}) collective-permute-start(bf16[480,768]{1,0:T(8,128)(2,1)} %get-tuple-element.223), channel_id=1, source_target_pairs={{0,8},{4,12},{8,0},{12,4},{16,24},{20,28},{24,16},{28,20},{1,9},{5... | collective-permute-start | bytes 2211848 | tf_op jit(solution)/shard_map/ppermute | solution.py:627
  130.3 15.9 %collective-permute-start.23 = (bf16[4,96,768]{2,1,0:T(8,128)(2,1)S(1)}, bf16[4,96,768]{2,1,0:T(8,128)(2,1)}, u32[]{:S(2)}, u32[]{:S(2)}) collective-permute-start(bf16[4,96,768]{2,1,0:T(8,128)(2,1)S(1)} %fusion), channel_id=1, source_target_pairs={{0,2},{1,3},{2,0},{3,1},{4,6},{5,7},{6,4},{7,5},{8,10},{9,11},{10,... | collective-permute-start | bytes 1769480 | tf_op jit(solution)/shard_map/ppermute | solution.py:627
  131.8 14.4 %collective-permute-start.25 = (bf16[256,768]{1,0:T(8,128)(2,1)}, bf16[256,768]{1,0:T(8,128)(2,1)}, u32[]{:S(2)}, u32[]{:S(2)}) collective-permute-start(bf16[256,768]{1,0:T(8,128)(2,1)} %pad_maximum_fusion.3), channel_id=1, source_target_pairs={{0,4},{4,0},{8,12},{12,8},{16,20},{20,16},{24,28},{28,24},{1,5},{5... | collective-permute-start | bytes 1179656 | tf_op jit(solution)/shard_map/ppermute | solution.py:627
  132.4 14.8 %collective-permute-start.26 = (bf16[2,256,768]{2,1,0:T(8,128)(2,1)}, bf16[2,256,768]{2,1,0:T(8,128)(2,1)S(1)}, u32[]{:S(2)}, u32[]{:S(2)}) collective-permute-start(bf16[2,256,768]{2,1,0:T(8,128)(2,1)} %get-tuple-element.225), channel_id=1, source_target_pairs={{0,1},{1,0},{2,3},{3,2},{4,5},{5,4},{6,7},{7,6},{8,9},{9,8},{10,11... | collective-permute-start | bytes 2359304 | tf_op jit(solution)/shard_map/ppermute | solution.py:627
  146.2 3.7 %copy-start.16 = (bf16[4,96,768]{2,1,0:T(8,128)(2,1)S(1)}, bf16[4,96,768]{2,1,0:T(8,128)(2,1)}, u32[]{:S(2)}) copy-start(bf16[4,96,768]{2,1,0:T(8,128)(2,1)} %get-tuple-element.229) | copy-start | bytes 1769476
  147.2 19.6 %collective-permute-start.32 = (bf16[2,256,768]{2,1,0:T(8,128)(2,1)}, bf16[2,256,768]{2,1,0:T(8,128)(2,1)}, u32[]{:S(2)}, u32[]{:S(2)}) collective-permute-start(bf16[2,256,768]{2,1,0:T(8,128)(2,1)} %get-tuple-element.246), channel_id=1, source_target_pairs={{0,1},{1,0},{2,3},{3,2},{4,5},{5,4},{6,7},{7,6},{8,9},{9,8},{10,11... | collective-permute-start | bytes 2359304 | tf_op jit(solution)/shard_map/ppermute | solution.py:627
  152.1 12.6 %collective-permute-start.28 = (bf16[256,768]{1,0:T(8,128)(2,1)S(1)}, bf16[256,768]{1,0:T(8,128)(2,1)S(1)}, u32[]{:S(2)}, u32[]{:S(2)}) collective-permute-start(bf16[256,768]{1,0:T(8,128)(2,1)S(1)} %pad_maximum_fusion.4), channel_id=1, source_target_pairs={{0,2},{1,3},{2,0},{3,1},{4,6},{5,7},{6,4},{7,5},{8,10},{9,11},{10,... | collective-permute-start | bytes 1179656 | tf_op jit(solution)/shard_map/ppermute | solution.py:627
  153.7 11.0 %collective-permute-start.29 = (bf16[2,120,768]{2,1,0:T(8,128)(2,1)}, bf16[2,120,768]{2,1,0:T(8,128)(2,1)}, u32[]{:S(2)}, u32[]{:S(2)}) collective-permute-start(bf16[2,120,768]{2,1,0:T(8,128)(2,1)} %fusion.10), channel_id=1, source_target_pairs={{0,4},{4,0},{8,12},{12,8},{16,20},{20,16},{24,28},{28,24},{1,5},{5... | collective-permute-start | bytes 1105928 | tf_op jit(solution)/shard_map/ppermute | solution.py:627
  154.3 9.7 %collective-permute-start.27 = (bf16[2,96,768]{2,1,0:T(8,128)(2,1)S(1)}, bf16[2,96,768]{2,1,0:T(8,128)(2,1)}, u32[]{:S(2)}, u32[]{:S(2)}) collective-permute-start(bf16[2,96,768]{2,1,0:T(8,128)(2,1)S(1)} %fusion.13), channel_id=1, source_target_pairs={{0,8},{4,12},{8,0},{12,4},{16,24},{20,28},{24,16},{28,20},{1,9},{5... | collective-permute-start | bytes 884744 | tf_op jit(solution)/shard_map/ppermute | solution.py:627
  155.9 8.0 %copy-start.10 = (bf16[2,256,768]{2,1,0:T(8,128)(2,1)S(1)}, bf16[2,256,768]{2,1,0:T(8,128)(2,1)}, u32[]{:S(2)}) copy-start(bf16[2,256,768]{2,1,0:T(8,128)(2,1)} %get-tuple-element.206) | copy-start | bytes 2359300
  155.9 10.9 %copy-start.11 = (bf16[2,256,768]{2,1,0:T(8,128)(2,1)S(1)}, bf16[2,256,768]{2,1,0:T(8,128)(2,1)}, u32[]{:S(2)}) copy-start(bf16[2,256,768]{2,1,0:T(8,128)(2,1)} %get-tuple-element.245) | copy-start | bytes 2359300
  164.8 11.8 %collective-permute-start.30 = (bf16[584,384]{1,0:T(8,128)(2,1)}, bf16[584,384]{1,0:T(8,128)(2,1)S(1)}, u32[]{:S(2)}, u32[]{:S(2)}) collective-permute-start(bf16[584,384]{1,0:T(8,128)(2,1)} %get-tuple-element.241), channel_id=1, source_target_pairs={{0,4},{4,0},{8,12},{12,8},{16,20},{20,16},{24,28},{28,24},{1,5},{5... | collective-permute-start | bytes 1345544 | tf_op jit(solution)/shard_map/ppermute | solution.py:627
  165.5 10.4 %collective-permute-start.31 = (bf16[256,768]{1,0:T(8,128)(2,1)S(1)}, bf16[256,768]{1,0:T(8,128)(2,1)S(1)}, u32[]{:S(2)}, u32[]{:S(2)}) collective-permute-start(bf16[256,768]{1,0:T(8,128)(2,1)S(1)} %fusion.6), channel_id=1, source_target_pairs={{0,2},{1,3},{2,0},{3,1},{4,6},{5,7},{6,4},{7,5},{8,10},{9,11},{10,... | collective-permute-start | bytes 1179656 | tf_op jit(solution)/shard_map/ppermute | solution.py:627
  168.7 9.8 %copy-start.22 = (f32[1,384]{1,0:T(1,128)S(1)}, f32[1,384]{1,0:T(1,128)}, u32[]{:S(2)}) copy-start(f32[1,384]{1,0:T(1,128)} %get-tuple-element.257) | copy-start | bytes 4612
  168.7 9.8 %copy-start.17 = (bf16[576,384]{1,0:T(8,128)(2,1)S(1)}, bf16[576,384]{1,0:T(8,128)(2,1)}, u32[]{:S(2)}) copy-start(bf16[576,384]{1,0:T(8,128)(2,1)} %get-tuple-element.251) | copy-start | bytes 1327108
  169.9 8.5 %collective-permute-start.34 = (bf16[96,768]{1,0:T(8,128)(2,1)S(1)}, bf16[96,768]{1,0:T(8,128)(2,1)S(1)}, u32[]{:S(2)}, u32[]{:S(2)}) collective-permute-start(bf16[96,768]{1,0:T(8,128)(2,1)S(1)} %fusion.15), channel_id=1, source_target_pairs={{0,16},{4,20},{8,24},{12,28},{16,0},{20,4},{24,8},{28,12},{1,17},{... | collective-permute-start | bytes 442376 | tf_op jit(solution)/shard_map/ppermute | solution.py:627
  175.9 2.7 %copy-start.18 = (bf16[256,768]{1,0:T(8,128)(2,1)}, bf16[256,768]{1,0:T(8,128)(2,1)S(1)}, u32[]{:S(2)}) copy-start(bf16[256,768]{1,0:T(8,128)(2,1)S(1)} %collective-permute-done.31) | copy-start | bytes 1179652
  178.4 0.7 copy-start.20
  179.1 10.6 %collective-permute-start.35 = (bf16[290,384]{1,0:T(8,128)(2,1)S(1)}, bf16[290,384]{1,0:T(8,128)(2,1)S(1)}, u32[]{:S(2)}, u32[]{:S(2)}) collective-permute-start(bf16[290,384]{1,0:T(8,128)(2,1)S(1)} %pad_maximum_fusion.6), channel_id=1, source_target_pairs={{0,8},{4,12},{8,0},{12,4},{16,24},{20,28},{24,16},{28,20},{1,9},{5... | collective-permute-start | bytes 668168 | tf_op jit(solution)/shard_map/ppermute | solution.py:627
  179.6 18.6 %collective-permute-start.33 = (bf16[256,768]{1,0:T(8,128)(2,1)}, bf16[256,768]{1,0:T(8,128)(2,1)S(1)}, u32[]{:S(2)}, u32[]{:S(2)}) collective-permute-start(bf16[256,768]{1,0:T(8,128)(2,1)} %fusion.7), channel_id=1, source_target_pairs={{0,2},{1,3},{2,0},{3,1},{4,6},{5,7},{6,4},{7,5},{8,10},{9,11},{10,... | collective-permute-start | bytes 1179656 | tf_op jit(solution)/shard_map/ppermute | solution.py:627
  180.7 12.4 %collective-permute-start.37 = (bf16[136,768]{1,0:T(8,128)(2,1)}, bf16[136,768]{1,0:T(8,128)(2,1)S(1)}, u32[]{:S(2)}, u32[]{:S(2)}) collective-permute-start(bf16[136,768]{1,0:T(8,128)(2,1)} %pad_maximum_fusion.7), channel_id=1, source_target_pairs={{0,16},{4,20},{8,24},{12,28},{16,0},{20,4},{24,8},{28,12},{1,17},{... | collective-permute-start | bytes 626696 | tf_op jit(solution)/shard_map/ppermute | solution.py:627
  189.7 6.6 %copy-start.21 = (bf16[96,768]{1,0:T(8,128)(2,1)S(1)}, bf16[96,768]{1,0:T(8,128)(2,1)}, u32[]{:S(2)}) copy-start(bf16[96,768]{1,0:T(8,128)(2,1)} %copy-done.20) | copy-start | bytes 442372
  190.7 7.4 %copy-start.9 = (f32[512,768]{1,0:T(8,128)S(1)}, f32[512,768]{1,0:T(8,128)}, u32[]{:S(2)}) copy-start(f32[512,768]{1,0:T(8,128)} %get-tuple-element.244) | copy-start | bytes 4718596
  190.8 7.4 %copy-start.12 = (bf16[2,256,768]{2,1,0:T(8,128)(2,1)S(1)}, bf16[2,256,768]{2,1,0:T(8,128)(2,1)}, u32[]{:S(2)}) copy-start(bf16[2,256,768]{2,1,0:T(8,128)(2,1)} %get-tuple-element.245) | copy-start | bytes 2359300
  190.8 7.4 %copy-start.19 = (bf16[256,768]{1,0:T(8,128)(2,1)S(1)}, bf16[256,768]{1,0:T(8,128)(2,1)}, u32[]{:S(2)}) copy-start(bf16[256,768]{1,0:T(8,128)(2,1)} %copy-done.18) | copy-start | bytes 1179652
  195.7 6.4 %collective-permute-start.36 = (bf16[146,384]{1,0:T(8,128)(2,1)S(1)}, bf16[146,384]{1,0:T(8,128)(2,1)S(1)}, u32[]{:S(2)}, u32[]{:S(2)}) collective-permute-start(bf16[146,384]{1,0:T(8,128)(2,1)S(1)} %pad_maximum_fusion.8), channel_id=1, source_target_pairs={{0,16},{4,20},{8,24},{12,28},{16,0},{20,4},{24,8},{28,12},{1,17},{... | collective-permute-start | bytes 336392 | tf_op jit(solution)/shard_map/ppermute | solution.py:627

commit v9 on v8

--- a/solution.py
+++ b/solution.py
@@ -904,8 +904,9 @@
         (summed([k[0], x[0], y]) + gfi[s * rows : (s + 1) * rows]).astype(bf16)
         for s, (k, x, y) in enumerate(((keep0, near0, far[0]), (keep1, near1, far[1])))
     ])
-    qkv_sum = summed(terms)
-    qkv_sum = jnp.concatenate([qkv_sum[:, :width], qkv_sum[:, width:]], axis=0).reshape(3, -1, width)
+    sides = [jnp.concatenate([x[:, :width], x[:, width:]], axis=0) for x in terms[:-1]]
+    last = jnp.concatenate([terms[-1][:, :width], terms[-1][:, width:]], axis=0)
+    qkv_sum = (summed(sides) + last.astype(f32)).reshape(3, -1, width)
     qkv_sum = jnp.transpose(qkv_sum, (1, 0, 2))
     db = db.reshape(2, width)
     return (

time: 205 us -> 200 us (0.976)
  other arithmetic: 19.4 us -> 11.7 us
  starting transfers between devices: 34.1 us -> 37 us
  waiting for transfers between devices: 39.4 us -> 36.6 us
    ppermute x38, starting transfers between devices: 34.1 us -> 37 us  [swap(): return lax.ppermute(x, axis, [(i, i ^ bit) for i in range(size)])]
    ppermute x38, waiting for transfers between devices: 39.4 us -> 36.6 us  [swap(): return lax.ppermute(x, axis, [(i, i ^ bit) for i in range(size)])]
    add x4 -> x3, other arithmetic: 4.22 us -> 2.12 us  [summed(): return sum((p.astype(f32) for p in parts))]
  transfers between devices with their start and end apart: 38 -> 38, of which waited for: 21 -> 16; matrix products, arithmetic and copies ran while one was open for 9% -> 7% of each run, Pallas kernels for 36% -> 38%
where the time goes in v9:
time: 200 us; the launch traced here: 199 us
  Pallas kernels  104 us (52%)
  starting transfers between devices  37 us (18%)
  waiting for transfers between devices  36.6 us (18%)
  other arithmetic  11.7 us (6%)
  local copies, waits for them, and re-layouts  8.03 us (4%)
    pallas_call x13, Pallas kernels, call(): pl.pallas_call(kernel, out_shape=[pltpu.HBM(o.shape, o.dtype) if i in far...  104 us
    ppermute x38, starting transfers between devices, swap(): return lax.ppermute(x, axis, [(i, i ^ bit) for i in range(size)])  37 us
    ppermute x38, waiting for transfers between devices, swap(): return lax.ppermute(x, axis, [(i, i ^ bit) for i in range(size)])  36.6 us
  transfers between devices with their start and end apart: 38, of which 16 were waited for; matrix products, arithmetic and copies ran while one was open for 7% of the time, Pallas kernels for 38%

profile of v9, /device:TPU:0, one launch (start us, length us, event | category | flops | bytes accessed | tf_op | source)
XLA Modules:
  0.0 199.0 jit_solution(13176603792432249946)
XLA Ops:
  0.6 3.4 %prepare.1 = (bf16[200,768]{1,0:T(8,128)(2,1)}, bf16[192,768]{1,0:T(8,128)(2,1)}, bf16[192,768]{1,0:T(8,128)(2,1)}) custom-call(s32[2]{0:T(128)} %lengths_ref.25, s32[1]{0:T(128)} %constant.384.clone.1.which_ref, bf16[192,768]{1,0:T(8,128)(2,1)} %refs_0_.7, bf16[768]{0:T(1024)(128)(2,1)} %refs_1_.4, bf16[768,768]{1,0:T(8,128)(2,1)} %refs_4_.6, ...), custom_call_target="tpu_custom_call" | custom-call | flops 1000 | bytes 1000 | tf_op jit(solution)/shard_map/prepare/pallas_call | solution.py:117
  4.6 2.6 %collective-permute-start.1 = (bf16[200,768]{1,0:T(8,128)(2,1)}, bf16[200,768]{1,0:T(8,128)(2,1)S(1)}, u32[]{:S(2)}, u32[]{:S(2)}) collective-permute-start(bf16[200,768]{1,0:T(8,128)(2,1)} %get-tuple-element.142.refs_11_.refs_4_.refs_16_), channel_id=1, source_target_pairs={{0,2},{1,3},{2,0},{3,1},{4,6},{5,7},{6,4},{7,5},{8,10},{9,11},{10,... | collective-permute-start | bytes 921608 | tf_op jit(solution)/shard_map/ppermute | solution.py:627
  7.2 1.9 collective-permute-start.3
  9.2 16.3 %attend_fwd.1 = (bf16[2,1024,256]{2,1,0:T(8,128)(2,1)}, bf16[2,1024,256]{2,1,0:T(8,128)(2,1)}, bf16[2,1024,192]{2,1,0:T(8,128)(2,1)}, f32[2,4,8,256]{3,2,1,0:T(8...) custom-call(s32[2]{0:T(128)} %lengths_ref.25, ...), custom_call_target="tpu_custom_call" | custom-call | flops 1000 | bytes 1000 | tf_op jit(solution)/shard_map/attend_fwd/pallas_call | solution.py:117
  25.6 2.3 %collective-permute-done.3 = bf16[192,768]{1,0:T(8,128)(2,1)S(1)} collective-permute-done((bf16[192,768]{1,0:T(8,128)(2,1)}, bf16[192,768]{1,0:T(8,128)(2,1)S(1)}, u32[]{:S(2)}, u32[]{:S(2)}) %collective-permute-start.3) | collective-permute-done | bytes 294944 | tf_op jit(solution)/shard_map/ppermute | solution.py:627
  27.9 1.7 collective-permute-start.7
  29.6 1.6 collective-permute-start.8
  31.2 1.5 collective-permute-start.5
  33.0 6.0 %collective-permute-done.5.refs_9_.refs_14_ = bf16[2,192,256]{2,1,0:T(8,128)(2,1)S(1)} collective-permute-done((bf16[2,192,256]{2,1,0:T(8,128)(2,1)}, bf16[2,192,256]{2,1,0:T(8,128)(2,1)S(1)}, u32[]{:S(2)}, u32[]{:S(2)}) %collective-permute-start.5) | collective-permute-done | bytes 196640 | tf_op jit(solution)/shard_map/ppermute | solution.py:627
  39.1 3.4 %collective-permute-done.6.refs_10_.refs_15_ = bf16[2,192,256]{2,1,0:T(8,128)(2,1)S(1)} collective-permute-done((bf16[2,192,256]{2,1,0:T(8,128)(2,1)}, bf16[2,192,256]{2,1,0:T(8,128)(2,1)S(1)}, u32[]{:S(2)}, u32[]{:S(2)}) %collective-permute-start.6) | collective-permute-done | bytes 196640 | tf_op jit(solution)/shard_map/ppermute | solution.py:627
  43.7 0.6 collective-permute-done.9.refs_14_.refs_19_
  44.3 4.2 %first_norm.1 = (f32[512,768]{1,0:T(8,128)S(1)}, f32[512,1]{1,0:T(8,128)S(1)}, bf16[256,768]{1,0:T(8,128)(2,1)S(1)}, bf16[256,768]{1,0:T(8,128)(2,1)S(1)}) custom-call(s32[2]{0:T(128)S(1)} %copy-done.2, s32[1]{0:T(128)} %constant.384.clone.1.which_ref, bf16[2,1024,768]{2,1,0:T(8,128)(2,1)} %refs_2_.11, bf16[768]{0:T(1024)(128)(2,1)S(1)} %copy-done.3, ...), custom_call_target="tpu_custom_call" | custom-call | flops 1000 | bytes 1000 | tf_op jit(solution)/shard_map/first_norm/pallas_call | solution.py:117
  49.1 1.2 collective-permute-done.10.refs_2_
  50.3 0.6 collective-permute-done.11.refs_3_
  50.9 7.2 %feed.2 = (bf16[1024,768]{1,0:T(8,128)(2,1)S(1)}, bf16[1024,768]{1,0:T(8,128)(2,1)S(1)}, f32[512,768]{1,0:T(8,128)S(1)}, f32[512,768]{1,0:T(8,128)S(1)}) custom-call(s32[2]{0:T(128)S(1)} %copy-done.2, s32[1]{0:T(128)} %constant.384.clone.1.which_ref, bf16[256,768]{1,0:T(8,128)(2,1)S(1)} %get-tuple-element.161.refs_0_, ...), custom_call_target="tpu_custom_call" | custom-call | flops 1000 | bytes 1000 | tf_op jit(solution)/shard_map/feed/pallas_call | solution.py:117
  58.6 6.5 %feed.3 = (bf16[1024,768]{1,0:T(8,128)(2,1)S(1)}, bf16[1024,768]{1,0:T(8,128)(2,1)S(1)}, f32[512,768]{1,0:T(8,128)S(1)}, bf16[512,768]{1,0:T(8,128)(2,1)S(1)}) custom-call(s32[2]{0:T(128)S(1)} %copy-done.2, s32[1]{0:T(128)} %constant.384.clone.1.which_ref, bf16[256,768]{1,0:T(8,128)(2,1)S(1)} %get-tuple-element.161.refs_0_, ...), custom_call_target="tpu_custom_call" | custom-call | flops 1000 | bytes 1000 | tf_op jit(solution)/shard_map/feed/pallas_call | solution.py:117
  65.2 2.3 %collective-permute-done.14.refs_9_ = bf16[512,768]{1,0:T(8,128)(2,1)S(1)} collective-permute-done((bf16[512,768]{1,0:T(8,128)(2,1)S(1)}, bf16[512,768]{1,0:T(8,128)(2,1)S(1)}, u32[]{:S(2)}, u32[]{:S(2)}) %collective-permute-start.14) | collective-permute-done | bytes 786464 | tf_op jit(solution)/shard_map/ppermute | solution.py:627
  67.5 4.0 %second_norm.1 = (bf16[2,256,768]{2,1,0:T(8,128)(2,1)}, f32[512,768]{1,0:T(8,128)S(1)}, bf16[512,768]{1,0:T(8,128)(2,1)S(1)}, f32[8,768]{1,0:T(8,128)S(1)}) custom-call(s32[2]{0:T(128)S(1)} %copy-done.2, s32[1]{0:T(128)} %constant.384.clone.1.which_ref, bf16[2,256,768]{2,1,0:T(8,128)(2,1)} %refs_0_.9, bf16[768]{0:T(1024)(128)(2,1)S(1)} %copy-done.3, ...), custom_call_target="tpu_custom_call" | custom-call | flops 1000 | bytes 1000 | tf_op jit(solution)/shard_map/second_norm/pallas_call | solution.py:117
  71.7 2.1 %collective-permute-done.15.refs_1_.refs_3_ = bf16[512,768]{1,0:T(8,128)(2,1)S(1)} collective-permute-done((bf16[512,768]{1,0:T(8,128)(2,1)S(1)}, bf16[512,768]{1,0:T(8,128)(2,1)S(1)}, u32[]{:S(2)}, u32[]{:S(2)}) %collective-permute-start.15) | collective-permute-done | bytes 786464 | tf_op jit(solution)/shard_map/ppermute | solution.py:627
  73.9 8.7 %feed_back.1 = (bf16[2,1024,768]{2,1,0:T(8,128)(2,1)S(1)}, f32[512,768]{1,0:T(8,128)S(1)}, bf16[512,768]{1,0:T(8,128)(2,1)S(1)}, f32[8,768]{1,0:T(8,128)S(1)}) custom-call(s32[2]{0:T(128)S(1)} %copy-done.2, s32[1]{0:T(128)} %constant.384.clone.1.which_ref, bf16[512,768]{1,0:T(8,128)(2,1)S(1)} %get-tuple-element.176.refs_0_.refs_2_, ...), custom_call_target="tpu_custom_call" | custom-call | flops 1000 | bytes 1000 | tf_op jit(solution)/shard_map/feed_back/pallas_call | solution.py:117
  82.8 5.5 %down_grads.1 = (bf16[4,96,768]{2,1,0:T(8,128)(2,1)}, bf16[4,96,768]{2,1,0:T(8,128)(2,1)}, bf16[2,4,96,768]{3,2,1,0:T(8,128)(2,1)}) custom-call(s32[2]{0:T(128)S(1)} %copy-done.2, s32[1]{0:T(128)} %constant.384.clone.1.which_ref, bf16[1024,768]{1,0:T(8,128)(2,1)S(1)} %get-tuple-element.181.refs_0_, bf16[1024,768]{1,0:T(8,128)(2,1)S(1)} %get-tuple-element.182.refs_1_, ...), custom_call_target="tpu_custom_call" | custom-call | flops 1000 | bytes 1000 | tf_op jit(solution)/shard_map/down_grads/pallas_call | solution.py:117
  88.3 7.0 %first_back.1 = (f32[512,768]{1,0:T(8,128)}, bf16[2,192,256]{2,1,0:T(8,128)(2,1)}, bf16[2,192,256]{2,1,0:T(8,128)(2,1)}, bf16[2,192,256]{2,1,0:T(8,128)(2,1)}, b...) custom-call(s32[2]{0:T(128)S(1)} %copy-done.2, ...), custom_call_target="tpu_custom_call" | custom-call | flops 1000 | bytes 1000 | tf_op jit(solution)/shard_map/first_back/pallas_call | solution.py:117
  95.9 1.5 collective-permute-start.18
  97.7 0.6 collective-permute-start.22
  98.3 1.9 copy-done.1
  100.2 5.9 %up_grads.1 = (bf16[480,768]{1,0:T(8,128)(2,1)}, bf16[496,768]{1,0:T(8,128)(2,1)}, bf16[480,768]{1,0:T(8,128)(2,1)}, bf16[480,768]{1,0:T(8,128)(2,1)}, f32[8,768]{1,0:T(8,128)S(1)}) custom-call(s32[2]{0:T(128)S(1)} %copy-done.2, s32[1]{0:T(128)} %constant.384.clone.1.which_ref, bf16[256,768]{1,0:T(8,128)(2,1)S(1)} %get-tuple-element.161.refs_0_, ...), custom_call_target="tpu_custom_call" | custom-call | flops 1000 | bytes 1000 | tf_op jit(solution)/shard_map/up_grads/pallas_call | solution.py:117
  106.1 1.0 collective-permute-done.19.refs_9_
  107.1 1.6 collective-permute-start.21
  108.7 14.0 %attend_bwd.2 = (bf16[2,256,768]{2,1,0:T(8,128)(2,1)}, bf16[2,256,768]{2,1,0:T(8,128)(2,1)}, bf16[3,1024,192]{2,1,0:T(8,128)(2,1)}, f32[1,384]{1,0:T(1,128)}) custom-call(s32[2]{0:T(128)} %lengths_ref.25, s32[1]{0:T(128)} %constant.384.clone.1.which_ref, bf16[3,192,768]{2,1,0:T(8,128)(2,1)} %bitcast.110, bf16[2,1024,256]{2,1,0:T(8,128)(2,1)} %get-tuple-element.170.refs_1_, ...), custom_call_target="tpu_custom_call" | custom-call | flops 20000000000 | bytes 1000 | tf_op jit(solution)/shard_map/attend_bwd/pallas_call | solution.py:117
  122.7 3.3 %collective-permute-done.22 = bf16[2,4,96,768]{3,2,1,0:T(8,128)(2,1)S(1)} collective-permute-done((bf16[2,4,96,768]{3,2,1,0:T(8,128)(2,1)S(1)}, bf16[2,4,96,768]{3,2,1,0:T(8,128)(2,1)S(1)}, u32[]{:S(2)}, u32[]{:S(2)}) %collective-permute-start.22) | collective-permute-done | bytes 1179680 | tf_op jit(solution)/shard_map/ppermute | solution.py:627
  126.0 0.8 collective-permute-done.21
  127.1 0.9 copy-done.12
  128.1 0.8 pad_maximum_fusion.3
  128.9 1.6 collective-permute-start.24
  130.5 1.5 collective-permute-start.23
  132.0 0.6 collective-permute-start.25
  132.6 13.7 %attend_bwd.3 = (bf16[2,256,768]{2,1,0:T(8,128)(2,1)}, bf16[2,256,768]{2,1,0:T(8,128)(2,1)}, bf16[3,1024,192]{2,1,0:T(8,128)(2,1)}, f32[1,384]{1,0:T(1,128)}) custom-call(s32[2]{0:T(128)} %lengths_ref.25, s32[1]{0:T(128)} %constant.385.clone.1.which_ref, bf16[3,192,768]{2,1,0:T(8,128)(2,1)} %bitcast.111, bf16[2,1024,256]{2,1,0:T(8,128)(2,1)} %get-tuple-element.170.refs_1_, ...), custom_call_target="tpu_custom_call" | custom-call | flops 20000000000 | bytes 1000 | tf_op jit(solution)/shard_map/attend_bwd/pallas_call | solution.py:117
  146.4 0.9 collective-permute-done.24
  147.3 0.9 copy-done.14
  148.2 0.8 add_add_fusion.1
  149.0 1.1 fusion.5
  150.1 0.9 fusion.10
  151.0 1.8 fusion.13
  152.9 1.6 collective-permute-start.28
  154.5 2.3 %collective-permute-start.29 = (bf16[2,120,768]{2,1,0:T(8,128)(2,1)}, bf16[2,120,768]{2,1,0:T(8,128)(2,1)S(1)}, u32[]{:S(2)}, u32[]{:S(2)}) collective-permute-start(bf16[2,120,768]{2,1,0:T(8,128)(2,1)} %fusion.10), channel_id=1, source_target_pairs={{0,4},{4,0},{8,12},{12,8},{16,20},{20,16},{24,28},{28,24},{1,5},{5... | collective-permute-start | bytes 1105928 | tf_op jit(solution)/shard_map/ppermute | solution.py:627
  156.7 8.0 %project_grads.1 = (bf16[576,384]{1,0:T(8,128)(2,1)}, bf16[584,384]{1,0:T(8,128)(2,1)}, f32[1,384]{1,0:T(1,128)}) custom-call(s32[2]{0:T(128)} %lengths_ref.25, s32[1]{0:T(128)} %constant.384.clone.1.which_ref, bf16[2,1024,768]{2,1,0:T(8,128)(2,1)} %refs_2_.11, bf16[3,1024,192]{2,1,0:T(8,128)(2,1)} %get-tuple-element.227.refs_1_, ...), custom_call_target="tpu_custom_call" | custom-call | flops 1000 | bytes 1000 | tf_op jit(solution)/shard_map/project_grads/pallas_call | solution.py:117
  164.7 1.0 dynamic-slice_bitcast_fusion.2
  166.0 1.4 collective-permute-start.30
  167.4 1.3 collective-permute-start.31
  168.9 1.1 fusion.15
  170.1 2.7 %collective-permute-start.34 = (bf16[96,768]{1,0:T(8,128)(2,1)S(1)}, bf16[96,768]{1,0:T(8,128)(2,1)S(1)}, u32[]{:S(2)}, u32[]{:S(2)}) collective-permute-start(bf16[96,768]{1,0:T(8,128)(2,1)S(1)} %fusion.15), channel_id=1, source_target_pairs={{0,16},{4,20},{8,24},{12,28},{16,0},{20,4},{24,8},{28,12},{1,17},{... | collective-permute-start | bytes 442376 | tf_op jit(solution)/shard_map/ppermute | solution.py:627
  172.7 0.7 collective-permute-start.33
  173.6 5.9 %collective-permute-done.31 = bf16[256,768]{1,0:T(8,128)(2,1)S(1)} collective-permute-done((bf16[256,768]{1,0:T(8,128)(2,1)S(1)}, bf16[256,768]{1,0:T(8,128)(2,1)S(1)}, u32[]{:S(2)}, u32[]{:S(2)}) %collective-permute-start.31) | collective-permute-done | bytes 393248 | tf_op jit(solution)/shard_map/ppermute | solution.py:627
  179.7 0.9 collective-permute-start.35
  180.6 3.1 %collective-permute-start.37 = (bf16[136,768]{1,0:T(8,128)(2,1)S(1)}, bf16[136,768]{1,0:T(8,128)(2,1)S(1)}, u32[]{:S(2)}, u32[]{:S(2)}) collective-permute-start(bf16[136,768]{1,0:T(8,128)(2,1)S(1)} %pad_maximum_fusion.6), channel_id=1, source_target_pairs={{0,16},{4,20},{8,24},{12,28},{16,0},{20,4},{24,8},{28,12},{1,17},{... | collective-permute-start | bytes 626696 | tf_op jit(solution)/shard_map/ppermute | solution.py:627
  183.8 5.6 %collective-permute-done.35 = bf16[290,384]{1,0:T(8,128)(2,1)S(1)} collective-permute-done((bf16[290,384]{1,0:T(8,128)(2,1)S(1)}, bf16[290,384]{1,0:T(8,128)(2,1)S(1)}, u32[]{:S(2)}, u32[]{:S(2)}) %collective-permute-start.35) | collective-permute-done | bytes 222752 | tf_op jit(solution)/shard_map/ppermute | solution.py:627
  189.7 0.7 slice.238
  190.4 0.6 slice.234
  191.0 2.4 %collective-permute-start.36 = (bf16[146,384]{1,0:T(8,128)(2,1)S(1)}, bf16[146,384]{1,0:T(8,128)(2,1)S(1)}, u32[]{:S(2)}, u32[]{:S(2)}) collective-permute-start(bf16[146,384]{1,0:T(8,128)(2,1)S(1)} %pad_maximum_fusion.7), channel_id=1, source_target_pairs={{0,16},{4,20},{8,24},{12,28},{16,0},{20,4},{24,8},{28,12},{1,17},{... | collective-permute-start | bytes 336392 | tf_op jit(solution)/shard_map/ppermute | solution.py:627
  193.6 0.7 slice_reduce_fusion
  194.2 1.8 fusion.14
  196.4 0.9 pad_maximum_fusion
  197.4 0.7 reshape.191
  198.2 0.8 convert_add_fusion.8
  (123 shorter events, 6.7 us)
Async XLA Ops:
  4.0 23.8 %collective-permute-start = (bf16[200,768]{1,0:T(8,128)(2,1)}, bf16[200,768]{1,0:T(8,128)(2,1)S(1)}, u32[]{:S(2)}, u32[]{:S(2)}) collective-permute-start(bf16[200,768]{1,0:T(8,128)(2,1)} %get-tuple-element.142.refs_11_.refs_4_.refs_16_), channel_id=1, source_target_pairs={{0,1},{1,0},{2,3},{3,2},{4,5},{5,4},{6,7},{7,6},{8,9},{9,8},{10,11... | collective-permute-start | bytes 921608 | tf_op jit(solution)/shard_map/ppermute | solution.py:627
  4.6 23.3 %collective-permute-start.1 = (bf16[200,768]{1,0:T(8,128)(2,1)}, bf16[200,768]{1,0:T(8,128)(2,1)S(1)}, u32[]{:S(2)}, u32[]{:S(2)}) collective-permute-start(bf16[200,768]{1,0:T(8,128)(2,1)} %get-tuple-element.142.refs_11_.refs_4_.refs_16_), channel_id=1, source_target_pairs={{0,2},{1,3},{2,0},{3,1},{4,6},{5,7},{6,4},{7,5},{8,10},{9,11},{10,... | collective-permute-start | bytes 921608 | tf_op jit(solution)/shard_map/ppermute | solution.py:627
  7.2 18.4 %collective-permute-start.2 = (bf16[192,768]{1,0:T(8,128)(2,1)}, bf16[192,768]{1,0:T(8,128)(2,1)S(1)}, u32[]{:S(2)}, u32[]{:S(2)}) collective-permute-start(bf16[192,768]{1,0:T(8,128)(2,1)} %get-tuple-element.143), channel_id=1, source_target_pairs={{0,2},{1,3},{2,0},{3,1},{4,6},{5,7},{6,4},{7,5},{8,10},{9,11},{10,... | collective-permute-start | bytes 884744 | tf_op jit(solution)/shard_map/ppermute | solution.py:627
  7.2 20.6 %collective-permute-start.3 = (bf16[192,768]{1,0:T(8,128)(2,1)}, bf16[192,768]{1,0:T(8,128)(2,1)S(1)}, u32[]{:S(2)}, u32[]{:S(2)}) collective-permute-start(bf16[192,768]{1,0:T(8,128)(2,1)} %get-tuple-element.144), channel_id=1, source_target_pairs={{0,2},{1,3},{2,0},{3,1},{4,6},{5,7},{6,4},{7,5},{8,10},{9,11},{10,... | collective-permute-start | bytes 884744 | tf_op jit(solution)/shard_map/ppermute | solution.py:627
  25.5 18.8 %copy-start.2 = (s32[2]{0:T(128)S(1)}, s32[2]{0:T(128)}, u32[]{:S(2)}) copy-start(s32[2]{0:T(128)} %lengths_ref.25) | copy-start | bytes 28
  25.5 18.8 %copy-start.3 = (bf16[768]{0:T(1024)(128)(2,1)S(1)}, bf16[768]{0:T(1024)(128)(2,1)}, u32[]{:S(2)}) copy-start(bf16[768]{0:T(1024)(128)(2,1)} %refs_0_.10) | copy-start | bytes 4612
  25.5 18.8 %copy-start.4 = (bf16[768]{0:T(1024)(128)(2,1)S(1)}, bf16[768]{0:T(1024)(128)(2,1)}, u32[]{:S(2)}) copy-start(bf16[768]{0:T(1024)(128)(2,1)} %refs_1_.7) | copy-start | bytes 4612
  25.5 18.8 %copy-start.5 = (bf16[768]{0:T(1024)(128)(2,1)S(1)}, bf16[768]{0:T(1024)(128)(2,1)}, u32[]{:S(2)}) copy-start(bf16[768]{0:T(1024)(128)(2,1)} %refs_2_.10) | copy-start | bytes 4612
  25.5 18.8 %copy-start.6 = (bf16[768]{0:T(1024)(128)(2,1)S(1)}, bf16[768]{0:T(1024)(128)(2,1)}, u32[]{:S(2)}) copy-start(bf16[768]{0:T(1024)(128)(2,1)} %refs_3_.7) | copy-start | bytes 4612
  25.6 18.8 %copy-start.7 = (bf16[768]{0:T(1024)(128)(2,1)S(1)}, bf16[768]{0:T(1024)(128)(2,1)}, u32[]{:S(2)}) copy-start(bf16[768]{0:T(1024)(128)(2,1)} %refs_4_.7) | copy-start | bytes 4612
  25.6 18.8 %copy-start.8 = (bf16[768]{0:T(1024)(128)(2,1)S(1)}, bf16[768]{0:T(1024)(128)(2,1)}, u32[]{:S(2)}) copy-start(bf16[768]{0:T(1024)(128)(2,1)} %refs_5_.9) | copy-start | bytes 4612
  27.9 14.7 %collective-permute-start.7 = (bf16[192,768]{1,0:T(8,128)(2,1)S(1)}, bf16[192,768]{1,0:T(8,128)(2,1)S(1)}, u32[]{:S(2)}, u32[]{:S(2)}) collective-permute-start(bf16[192,768]{1,0:T(8,128)(2,1)S(1)} %collective-permute-done.2), channel_id=1, source_target_pairs={{0,4},{4,0},{8,12},{12,8},{16,20},{20,16},{24,28},{28,24},{1,5},{5... | collective-permute-start | bytes 884744 | tf_op jit(solution)/shard_map/ppermute | solution.py:627
  29.6 12.9 %collective-permute-start.8 = (bf16[192,768]{1,0:T(8,128)(2,1)S(1)}, bf16[192,768]{1,0:T(8,128)(2,1)S(1)}, u32[]{:S(2)}, u32[]{:S(2)}) collective-permute-start(bf16[192,768]{1,0:T(8,128)(2,1)S(1)} %collective-permute-done.3), channel_id=1, source_target_pairs={{0,8},{4,12},{8,0},{12,4},{16,24},{20,28},{24,16},{28,20},{1,9},{5... | collective-permute-start | bytes 884744 | tf_op jit(solution)/shard_map/ppermute | solution.py:627
  31.2 1.9 collective-permute-start.4
  31.2 7.9 %collective-permute-start.5 = (bf16[2,192,256]{2,1,0:T(8,128)(2,1)}, bf16[2,192,256]{2,1,0:T(8,128)(2,1)S(1)}, u32[]{:S(2)}, u32[]{:S(2)}) collective-permute-start(bf16[2,192,256]{2,1,0:T(8,128)(2,1)} %get-tuple-element.147), channel_id=1, source_target_pairs={{0,2},{1,3},{2,0},{3,1},{4,6},{5,7},{6,4},{7,5},{8,10},{9,11},{10,... | collective-permute-start | bytes 589832 | tf_op jit(solution)/shard_map/ppermute | solution.py:627
  32.7 9.8 %collective-permute-start.6 = (bf16[2,192,256]{2,1,0:T(8,128)(2,1)}, bf16[2,192,256]{2,1,0:T(8,128)(2,1)S(1)}, u32[]{:S(2)}, u32[]{:S(2)}) collective-permute-start(bf16[2,192,256]{2,1,0:T(8,128)(2,1)} %get-tuple-element.148), channel_id=1, source_target_pairs={{0,3},{1,2},{2,1},{3,0},{4,7},{5,6},{6,5},{7,4},{8,11},{9,10},{10,... | collective-permute-start | bytes 589832 | tf_op jit(solution)/shard_map/ppermute | solution.py:627
  42.6 1.7 collective-permute-start.9
  42.9 15.5 %collective-permute-start.12 = (bf16[384,768]{1,0:T(8,128)(2,1)S(1)}, bf16[384,768]{1,0:T(8,128)(2,1)S(1)}, u32[]{:S(2)}, u32[]{:S(2)}) collective-permute-start(bf16[384,768]{1,0:T(8,128)(2,1)S(1)} %get-tuple-element.163.refs_5_.refs_6_), channel_id=1, source_target_pairs={{0,8},{4,12},{8,0},{12,4},{16,24},{20,28},{24,16},{28,20},{1,9},{5... | collective-permute-start | bytes 1769480 | tf_op jit(solution)/shard_map/ppermute | solution.py:627
  43.4 15.3 %collective-permute-start.13 = (bf16[384,768]{1,0:T(8,128)(2,1)S(1)}, bf16[384,768]{1,0:T(8,128)(2,1)S(1)}, u32[]{:S(2)}, u32[]{:S(2)}) collective-permute-start(bf16[384,768]{1,0:T(8,128)(2,1)S(1)} %get-tuple-element.164.refs_7_.refs_8_), channel_id=1, source_target_pairs={{0,4},{4,0},{8,12},{12,8},{16,20},{20,16},{24,28},{28,24},{1,5},{5... | collective-permute-start | bytes 1769480 | tf_op jit(solution)/shard_map/ppermute | solution.py:627
  48.5 1.8 collective-permute-start.10
  48.8 2.1 %collective-permute-start.11 = (bf16[256,768]{1,0:T(8,128)(2,1)S(1)}, bf16[256,768]{1,0:T(8,128)(2,1)S(1)}, u32[]{:S(2)}, u32[]{:S(2)}) collective-permute-start(bf16[256,768]{1,0:T(8,128)(2,1)S(1)} %get-tuple-element.162.refs_1_), channel_id=1, source_target_pairs={{0,1},{1,0},{2,3},{3,2},{4,5},{5,4},{6,7},{7,6},{8,9},{9,8},{10,11... | collective-permute-start | bytes 1179656 | tf_op jit(solution)/shard_map/ppermute | solution.py:627
  65.1 2.4 %collective-permute-start.14 = (bf16[512,768]{1,0:T(8,128)(2,1)S(1)}, bf16[512,768]{1,0:T(8,128)(2,1)S(1)}, u32[]{:S(2)}, u32[]{:S(2)}) collective-permute-start(bf16[512,768]{1,0:T(8,128)(2,1)S(1)} %get-tuple-element.168), channel_id=1, source_target_pairs={{0,1},{1,0},{2,3},{3,2},{4,5},{5,4},{6,7},{7,6},{8,9},{9,8},{10,11... | collective-permute-start | bytes 2359304 | tf_op jit(solution)/shard_map/ppermute | solution.py:627
  71.5 2.4 %collective-permute-start.15 = (bf16[512,768]{1,0:T(8,128)(2,1)S(1)}, bf16[512,768]{1,0:T(8,128)(2,1)S(1)}, u32[]{:S(2)}, u32[]{:S(2)}) collective-permute-start(bf16[512,768]{1,0:T(8,128)(2,1)S(1)} %get-tuple-element.176.refs_0_.refs_2_), channel_id=1, source_target_pairs={{0,1},{1,0},{2,3},{3,2},{4,5},{5,4},{6,7},{7,6},{8,9},{9,8},{10,11... | collective-permute-start | bytes 2359304 | tf_op jit(solution)/shard_map/ppermute | solution.py:627
  82.6 5.8 %copy-start = (bf16[2,1024,768]{2,1,0:T(8,128)(2,1)}, bf16[2,1024,768]{2,1,0:T(8,128)(2,1)S(1)}, u32[]{:S(2)}) copy-start(bf16[2,1024,768]{2,1,0:T(8,128)(2,1)S(1)} %get-tuple-element.191.refs_4_) | copy-start | bytes 9437188
  82.6 5.8 %collective-permute-start.16 = (bf16[512,768]{1,0:T(8,128)(2,1)S(1)}, bf16[512,768]{1,0:T(8,128)(2,1)S(1)}, u32[]{:S(2)}, u32[]{:S(2)}) collective-permute-start(bf16[512,768]{1,0:T(8,128)(2,1)S(1)} %get-tuple-element.180), channel_id=1, source_target_pairs={{0,1},{1,0},{2,3},{3,2},{4,5},{5,4},{6,7},{7,6},{8,9},{9,8},{10,11... | collective-permute-start | bytes 2359304 | tf_op jit(solution)/shard_map/ppermute | solution.py:627
  88.3 9.4 %copy-start.22 = (bf16[2,4,96,768]{3,2,1,0:T(8,128)(2,1)S(1)}, bf16[2,4,96,768]{3,2,1,0:T(8,128)(2,1)}, u32[]{:S(2)}) copy-start(bf16[2,4,96,768]{3,2,1,0:T(8,128)(2,1)} %get-tuple-element.210) | copy-start | bytes 3538948
  95.4 2.9 %collective-permute-start.20 = (bf16[2,200,768]{2,1,0:T(8,128)(2,1)}, bf16[2,200,768]{2,1,0:T(8,128)(2,1)S(1)}, u32[]{:S(2)}, u32[]{:S(2)}) collective-permute-start(bf16[2,200,768]{2,1,0:T(8,128)(2,1)} %get-tuple-element.193), channel_id=1, source_target_pairs={{0,1},{1,0},{2,3},{3,2},{4,5},{5,4},{6,7},{7,6},{8,9},{9,8},{10,11... | collective-permute-start | bytes 1843208 | tf_op jit(solution)/shard_map/ppermute | solution.py:627
  95.8 10.3 %collective-permute-start.17 = (bf16[2,192,256]{2,1,0:T(8,128)(2,1)}, bf16[2,192,256]{2,1,0:T(8,128)(2,1)}, u32[]{:S(2)}, u32[]{:S(2)}) collective-permute-start(bf16[2,192,256]{2,1,0:T(8,128)(2,1)} %get-tuple-element.188), channel_id=1, source_target_pairs={{0,1},{1,0},{2,3},{3,2},{4,5},{5,4},{6,7},{7,6},{8,9},{9,8},{10,11... | collective-permute-start | bytes 589832 | tf_op jit(solution)/shard_map/ppermute | solution.py:627
  95.9 10.2 %collective-permute-start.18 = (bf16[2,192,256]{2,1,0:T(8,128)(2,1)}, bf16[2,192,256]{2,1,0:T(8,128)(2,1)}, u32[]{:S(2)}, u32[]{:S(2)}) collective-permute-start(bf16[2,192,256]{2,1,0:T(8,128)(2,1)} %get-tuple-element.189), channel_id=1, source_target_pairs={{0,2},{1,3},{2,0},{3,1},{4,6},{5,7},{6,4},{7,5},{8,10},{9,11},{10,... | collective-permute-start | bytes 589832 | tf_op jit(solution)/shard_map/ppermute | solution.py:627
  97.5 9.6 %collective-permute-start.19 = (bf16[2,192,256]{2,1,0:T(8,128)(2,1)}, bf16[2,192,256]{2,1,0:T(8,128)(2,1)}, u32[]{:S(2)}, u32[]{:S(2)}) collective-permute-start(bf16[2,192,256]{2,1,0:T(8,128)(2,1)} %get-tuple-element.190), channel_id=1, source_target_pairs={{0,3},{1,2},{2,1},{3,0},{4,7},{5,6},{6,5},{7,4},{8,11},{9,10},{10,... | collective-permute-start | bytes 589832 | tf_op jit(solution)/shard_map/ppermute | solution.py:627
  97.7 28.3 %collective-permute-start.22 = (bf16[2,4,96,768]{3,2,1,0:T(8,128)(2,1)S(1)}, bf16[2,4,96,768]{3,2,1,0:T(8,128)(2,1)S(1)}, u32[]{:S(2)}, u32[]{:S(2)}) collective-permute-start(bf16[2,4,96,768]{3,2,1,0:T(8,128)(2,1)S(1)} %copy-done.22), channel_id=1, source_target_pairs={{0,4},{4,0},{8,12},{12,8},{16,20},{20,16},{24,28},{28,24},{1,5},{5... | collective-permute-start | bytes 3538952 | tf_op jit(solution)/shard_map/ppermute | solution.py:627
  98.3 1.9 copy-start.1
  107.1 19.7 %collective-permute-start.21 = (bf16[496,768]{1,0:T(8,128)(2,1)}, bf16[496,768]{1,0:T(8,128)(2,1)S(1)}, u32[]{:S(2)}, u32[]{:S(2)}) collective-permute-start(bf16[496,768]{1,0:T(8,128)(2,1)} %get-tuple-element.209), channel_id=1, source_target_pairs={{0,8},{4,12},{8,0},{12,4},{16,24},{20,28},{24,16},{28,20},{1,9},{5... | collective-permute-start | bytes 2285576 | tf_op jit(solution)/shard_map/ppermute | solution.py:627
  122.7 4.2 %copy-start.17 = (bf16[4,96,768]{2,1,0:T(8,128)(2,1)S(1)}, bf16[4,96,768]{2,1,0:T(8,128)(2,1)}, u32[]{:S(2)}) copy-start(bf16[4,96,768]{2,1,0:T(8,128)(2,1)} %get-tuple-element.207) | copy-start | bytes 1769476
  126.8 1.1 copy-start.12
  128.9 18.4 %collective-permute-start.24 = (bf16[480,768]{1,0:T(8,128)(2,1)}, bf16[480,768]{1,0:T(8,128)(2,1)S(1)}, u32[]{:S(2)}, u32[]{:S(2)}) collective-permute-start(bf16[480,768]{1,0:T(8,128)(2,1)} %get-tuple-element.223), channel_id=1, source_target_pairs={{0,8},{4,12},{8,0},{12,4},{16,24},{20,28},{24,16},{28,20},{1,9},{5... | collective-permute-start | bytes 2211848 | tf_op jit(solution)/shard_map/ppermute | solution.py:627
  130.5 15.9 %collective-permute-start.23 = (bf16[4,96,768]{2,1,0:T(8,128)(2,1)S(1)}, bf16[4,96,768]{2,1,0:T(8,128)(2,1)}, u32[]{:S(2)}, u32[]{:S(2)}) collective-permute-start(bf16[4,96,768]{2,1,0:T(8,128)(2,1)S(1)} %fusion), channel_id=1, source_target_pairs={{0,2},{1,3},{2,0},{3,1},{4,6},{5,7},{6,4},{7,5},{8,10},{9,11},{10,... | collective-permute-start | bytes 1769480 | tf_op jit(solution)/shard_map/ppermute | solution.py:627
  132.0 14.4 %collective-permute-start.25 = (bf16[256,768]{1,0:T(8,128)(2,1)}, bf16[256,768]{1,0:T(8,128)(2,1)}, u32[]{:S(2)}, u32[]{:S(2)}) collective-permute-start(bf16[256,768]{1,0:T(8,128)(2,1)} %pad_maximum_fusion.3), channel_id=1, source_target_pairs={{0,4},{4,0},{8,12},{12,8},{16,20},{20,16},{24,28},{28,24},{1,5},{5... | collective-permute-start | bytes 1179656 | tf_op jit(solution)/shard_map/ppermute | solution.py:627
  132.6 14.7 %collective-permute-start.26 = (bf16[2,256,768]{2,1,0:T(8,128)(2,1)}, bf16[2,256,768]{2,1,0:T(8,128)(2,1)S(1)}, u32[]{:S(2)}, u32[]{:S(2)}) collective-permute-start(bf16[2,256,768]{2,1,0:T(8,128)(2,1)} %get-tuple-element.225), channel_id=1, source_target_pairs={{0,1},{1,0},{2,3},{3,2},{4,5},{5,4},{6,7},{7,6},{8,9},{9,8},{10,11... | collective-permute-start | bytes 2359304 | tf_op jit(solution)/shard_map/ppermute | solution.py:627
  146.4 3.8 %copy-start.13 = (bf16[480,768]{1,0:T(8,128)(2,1)S(1)}, bf16[480,768]{1,0:T(8,128)(2,1)}, u32[]{:S(2)}) copy-start(bf16[480,768]{1,0:T(8,128)(2,1)} %get-tuple-element.232) | copy-start | bytes 2211844
  146.4 4.6 %copy-start.18 = (bf16[4,96,768]{2,1,0:T(8,128)(2,1)S(1)}, bf16[4,96,768]{2,1,0:T(8,128)(2,1)}, u32[]{:S(2)}) copy-start(bf16[4,96,768]{2,1,0:T(8,128)(2,1)} %get-tuple-element.229) | copy-start | bytes 1769476
  147.3 0.9 copy-start.14
  148.2 1.9 copy-start.15
  148.2 20.6 %collective-permute-start.32 = (bf16[2,256,768]{2,1,0:T(8,128)(2,1)}, bf16[2,256,768]{2,1,0:T(8,128)(2,1)S(1)}, u32[]{:S(2)}, u32[]{:S(2)}) collective-permute-start(bf16[2,256,768]{2,1,0:T(8,128)(2,1)} %get-tuple-element.246), channel_id=1, source_target_pairs={{0,1},{1,0},{2,3},{3,2},{4,5},{5,4},{6,7},{7,6},{8,9},{9,8},{10,11... | collective-permute-start | bytes 2359304 | tf_op jit(solution)/shard_map/ppermute | solution.py:627
  152.9 13.1 %collective-permute-start.28 = (bf16[256,768]{1,0:T(8,128)(2,1)S(1)}, bf16[256,768]{1,0:T(8,128)(2,1)S(1)}, u32[]{:S(2)}, u32[]{:S(2)}) collective-permute-start(bf16[256,768]{1,0:T(8,128)(2,1)S(1)} %pad_maximum_fusion.4), channel_id=1, source_target_pairs={{0,2},{1,3},{2,0},{3,1},{4,6},{5,7},{6,4},{7,5},{8,10},{9,11},{10,... | collective-permute-start | bytes 1179656 | tf_op jit(solution)/shard_map/ppermute | solution.py:627
  154.5 11.5 %collective-permute-start.29 = (bf16[2,120,768]{2,1,0:T(8,128)(2,1)}, bf16[2,120,768]{2,1,0:T(8,128)(2,1)S(1)}, u32[]{:S(2)}, u32[]{:S(2)}) collective-permute-start(bf16[2,120,768]{2,1,0:T(8,128)(2,1)} %fusion.10), channel_id=1, source_target_pairs={{0,4},{4,0},{8,12},{12,8},{16,20},{20,16},{24,28},{28,24},{1,5},{5... | collective-permute-start | bytes 1105928 | tf_op jit(solution)/shard_map/ppermute | solution.py:627
  156.7 9.3 %collective-permute-start.27 = (bf16[2,96,768]{2,1,0:T(8,128)(2,1)}, bf16[2,96,768]{2,1,0:T(8,128)(2,1)}, u32[]{:S(2)}, u32[]{:S(2)}) collective-permute-start(bf16[2,96,768]{2,1,0:T(8,128)(2,1)} %fusion.13), channel_id=1, source_target_pairs={{0,8},{4,12},{8,0},{12,4},{16,24},{20,28},{24,16},{28,20},{1,9},{5... | collective-permute-start | bytes 884744 | tf_op jit(solution)/shard_map/ppermute | solution.py:627
  156.7 9.1 %copy-start.10 = (bf16[2,256,768]{2,1,0:T(8,128)(2,1)S(1)}, bf16[2,256,768]{2,1,0:T(8,128)(2,1)}, u32[]{:S(2)}) copy-start(bf16[2,256,768]{2,1,0:T(8,128)(2,1)} %get-tuple-element.206) | copy-start | bytes 2359300
  164.7 1.3 copy-start.23
  164.7 4.0 %copy-start.11 = (bf16[2,256,768]{2,1,0:T(8,128)(2,1)S(1)}, bf16[2,256,768]{2,1,0:T(8,128)(2,1)}, u32[]{:S(2)}) copy-start(bf16[2,256,768]{2,1,0:T(8,128)(2,1)} %get-tuple-element.245) | copy-start | bytes 2359300
  165.8 3.1 %copy-start.19 = (bf16[4,96,768]{2,1,0:T(8,128)(2,1)S(1)}, bf16[4,96,768]{2,1,0:T(8,128)(2,1)}, u32[]{:S(2)}) copy-start(bf16[4,96,768]{2,1,0:T(8,128)(2,1)} %get-tuple-element.229) | copy-start | bytes 1769476
  166.0 7.5 %copy-start.16 = (bf16[480,768]{1,0:T(8,128)(2,1)S(1)}, bf16[480,768]{1,0:T(8,128)(2,1)}, u32[]{:S(2)}) copy-start(bf16[480,768]{1,0:T(8,128)(2,1)} %copy-done.14) | copy-start | bytes 2211844
  166.0 13.4 %collective-permute-start.30 = (bf16[584,384]{1,0:T(8,128)(2,1)S(1)}, bf16[584,384]{1,0:T(8,128)(2,1)S(1)}, u32[]{:S(2)}, u32[]{:S(2)}) collective-permute-start(bf16[584,384]{1,0:T(8,128)(2,1)S(1)} %copy-done.23), channel_id=1, source_target_pairs={{0,4},{4,0},{8,12},{12,8},{16,20},{20,16},{24,28},{28,24},{1,5},{5... | collective-permute-start | bytes 1345544 | tf_op jit(solution)/shard_map/ppermute | solution.py:627
  167.4 12.1 %collective-permute-start.31 = (bf16[256,768]{1,0:T(8,128)(2,1)S(1)}, bf16[256,768]{1,0:T(8,128)(2,1)S(1)}, u32[]{:S(2)}, u32[]{:S(2)}) collective-permute-start(bf16[256,768]{1,0:T(8,128)(2,1)S(1)} %fusion.6), channel_id=1, source_target_pairs={{0,2},{1,3},{2,0},{3,1},{4,6},{5,7},{6,4},{7,5},{8,10},{9,11},{10,... | collective-permute-start | bytes 1179656 | tf_op jit(solution)/shard_map/ppermute | solution.py:627
  168.9 10.6 %copy-start.20 = (bf16[576,384]{1,0:T(8,128)(2,1)S(1)}, bf16[576,384]{1,0:T(8,128)(2,1)}, u32[]{:S(2)}) copy-start(bf16[576,384]{1,0:T(8,128)(2,1)} %get-tuple-element.251) | copy-start | bytes 1327108
  170.1 9.4 %collective-permute-start.34 = (bf16[96,768]{1,0:T(8,128)(2,1)S(1)}, bf16[96,768]{1,0:T(8,128)(2,1)S(1)}, u32[]{:S(2)}, u32[]{:S(2)}) collective-permute-start(bf16[96,768]{1,0:T(8,128)(2,1)S(1)} %fusion.15), channel_id=1, source_target_pairs={{0,16},{4,20},{8,24},{12,28},{16,0},{20,4},{24,8},{28,12},{1,17},{... | collective-permute-start | bytes 442376 | tf_op jit(solution)/shard_map/ppermute | solution.py:627
  172.7 23.3 %collective-permute-start.33 = (bf16[256,768]{1,0:T(8,128)(2,1)S(1)}, bf16[256,768]{1,0:T(8,128)(2,1)S(1)}, u32[]{:S(2)}, u32[]{:S(2)}) collective-permute-start(bf16[256,768]{1,0:T(8,128)(2,1)S(1)} %fusion.7), channel_id=1, source_target_pairs={{0,2},{1,3},{2,0},{3,1},{4,6},{5,7},{6,4},{7,5},{8,10},{9,11},{10,... | collective-permute-start | bytes 1179656 | tf_op jit(solution)/shard_map/ppermute | solution.py:627
  173.4 6.2 %copy-start.21 = (f32[1,384]{1,0:T(1,128)S(1)}, f32[1,384]{1,0:T(1,128)}, u32[]{:S(2)}) copy-start(f32[1,384]{1,0:T(1,128)} %get-tuple-element.257) | copy-start | bytes 4612
  179.7 9.6 %collective-permute-start.35 = (bf16[290,384]{1,0:T(8,128)(2,1)S(1)}, bf16[290,384]{1,0:T(8,128)(2,1)S(1)}, u32[]{:S(2)}, u32[]{:S(2)}) collective-permute-start(bf16[290,384]{1,0:T(8,128)(2,1)S(1)} %pad_maximum_fusion.5), channel_id=1, source_target_pairs={{0,8},{4,12},{8,0},{12,4},{16,24},{20,28},{24,16},{28,20},{1,9},{5... | collective-permute-start | bytes 668168 | tf_op jit(solution)/shard_map/ppermute | solution.py:627
  180.6 8.9 %collective-permute-start.37 = (bf16[136,768]{1,0:T(8,128)(2,1)S(1)}, bf16[136,768]{1,0:T(8,128)(2,1)S(1)}, u32[]{:S(2)}, u32[]{:S(2)}) collective-permute-start(bf16[136,768]{1,0:T(8,128)(2,1)S(1)} %pad_maximum_fusion.6), channel_id=1, source_target_pairs={{0,16},{4,20},{8,24},{12,28},{16,0},{20,4},{24,8},{28,12},{1,17},{... | collective-permute-start | bytes 626696 | tf_op jit(solution)/shard_map/ppermute | solution.py:627
  189.5 6.5 %copy-start.9 = (f32[512,768]{1,0:T(8,128)S(1)}, f32[512,768]{1,0:T(8,128)}, u32[]{:S(2)}) copy-start(f32[512,768]{1,0:T(8,128)} %get-tuple-element.244) | copy-start | bytes 4718596
  191.0 6.4 %collective-permute-start.36 = (bf16[146,384]{1,0:T(8,128)(2,1)S(1)}, bf16[146,384]{1,0:T(8,128)(2,1)S(1)}, u32[]{:S(2)}, u32[]{:S(2)}) collective-permute-start(bf16[146,384]{1,0:T(8,128)(2,1)S(1)} %pad_maximum_fusion.7), channel_id=1, source_target_pairs={{0,16},{4,20},{8,24},{12,28},{16,0},{20,4},{24,8},{28,12},{1,17},{... | collective-permute-start | bytes 336392 | tf_op jit(solution)/shard_map/ppermute | solution.py:627

commit v10 on v9

--- a/solution.py
+++ b/solution.py
@@ -898,7 +898,7 @@
         terms, db = kept, db + more
     down_terms, up_terms, small = with_received(down_terms, down_got, up_terms, up_got, sent, small)
     down_sum = summed(down_terms)
-    up_sum = summed(up_terms)
+    up_sum, out_sum = summed([x[:block] for x in up_terms]), summed([x[block:] for x in up_terms])
     mine = small
     input_grad = jnp.stack([
         (summed([k[0], x[0], y]) + gfi[s * rows : (s + 1) * rows]).astype(bf16)
@@ -914,11 +914,11 @@
         input_grad,
         qkv_sum,
         db,
-        up_sum[block:],
+        out_sum,
         mine[0],
         mine[1],
         mine[2],
-        up_sum[:block],
+        up_sum,
         mine[6],
         down_sum,
         mine[3],

time: 200 us -> 200 us (level)
  starting transfers between devices: 37 us -> 33.7 us
  Pallas kernels: 104 us -> 107 us
    ppermute x38, starting transfers between devices: 37 us -> 33.7 us  [swap(): return lax.ppermute(x, axis, [(i, i ^ bit) for i in range(size)])]
    pallas_call x13, Pallas kernels: 104 us -> 107 us  [call(): pl.pallas_call(kernel, out_shape=[pltpu.HBM(o.shape, o.dtype) if i in far...]
  transfers between devices with their start and end apart: 38 -> 38, of which waited for: 16 -> 16; matrix products, arithmetic and copies ran while one was open for 7% -> 7% of each run, Pallas kernels for 38% -> 39%
where the time goes in v10:
time: 200 us; the launch traced here: 199 us
  Pallas kernels  107 us (54%)
  waiting for transfers between devices  37.3 us (19%)
  starting transfers between devices  33.7 us (17%)
  other arithmetic  12.9 us (6%)
  local copies, waits for them, and re-layouts  6.64 us (3%)
    pallas_call x13, Pallas kernels, call(): pl.pallas_call(kernel, out_shape=[pltpu.HBM(o.shape, o.dtype) if i in far...  107 us
    ppermute x38, waiting for transfers between devices, swap(): return lax.ppermute(x, axis, [(i, i ^ bit) for i in range(size)])  37.3 us
    ppermute x38, starting transfers between devices, swap(): return lax.ppermute(x, axis, [(i, i ^ bit) for i in range(size)])  33.7 us
  transfers between devices with their start and end apart: 38, of which 16 were waited for; matrix products, arithmetic and copies ran while one was open for 7% of the time, Pallas kernels for 39%

profile of v10, /device:TPU:0, one launch (start us, length us, event | category | flops | bytes accessed | tf_op | source)
XLA Modules:
  0.0 198.6 jit_solution(11948802324768052719)
XLA Ops:
  0.6 3.4 %prepare.1 = (bf16[200,768]{1,0:T(8,128)(2,1)}, bf16[192,768]{1,0:T(8,128)(2,1)}, bf16[192,768]{1,0:T(8,128)(2,1)}) custom-call(s32[2]{0:T(128)} %lengths_ref.25, s32[1]{0:T(128)} %constant.384.clone.1.which_ref, bf16[192,768]{1,0:T(8,128)(2,1)} %refs_0_.7, bf16[768]{0:T(1024)(128)(2,1)} %refs_1_.4, bf16[768,768]{1,0:T(8,128)(2,1)} %refs_4_.6, ...), custom_call_target="tpu_custom_call" | custom-call | flops 1000 | bytes 1000 | tf_op jit(solution)/shard_map/prepare/pallas_call | solution.py:117
  4.6 2.6 %collective-permute-start.1 = (bf16[200,768]{1,0:T(8,128)(2,1)}, bf16[200,768]{1,0:T(8,128)(2,1)S(1)}, u32[]{:S(2)}, u32[]{:S(2)}) collective-permute-start(bf16[200,768]{1,0:T(8,128)(2,1)} %get-tuple-element.142.refs_11_.refs_4_.refs_16_), channel_id=1, source_target_pairs={{0,2},{1,3},{2,0},{3,1},{4,6},{5,7},{6,4},{7,5},{8,10},{9,11},{10,... | collective-permute-start | bytes 921608 | tf_op jit(solution)/shard_map/ppermute | solution.py:627
  7.2 1.9 collective-permute-start.3
  9.2 16.3 %attend_fwd.1 = (bf16[2,1024,256]{2,1,0:T(8,128)(2,1)}, bf16[2,1024,256]{2,1,0:T(8,128)(2,1)}, bf16[2,1024,192]{2,1,0:T(8,128)(2,1)}, f32[2,4,8,256]{3,2,1,0:T(8...) custom-call(s32[2]{0:T(128)} %lengths_ref.25, ...), custom_call_target="tpu_custom_call" | custom-call | flops 1000 | bytes 1000 | tf_op jit(solution)/shard_map/attend_fwd/pallas_call | solution.py:117
  25.6 2.3 %collective-permute-done.3 = bf16[192,768]{1,0:T(8,128)(2,1)S(1)} collective-permute-done((bf16[192,768]{1,0:T(8,128)(2,1)}, bf16[192,768]{1,0:T(8,128)(2,1)S(1)}, u32[]{:S(2)}, u32[]{:S(2)}) %collective-permute-start.3) | collective-permute-done | bytes 294944 | tf_op jit(solution)/shard_map/ppermute | solution.py:627
  27.9 1.7 collective-permute-start.7
  29.6 1.6 collective-permute-start.8
  31.2 1.5 collective-permute-start.5
  33.0 6.0 %collective-permute-done.5.refs_9_.refs_14_ = bf16[2,192,256]{2,1,0:T(8,128)(2,1)S(1)} collective-permute-done((bf16[2,192,256]{2,1,0:T(8,128)(2,1)}, bf16[2,192,256]{2,1,0:T(8,128)(2,1)S(1)}, u32[]{:S(2)}, u32[]{:S(2)}) %collective-permute-start.5) | collective-permute-done | bytes 196640 | tf_op jit(solution)/shard_map/ppermute | solution.py:627
  39.1 3.4 %collective-permute-done.6.refs_10_.refs_15_ = bf16[2,192,256]{2,1,0:T(8,128)(2,1)S(1)} collective-permute-done((bf16[2,192,256]{2,1,0:T(8,128)(2,1)}, bf16[2,192,256]{2,1,0:T(8,128)(2,1)S(1)}, u32[]{:S(2)}, u32[]{:S(2)}) %collective-permute-start.6) | collective-permute-done | bytes 196640 | tf_op jit(solution)/shard_map/ppermute | solution.py:627
  43.7 0.6 collective-permute-done.9.refs_14_.refs_19_
  44.3 4.2 %first_norm.1 = (f32[512,768]{1,0:T(8,128)S(1)}, f32[512,1]{1,0:T(8,128)S(1)}, bf16[256,768]{1,0:T(8,128)(2,1)S(1)}, bf16[256,768]{1,0:T(8,128)(2,1)S(1)}) custom-call(s32[2]{0:T(128)S(1)} %copy-done.2, s32[1]{0:T(128)} %constant.384.clone.1.which_ref, bf16[2,1024,768]{2,1,0:T(8,128)(2,1)} %refs_2_.11, bf16[768]{0:T(1024)(128)(2,1)S(1)} %copy-done.3, ...), custom_call_target="tpu_custom_call" | custom-call | flops 1000 | bytes 1000 | tf_op jit(solution)/shard_map/first_norm/pallas_call | solution.py:117
  49.1 1.2 collective-permute-done.10.refs_2_
  50.3 0.6 collective-permute-done.11.refs_3_
  50.9 7.2 %feed.2 = (bf16[1024,768]{1,0:T(8,128)(2,1)S(1)}, bf16[1024,768]{1,0:T(8,128)(2,1)S(1)}, f32[512,768]{1,0:T(8,128)S(1)}, f32[512,768]{1,0:T(8,128)S(1)}) custom-call(s32[2]{0:T(128)S(1)} %copy-done.2, s32[1]{0:T(128)} %constant.384.clone.1.which_ref, bf16[256,768]{1,0:T(8,128)(2,1)S(1)} %get-tuple-element.161.refs_0_, ...), custom_call_target="tpu_custom_call" | custom-call | flops 1000 | bytes 1000 | tf_op jit(solution)/shard_map/feed/pallas_call | solution.py:117
  58.6 6.5 %feed.3 = (bf16[1024,768]{1,0:T(8,128)(2,1)S(1)}, bf16[1024,768]{1,0:T(8,128)(2,1)S(1)}, f32[512,768]{1,0:T(8,128)S(1)}, bf16[512,768]{1,0:T(8,128)(2,1)S(1)}) custom-call(s32[2]{0:T(128)S(1)} %copy-done.2, s32[1]{0:T(128)} %constant.384.clone.1.which_ref, bf16[256,768]{1,0:T(8,128)(2,1)S(1)} %get-tuple-element.161.refs_0_, ...), custom_call_target="tpu_custom_call" | custom-call | flops 1000 | bytes 1000 | tf_op jit(solution)/shard_map/feed/pallas_call | solution.py:117
  65.2 2.3 %collective-permute-done.14.refs_9_ = bf16[512,768]{1,0:T(8,128)(2,1)S(1)} collective-permute-done((bf16[512,768]{1,0:T(8,128)(2,1)S(1)}, bf16[512,768]{1,0:T(8,128)(2,1)S(1)}, u32[]{:S(2)}, u32[]{:S(2)}) %collective-permute-start.14) | collective-permute-done | bytes 786464 | tf_op jit(solution)/shard_map/ppermute | solution.py:627
  67.5 4.0 %second_norm.1 = (bf16[2,256,768]{2,1,0:T(8,128)(2,1)}, f32[512,768]{1,0:T(8,128)S(1)}, bf16[512,768]{1,0:T(8,128)(2,1)S(1)}, f32[8,768]{1,0:T(8,128)S(1)}) custom-call(s32[2]{0:T(128)S(1)} %copy-done.2, s32[1]{0:T(128)} %constant.384.clone.1.which_ref, bf16[2,256,768]{2,1,0:T(8,128)(2,1)} %refs_0_.9, bf16[768]{0:T(1024)(128)(2,1)S(1)} %copy-done.3, ...), custom_call_target="tpu_custom_call" | custom-call | flops 1000 | bytes 1000 | tf_op jit(solution)/shard_map/second_norm/pallas_call | solution.py:117
  71.7 2.1 %collective-permute-done.15.refs_1_.refs_3_ = bf16[512,768]{1,0:T(8,128)(2,1)S(1)} collective-permute-done((bf16[512,768]{1,0:T(8,128)(2,1)S(1)}, bf16[512,768]{1,0:T(8,128)(2,1)S(1)}, u32[]{:S(2)}, u32[]{:S(2)}) %collective-permute-start.15) | collective-permute-done | bytes 786464 | tf_op jit(solution)/shard_map/ppermute | solution.py:627
  73.9 8.7 %feed_back.1 = (bf16[2,1024,768]{2,1,0:T(8,128)(2,1)S(1)}, f32[512,768]{1,0:T(8,128)S(1)}, bf16[512,768]{1,0:T(8,128)(2,1)S(1)}, f32[8,768]{1,0:T(8,128)S(1)}) custom-call(s32[2]{0:T(128)S(1)} %copy-done.2, s32[1]{0:T(128)} %constant.384.clone.1.which_ref, bf16[512,768]{1,0:T(8,128)(2,1)S(1)} %get-tuple-element.176.refs_0_.refs_2_, ...), custom_call_target="tpu_custom_call" | custom-call | flops 1000 | bytes 1000 | tf_op jit(solution)/shard_map/feed_back/pallas_call | solution.py:117
  82.8 5.5 %down_grads.1 = (bf16[4,96,768]{2,1,0:T(8,128)(2,1)}, bf16[4,96,768]{2,1,0:T(8,128)(2,1)}, bf16[2,4,96,768]{3,2,1,0:T(8,128)(2,1)}) custom-call(s32[2]{0:T(128)S(1)} %copy-done.2, s32[1]{0:T(128)} %constant.384.clone.1.which_ref, bf16[1024,768]{1,0:T(8,128)(2,1)S(1)} %get-tuple-element.181.refs_0_, bf16[1024,768]{1,0:T(8,128)(2,1)S(1)} %get-tuple-element.182.refs_1_, ...), custom_call_target="tpu_custom_call" | custom-call | flops 1000 | bytes 1000 | tf_op jit(solution)/shard_map/down_grads/pallas_call | solution.py:117
  88.3 7.0 %first_back.1 = (f32[512,768]{1,0:T(8,128)}, bf16[2,192,256]{2,1,0:T(8,128)(2,1)}, bf16[2,192,256]{2,1,0:T(8,128)(2,1)}, bf16[2,192,256]{2,1,0:T(8,128)(2,1)}, b...) custom-call(s32[2]{0:T(128)S(1)} %copy-done.2, ...), custom_call_target="tpu_custom_call" | custom-call | flops 1000 | bytes 1000 | tf_op jit(solution)/shard_map/first_back/pallas_call | solution.py:117
  95.9 1.5 collective-permute-start.18
  97.7 0.6 collective-permute-start.22
  98.3 1.9 copy-done.1
  100.2 5.9 %up_grads.1 = (bf16[480,768]{1,0:T(8,128)(2,1)}, bf16[496,768]{1,0:T(8,128)(2,1)}, bf16[480,768]{1,0:T(8,128)(2,1)}, bf16[480,768]{1,0:T(8,128)(2,1)}, f32[8,768]{1,0:T(8,128)S(1)}) custom-call(s32[2]{0:T(128)S(1)} %copy-done.2, s32[1]{0:T(128)} %constant.384.clone.1.which_ref, bf16[256,768]{1,0:T(8,128)(2,1)S(1)} %get-tuple-element.161.refs_0_, ...), custom_call_target="tpu_custom_call" | custom-call | flops 1000 | bytes 1000 | tf_op jit(solution)/shard_map/up_grads/pallas_call | solution.py:117
  106.1 1.0 collective-permute-done.19.refs_9_
  107.1 1.6 collective-permute-start.21
  108.7 14.0 %attend_bwd.2 = (bf16[2,256,768]{2,1,0:T(8,128)(2,1)}, bf16[2,256,768]{2,1,0:T(8,128)(2,1)}, bf16[3,1024,192]{2,1,0:T(8,128)(2,1)}, f32[1,384]{1,0:T(1,128)}) custom-call(s32[2]{0:T(128)} %lengths_ref.25, s32[1]{0:T(128)} %constant.384.clone.1.which_ref, bf16[3,192,768]{2,1,0:T(8,128)(2,1)} %bitcast.131, bf16[2,1024,256]{2,1,0:T(8,128)(2,1)} %get-tuple-element.170.refs_1_, ...), custom_call_target="tpu_custom_call" | custom-call | flops 20000000000 | bytes 1000 | tf_op jit(solution)/shard_map/attend_bwd/pallas_call | solution.py:117
  122.7 3.3 %collective-permute-done.22 = bf16[2,4,96,768]{3,2,1,0:T(8,128)(2,1)S(1)} collective-permute-done((bf16[2,4,96,768]{3,2,1,0:T(8,128)(2,1)S(1)}, bf16[2,4,96,768]{3,2,1,0:T(8,128)(2,1)S(1)}, u32[]{:S(2)}, u32[]{:S(2)}) %collective-permute-start.22) | collective-permute-done | bytes 1179680 | tf_op jit(solution)/shard_map/ppermute | solution.py:627
  126.0 0.8 collective-permute-done.21
  127.1 0.9 copy-done.16
  128.1 0.8 pad_maximum_fusion.3
  128.9 1.6 collective-permute-start.24
  130.5 1.5 collective-permute-start.23
  132.0 0.6 collective-permute-start.25
  132.6 16.0 %attend_bwd.3 = (bf16[2,256,768]{2,1,0:T(8,128)(2,1)}, bf16[2,256,768]{2,1,0:T(8,128)(2,1)}, bf16[3,1024,192]{2,1,0:T(8,128)(2,1)}, f32[1,384]{1,0:T(1,128)}) custom-call(s32[2]{0:T(128)} %lengths_ref.25, s32[1]{0:T(128)} %constant.385.clone.1.which_ref, bf16[3,192,768]{2,1,0:T(8,128)(2,1)} %bitcast.132, bf16[2,1024,256]{2,1,0:T(8,128)(2,1)} %get-tuple-element.170.refs_1_, ...), custom_call_target="tpu_custom_call" | custom-call | flops 20000000000 | bytes 1000 | tf_op jit(solution)/shard_map/attend_bwd/pallas_call | solution.py:117
  148.8 0.8 copy-done.13
  150.1 0.7 add_add_fusion.1
  150.9 1.1 fusion.5
  152.0 0.9 fusion.10
  152.9 1.8 fusion.12
  154.8 0.6 collective-permute-start.28
  155.3 1.4 collective-permute-start.29
  156.7 8.0 %project_grads.1 = (bf16[576,384]{1,0:T(8,128)(2,1)}, bf16[584,384]{1,0:T(8,128)(2,1)}, f32[1,384]{1,0:T(1,128)}) custom-call(s32[2]{0:T(128)} %lengths_ref.25, s32[1]{0:T(128)} %constant.384.clone.1.which_ref, bf16[2,1024,768]{2,1,0:T(8,128)(2,1)} %refs_2_.11, bf16[3,1024,192]{2,1,0:T(8,128)(2,1)} %get-tuple-element.227.refs_1_, ...), custom_call_target="tpu_custom_call" | custom-call | flops 1000 | bytes 1000 | tf_op jit(solution)/shard_map/project_grads/pallas_call | solution.py:117
  164.7 1.0 dynamic-slice_bitcast_fusion.4
  166.0 1.4 collective-permute-start.30
  167.4 1.3 collective-permute-start.31
  168.9 1.1 fusion.15
  170.1 2.7 %collective-permute-start.34 = (bf16[96,768]{1,0:T(8,128)(2,1)S(1)}, bf16[96,768]{1,0:T(8,128)(2,1)S(1)}, u32[]{:S(2)}, u32[]{:S(2)}) collective-permute-start(bf16[96,768]{1,0:T(8,128)(2,1)S(1)} %fusion.15), channel_id=1, source_target_pairs={{0,16},{4,20},{8,24},{12,28},{16,0},{20,4},{24,8},{28,12},{1,17},{... | collective-permute-start | bytes 442376 | tf_op jit(solution)/shard_map/ppermute | solution.py:627
  172.7 0.7 collective-permute-start.33
  173.6 5.9 %collective-permute-done.31 = bf16[256,768]{1,0:T(8,128)(2,1)S(1)} collective-permute-done((bf16[256,768]{1,0:T(8,128)(2,1)S(1)}, bf16[256,768]{1,0:T(8,128)(2,1)S(1)}, u32[]{:S(2)}, u32[]{:S(2)}) %collective-permute-start.31) | collective-permute-done | bytes 393248 | tf_op jit(solution)/shard_map/ppermute | solution.py:627
  179.7 1.4 collective-permute-start.35
  181.1 2.1 %collective-permute-start.37 = (bf16[136,768]{1,0:T(8,128)(2,1)S(1)}, bf16[136,768]{1,0:T(8,128)(2,1)S(1)}, u32[]{:S(2)}, u32[]{:S(2)}) collective-permute-start(bf16[136,768]{1,0:T(8,128)(2,1)S(1)} %pad_maximum_fusion.6), channel_id=1, source_target_pairs={{0,16},{4,20},{8,24},{12,28},{16,0},{20,4},{24,8},{28,12},{1,17},{... | collective-permute-start | bytes 626696 | tf_op jit(solution)/shard_map/ppermute | solution.py:627
  183.3 6.6 %collective-permute-done.35 = bf16[290,384]{1,0:T(8,128)(2,1)S(1)} collective-permute-done((bf16[290,384]{1,0:T(8,128)(2,1)S(1)}, bf16[290,384]{1,0:T(8,128)(2,1)S(1)}, u32[]{:S(2)}, u32[]{:S(2)}) %collective-permute-start.35) | collective-permute-done | bytes 222752 | tf_op jit(solution)/shard_map/ppermute | solution.py:627
  190.0 1.1 collective-permute-start.36
  191.1 0.8 fusion.14
  191.9 0.7 fusion.17
  192.7 0.7 slice_reduce_fusion
  193.3 1.8 fusion.13
  195.5 0.9 pad_maximum_fusion
  196.5 0.5 collective-permute-done.36
  197.0 0.7 reshape.206
  197.8 0.8 convert_add_fusion.8
  (122 shorter events, 7.1 us)
Async XLA Ops:
  4.0 23.8 %collective-permute-start = (bf16[200,768]{1,0:T(8,128)(2,1)}, bf16[200,768]{1,0:T(8,128)(2,1)S(1)}, u32[]{:S(2)}, u32[]{:S(2)}) collective-permute-start(bf16[200,768]{1,0:T(8,128)(2,1)} %get-tuple-element.142.refs_11_.refs_4_.refs_16_), channel_id=1, source_target_pairs={{0,1},{1,0},{2,3},{3,2},{4,5},{5,4},{6,7},{7,6},{8,9},{9,8},{10,11... | collective-permute-start | bytes 921608 | tf_op jit(solution)/shard_map/ppermute | solution.py:627
  4.6 23.3 %collective-permute-start.1 = (bf16[200,768]{1,0:T(8,128)(2,1)}, bf16[200,768]{1,0:T(8,128)(2,1)S(1)}, u32[]{:S(2)}, u32[]{:S(2)}) collective-permute-start(bf16[200,768]{1,0:T(8,128)(2,1)} %get-tuple-element.142.refs_11_.refs_4_.refs_16_), channel_id=1, source_target_pairs={{0,2},{1,3},{2,0},{3,1},{4,6},{5,7},{6,4},{7,5},{8,10},{9,11},{10,... | collective-permute-start | bytes 921608 | tf_op jit(solution)/shard_map/ppermute | solution.py:627
  7.2 18.4 %collective-permute-start.2 = (bf16[192,768]{1,0:T(8,128)(2,1)}, bf16[192,768]{1,0:T(8,128)(2,1)S(1)}, u32[]{:S(2)}, u32[]{:S(2)}) collective-permute-start(bf16[192,768]{1,0:T(8,128)(2,1)} %get-tuple-element.143), channel_id=1, source_target_pairs={{0,2},{1,3},{2,0},{3,1},{4,6},{5,7},{6,4},{7,5},{8,10},{9,11},{10,... | collective-permute-start | bytes 884744 | tf_op jit(solution)/shard_map/ppermute | solution.py:627
  7.2 20.6 %collective-permute-start.3 = (bf16[192,768]{1,0:T(8,128)(2,1)}, bf16[192,768]{1,0:T(8,128)(2,1)S(1)}, u32[]{:S(2)}, u32[]{:S(2)}) collective-permute-start(bf16[192,768]{1,0:T(8,128)(2,1)} %get-tuple-element.144), channel_id=1, source_target_pairs={{0,2},{1,3},{2,0},{3,1},{4,6},{5,7},{6,4},{7,5},{8,10},{9,11},{10,... | collective-permute-start | bytes 884744 | tf_op jit(solution)/shard_map/ppermute | solution.py:627
  25.5 18.8 %copy-start.2 = (s32[2]{0:T(128)S(1)}, s32[2]{0:T(128)}, u32[]{:S(2)}) copy-start(s32[2]{0:T(128)} %lengths_ref.25) | copy-start | bytes 28
  25.5 18.8 %copy-start.3 = (bf16[768]{0:T(1024)(128)(2,1)S(1)}, bf16[768]{0:T(1024)(128)(2,1)}, u32[]{:S(2)}) copy-start(bf16[768]{0:T(1024)(128)(2,1)} %refs_0_.10) | copy-start | bytes 4612
  25.5 18.8 %copy-start.4 = (bf16[768]{0:T(1024)(128)(2,1)S(1)}, bf16[768]{0:T(1024)(128)(2,1)}, u32[]{:S(2)}) copy-start(bf16[768]{0:T(1024)(128)(2,1)} %refs_1_.7) | copy-start | bytes 4612
  25.5 18.8 %copy-start.5 = (bf16[768]{0:T(1024)(128)(2,1)S(1)}, bf16[768]{0:T(1024)(128)(2,1)}, u32[]{:S(2)}) copy-start(bf16[768]{0:T(1024)(128)(2,1)} %refs_2_.10) | copy-start | bytes 4612
  25.5 18.8 %copy-start.6 = (bf16[768]{0:T(1024)(128)(2,1)S(1)}, bf16[768]{0:T(1024)(128)(2,1)}, u32[]{:S(2)}) copy-start(bf16[768]{0:T(1024)(128)(2,1)} %refs_3_.7) | copy-start | bytes 4612
  25.6 18.8 %copy-start.7 = (bf16[768]{0:T(1024)(128)(2,1)S(1)}, bf16[768]{0:T(1024)(128)(2,1)}, u32[]{:S(2)}) copy-start(bf16[768]{0:T(1024)(128)(2,1)} %refs_4_.7) | copy-start | bytes 4612
  25.6 18.8 %copy-start.8 = (bf16[768]{0:T(1024)(128)(2,1)S(1)}, bf16[768]{0:T(1024)(128)(2,1)}, u32[]{:S(2)}) copy-start(bf16[768]{0:T(1024)(128)(2,1)} %refs_5_.9) | copy-start | bytes 4612
  27.9 14.7 %collective-permute-start.7 = (bf16[192,768]{1,0:T(8,128)(2,1)S(1)}, bf16[192,768]{1,0:T(8,128)(2,1)S(1)}, u32[]{:S(2)}, u32[]{:S(2)}) collective-permute-start(bf16[192,768]{1,0:T(8,128)(2,1)S(1)} %collective-permute-done.2), channel_id=1, source_target_pairs={{0,4},{4,0},{8,12},{12,8},{16,20},{20,16},{24,28},{28,24},{1,5},{5... | collective-permute-start | bytes 884744 | tf_op jit(solution)/shard_map/ppermute | solution.py:627
  29.6 12.9 %collective-permute-start.8 = (bf16[192,768]{1,0:T(8,128)(2,1)S(1)}, bf16[192,768]{1,0:T(8,128)(2,1)S(1)}, u32[]{:S(2)}, u32[]{:S(2)}) collective-permute-start(bf16[192,768]{1,0:T(8,128)(2,1)S(1)} %collective-permute-done.3), channel_id=1, source_target_pairs={{0,8},{4,12},{8,0},{12,4},{16,24},{20,28},{24,16},{28,20},{1,9},{5... | collective-permute-start | bytes 884744 | tf_op jit(solution)/shard_map/ppermute | solution.py:627
  31.2 1.9 collective-permute-start.4
  31.2 7.9 %collective-permute-start.5 = (bf16[2,192,256]{2,1,0:T(8,128)(2,1)}, bf16[2,192,256]{2,1,0:T(8,128)(2,1)S(1)}, u32[]{:S(2)}, u32[]{:S(2)}) collective-permute-start(bf16[2,192,256]{2,1,0:T(8,128)(2,1)} %get-tuple-element.147), channel_id=1, source_target_pairs={{0,2},{1,3},{2,0},{3,1},{4,6},{5,7},{6,4},{7,5},{8,10},{9,11},{10,... | collective-permute-start | bytes 589832 | tf_op jit(solution)/shard_map/ppermute | solution.py:627
  32.7 9.8 %collective-permute-start.6 = (bf16[2,192,256]{2,1,0:T(8,128)(2,1)}, bf16[2,192,256]{2,1,0:T(8,128)(2,1)S(1)}, u32[]{:S(2)}, u32[]{:S(2)}) collective-permute-start(bf16[2,192,256]{2,1,0:T(8,128)(2,1)} %get-tuple-element.148), channel_id=1, source_target_pairs={{0,3},{1,2},{2,1},{3,0},{4,7},{5,6},{6,5},{7,4},{8,11},{9,10},{10,... | collective-permute-start | bytes 589832 | tf_op jit(solution)/shard_map/ppermute | solution.py:627
  42.6 1.7 collective-permute-start.9
  42.9 15.5 %collective-permute-start.12 = (bf16[384,768]{1,0:T(8,128)(2,1)S(1)}, bf16[384,768]{1,0:T(8,128)(2,1)S(1)}, u32[]{:S(2)}, u32[]{:S(2)}) collective-permute-start(bf16[384,768]{1,0:T(8,128)(2,1)S(1)} %get-tuple-element.163.refs_5_.refs_6_), channel_id=1, source_target_pairs={{0,8},{4,12},{8,0},{12,4},{16,24},{20,28},{24,16},{28,20},{1,9},{5... | collective-permute-start | bytes 1769480 | tf_op jit(solution)/shard_map/ppermute | solution.py:627
  43.4 15.3 %collective-permute-start.13 = (bf16[384,768]{1,0:T(8,128)(2,1)S(1)}, bf16[384,768]{1,0:T(8,128)(2,1)S(1)}, u32[]{:S(2)}, u32[]{:S(2)}) collective-permute-start(bf16[384,768]{1,0:T(8,128)(2,1)S(1)} %get-tuple-element.164.refs_7_.refs_8_), channel_id=1, source_target_pairs={{0,4},{4,0},{8,12},{12,8},{16,20},{20,16},{24,28},{28,24},{1,5},{5... | collective-permute-start | bytes 1769480 | tf_op jit(solution)/shard_map/ppermute | solution.py:627
  48.5 1.8 collective-permute-start.10
  48.8 2.1 %collective-permute-start.11 = (bf16[256,768]{1,0:T(8,128)(2,1)S(1)}, bf16[256,768]{1,0:T(8,128)(2,1)S(1)}, u32[]{:S(2)}, u32[]{:S(2)}) collective-permute-start(bf16[256,768]{1,0:T(8,128)(2,1)S(1)} %get-tuple-element.162.refs_1_), channel_id=1, source_target_pairs={{0,1},{1,0},{2,3},{3,2},{4,5},{5,4},{6,7},{7,6},{8,9},{9,8},{10,11... | collective-permute-start | bytes 1179656 | tf_op jit(solution)/shard_map/ppermute | solution.py:627
  65.1 2.4 %collective-permute-start.14 = (bf16[512,768]{1,0:T(8,128)(2,1)S(1)}, bf16[512,768]{1,0:T(8,128)(2,1)S(1)}, u32[]{:S(2)}, u32[]{:S(2)}) collective-permute-start(bf16[512,768]{1,0:T(8,128)(2,1)S(1)} %get-tuple-element.168), channel_id=1, source_target_pairs={{0,1},{1,0},{2,3},{3,2},{4,5},{5,4},{6,7},{7,6},{8,9},{9,8},{10,11... | collective-permute-start | bytes 2359304 | tf_op jit(solution)/shard_map/ppermute | solution.py:627
  71.5 2.4 %collective-permute-start.15 = (bf16[512,768]{1,0:T(8,128)(2,1)S(1)}, bf16[512,768]{1,0:T(8,128)(2,1)S(1)}, u32[]{:S(2)}, u32[]{:S(2)}) collective-permute-start(bf16[512,768]{1,0:T(8,128)(2,1)S(1)} %get-tuple-element.176.refs_0_.refs_2_), channel_id=1, source_target_pairs={{0,1},{1,0},{2,3},{3,2},{4,5},{5,4},{6,7},{7,6},{8,9},{9,8},{10,11... | collective-permute-start | bytes 2359304 | tf_op jit(solution)/shard_map/ppermute | solution.py:627
  82.6 5.8 %copy-start = (bf16[2,1024,768]{2,1,0:T(8,128)(2,1)}, bf16[2,1024,768]{2,1,0:T(8,128)(2,1)S(1)}, u32[]{:S(2)}) copy-start(bf16[2,1024,768]{2,1,0:T(8,128)(2,1)S(1)} %get-tuple-element.191.refs_4_) | copy-start | bytes 9437188
  82.6 5.8 %collective-permute-start.16 = (bf16[512,768]{1,0:T(8,128)(2,1)S(1)}, bf16[512,768]{1,0:T(8,128)(2,1)S(1)}, u32[]{:S(2)}, u32[]{:S(2)}) collective-permute-start(bf16[512,768]{1,0:T(8,128)(2,1)S(1)} %get-tuple-element.180), channel_id=1, source_target_pairs={{0,1},{1,0},{2,3},{3,2},{4,5},{5,4},{6,7},{7,6},{8,9},{9,8},{10,11... | collective-permute-start | bytes 2359304 | tf_op jit(solution)/shard_map/ppermute | solution.py:627
  88.3 9.4 %copy-start.22 = (bf16[2,4,96,768]{3,2,1,0:T(8,128)(2,1)S(1)}, bf16[2,4,96,768]{3,2,1,0:T(8,128)(2,1)}, u32[]{:S(2)}) copy-start(bf16[2,4,96,768]{3,2,1,0:T(8,128)(2,1)} %get-tuple-element.210) | copy-start | bytes 3538948
  95.4 2.9 %collective-permute-start.20 = (bf16[2,200,768]{2,1,0:T(8,128)(2,1)}, bf16[2,200,768]{2,1,0:T(8,128)(2,1)S(1)}, u32[]{:S(2)}, u32[]{:S(2)}) collective-permute-start(bf16[2,200,768]{2,1,0:T(8,128)(2,1)} %get-tuple-element.193), channel_id=1, source_target_pairs={{0,1},{1,0},{2,3},{3,2},{4,5},{5,4},{6,7},{7,6},{8,9},{9,8},{10,11... | collective-permute-start | bytes 1843208 | tf_op jit(solution)/shard_map/ppermute | solution.py:627
  95.8 10.3 %collective-permute-start.17 = (bf16[2,192,256]{2,1,0:T(8,128)(2,1)}, bf16[2,192,256]{2,1,0:T(8,128)(2,1)}, u32[]{:S(2)}, u32[]{:S(2)}) collective-permute-start(bf16[2,192,256]{2,1,0:T(8,128)(2,1)} %get-tuple-element.188), channel_id=1, source_target_pairs={{0,1},{1,0},{2,3},{3,2},{4,5},{5,4},{6,7},{7,6},{8,9},{9,8},{10,11... | collective-permute-start | bytes 589832 | tf_op jit(solution)/shard_map/ppermute | solution.py:627
  95.9 10.2 %collective-permute-start.18 = (bf16[2,192,256]{2,1,0:T(8,128)(2,1)}, bf16[2,192,256]{2,1,0:T(8,128)(2,1)}, u32[]{:S(2)}, u32[]{:S(2)}) collective-permute-start(bf16[2,192,256]{2,1,0:T(8,128)(2,1)} %get-tuple-element.189), channel_id=1, source_target_pairs={{0,2},{1,3},{2,0},{3,1},{4,6},{5,7},{6,4},{7,5},{8,10},{9,11},{10,... | collective-permute-start | bytes 589832 | tf_op jit(solution)/shard_map/ppermute | solution.py:627
  97.5 9.6 %collective-permute-start.19 = (bf16[2,192,256]{2,1,0:T(8,128)(2,1)}, bf16[2,192,256]{2,1,0:T(8,128)(2,1)}, u32[]{:S(2)}, u32[]{:S(2)}) collective-permute-start(bf16[2,192,256]{2,1,0:T(8,128)(2,1)} %get-tuple-element.190), channel_id=1, source_target_pairs={{0,3},{1,2},{2,1},{3,0},{4,7},{5,6},{6,5},{7,4},{8,11},{9,10},{10,... | collective-permute-start | bytes 589832 | tf_op jit(solution)/shard_map/ppermute | solution.py:627
  97.7 28.3 %collective-permute-start.22 = (bf16[2,4,96,768]{3,2,1,0:T(8,128)(2,1)S(1)}, bf16[2,4,96,768]{3,2,1,0:T(8,128)(2,1)S(1)}, u32[]{:S(2)}, u32[]{:S(2)}) collective-permute-start(bf16[2,4,96,768]{3,2,1,0:T(8,128)(2,1)S(1)} %copy-done.22), channel_id=1, source_target_pairs={{0,4},{4,0},{8,12},{12,8},{16,20},{20,16},{24,28},{28,24},{1,5},{5... | collective-permute-start | bytes 3538952 | tf_op jit(solution)/shard_map/ppermute | solution.py:627
  98.3 1.9 copy-start.1
  107.1 19.7 %collective-permute-start.21 = (bf16[496,768]{1,0:T(8,128)(2,1)}, bf16[496,768]{1,0:T(8,128)(2,1)S(1)}, u32[]{:S(2)}, u32[]{:S(2)}) collective-permute-start(bf16[496,768]{1,0:T(8,128)(2,1)} %get-tuple-element.209), channel_id=1, source_target_pairs={{0,8},{4,12},{8,0},{12,4},{16,24},{20,28},{24,16},{28,20},{1,9},{5... | collective-permute-start | bytes 2285576 | tf_op jit(solution)/shard_map/ppermute | solution.py:627
  122.7 4.2 %copy-start.17 = (bf16[4,96,768]{2,1,0:T(8,128)(2,1)S(1)}, bf16[4,96,768]{2,1,0:T(8,128)(2,1)}, u32[]{:S(2)}) copy-start(bf16[4,96,768]{2,1,0:T(8,128)(2,1)} %get-tuple-element.207) | copy-start | bytes 1769476
  126.8 1.1 copy-start.16
  128.9 19.8 %collective-permute-start.24 = (bf16[480,768]{1,0:T(8,128)(2,1)}, bf16[480,768]{1,0:T(8,128)(2,1)S(1)}, u32[]{:S(2)}, u32[]{:S(2)}) collective-permute-start(bf16[480,768]{1,0:T(8,128)(2,1)} %get-tuple-element.223), channel_id=1, source_target_pairs={{0,8},{4,12},{8,0},{12,4},{16,24},{20,28},{24,16},{28,20},{1,9},{5... | collective-permute-start | bytes 2211848 | tf_op jit(solution)/shard_map/ppermute | solution.py:627
  130.5 18.3 %collective-permute-start.23 = (bf16[4,96,768]{2,1,0:T(8,128)(2,1)S(1)}, bf16[4,96,768]{2,1,0:T(8,128)(2,1)}, u32[]{:S(2)}, u32[]{:S(2)}) collective-permute-start(bf16[4,96,768]{2,1,0:T(8,128)(2,1)S(1)} %fusion), channel_id=1, source_target_pairs={{0,2},{1,3},{2,0},{3,1},{4,6},{5,7},{6,4},{7,5},{8,10},{9,11},{10,... | collective-permute-start | bytes 1769480 | tf_op jit(solution)/shard_map/ppermute | solution.py:627
  132.0 16.7 %collective-permute-start.25 = (bf16[256,768]{1,0:T(8,128)(2,1)}, bf16[256,768]{1,0:T(8,128)(2,1)}, u32[]{:S(2)}, u32[]{:S(2)}) collective-permute-start(bf16[256,768]{1,0:T(8,128)(2,1)} %pad_maximum_fusion.3), channel_id=1, source_target_pairs={{0,4},{4,0},{8,12},{12,8},{16,20},{20,16},{24,28},{28,24},{1,5},{5... | collective-permute-start | bytes 1179656 | tf_op jit(solution)/shard_map/ppermute | solution.py:627
  132.6 16.1 %collective-permute-start.26 = (bf16[2,256,768]{2,1,0:T(8,128)(2,1)}, bf16[2,256,768]{2,1,0:T(8,128)(2,1)S(1)}, u32[]{:S(2)}, u32[]{:S(2)}) collective-permute-start(bf16[2,256,768]{2,1,0:T(8,128)(2,1)} %get-tuple-element.225), channel_id=1, source_target_pairs={{0,1},{1,0},{2,3},{3,2},{4,5},{5,4},{6,7},{7,6},{8,9},{9,8},{10,11... | collective-permute-start | bytes 2359304 | tf_op jit(solution)/shard_map/ppermute | solution.py:627
  148.7 3.3 %copy-start.12 = (bf16[480,768]{1,0:T(8,128)(2,1)S(1)}, bf16[480,768]{1,0:T(8,128)(2,1)}, u32[]{:S(2)}) copy-start(bf16[480,768]{1,0:T(8,128)(2,1)} %get-tuple-element.232) | copy-start | bytes 2211844
  148.7 4.2 %copy-start.18 = (bf16[4,96,768]{2,1,0:T(8,128)(2,1)S(1)}, bf16[4,96,768]{2,1,0:T(8,128)(2,1)}, u32[]{:S(2)}) copy-start(bf16[4,96,768]{2,1,0:T(8,128)(2,1)} %get-tuple-element.229) | copy-start | bytes 1769476
  148.8 0.9 copy-start.13
  149.6 2.4 %copy-start.14 = (bf16[480,768]{1,0:T(8,128)(2,1)S(1)}, bf16[480,768]{1,0:T(8,128)(2,1)}, u32[]{:S(2)}) copy-start(bf16[480,768]{1,0:T(8,128)(2,1)} %copy-done.13) | copy-start | bytes 2211844
  149.6 19.1 %collective-permute-start.32 = (bf16[2,256,768]{2,1,0:T(8,128)(2,1)}, bf16[2,256,768]{2,1,0:T(8,128)(2,1)S(1)}, u32[]{:S(2)}, u32[]{:S(2)}) collective-permute-start(bf16[2,256,768]{2,1,0:T(8,128)(2,1)} %get-tuple-element.246), channel_id=1, source_target_pairs={{0,1},{1,0},{2,3},{3,2},{4,5},{5,4},{6,7},{7,6},{8,9},{9,8},{10,11... | collective-permute-start | bytes 2359304 | tf_op jit(solution)/shard_map/ppermute | solution.py:627
  154.8 11.2 %collective-permute-start.28 = (bf16[256,768]{1,0:T(8,128)(2,1)S(1)}, bf16[256,768]{1,0:T(8,128)(2,1)S(1)}, u32[]{:S(2)}, u32[]{:S(2)}) collective-permute-start(bf16[256,768]{1,0:T(8,128)(2,1)S(1)} %pad_maximum_fusion.4), channel_id=1, source_target_pairs={{0,2},{1,3},{2,0},{3,1},{4,6},{5,7},{6,4},{7,5},{8,10},{9,11},{10,... | collective-permute-start | bytes 1179656 | tf_op jit(solution)/shard_map/ppermute | solution.py:627
  155.3 10.7 %collective-permute-start.29 = (bf16[2,120,768]{2,1,0:T(8,128)(2,1)}, bf16[2,120,768]{2,1,0:T(8,128)(2,1)S(1)}, u32[]{:S(2)}, u32[]{:S(2)}) collective-permute-start(bf16[2,120,768]{2,1,0:T(8,128)(2,1)} %fusion.10), channel_id=1, source_target_pairs={{0,4},{4,0},{8,12},{12,8},{16,20},{20,16},{24,28},{28,24},{1,5},{5... | collective-permute-start | bytes 1105928 | tf_op jit(solution)/shard_map/ppermute | solution.py:627
  156.7 9.3 %collective-permute-start.27 = (bf16[2,96,768]{2,1,0:T(8,128)(2,1)}, bf16[2,96,768]{2,1,0:T(8,128)(2,1)}, u32[]{:S(2)}, u32[]{:S(2)}) collective-permute-start(bf16[2,96,768]{2,1,0:T(8,128)(2,1)} %fusion.12), channel_id=1, source_target_pairs={{0,8},{4,12},{8,0},{12,4},{16,24},{20,28},{24,16},{28,20},{1,9},{5... | collective-permute-start | bytes 884744 | tf_op jit(solution)/shard_map/ppermute | solution.py:627
  156.7 9.1 %copy-start.10 = (bf16[2,256,768]{2,1,0:T(8,128)(2,1)S(1)}, bf16[2,256,768]{2,1,0:T(8,128)(2,1)}, u32[]{:S(2)}) copy-start(bf16[2,256,768]{2,1,0:T(8,128)(2,1)} %get-tuple-element.206) | copy-start | bytes 2359300
  164.7 1.3 copy-start.23
  164.7 4.0 %copy-start.11 = (bf16[2,256,768]{2,1,0:T(8,128)(2,1)S(1)}, bf16[2,256,768]{2,1,0:T(8,128)(2,1)}, u32[]{:S(2)}) copy-start(bf16[2,256,768]{2,1,0:T(8,128)(2,1)} %get-tuple-element.245) | copy-start | bytes 2359300
  165.8 3.1 %copy-start.19 = (bf16[4,96,768]{2,1,0:T(8,128)(2,1)S(1)}, bf16[4,96,768]{2,1,0:T(8,128)(2,1)}, u32[]{:S(2)}) copy-start(bf16[4,96,768]{2,1,0:T(8,128)(2,1)} %get-tuple-element.229) | copy-start | bytes 1769476
  166.0 7.5 %copy-start.15 = (bf16[480,768]{1,0:T(8,128)(2,1)S(1)}, bf16[480,768]{1,0:T(8,128)(2,1)}, u32[]{:S(2)}) copy-start(bf16[480,768]{1,0:T(8,128)(2,1)} %copy-done.13) | copy-start | bytes 2211844
  166.0 13.4 %collective-permute-start.30 = (bf16[584,384]{1,0:T(8,128)(2,1)S(1)}, bf16[584,384]{1,0:T(8,128)(2,1)S(1)}, u32[]{:S(2)}, u32[]{:S(2)}) collective-permute-start(bf16[584,384]{1,0:T(8,128)(2,1)S(1)} %copy-done.23), channel_id=1, source_target_pairs={{0,4},{4,0},{8,12},{12,8},{16,20},{20,16},{24,28},{28,24},{1,5},{5... | collective-permute-start | bytes 1345544 | tf_op jit(solution)/shard_map/ppermute | solution.py:627
  167.4 12.1 %collective-permute-start.31 = (bf16[256,768]{1,0:T(8,128)(2,1)S(1)}, bf16[256,768]{1,0:T(8,128)(2,1)S(1)}, u32[]{:S(2)}, u32[]{:S(2)}) collective-permute-start(bf16[256,768]{1,0:T(8,128)(2,1)S(1)} %fusion.6), channel_id=1, source_target_pairs={{0,2},{1,3},{2,0},{3,1},{4,6},{5,7},{6,4},{7,5},{8,10},{9,11},{10,... | collective-permute-start | bytes 1179656 | tf_op jit(solution)/shard_map/ppermute | solution.py:627
  168.9 10.6 %copy-start.20 = (bf16[576,384]{1,0:T(8,128)(2,1)S(1)}, bf16[576,384]{1,0:T(8,128)(2,1)}, u32[]{:S(2)}) copy-start(bf16[576,384]{1,0:T(8,128)(2,1)} %get-tuple-element.251) | copy-start | bytes 1327108
  170.1 9.4 %collective-permute-start.34 = (bf16[96,768]{1,0:T(8,128)(2,1)S(1)}, bf16[96,768]{1,0:T(8,128)(2,1)S(1)}, u32[]{:S(2)}, u32[]{:S(2)}) collective-permute-start(bf16[96,768]{1,0:T(8,128)(2,1)S(1)} %fusion.15), channel_id=1, source_target_pairs={{0,16},{4,20},{8,24},{12,28},{16,0},{20,4},{24,8},{28,12},{1,17},{... | collective-permute-start | bytes 442376 | tf_op jit(solution)/shard_map/ppermute | solution.py:627
  172.7 22.4 %collective-permute-start.33 = (bf16[256,768]{1,0:T(8,128)(2,1)S(1)}, bf16[256,768]{1,0:T(8,128)(2,1)S(1)}, u32[]{:S(2)}, u32[]{:S(2)}) collective-permute-start(bf16[256,768]{1,0:T(8,128)(2,1)S(1)} %fusion.7), channel_id=1, source_target_pairs={{0,2},{1,3},{2,0},{3,1},{4,6},{5,7},{6,4},{7,5},{8,10},{9,11},{10,... | collective-permute-start | bytes 1179656 | tf_op jit(solution)/shard_map/ppermute | solution.py:627
  173.4 6.2 %copy-start.21 = (f32[1,384]{1,0:T(1,128)S(1)}, f32[1,384]{1,0:T(1,128)}, u32[]{:S(2)}) copy-start(f32[1,384]{1,0:T(1,128)} %get-tuple-element.257) | copy-start | bytes 4612
  179.7 10.1 %collective-permute-start.35 = (bf16[290,384]{1,0:T(8,128)(2,1)S(1)}, bf16[290,384]{1,0:T(8,128)(2,1)S(1)}, u32[]{:S(2)}, u32[]{:S(2)}) collective-permute-start(bf16[290,384]{1,0:T(8,128)(2,1)S(1)} %pad_maximum_fusion.5), channel_id=1, source_target_pairs={{0,8},{4,12},{8,0},{12,4},{16,24},{20,28},{24,16},{28,20},{1,9},{5... | collective-permute-start | bytes 668168 | tf_op jit(solution)/shard_map/ppermute | solution.py:627
  181.1 10.0 %collective-permute-start.37 = (bf16[136,768]{1,0:T(8,128)(2,1)S(1)}, bf16[136,768]{1,0:T(8,128)(2,1)S(1)}, u32[]{:S(2)}, u32[]{:S(2)}) collective-permute-start(bf16[136,768]{1,0:T(8,128)(2,1)S(1)} %pad_maximum_fusion.6), channel_id=1, source_target_pairs={{0,16},{4,20},{8,24},{12,28},{16,0},{20,4},{24,8},{28,12},{1,17},{... | collective-permute-start | bytes 626696 | tf_op jit(solution)/shard_map/ppermute | solution.py:627
  189.9 5.2 %copy-start.9 = (f32[512,768]{1,0:T(8,128)S(1)}, f32[512,768]{1,0:T(8,128)}, u32[]{:S(2)}) copy-start(f32[512,768]{1,0:T(8,128)} %get-tuple-element.244) | copy-start | bytes 4718596
  190.0 7.0 %collective-permute-start.36 = (bf16[146,384]{1,0:T(8,128)(2,1)S(1)}, bf16[146,384]{1,0:T(8,128)(2,1)S(1)}, u32[]{:S(2)}, u32[]{:S(2)}) collective-permute-start(bf16[146,384]{1,0:T(8,128)(2,1)S(1)} %pad_maximum_fusion.7), channel_id=1, source_target_pairs={{0,16},{4,20},{8,24},{12,28},{16,0},{20,4},{24,8},{28,12},{1,17},{... | collective-permute-start | bytes 336392 | tf_op jit(solution)/shard_map/ppermute | solution.py:627
